TPU v7x, 32 devices: a whole 2x2x4 slice. The times are simulated.
32 devices in a mesh: feat: 4 (over z), tok: 8 (over y, x, core).
Axes of the slice: x: 2, y: 2, z: 4, core: 2. Of those that a mesh axis runs over, the one named last changes fastest.
Arguments:
- tokens: bfloat16 [512, 8192], P('tok'), may hold values from -6 to 6
- dec_bias: bfloat16 [8192], replicated, may hold values from -3 to 3
- enc_weight: bfloat16 [8192, 8192], P('tok', 'feat'), may hold values from -0.0625 to 0.0625
- enc_bias: bfloat16 [8192], P('feat'), may hold values from -3 to 3
- dec_weight: bfloat16 [8192, 8192], P('feat', 'tok'), may hold values from -0.25 to 0.25
- block_ids: int32 [8, 4, 4], P(None, 'feat'), may hold values from 0 to 31, as said below
- block_counts: int32 [8, 4], P(None, 'feat'), may hold values from 1 to 4, as said below
Outputs:
- code_values: bfloat16 [512, 1024], P('tok', 'feat')
- rebuilt: bfloat16 [512, 8192], P('tok', 'feat')
Inputs may be any that keep to these rules, and one draw needn't show every extreme that they name: `block_ids`: the 4 entries of one list are distinct; they number the owner's 32 blocks. `block_counts`: for every owner some tile has all 4 slots active.
All inputs are finite; a program needn't handle non-finite values.
Results may differ from a plain program's by a relative error of at most 0.029.
Values may be sent and summed in bfloat16 or wider, within the bound.
No kernel may reach another device: no remote copies, remote signals or barrier semaphores. Data moves between devices by JAX's collectives and lax.ppermute only.
A program may use at most 64 MiB of HBM per device.

v0:
```python
import jax
import jax.numpy as jnp
from jax import lax
from jax.sharding import PartitionSpec as P

BLOCK = 64
SLOTS = 4


def on_device(tokens, dec_bias, enc_weight, enc_bias, dec_weight, block_ids, block_counts):
    tile_count = lax.axis_size("tok")
    tok_rows = tokens.shape[0]
    width = tokens.shape[1]
    wslice = width // tile_count
    nblocks = enc_weight.shape[1] // BLOCK
    active_cols = SLOTS * BLOCK
    listed = block_ids[:, 0, :].reshape(-1)
    centered = (tokens.astype(jnp.float32) - dec_bias.astype(jnp.float32)).astype(jnp.bfloat16)
    chosen = jnp.take(enc_weight.reshape(wslice, nblocks, BLOCK), listed, axis=1)
    chosen = chosen.reshape(wslice, tile_count, active_cols)
    gathered = lax.all_to_all(centered, "tok", split_axis=1, concat_axis=0, tiled=True)
    gathered = gathered.reshape(tile_count, tok_rows, wslice)
    pre = lax.psum_scatter(
        jnp.einsum("tri,itc->trc", gathered, chosen, preferred_element_type=jnp.float32).astype(
            jnp.bfloat16
        ),
        "tok",
        scatter_dimension=0,
        tiled=True,
    ).astype(jnp.float32)[0]
    my_tile = lax.axis_index("tok")
    my_ids = lax.dynamic_slice_in_dim(block_ids[:, 0, :], my_tile, 1, 0)[0]
    my_count = lax.dynamic_slice_in_dim(block_counts[:, 0], my_tile, 1, 0)[0]
    bias_cols = jnp.take(enc_bias.reshape(nblocks, BLOCK), my_ids, axis=0).reshape(active_cols)
    live_mask = jnp.repeat(jnp.arange(SLOTS, dtype=jnp.int32) < my_count, BLOCK)
    code_values = jnp.where(
        live_mask[None, :], jnp.maximum(pre + bias_cols.astype(jnp.float32)[None, :], 0.0), 0.0
    )
    code_values = code_values.astype(jnp.bfloat16)
    outgoing = jnp.take(dec_weight.reshape(nblocks, BLOCK, wslice), listed, axis=0)
    outgoing = outgoing.reshape(tile_count, active_cols, wslice)
    owner_part = jnp.einsum(
        "rc,uci->rui",
        code_values,
        lax.all_to_all(outgoing, "tok", split_axis=0, concat_axis=0, tiled=True),
        preferred_element_type=jnp.float32,
    )
    owner_part = owner_part.reshape(tok_rows, width)
    summed = lax.psum_scatter(
        owner_part.astype(jnp.bfloat16), "feat", scatter_dimension=1, tiled=True
    ).astype(jnp.float32)
    share = summed.shape[1]
    bias_share = lax.dynamic_slice_in_dim(dec_bias, lax.axis_index("feat") * share, share, 0)
    rebuilt = (summed + bias_share.astype(jnp.float32)[None, :]).astype(jnp.bfloat16)
    return (code_values, rebuilt)


def solution(mesh):
    in_specs = (
        P("tok", None),
        P(),
        P("tok", "feat"),
        P("feat"),
        P("feat", "tok"),
        P(None, "feat", None),
        P(None, "feat"),
    )
    out_specs = (P("tok", "feat"), P("tok", "feat"))
    return jax.shard_map(
        on_device, mesh=mesh, in_specs=in_specs, out_specs=out_specs, check_vma=False
    )
```

profile of v0, /device:TPU:0, one launch (start us, length us, event | category | flops | bytes accessed | tf_op | source)
XLA Modules:
  0.0 131.7 jit_solution(5689210240074162982)
XLA Ops:
  7.2 0.7 convert_element_type.46
  7.9 1.4 %subtract_convert_fusion = bf16[64,8192]{1,0:T(8,128)(2,1)S(1)} fusion(bf16[64,8192]{1,0:T(8,128)(2,1)} %param.7, f32[8192]{0:T(1024)S(1)} %convert_element_type.46), kind=kLoop, calls=%fused_computation.9 | loop fusion | flops 1572864 | bytes 2129920 | tf_op jit(solution)/shard_map/convert_element_type | solution.py:18
  9.3 1.1 copy.25
  10.4 5.2 %all-to-all-start = ((bf16[64,8,1024]{2,0,1:T(8,128)(2,1)}), bf16[64,8,1024]{2,0,1:T(8,128)(2,1)S(1)}, u32[]{:S(2)}, u32[]{:S(2)}) async-start(bf16[64,8,1024]{2,0,1:T(8,128)(2,1)} %bitcast.42), calls=%async_computation | async-start | bytes 2097152 | tf_op jit(solution)/shard_map/all_to_all | solution.py:21
  15.6 0.1 copy.19
  15.7 0.1 reshape_squeeze.6
  15.8 0.1 copy.17
  15.9 0.1 broadcast_in_dim.57
  16.0 0.1 broadcast_in_dim.58
  16.1 5.0 %gather_fusion.2 = bf16[32,64,1024]{2,1,0:T(8,128)(2,1)} fusion(bf16[32,64,1024]{2,1,0:T(8,128)(2,1)} %bitcast.48, s32[1024]{0:T(1024)S(1)} %pad_clamp_fusion.1), kind=kCustom, calls=%fused_computation.2 | custom fusion | bytes 8388736 | tf_op jit(solution)/shard_map/jit(_take)/gather | solution.py:40
  21.1 3.8 %bitcast_select_fusion = bf16[8,256,1024]{2,1,0:T(8,128)(2,1)} fusion(pred[8,256]{1,0:T(8,128)(4,1)S(1)} %broadcast_in_dim.58, bf16[8,256,1024]{2,1,0:T(8,128)(2,1)} %bitcast.46), kind=kLoop, calls=%fused_computation.4 | loop fusion | flops 2097152 | bytes 8390656 | tf_op jit(solution)/shard_map/jit(_take)/select_n | solution.py:40
  24.9 6.1 %all-to-all-done = bf16[64,8,1024]{2,0,1:T(8,128)(2,1)S(1)} async-done(((bf16[64,8,1024]{2,0,1:T(8,128)(2,1)}), bf16[64,8,1024]{2,0,1:T(8,128)(2,1)S(1)}, u32[]{:S(2)}, u32[]{:S(2)}) %all-to-all-start) | async-done | bytes 1048608 | tf_op jit(solution)/shard_map/all_to_all | solution.py:21
  31.0 4.6 %all-to-all-start.1 = ((bf16[8,256,1024]{2,1,0:T(8,128)(2,1)}), bf16[8,256,1024]{2,1,0:T(8,128)(2,1)}, u32[]{:S(2)}, u32[]{:S(2)}) async-start(bf16[8,256,1024]{2,1,0:T(8,128)(2,1)} %bitcast_select_fusion), calls=%async_computation.2 | async-start | bytes 8388608 | tf_op jit(solution)/shard_map/all_to_all | solution.py:45
  35.7 0.2 dynamic-slice_reduce_fusion
  35.8 0.1 reshape.137
  35.9 6.4 %copy.18 = bf16[1024,2048]{0,1:T(8,128)(2,1)} copy(bf16[1024,2048]{1,0:T(8,128)(2,1)} %param.9) | data formatting | bytes 8388608 | tf_op args[2]
  42.3 4.9 %gather_fusion = bf16[32,1024,64]{1,2,0:T(8,128)(2,1)} fusion(bf16[1024,32,64]{0,2,1:T(8,128)(2,1)} %bitcast.44, s32[1024]{0:T(1024)S(1)} %pad_clamp_fusion.1), kind=kCustom, calls=%fused_computation | custom fusion | bytes 8388736 | tf_op jit(solution)/shard_map/jit(_take)/gather | solution.py:19
  47.3 4.4 %fusion.4 = bf16[8,64,256]{2,1,0:T(8,128)(2,1)} fusion(bf16[1024,8,256]{0,2,1:T(8,128)(2,1)} %bitcast.45, pred[8,256]{1,0:T(8,128)(4,1)S(1)} %broadcast_in_dim.58, bf16[64,8,1024]{2,0,1:T(8,128)(2,1)S(1)} %all-to-all-done), kind=kOutput, calls=%fused_computation.10 | convolution fusion | flops 270663680 | bytes 5507072 | tf_op jit(solution)/shard_map/tri,itc->trc/dot_general | solution.py:24
  51.8 0.6 gather_fusion.1
  52.3 0.1 select_convert_fusion
  52.4 0.1 reshape.139
  52.5 0.6 constant_dynamic-slice_fusion
  53.1 0.6 iota_compare_fusion
  53.7 0.1 broadcast_in_dim.54
  53.8 0.1 broadcast_in_dim.55
  53.9 31.6 %all-to-all-done.1 = bf16[8,256,1024]{2,1,0:T(8,128)(2,1)} async-done(((bf16[8,256,1024]{2,1,0:T(8,128)(2,1)}), bf16[8,256,1024]{2,1,0:T(8,128)(2,1)}, u32[]{:S(2)}, u32[]{:S(2)}) %all-to-all-start.1) | async-done | bytes 4194336 | tf_op jit(solution)/shard_map/all_to_all | solution.py:45
  85.5 6.4 %copy.21 = bf16[8,1024,256]{2,1,0:T(8,128)(2,1)} copy(bf16[8,1024,256]{1,2,0:T(8,128)(2,1)} %bitcast.12) | data formatting | bytes 8388608 | tf_op jit(solution)/shard_map/rc,uci->rui/dot_general | solution.py:42
  91.9 4.6 %convolution_convert_fusion = bf16[64,8192]{1,0:T(8,128)(2,1)} fusion(bf16[8192,256]{1,0:T(8,128)(2,1)} %bitcast.47, bf16[1,64,256]{2,1,0:T(8,128)(2,1)} %reduce-scatter.3.cloned.1.call-done, f32[256]{0:T(256)S(1)} %reshape.139, pred[256]{0:T(512)(128)(4,1)S(1)} %broadcast_in_dim.55), kind=kOutput, calls=%fused_computation.3 | convolution fusion | flops 269041664 | bytes 5276928 | tf_op jit(solution)/shard_map/rc,uci->rui/dot_general | solution.py:42
  96.5 0.7 dynamic-slice_convert_fusion
  97.2 0.6 fusion.11
  97.8 25.4 %reduce-scatter.5.cloned.1.call-done = bf16[64,2048]{1,0:T(8,128)(2,1)} async-done(((bf16[64,8192]{1,0:T(8,128)(2,1)}), bf16[64,2048]{1,0:T(8,128)(2,1)}) %reduce-scatter.5.cloned.1.call-update) | async-done | bytes 262160 | tf_op jit(solution)/shard_map/reduce_scatter | solution.py:49
  123.2 1.7 %add_convert_fusion = bf16[64,2048]{1,0:T(8,128)(2,1)} fusion(bf16[64,2048]{1,0:T(8,128)(2,1)} %reduce-scatter.5.cloned.1.call-done, f32[2048]{0:T(1024)S(1)} %dynamic-slice_convert_fusion), kind=kLoop, calls=%fused_computation.13 | loop fusion | flops 393216 | bytes 532480 | tf_op jit(solution)/shard_map/convert_element_type | solution.py:54
  (19 shorter events, 0.2 us)
Async XLA Ops:
  7.2 45.3 %copy-start = (s32[8,1]{0,1:T(1,128)S(1)}, s32[8,1]{0,1:T(1,128)}, u32[]{:S(2)}) copy-start(s32[8,1]{0,1:T(1,128)} %param.13) | copy-start | bytes 100
  7.2 8.4 %copy-start.2 = (s32[8,1,4]{0,2,1:T(4,128)S(1)}, s32[8,1,4]{0,2,1:T(4,128)}, u32[]{:S(2)}) copy-start(s32[8,1,4]{0,2,1:T(4,128)} %param.12) | copy-start | bytes 388
  10.4 20.6 %all-to-all-start = ((bf16[64,8,1024]{2,0,1:T(8,128)(2,1)}), bf16[64,8,1024]{2,0,1:T(8,128)(2,1)S(1)}, u32[]{:S(2)}, u32[]{:S(2)}) async-start(bf16[64,8,1024]{2,0,1:T(8,128)(2,1)} %bitcast.42), calls=%async_computation | async-start | bytes 2097152 | tf_op jit(solution)/shard_map/all_to_all | solution.py:21
  24.9 11.0 %copy-start.3 = (bf16[2048]{0:T(1024)(128)(2,1)S(1)}, bf16[2048]{0:T(1024)(128)(2,1)}, u32[]{:S(2)}) copy-start(bf16[2048]{0:T(1024)(128)(2,1)} %param.10) | copy-start | bytes 12292
  31.0 54.4 %all-to-all-start.1 = ((bf16[8,256,1024]{2,1,0:T(8,128)(2,1)}), bf16[8,256,1024]{2,1,0:T(8,128)(2,1)}, u32[]{:S(2)}, u32[]{:S(2)}) async-start(bf16[8,256,1024]{2,1,0:T(8,128)(2,1)} %bitcast_select_fusion), calls=%async_computation.2 | async-start | bytes 8388608 | tf_op jit(solution)/shard_map/all_to_all | solution.py:45
  35.6 56.3 %reduce-scatter.3.cloned.1.call-start = ((), (), s32[]{:S(2)}) async-start(), calls=%async_computation.4 | async-start | bytes 294912 | tf_op jit(solution)/shard_map/reduce_scatter | solution.py:23
  51.7 71.5 %reduce-scatter.5.cloned.1.call-start = ((), (), s32[]{:S(2)}) async-start(), calls=%async_computation.5 | async-start | bytes 1310720 | tf_op jit(solution)/shard_map/reduce_scatter | solution.py:49
  91.9 5.3 %copy-start.1 = (bf16[1,64,256]{2,1,0:T(8,128)(2,1)S(1)}, bf16[1,64,256]{2,1,0:T(8,128)(2,1)}, u32[]{:S(2)}) copy-start(bf16[1,64,256]{2,1,0:T(8,128)(2,1)} %reduce-scatter.3.cloned.1.call-done) | copy-start | bytes 98308
Sparse Core Ops, SparseCore 0:
  51.8 35.4 reduce-scatter.2
  96.6 26.5 reduce-scatter.4
where the time goes:
time: 133 us; the launch traced here: 132 us
  waiting for transfers between devices  63.1 us (47%)
  local copies, waits for them, and re-layouts  26 us (20%)
  between operations  14.1 us (11%)
  starting transfers between devices  9.82 us (7%)
  other arithmetic  9.73 us (7%)
  matrix products  8.96 us (7%)
    all_to_all x1, waiting for transfers between devices, on_device(): lax.all_to_all(outgoing, 'tok', split_axis=0, concat_axis=0, tiled=True)  31.6 us
    reduce_scatter x1, waiting for transfers between devices, on_device(): lax.psum_scatter(owner_part.astype(jnp.bfloat16), 'feat', scatter_dimensi...  25.4 us
    unnamed x10, local copies, waits for them, and re-layouts  6.51 us
    dot_general x1, local copies, waits for them, and re-layouts, on_device(): jnp.einsum('rc,uci->rui', code_values, lax.all_to_all(outgoing, 'tok', sp...  6.44 us
    all_to_all x1, waiting for transfers between devices, on_device(): lax.all_to_all(centered, 'tok', split_axis=1, concat_axis=0, tiled=True)  6.14 us
    all_to_all x1, starting transfers between devices, on_device(): lax.all_to_all(centered, 'tok', split_axis=1, concat_axis=0, tiled=True)  5.17 us
    gather x1, local copies, waits for them, and re-layouts, on_device(): jnp.take(dec_weight.reshape(nblocks, BLOCK, wslice), listed, axis=0)  4.98 us
    gather x1, local copies, waits for them, and re-layouts, on_device(): jnp.take(enc_weight.reshape(wslice, nblocks, BLOCK), listed, axis=1)  4.95 us
  transfers between devices with their start and end apart: 4, of which 3 were waited for; matrix products, arithmetic and copies ran while one was open for 27% of the time, Pallas kernels for 0%

commit v1 on v0

v1 whole, which is shorter than its diff:
```python
import functools

import jax
import jax.numpy as jnp
from jax import lax
from jax.experimental import pallas as pl
from jax.experimental.pallas import tpu as pltpu
from jax.sharding import PartitionSpec as P

BLOCK = 64
SLOTS = 4
LANES = 128
ACTIVE = SLOTS * BLOCK
VMEM = pltpu.VMEM
SMEM = pltpu.SMEM
BF16 = jnp.bfloat16
F32 = jnp.float32


def spec(space):
    return pl.BlockSpec(memory_space=space)


def params(mib):
    return pltpu.CompilerParams(vmem_limit_bytes=mib << 20)


def cost(flops, nbytes):
    return pl.CostEstimate(flops=flops, bytes_accessed=nbytes, transcendentals=0)


def place():
    tok = lax.axis_index("tok")
    return lax.axis_index("feat"), tok >> 1, tok & 1


def center_kernel(groups, wslice, tok_ref, bias_ref, *outs):
    _, c, k = place()
    for p in range(groups):
        for half in range(2):
            u = ((c ^ p) << 1) + (k ^ half)
            cols = pl.ds(pl.multiple_of(u * wslice, wslice), wslice)
            rows = tok_ref[:, cols].astype(F32) - bias_ref[pl.ds(u, 1), :]
            outs[p][half] = rows.astype(BF16)


def pick_pair(first, second, odd_first, odd_second):
    low = lax.broadcasted_iota(jnp.int32, first.shape, 1) < BLOCK
    a = jnp.where(odd_first, pltpu.roll(first, BLOCK, 1), first)
    b = jnp.where(odd_second, second, pltpu.roll(second, BLOCK, 1))
    return jnp.where(low, a, b)


def gather_kernel(groups, ids_ref, w_ref, out_ref):
    _, c, k = place()
    for p in range(groups):
        tile = ((c ^ p) << 1) + k
        for pair in range(SLOTS // 2):
            windows = []
            odds = []
            for slot in (2 * pair, 2 * pair + 1):
                block = ids_ref[tile, slot]
                start = pl.multiple_of((block >> 1) * LANES, LANES)
                windows.append(w_ref[:, pl.ds(start, LANES)])
                odds.append((block & 1) == 1)
            picked = pick_pair(windows[0].astype(F32), windows[1].astype(F32), *odds)
            out_ref[p, :, pair * LANES : (pair + 1) * LANES] = picked.astype(BF16)


def encode_kernel(groups, *refs):
    pieces, (own_ref, oth_ref, out_ref) = refs[:groups], refs[groups:]
    step = pl.program_id(0)
    for p in range(groups):

        @pl.when(step == p)
        def _(p=p):
            acc = jnp.dot(pieces[p][0], own_ref[0], preferred_element_type=F32)
            acc += jnp.dot(pieces[p][1], oth_ref[0], preferred_element_type=F32)
            out_ref[0] = acc.astype(BF16)


def decode_kernel(groups, *refs):
    ids_ref, counts_ref, bias_ref = refs[:3]
    parts = refs[3 : 3 + groups]
    own_ref, oth_ref = refs[3 + groups : 5 + groups]
    code_ref = refs[5 + groups]
    outs = refs[6 + groups : 6 + 2 * groups]
    codes, own_rows, oth_rows, sems = refs[6 + 2 * groups :]
    f, c, k = place()
    copies = []
    for s in range(groups):
        tile = ((c ^ f ^ s) << 1) + k
        for slot in range(SLOTS):
            rows = pl.ds(pl.multiple_of(ids_ref[tile, slot] * BLOCK, BLOCK), BLOCK)
            into = pl.ds(slot * BLOCK, BLOCK)
            for which, (src, dst) in enumerate(((own_ref, own_rows), (oth_ref, oth_rows))):
                copy = pltpu.make_async_copy(
                    src.at[rows, :], dst.at[s, into, :], sems.at[s, slot, which]
                )
                copy.start()
                copies.append(copy)
    lane = lax.broadcasted_iota(jnp.int32, (1, LANES), 1)
    for p in range(groups):
        tile = ((c ^ p) << 1) + k
        count = counts_ref[tile]
        for pair in range(SLOTS // 2):
            cols = slice(pair * LANES, (pair + 1) * LANES)
            pre = parts[0][p, :, cols].astype(F32)
            for q in range(1, groups):
                pre += parts[q][p ^ q, :, cols].astype(F32)
            bias = []
            odds = []
            for slot in (2 * pair, 2 * pair + 1):
                block = ids_ref[tile, slot]
                bias.append(bias_ref[pl.ds(block >> 1, 1), :])
                odds.append((block & 1) == 1)
            row = pick_pair(bias[0], bias[1], *odds)
            live = (lane >= BLOCK).astype(jnp.int32) + 2 * pair < count
            value = jnp.where(live, jnp.maximum(pre + row, 0.0), 0.0).astype(BF16)
            codes[p, :, cols] = value
    code_ref[...] = codes[0]
    per_step = 2 * SLOTS
    for s in range(groups):
        for copy in copies[s * per_step : (s + 1) * per_step]:
            copy.wait()
        code = codes[f ^ s]
        own = jnp.dot(code, own_rows[s], preferred_element_type=F32)
        outs[s][k] = own.astype(BF16)
        oth = jnp.dot(code, oth_rows[s], preferred_element_type=F32)
        outs[s][1 - k] = oth.astype(BF16)


def finish_kernel(groups, *refs):
    arrived, (bias_ref, out_ref) = refs[:groups], refs[groups:]
    f, _, _ = place()
    wslice = arrived[0].shape[2]
    for half in range(2):
        total = arrived[0][half].astype(F32)
        for ref in arrived[1:]:
            total += ref[half].astype(F32)
        total += bias_ref[pl.ds(2 * f + half, 1), :]
        out_ref[:, half * wslice : (half + 1) * wslice] = total.astype(BF16)


def on_device(tokens, dec_bias, enc_weight, enc_bias, dec_weight, block_ids, block_counts):
    tile_count = lax.axis_size("tok")
    groups = lax.axis_size("feat")
    tok_rows, width = tokens.shape
    wslice = width // tile_count
    feats = enc_weight.shape[1]
    ids = block_ids[:, 0, :]
    counts = block_counts[:, 0]
    bias_rows = dec_bias.astype(F32).reshape(tile_count, wslice)
    enc_bias_rows = enc_bias.astype(F32).reshape(feats // LANES, LANES)

    def swap(value, p):
        pairs = [(i, i ^ (2 * p)) for i in range(tile_count)]
        return lax.ppermute(value, "tok", pairs)

    cores = [(i, i ^ 1) for i in range(tile_count)]
    enc_other = lax.ppermute(enc_weight, "tok", cores)
    dec_other = lax.ppermute(dec_weight, "tok", cores)

    piece = jax.ShapeDtypeStruct((2, tok_rows, wslice), BF16)
    sent = pl.pallas_call(
        functools.partial(center_kernel, groups, wslice),
        out_shape=[piece] * groups,
        in_specs=[spec(VMEM)] * 2,
        out_specs=[spec(VMEM)] * groups,
        compiler_params=params(16),
        cost_estimate=cost(width * tok_rows, 4 * width * tok_rows),
        name="center",
    )(tokens, bias_rows)
    pieces = [sent[0]] + [swap(sent[p], p) for p in range(1, groups)]

    chunk = min(wslice, 256)

    def gather(weight):
        return pl.pallas_call(
            functools.partial(gather_kernel, groups),
            out_shape=jax.ShapeDtypeStruct((groups, wslice, ACTIVE), BF16),
            grid=(wslice // chunk,),
            in_specs=[spec(SMEM), pl.BlockSpec((chunk, feats), lambda i: (i, 0))],
            out_specs=pl.BlockSpec((groups, chunk, ACTIVE), lambda i: (0, i, 0)),
            compiler_params=params(32),
            cost_estimate=cost(0, 2 * wslice * (feats + groups * ACTIVE)),
            name="pick_columns",
        )(ids, weight)

    own_cols = gather(enc_weight)
    oth_cols = gather(enc_other)
    col_spec = pl.BlockSpec((1, wslice, ACTIVE), lambda i: (i, 0, 0))
    part = pl.pallas_call(
        functools.partial(encode_kernel, groups),
        out_shape=jax.ShapeDtypeStruct((groups, tok_rows, ACTIVE), BF16),
        grid=(groups,),
        in_specs=[spec(VMEM)] * groups + [col_spec] * 2,
        out_specs=pl.BlockSpec((1, tok_rows, ACTIVE), lambda i: (i, 0, 0)),
        compiler_params=params(32),
        cost_estimate=cost(
            4 * groups * tok_rows * wslice * ACTIVE, 4 * groups * wslice * ACTIVE
        ),
        name="encode",
    )(*pieces, own_cols, oth_cols)
    parts = [part] + [swap(part, p) for p in range(1, groups)]

    decoded = pl.pallas_call(
        functools.partial(decode_kernel, groups),
        out_shape=[jax.ShapeDtypeStruct((tok_rows, ACTIVE), BF16)] + [piece] * groups,
        in_specs=[spec(SMEM)] * 2 + [spec(VMEM)] * (1 + groups) + [spec(pl.ANY)] * 2,
        out_specs=[spec(VMEM)] * (1 + groups),
        scratch_shapes=[
            VMEM((groups, tok_rows, ACTIVE), BF16),
            VMEM((groups, ACTIVE, wslice), BF16),
            VMEM((groups, ACTIVE, wslice), BF16),
            pltpu.SemaphoreType.DMA((groups, SLOTS, 2)),
        ],
        compiler_params=params(40),
        cost_estimate=cost(
            4 * groups * tok_rows * wslice * ACTIVE, 4 * groups * wslice * ACTIVE
        ),
        name="decode",
    )(ids, counts, enc_bias_rows, *parts, dec_weight, dec_other)
    code_values, outgoing = decoded[0], decoded[1:]

    arrived = []
    for s in range(groups):
        plane = []
        line = []
        for f in range(groups):
            for i in range(tile_count):
                here = f * tile_count + i
                plane.append((here, f * tile_count + (i ^ (2 * (f ^ s)))))
                line.append((here, ((i >> 1) ^ f ^ s) * tile_count + i))
        moved = lax.ppermute(outgoing[s], ("feat", "tok"), plane)
        arrived.append(lax.ppermute(moved, ("feat", "tok"), line))

    rebuilt = pl.pallas_call(
        functools.partial(finish_kernel, groups),
        out_shape=jax.ShapeDtypeStruct((tok_rows, 2 * wslice), BF16),
        in_specs=[spec(VMEM)] * (groups + 1),
        out_specs=spec(VMEM),
        compiler_params=params(16),
        cost_estimate=cost(0, 2 * (groups + 1) * 2 * tok_rows * wslice),
        name="finish",
    )(*arrived, bias_rows)
    return (code_values, rebuilt)


def solution(mesh):
    in_specs = (
        P("tok", None),
        P(),
        P("tok", "feat"),
        P("feat"),
        P("feat", "tok"),
        P(None, "feat", None),
        P(None, "feat"),
    )
    out_specs = (P("tok", "feat"), P("tok", "feat"))
    return jax.shard_map(
        on_device, mesh=mesh, in_specs=in_specs, out_specs=out_specs, check_vma=False
    )
```

time: 133 us -> 72.1 us (0.54)
  waiting for transfers between devices: 63.1 us -> 23.2 us
  local copies, waits for them, and re-layouts: 26 us -> 4.91 us
  starting transfers between devices: 9.82 us -> 27.3 us
  Pallas kernels: 0 us -> 15.1 us
  between operations: 14.1 us -> 0.83 us
  other arithmetic: 9.73 us -> 0.01 us
  matrix products: 8.96 us -> 0 us
    all_to_all x2 -> x0, waiting for transfers between devices: 37.7 us -> none  [the longest x1 31.6 us: on_device(): lax.all_to_all(outgoing, 'tok', split_axis=0, concat_axis=0, tiled=True)]
    ppermute x0 -> x16, starting transfers between devices: none -> 27.3 us  [the longest x4 9.89 us: on_device(): moved = lax.ppermute(outgoing[s], ('feat', 'tok'), plane)]
    reduce_scatter x2 -> x0, waiting for transfers between devices: 25.4 us -> none  [the longest x1 25.4 us: on_device(): lax.psum_scatter(owner_part.astype(jnp.bfloat16), 'feat', scatter_dimensi...]
    ppermute x0 -> x16, waiting for transfers between devices: none -> 23.2 us  [the longest x4 12.9 us: on_device(): arrived.append(lax.ppermute(moved, ('feat', 'tok'), line))]
    pallas_call x0 -> x6, Pallas kernels: none -> 15.1 us  [the longest x2 7.3 us: gather(): pl.pallas_call(functools.partial(gather_kernel, groups), out_shape=jax.Sh...]
    gather x3 -> x0, local copies, waits for them, and re-layouts: 10.5 us -> none  [the longest x1 4.98 us: on_device(): jnp.take(dec_weight.reshape(nblocks, BLOCK, wslice), listed, axis=0)]
    all_to_all x2 -> x0, starting transfers between devices: 9.73 us -> none  [the longest x1 5.17 us: on_device(): lax.all_to_all(centered, 'tok', split_axis=1, concat_axis=0, tiled=True)]
    dot_general x2 -> x0, matrix products: 8.96 us -> none  [the longest x1 4.57 us: on_device(): jnp.einsum('rc,uci->rui', code_values, lax.all_to_all(outgoing, 'tok', sp...]
  transfers between devices with their start and end apart: 4 -> 16, of which waited for: 3 -> 5; matrix products, arithmetic and copies ran while one was open for 27% -> 2% of each run, Pallas kernels for 0% -> 12%
where the time goes in v1:
time: 72.1 us; the launch traced here: 71.3 us
  starting transfers between devices  27.3 us (38%)
  waiting for transfers between devices  23.2 us (32%)
  Pallas kernels  15.1 us (21%)
  local copies, waits for them, and re-layouts  4.91 us (7%)
  between operations  0.83 us (1%)
    ppermute x4, waiting for transfers between devices, on_device(): arrived.append(lax.ppermute(moved, ('feat', 'tok'), line))  12.9 us
    ppermute x4, starting transfers between devices, on_device(): moved = lax.ppermute(outgoing[s], ('feat', 'tok'), plane)  9.89 us
    ppermute x4, starting transfers between devices, on_device(): arrived.append(lax.ppermute(moved, ('feat', 'tok'), line))  8.74 us
    ppermute x6, starting transfers between devices, swap(): return lax.ppermute(value, 'tok', pairs)  8.07 us
    pallas_call x2, Pallas kernels, gather(): pl.pallas_call(functools.partial(gather_kernel, groups), out_shape=jax.Sh...  7.3 us
    ppermute x6, waiting for transfers between devices, swap(): return lax.ppermute(value, 'tok', pairs)  6.68 us
    pallas_call x1, Pallas kernels, on_device(): pl.pallas_call(functools.partial(decode_kernel, groups), out_shape=[jax.S...  5.42 us
    ppermute x4, waiting for transfers between devices, on_device(): moved = lax.ppermute(outgoing[s], ('feat', 'tok'), plane)  3.64 us
  transfers between devices with their start and end apart: 16, of which 5 were waited for; matrix products, arithmetic and copies ran while one was open for 2% of the time, Pallas kernels for 12%

profile of v1, /device:TPU:0, one launch (start us, length us, event | category | flops | bytes accessed | tf_op | source)
XLA Modules:
  0.0 71.3 jit_solution(7892137595391958253)
XLA Ops:
  0.6 0.5 collective-permute-start.3
  1.1 0.1 collective-permute-start.7
  1.2 0.7 %reshape.21.bias_ref.refs_4_ = f32[8,1024]{1,0:T(8,128)S(1)} reshape(bf16[8192]{0:T(1024)(128)(2,1)} %param.8) | data formatting | bytes 49152 | tf_op jit(solution)/shard_map/reshape | solution.py:153
  2.0 0.0 copy-start.2
  2.0 1.2 %copy-done.2 = bf16[64,8192]{1,0:T(8,128)(2,1)S(1)} copy-done((bf16[64,8192]{1,0:T(8,128)(2,1)S(1)}, bf16[64,8192]{1,0:T(8,128)(2,1)}, u32[]{:S(2)}) %copy-start.2) | copy-done | bytes 1048600
  3.2 0.2 center.1
  3.4 3.0 %collective-permute-start = (bf16[2,64,1024]{2,1,0:T(8,128)(2,1)S(1)}, bf16[2,64,1024]{2,1,0:T(8,128)(2,1)S(1)}, u32[]{:S(2)}, u32[]{:S(2)}) collective-permute-start(bf16[2,64,1024]{2,1,0:T(8,128)(2,1)S(1)} %get-tuple-element.12), channel_id=1, source_target_pairs={{0,2},{1,3},{2,0},{3,1},{4,6},{5,7},{6,4},{7,5},{8,10},{9,11},{10,... | collective-permute-start | bytes 786440 | tf_op jit(solution)/shard_map/ppermute | solution.py:158
  6.4 1.5 %collective-permute-start.1 = (bf16[2,64,1024]{2,1,0:T(8,128)(2,1)S(1)}, bf16[2,64,1024]{2,1,0:T(8,128)(2,1)S(1)}, u32[]{:S(2)}, u32[]{:S(2)}) collective-permute-start(bf16[2,64,1024]{2,1,0:T(8,128)(2,1)S(1)} %get-tuple-element.13), channel_id=1, source_target_pairs={{0,4},{1,5},{2,6},{3,7},{4,0},{5,1},{6,2},{7,3},{8,12},{9,13},{10,... | collective-permute-start | bytes 786440 | tf_op jit(solution)/shard_map/ppermute | solution.py:158
  7.9 0.0 collective-permute-start.2
  7.9 0.8 %copy.11.ids_ref.refs_0_ = s32[8,4]{1,0:T(8,128)S(1)} copy(s32[8,4]{0,1:T(4,128)} %bitcast.6) | data formatting | bytes 256 | tf_op jit(solution)/shard_map/squeeze | solution.py:151
  8.7 2.2 %copy-done.1 = bf16[1024,2048]{1,0:T(8,128)(2,1)S(1)} copy-done((bf16[1024,2048]{1,0:T(8,128)(2,1)S(1)}, bf16[1024,2048]{1,0:T(8,128)(2,1)}, u32[]{:S(2)}) %copy-start.1) | copy-done | bytes 4194328
  10.8 3.0 %pick_columns.2.refs_4_ = bf16[4,1024,256]{2,1,0:T(8,128)(2,1)S(1)} custom-call(s32[8,4]{1,0:T(8,128)S(1)} %copy.11.ids_ref.refs_0_, bf16[1024,2048]{1,0:T(8,128)(2,1)S(1)} %copy-done.1), custom_call_target="tpu_custom_call" | custom-call | bytes 6291456 | tf_op jit(solution)/shard_map/pick_columns/pallas_call | solution.py:179
  13.8 4.3 %pick_columns.3.refs_5_ = bf16[4,1024,256]{2,1,0:T(8,128)(2,1)S(1)} custom-call(s32[8,4]{1,0:T(8,128)S(1)} %copy.11.ids_ref.refs_0_, bf16[1024,2048]{1,0:T(8,128)(2,1)} %collective-permute-done.3.w_ref), custom_call_target="tpu_custom_call" | custom-call | bytes 6291456 | tf_op jit(solution)/shard_map/pick_columns/pallas_call | solution.py:179
  18.2 1.8 %collective-permute-done.1.refs_2_ = bf16[2,64,1024]{2,1,0:T(8,128)(2,1)S(1)} collective-permute-done((bf16[2,64,1024]{2,1,0:T(8,128)(2,1)S(1)}, bf16[2,64,1024]{2,1,0:T(8,128)(2,1)S(1)}, u32[]{:S(2)}, u32[]{:S(2)}) %collective-permute-start.1) | collective-permute-done | bytes 262176 | tf_op jit(solution)/shard_map/ppermute | solution.py:158
  20.0 1.3 %encode.1.refs_3_ = bf16[4,64,256]{2,1,0:T(8,128)(2,1)S(1)} custom-call(bf16[2,64,1024]{2,1,0:T(8,128)(2,1)S(1)} %get-tuple-element.11.refs_0_, bf16[2,64,1024]{2,1,0:T(8,128)(2,1)S(1)} %collective-permute-done.refs_1_, bf16[2,64,1024]{2,1,0:T(8,128)(2,1)S(1)} %collective-permute-done.1.refs_2_, bf16[2,64,1024]{2,1,0:T(8,128)(2,1)S(1)} %collective-permute-done.2.refs_3_, ...), custom_call_target="tpu_custom_call" | custom-call | flops 268435456 | bytes 4194304 | tf_op jit(solution)/shard_map/encode/pallas_call | solution.py:193
  21.3 1.3 %collective-permute-start.4 = (bf16[4,64,256]{2,1,0:T(8,128)(2,1)S(1)}, bf16[4,64,256]{2,1,0:T(8,128)(2,1)S(1)}, u32[]{:S(2)}, u32[]{:S(2)}) collective-permute-start(bf16[4,64,256]{2,1,0:T(8,128)(2,1)S(1)} %encode.1.refs_3_), channel_id=1, source_target_pairs={{0,2},{1,3},{2,0},{3,1},{4,6},{5,7},{6,4},{7,5},{8,10},{9,11},{10,... | collective-permute-start | bytes 393224 | tf_op jit(solution)/shard_map/ppermute | solution.py:158
  22.6 0.8 %collective-permute-start.5 = (bf16[4,64,256]{2,1,0:T(8,128)(2,1)S(1)}, bf16[4,64,256]{2,1,0:T(8,128)(2,1)S(1)}, u32[]{:S(2)}, u32[]{:S(2)}) collective-permute-start(bf16[4,64,256]{2,1,0:T(8,128)(2,1)S(1)} %encode.1.refs_3_), channel_id=1, source_target_pairs={{0,4},{1,5},{2,6},{3,7},{4,0},{5,1},{6,2},{7,3},{8,12},{9,13},{10,... | collective-permute-start | bytes 393224 | tf_op jit(solution)/shard_map/ppermute | solution.py:158
  23.4 1.4 %collective-permute-start.6 = (bf16[4,64,256]{2,1,0:T(8,128)(2,1)S(1)}, bf16[4,64,256]{2,1,0:T(8,128)(2,1)S(1)}, u32[]{:S(2)}, u32[]{:S(2)}) collective-permute-start(bf16[4,64,256]{2,1,0:T(8,128)(2,1)S(1)} %encode.1.refs_3_), channel_id=1, source_target_pairs={{0,6},{1,7},{2,4},{3,5},{4,2},{5,3},{6,0},{7,1},{8,14},{9,15},{10,... | collective-permute-start | bytes 393224 | tf_op jit(solution)/shard_map/ppermute | solution.py:158
  24.9 2.5 %collective-permute-done.4.refs_4_ = bf16[4,64,256]{2,1,0:T(8,128)(2,1)S(1)} collective-permute-done((bf16[4,64,256]{2,1,0:T(8,128)(2,1)S(1)}, bf16[4,64,256]{2,1,0:T(8,128)(2,1)S(1)}, u32[]{:S(2)}, u32[]{:S(2)}) %collective-permute-start.4) | collective-permute-done | bytes 131104 | tf_op jit(solution)/shard_map/ppermute | solution.py:158
  27.4 2.4 %collective-permute-done.5.refs_5_ = bf16[4,64,256]{2,1,0:T(8,128)(2,1)S(1)} collective-permute-done((bf16[4,64,256]{2,1,0:T(8,128)(2,1)S(1)}, bf16[4,64,256]{2,1,0:T(8,128)(2,1)S(1)}, u32[]{:S(2)}, u32[]{:S(2)}) %collective-permute-start.5) | collective-permute-done | bytes 131104 | tf_op jit(solution)/shard_map/ppermute | solution.py:158
  29.8 5.4 %decode.1 = (bf16[64,256]{1,0:T(8,128)(2,1)}, bf16[2,64,1024]{2,1,0:T(8,128)(2,1)S(1)}, bf16[2,64,1024]{2,1,0:T(8,128)(2,1)S(1)}, bf16[2,64,1024]{2,1,0:T(8,128)(2,1)S(1)}, bf16[2,64,1024]{2,1,0:T(8,128)(2,1)S(1)}) custom-call(s32[8,4]{1,0:T(8,128)S(1)} %copy.11.ids_ref.refs_0_, s32[8]{0:T(128)S(1)} %bitcast.5, f32[16,128]{1,0:T(8,128)S(1)} %bitcast_convert_fusion.refs_2_, ...), custom_call_target="tpu_custom_call" | custom-call | flops 268435456 | bytes 4194304 | tf_op jit(solution)/shard_map/decode/pallas_call | solution.py:207
  35.2 3.2 %collective-permute-start.10 = (bf16[2,64,1024]{2,1,0:T(8,128)(2,1)S(1)}, bf16[2,64,1024]{2,1,0:T(8,128)(2,1)S(1)}, u32[]{:S(2)}, u32[]{:S(2)}) collective-permute-start(bf16[2,64,1024]{2,1,0:T(8,128)(2,1)S(1)} %get-tuple-element.17), channel_id=1, source_target_pairs={{0,2},{1,3},{2,0},{3,1},{4,6},{5,7},{6,4},{7,5},{8,8},{9,9},{10,10... | collective-permute-start | bytes 786440 | tf_op jit(solution)/shard_map/ppermute | solution.py:235
  38.4 2.9 %collective-permute-start.12 = (bf16[2,64,1024]{2,1,0:T(8,128)(2,1)S(1)}, bf16[2,64,1024]{2,1,0:T(8,128)(2,1)S(1)}, u32[]{:S(2)}, u32[]{:S(2)}) collective-permute-start(bf16[2,64,1024]{2,1,0:T(8,128)(2,1)S(1)} %get-tuple-element.18), channel_id=1, source_target_pairs={{0,4},{1,5},{2,6},{3,7},{4,0},{5,1},{6,2},{7,3},{8,14},{9,15},{10,... | collective-permute-start | bytes 786440 | tf_op jit(solution)/shard_map/ppermute | solution.py:235
  41.3 3.1 %collective-permute-start.14 = (bf16[2,64,1024]{2,1,0:T(8,128)(2,1)S(1)}, bf16[2,64,1024]{2,1,0:T(8,128)(2,1)S(1)}, u32[]{:S(2)}, u32[]{:S(2)}) collective-permute-start(bf16[2,64,1024]{2,1,0:T(8,128)(2,1)S(1)} %get-tuple-element.19), channel_id=1, source_target_pairs={{0,6},{1,7},{2,4},{3,5},{4,2},{5,3},{6,0},{7,1},{8,12},{9,13},{10,... | collective-permute-start | bytes 786440 | tf_op jit(solution)/shard_map/ppermute | solution.py:235
  44.5 0.7 collective-permute-start.8
  45.1 3.5 %collective-permute-start.11 = (bf16[2,64,1024]{2,1,0:T(8,128)(2,1)S(1)}, bf16[2,64,1024]{2,1,0:T(8,128)(2,1)S(1)}, u32[]{:S(2)}, u32[]{:S(2)}) collective-permute-start(bf16[2,64,1024]{2,1,0:T(8,128)(2,1)S(1)} %collective-permute-done.10), channel_id=1, source_target_pairs={{0,8},{1,9},{2,2},{3,3},{4,28},{5,29},{6,22},{7,23},{8,0},{9,1},{1... | collective-permute-start | bytes 786440 | tf_op jit(solution)/shard_map/ppermute | solution.py:236
  48.6 3.6 %collective-permute-done.12 = bf16[2,64,1024]{2,1,0:T(8,128)(2,1)S(1)} collective-permute-done((bf16[2,64,1024]{2,1,0:T(8,128)(2,1)S(1)}, bf16[2,64,1024]{2,1,0:T(8,128)(2,1)S(1)}, u32[]{:S(2)}, u32[]{:S(2)}) %collective-permute-start.12) | collective-permute-done | bytes 262176 | tf_op jit(solution)/shard_map/ppermute | solution.py:235
  52.3 1.9 %collective-permute-start.13 = (bf16[2,64,1024]{2,1,0:T(8,128)(2,1)S(1)}, bf16[2,64,1024]{2,1,0:T(8,128)(2,1)S(1)}, u32[]{:S(2)}, u32[]{:S(2)}) collective-permute-start(bf16[2,64,1024]{2,1,0:T(8,128)(2,1)S(1)} %collective-permute-done.12), channel_id=1, source_target_pairs={{0,16},{1,17},{2,26},{3,27},{4,4},{5,5},{6,14},{7,15},{8,24},{9,25... | collective-permute-start | bytes 786440 | tf_op jit(solution)/shard_map/ppermute | solution.py:236
  54.2 2.7 %collective-permute-start.15 = (bf16[2,64,1024]{2,1,0:T(8,128)(2,1)S(1)}, bf16[2,64,1024]{2,1,0:T(8,128)(2,1)S(1)}, u32[]{:S(2)}, u32[]{:S(2)}) collective-permute-start(bf16[2,64,1024]{2,1,0:T(8,128)(2,1)S(1)} %collective-permute-done.14), channel_id=1, source_target_pairs={{0,24},{1,25},{2,18},{3,19},{4,12},{5,13},{6,6},{7,7},{8,16},{9,17... | collective-permute-start | bytes 786440 | tf_op jit(solution)/shard_map/ppermute | solution.py:236
  56.9 0.7 collective-permute-start.9
  57.6 12.8 %collective-permute-done.13.refs_2_ = bf16[2,64,1024]{2,1,0:T(8,128)(2,1)S(1)} collective-permute-done((bf16[2,64,1024]{2,1,0:T(8,128)(2,1)S(1)}, bf16[2,64,1024]{2,1,0:T(8,128)(2,1)S(1)}, u32[]{:S(2)}, u32[]{:S(2)}) %collective-permute-start.13) | collective-permute-done | bytes 262176 | tf_op jit(solution)/shard_map/ppermute | solution.py:236
  70.4 0.9 %finish.1 = bf16[64,2048]{1,0:T(8,128)(2,1)} custom-call(bf16[2,64,1024]{2,1,0:T(8,128)(2,1)S(1)} %collective-permute-done.9.refs_0_, bf16[2,64,1024]{2,1,0:T(8,128)(2,1)S(1)} %collective-permute-done.11.refs_1_, bf16[2,64,1024]{2,1,0:T(8,128)(2,1)S(1)} %collective-permute-done.13.refs_2_, bf16[2,64,1024]{2,1,0:T(8,128)(2,1)S(1)} %collective-permute-done.15.refs_3_, ...), custom_call_target="tpu_custom_call" | custom-call | bytes 1310720 | tf_op jit(solution)/shard_map/finish/pallas_call | solution.py:238
  (19 shorter events, 0.1 us)
Async XLA Ops:
  0.6 13.2 %collective-permute-start.3 = (bf16[1024,2048]{1,0:T(8,128)(2,1)}, bf16[1024,2048]{1,0:T(8,128)(2,1)}, u32[]{:S(2)}, u32[]{:S(2)}) collective-permute-start(bf16[1024,2048]{1,0:T(8,128)(2,1)} %w_ref.1), channel_id=1, source_target_pairs={{0,1},{1,0},{2,3},{3,2},{4,5},{5,4},{6,7},{7,6},{8,9},{9,8},{10,11... | collective-permute-start | bytes 12582920 | tf_op jit(solution)/shard_map/ppermute | solution.py:161
  1.1 23.7 %collective-permute-start.7 = (bf16[2048,1024]{1,0:T(8,128)(2,1)}, bf16[2048,1024]{1,0:T(8,128)(2,1)}, u32[]{:S(2)}, u32[]{:S(2)}) collective-permute-start(bf16[2048,1024]{1,0:T(8,128)(2,1)} %refs_7_.1), channel_id=1, source_target_pairs={{0,1},{1,0},{2,3},{3,2},{4,5},{5,4},{6,7},{7,6},{8,9},{9,8},{10,11... | collective-permute-start | bytes 12582920 | tf_op jit(solution)/shard_map/ppermute | solution.py:162
  2.0 1.2 %copy-start.2 = (bf16[64,8192]{1,0:T(8,128)(2,1)S(1)}, bf16[64,8192]{1,0:T(8,128)(2,1)}, u32[]{:S(2)}) copy-start(bf16[64,8192]{1,0:T(8,128)(2,1)} %tok_ref.1) | copy-start | bytes 3145732
  3.4 14.8 %collective-permute-start = (bf16[2,64,1024]{2,1,0:T(8,128)(2,1)S(1)}, bf16[2,64,1024]{2,1,0:T(8,128)(2,1)S(1)}, u32[]{:S(2)}, u32[]{:S(2)}) collective-permute-start(bf16[2,64,1024]{2,1,0:T(8,128)(2,1)S(1)} %get-tuple-element.12), channel_id=1, source_target_pairs={{0,2},{1,3},{2,0},{3,1},{4,6},{5,7},{6,4},{7,5},{8,10},{9,11},{10,... | collective-permute-start | bytes 786440 | tf_op jit(solution)/shard_map/ppermute | solution.py:158
  6.4 13.6 %collective-permute-start.1 = (bf16[2,64,1024]{2,1,0:T(8,128)(2,1)S(1)}, bf16[2,64,1024]{2,1,0:T(8,128)(2,1)S(1)}, u32[]{:S(2)}, u32[]{:S(2)}) collective-permute-start(bf16[2,64,1024]{2,1,0:T(8,128)(2,1)S(1)} %get-tuple-element.13), channel_id=1, source_target_pairs={{0,4},{1,5},{2,6},{3,7},{4,0},{5,1},{6,2},{7,3},{8,12},{9,13},{10,... | collective-permute-start | bytes 786440 | tf_op jit(solution)/shard_map/ppermute | solution.py:158
  7.9 12.1 %collective-permute-start.2 = (bf16[2,64,1024]{2,1,0:T(8,128)(2,1)S(1)}, bf16[2,64,1024]{2,1,0:T(8,128)(2,1)S(1)}, u32[]{:S(2)}, u32[]{:S(2)}) collective-permute-start(bf16[2,64,1024]{2,1,0:T(8,128)(2,1)S(1)} %get-tuple-element.14), channel_id=1, source_target_pairs={{0,6},{1,7},{2,4},{3,5},{4,2},{5,3},{6,0},{7,1},{8,14},{9,15},{10,... | collective-permute-start | bytes 786440 | tf_op jit(solution)/shard_map/ppermute | solution.py:158
  8.7 2.2 %copy-start.1 = (bf16[1024,2048]{1,0:T(8,128)(2,1)S(1)}, bf16[1024,2048]{1,0:T(8,128)(2,1)}, u32[]{:S(2)}) copy-start(bf16[1024,2048]{1,0:T(8,128)(2,1)} %w_ref.1) | copy-start | bytes 12582916
  18.2 6.7 %copy-start.4 = (bf16[2048]{0:T(1024)(128)(2,1)S(1)}, bf16[2048]{0:T(1024)(128)(2,1)}, u32[]{:S(2)}) copy-start(bf16[2048]{0:T(1024)(128)(2,1)} %param.10) | copy-start | bytes 12292
  18.2 11.6 %copy-start = (bf16[2048,1024]{1,0:T(8,128)(2,1)S(1)}, bf16[2048,1024]{1,0:T(8,128)(2,1)}, u32[]{:S(2)}) copy-start(bf16[2048,1024]{1,0:T(8,128)(2,1)} %refs_7_.1) | copy-start | bytes 12582916
  18.2 11.6 %copy-start.3 = (s32[8,1]{0,1:T(1,128)S(1)}, s32[8,1]{0,1:T(1,128)}, u32[]{:S(2)}) copy-start(s32[8,1]{0,1:T(1,128)} %param.13) | copy-start | bytes 100
  21.3 6.1 %collective-permute-start.4 = (bf16[4,64,256]{2,1,0:T(8,128)(2,1)S(1)}, bf16[4,64,256]{2,1,0:T(8,128)(2,1)S(1)}, u32[]{:S(2)}, u32[]{:S(2)}) collective-permute-start(bf16[4,64,256]{2,1,0:T(8,128)(2,1)S(1)} %encode.1.refs_3_), channel_id=1, source_target_pairs={{0,2},{1,3},{2,0},{3,1},{4,6},{5,7},{6,4},{7,5},{8,10},{9,11},{10,... | collective-permute-start | bytes 393224 | tf_op jit(solution)/shard_map/ppermute | solution.py:158
  22.6 7.2 %collective-permute-start.5 = (bf16[4,64,256]{2,1,0:T(8,128)(2,1)S(1)}, bf16[4,64,256]{2,1,0:T(8,128)(2,1)S(1)}, u32[]{:S(2)}, u32[]{:S(2)}) collective-permute-start(bf16[4,64,256]{2,1,0:T(8,128)(2,1)S(1)} %encode.1.refs_3_), channel_id=1, source_target_pairs={{0,4},{1,5},{2,6},{3,7},{4,0},{5,1},{6,2},{7,3},{8,12},{9,13},{10,... | collective-permute-start | bytes 393224 | tf_op jit(solution)/shard_map/ppermute | solution.py:158
  23.4 6.4 %collective-permute-start.6 = (bf16[4,64,256]{2,1,0:T(8,128)(2,1)S(1)}, bf16[4,64,256]{2,1,0:T(8,128)(2,1)S(1)}, u32[]{:S(2)}, u32[]{:S(2)}) collective-permute-start(bf16[4,64,256]{2,1,0:T(8,128)(2,1)S(1)} %encode.1.refs_3_), channel_id=1, source_target_pairs={{0,6},{1,7},{2,4},{3,5},{4,2},{5,3},{6,0},{7,1},{8,14},{9,15},{10,... | collective-permute-start | bytes 393224 | tf_op jit(solution)/shard_map/ppermute | solution.py:158
  35.2 9.9 %collective-permute-start.10 = (bf16[2,64,1024]{2,1,0:T(8,128)(2,1)S(1)}, bf16[2,64,1024]{2,1,0:T(8,128)(2,1)S(1)}, u32[]{:S(2)}, u32[]{:S(2)}) collective-permute-start(bf16[2,64,1024]{2,1,0:T(8,128)(2,1)S(1)} %get-tuple-element.17), channel_id=1, source_target_pairs={{0,2},{1,3},{2,0},{3,1},{4,6},{5,7},{6,4},{7,5},{8,8},{9,9},{10,10... | collective-permute-start | bytes 786440 | tf_op jit(solution)/shard_map/ppermute | solution.py:235
  38.4 13.9 %collective-permute-start.12 = (bf16[2,64,1024]{2,1,0:T(8,128)(2,1)S(1)}, bf16[2,64,1024]{2,1,0:T(8,128)(2,1)S(1)}, u32[]{:S(2)}, u32[]{:S(2)}) collective-permute-start(bf16[2,64,1024]{2,1,0:T(8,128)(2,1)S(1)} %get-tuple-element.18), channel_id=1, source_target_pairs={{0,4},{1,5},{2,6},{3,7},{4,0},{5,1},{6,2},{7,3},{8,14},{9,15},{10,... | collective-permute-start | bytes 786440 | tf_op jit(solution)/shard_map/ppermute | solution.py:235
  41.3 12.9 %collective-permute-start.14 = (bf16[2,64,1024]{2,1,0:T(8,128)(2,1)S(1)}, bf16[2,64,1024]{2,1,0:T(8,128)(2,1)S(1)}, u32[]{:S(2)}, u32[]{:S(2)}) collective-permute-start(bf16[2,64,1024]{2,1,0:T(8,128)(2,1)S(1)} %get-tuple-element.19), channel_id=1, source_target_pairs={{0,6},{1,7},{2,4},{3,5},{4,2},{5,3},{6,0},{7,1},{8,12},{9,13},{10,... | collective-permute-start | bytes 786440 | tf_op jit(solution)/shard_map/ppermute | solution.py:235
  44.5 12.4 %collective-permute-start.8 = (bf16[2,64,1024]{2,1,0:T(8,128)(2,1)S(1)}, bf16[2,64,1024]{2,1,0:T(8,128)(2,1)S(1)}, u32[]{:S(2)}, u32[]{:S(2)}) collective-permute-start(bf16[2,64,1024]{2,1,0:T(8,128)(2,1)S(1)} %get-tuple-element.16), channel_id=1, source_target_pairs={{0,0},{1,1},{2,2},{3,3},{4,4},{5,5},{6,6},{7,7},{8,10},{9,11},{10,... | collective-permute-start | bytes 786440 | tf_op jit(solution)/shard_map/ppermute | solution.py:235
  45.1 12.4 %collective-permute-start.11 = (bf16[2,64,1024]{2,1,0:T(8,128)(2,1)S(1)}, bf16[2,64,1024]{2,1,0:T(8,128)(2,1)S(1)}, u32[]{:S(2)}, u32[]{:S(2)}) collective-permute-start(bf16[2,64,1024]{2,1,0:T(8,128)(2,1)S(1)} %collective-permute-done.10), channel_id=1, source_target_pairs={{0,8},{1,9},{2,2},{3,3},{4,28},{5,29},{6,22},{7,23},{8,0},{9,1},{1... | collective-permute-start | bytes 786440 | tf_op jit(solution)/shard_map/ppermute | solution.py:236
  52.3 18.1 %collective-permute-start.13 = (bf16[2,64,1024]{2,1,0:T(8,128)(2,1)S(1)}, bf16[2,64,1024]{2,1,0:T(8,128)(2,1)S(1)}, u32[]{:S(2)}, u32[]{:S(2)}) collective-permute-start(bf16[2,64,1024]{2,1,0:T(8,128)(2,1)S(1)} %collective-permute-done.12), channel_id=1, source_target_pairs={{0,16},{1,17},{2,26},{3,27},{4,4},{5,5},{6,14},{7,15},{8,24},{9,25... | collective-permute-start | bytes 786440 | tf_op jit(solution)/shard_map/ppermute | solution.py:236
  54.2 16.2 %collective-permute-start.15 = (bf16[2,64,1024]{2,1,0:T(8,128)(2,1)S(1)}, bf16[2,64,1024]{2,1,0:T(8,128)(2,1)S(1)}, u32[]{:S(2)}, u32[]{:S(2)}) collective-permute-start(bf16[2,64,1024]{2,1,0:T(8,128)(2,1)S(1)} %collective-permute-done.14), channel_id=1, source_target_pairs={{0,24},{1,25},{2,18},{3,19},{4,12},{5,13},{6,6},{7,7},{8,16},{9,17... | collective-permute-start | bytes 786440 | tf_op jit(solution)/shard_map/ppermute | solution.py:236
  56.9 13.5 %collective-permute-start.9 = (bf16[2,64,1024]{2,1,0:T(8,128)(2,1)S(1)}, bf16[2,64,1024]{2,1,0:T(8,128)(2,1)S(1)}, u32[]{:S(2)}, u32[]{:S(2)}) collective-permute-start(bf16[2,64,1024]{2,1,0:T(8,128)(2,1)S(1)} %collective-permute-done.8), channel_id=1, source_target_pairs={{0,0},{1,1},{2,10},{3,11},{4,20},{5,21},{6,30},{7,31},{8,8},{9,9},... | collective-permute-start | bytes 786440 | tf_op jit(solution)/shard_map/ppermute | solution.py:236

commit v2 on v1

v2 whole, which is shorter than its diff:
```python
import functools

import jax
import jax.numpy as jnp
from jax import lax
from jax.experimental import pallas as pl
from jax.experimental.pallas import tpu as pltpu
from jax.sharding import PartitionSpec as P

BLOCK = 64
SLOTS = 4
LANES = 128
ACTIVE = SLOTS * BLOCK
CHUNKS = 2
VMEM = pltpu.VMEM
SMEM = pltpu.SMEM
BF16 = jnp.bfloat16
F32 = jnp.float32


def spec(space):
    return pl.BlockSpec(memory_space=space)


def params(mib):
    return pltpu.CompilerParams(vmem_limit_bytes=mib << 20)


def cost(flops, nbytes):
    return pl.CostEstimate(flops=flops, bytes_accessed=nbytes, transcendentals=0)


def place():
    tok = lax.axis_index("tok")
    return lax.axis_index("feat"), tok >> 1, tok & 1


def center_kernel(groups, wslice, chunks, tok_ref, bias_ref, *outs):
    _, c, k = place()
    rows = tok_ref.shape[0] // chunks
    for h in range(chunks):
        for p in range(groups):
            for half in range(2):
                u = ((c ^ p) << 1) + (k ^ half)
                cols = pl.ds(pl.multiple_of(u * wslice, wslice), wslice)
                value = tok_ref[h * rows : (h + 1) * rows, cols].astype(F32)
                value -= bias_ref[pl.ds(u, 1), :]
                outs[h * groups + p][half] = value.astype(BF16)


def pick_pair(first, second, odd_first, odd_second):
    low = lax.broadcasted_iota(jnp.int32, first.shape, 1) < BLOCK
    a = jnp.where(odd_first, pltpu.roll(first, BLOCK, 1), first)
    b = jnp.where(odd_second, second, pltpu.roll(second, BLOCK, 1))
    return jnp.where(low, a, b)


def columns_kernel(groups, ids_ref, w_ref, out_ref):
    _, c, k = place()
    for p in range(groups):
        tile = ((c ^ p) << 1) + k
        for pair in range(SLOTS // 2):
            windows = []
            odds = []
            for slot in (2 * pair, 2 * pair + 1):
                block = ids_ref[tile, slot]
                start = pl.multiple_of((block >> 1) * LANES, LANES)
                windows.append(w_ref[:, pl.ds(start, LANES)])
                odds.append((block & 1) == 1)
            picked = pick_pair(windows[0].astype(F32), windows[1].astype(F32), *odds)
            out_ref[p, :, pair * LANES : (pair + 1) * LANES] = picked.astype(BF16)


def rows_kernel(groups, ids_ref, own_ref, oth_ref, own_rows, oth_rows, sems):
    _, c, k = place()
    copies = []
    for p in range(groups):
        tile = ((c ^ p) << 1) + k
        for slot in range(SLOTS):
            rows = pl.ds(pl.multiple_of(ids_ref[tile, slot] * BLOCK, BLOCK), BLOCK)
            into = pl.ds(slot * BLOCK, BLOCK)
            for which, (src, dst) in enumerate(((own_ref, own_rows), (oth_ref, oth_rows))):
                copy = pltpu.make_async_copy(
                    src.at[rows, :], dst.at[p, into, :], sems.at[p, slot, which]
                )
                copy.start()
                copies.append(copy)
    for copy in copies:
        copy.wait()


def encode_kernel(groups, *refs):
    pieces, (own_ref, oth_ref, out_ref) = refs[:groups], refs[groups:]
    for p in range(groups):
        acc = jnp.dot(pieces[p][0], own_ref[p], preferred_element_type=F32)
        acc += jnp.dot(pieces[p][1], oth_ref[p], preferred_element_type=F32)
        out_ref[p] = acc.astype(BF16)


def decode_kernel(groups, *refs):
    ids_ref, counts_ref, bias_ref = refs[:3]
    parts = refs[3 : 3 + groups]
    own_rows, oth_rows = refs[3 + groups : 5 + groups]
    code_ref = refs[5 + groups]
    outs = refs[6 + groups :]
    _, c, k = place()
    lane = lax.broadcasted_iota(jnp.int32, (1, LANES), 1)
    for p in range(groups):
        tile = ((c ^ p) << 1) + k
        count = counts_ref[tile]
        code = []
        for pair in range(SLOTS // 2):
            cols = slice(pair * LANES, (pair + 1) * LANES)
            pre = parts[0][p, :, cols].astype(F32)
            for q in range(1, groups):
                pre += parts[q][p ^ q, :, cols].astype(F32)
            bias = []
            odds = []
            for slot in (2 * pair, 2 * pair + 1):
                block = ids_ref[tile, slot]
                bias.append(bias_ref[pl.ds(block >> 1, 1), :])
                odds.append((block & 1) == 1)
            row = pick_pair(bias[0], bias[1], *odds)
            live = (lane >= BLOCK).astype(jnp.int32) + 2 * pair < count
            value = jnp.where(live, jnp.maximum(pre + row, 0.0), 0.0).astype(BF16)
            code.append(value)
        code = jnp.concatenate(code, axis=1)
        if p == 0:
            code_ref[...] = code
        outs[p][k] = jnp.dot(code, own_rows[p], preferred_element_type=F32).astype(BF16)
        outs[p][1 - k] = jnp.dot(code, oth_rows[p], preferred_element_type=F32).astype(BF16)


def route_kernel(groups, *refs):
    came, outs, held = refs[:groups], refs[groups : 2 * groups], refs[2 * groups]
    f, c, _ = place()
    for p in range(groups):
        held[p] = came[p][...]
    for m in range(groups):
        outs[m][...] = held[c ^ f ^ m]


def finish_kernel(groups, chunks, *refs):
    arrived, (bias_ref, out_ref) = refs[: groups * chunks], refs[groups * chunks :]
    f, _, _ = place()
    _, rows, wslice = arrived[0].shape
    for h in range(chunks):
        for half in range(2):
            total = arrived[h * groups][half].astype(F32)
            for ref in arrived[h * groups + 1 : (h + 1) * groups]:
                total += ref[half].astype(F32)
            total += bias_ref[pl.ds(2 * f + half, 1), :]
            out_ref[h * rows : (h + 1) * rows, half * wslice : (half + 1) * wslice] = (
                total.astype(BF16)
            )


def on_device(tokens, dec_bias, enc_weight, enc_bias, dec_weight, block_ids, block_counts):
    tile_count = lax.axis_size("tok")
    groups = lax.axis_size("feat")
    tok_rows, width = tokens.shape
    wslice = width // tile_count
    feats = enc_weight.shape[1]
    rows = tok_rows // CHUNKS
    ids = block_ids[:, 0, :]
    counts = block_counts[:, 0]
    bias_rows = dec_bias.astype(F32).reshape(tile_count, wslice)
    enc_bias_rows = enc_bias.astype(F32).reshape(feats // LANES, LANES)

    def swap(value, p):
        pairs = [(i, i ^ (2 * p)) for i in range(tile_count)]
        return lax.ppermute(value, "tok", pairs)

    def lift(value, m):
        return lax.ppermute(value, "feat", [(i, i ^ m) for i in range(groups)])

    cores = [(i, i ^ 1) for i in range(tile_count)]
    enc_other = lax.ppermute(enc_weight, "tok", cores)
    dec_other = lax.ppermute(dec_weight, "tok", cores)

    piece = jax.ShapeDtypeStruct((2, rows, wslice), BF16)
    sent = pl.pallas_call(
        functools.partial(center_kernel, groups, wslice, CHUNKS),
        out_shape=[piece] * (groups * CHUNKS),
        in_specs=[spec(VMEM)] * 2,
        out_specs=[spec(VMEM)] * (groups * CHUNKS),
        compiler_params=params(8),
        cost_estimate=cost(width * tok_rows, 4 * width * tok_rows),
        name="center",
    )(tokens, bias_rows)

    def columns(weight):
        return pl.pallas_call(
            functools.partial(columns_kernel, groups),
            out_shape=jax.ShapeDtypeStruct((groups, wslice, ACTIVE), BF16),
            in_specs=[spec(SMEM), spec(VMEM)],
            out_specs=spec(VMEM),
            compiler_params=params(8),
            cost_estimate=cost(0, 2 * wslice * (feats + groups * ACTIVE)),
            name="columns",
        )(ids, weight)

    own_cols = columns(enc_weight)
    oth_cols = columns(enc_other)

    listed = jax.ShapeDtypeStruct((groups, ACTIVE, wslice), BF16)
    own_rows, oth_rows = pl.pallas_call(
        functools.partial(rows_kernel, groups),
        out_shape=[listed] * 2,
        in_specs=[spec(SMEM)] + [spec(pl.ANY)] * 2,
        out_specs=[spec(VMEM)] * 2,
        scratch_shapes=[pltpu.SemaphoreType.DMA((groups, SLOTS, 2))],
        compiler_params=params(8),
        cost_estimate=cost(0, 8 * groups * ACTIVE * wslice),
        name="rows",
    )(ids, dec_weight, dec_other)

    flops = 4 * groups * rows * wslice * ACTIVE
    codes = []
    arrived = []
    for h in range(CHUNKS):
        first = sent[h * groups : (h + 1) * groups]
        pieces = [first[0]] + [swap(first[p], p) for p in range(1, groups)]
        part = pl.pallas_call(
            functools.partial(encode_kernel, groups),
            out_shape=jax.ShapeDtypeStruct((groups, rows, ACTIVE), BF16),
            in_specs=[spec(VMEM)] * (groups + 2),
            out_specs=spec(VMEM),
            compiler_params=params(8),
            cost_estimate=cost(flops, 4 * groups * wslice * ACTIVE),
            name="encode",
        )(*pieces, own_cols, oth_cols)
        parts = [part] + [swap(part, p) for p in range(1, groups)]
        decoded = pl.pallas_call(
            functools.partial(decode_kernel, groups),
            out_shape=[jax.ShapeDtypeStruct((rows, ACTIVE), BF16)] + [piece] * groups,
            in_specs=[spec(SMEM)] * 2 + [spec(VMEM)] * (3 + groups),
            out_specs=[spec(VMEM)] * (1 + groups),
            compiler_params=params(8),
            cost_estimate=cost(flops, 4 * groups * wslice * ACTIVE),
            name="decode",
        )(ids, counts, enc_bias_rows, *parts, own_rows, oth_rows)
        codes.append(decoded[0])
        came = [decoded[1]] + [swap(decoded[1 + p], p) for p in range(1, groups)]
        routed = pl.pallas_call(
            functools.partial(route_kernel, groups),
            out_shape=[piece] * groups,
            in_specs=[spec(VMEM)] * groups,
            out_specs=[spec(VMEM)] * groups,
            scratch_shapes=[VMEM((groups, 2, rows, wslice), BF16)],
            compiler_params=params(8),
            cost_estimate=cost(0, 8 * groups * rows * wslice),
            name="route",
        )(*came)
        arrived += [routed[0]] + [lift(routed[m], m) for m in range(1, groups)]

    rebuilt = pl.pallas_call(
        functools.partial(finish_kernel, groups, CHUNKS),
        out_shape=jax.ShapeDtypeStruct((tok_rows, 2 * wslice), BF16),
        in_specs=[spec(VMEM)] * (groups * CHUNKS + 1),
        out_specs=spec(VMEM),
        compiler_params=params(8),
        cost_estimate=cost(0, 4 * (groups + 1) * tok_rows * wslice),
        name="finish",
    )(*arrived, bias_rows)
    return (jnp.concatenate(codes, axis=0), rebuilt)


def solution(mesh):
    in_specs = (
        P("tok", None),
        P(),
        P("tok", "feat"),
        P("feat"),
        P("feat", "tok"),
        P(None, "feat", None),
        P(None, "feat"),
    )
    out_specs = (P("tok", "feat"), P("tok", "feat"))
    return jax.shard_map(
        on_device, mesh=mesh, in_specs=in_specs, out_specs=out_specs, check_vma=False
    )
```

time: 72.1 us -> 73.4 us (1.018)
  waiting for transfers between devices: 23.2 us -> 14.6 us
  starting transfers between devices: 27.3 us -> 34.9 us
  Pallas kernels: 15.1 us -> 17.4 us
    ppermute x6 -> x18, starting transfers between devices: 8.07 us -> 23.1 us  [swap(): return lax.ppermute(value, 'tok', pairs)]
    ppermute x8 -> x6, waiting for transfers between devices: 16.5 us -> 6.98 us  [lift(): return lax.ppermute(value, 'feat', [(i, i ^ m) for i in range(groups)])]
    ppermute x8 -> x6, starting transfers between devices: 18.6 us -> 11.2 us  [lift(): return lax.ppermute(value, 'feat', [(i, i ^ m) for i in range(groups)])]
    pallas_call x4 -> x7, Pallas kernels: 8.34 us -> 12.7 us  [the longest x2 6.88 us: columns(): pl.pallas_call(functools.partial(columns_kernel, groups), out_shape=jax.S...]
    pallas_call x1 -> x2, Pallas kernels: 5.42 us -> 2.99 us  [on_device(): pl.pallas_call(functools.partial(decode_kernel, groups), out_shape=[jax.S...]
    ppermute x6 -> x18, waiting for transfers between devices: 6.68 us -> 7.56 us  [swap(): return lax.ppermute(value, 'tok', pairs)]
    pallas_call x1 -> x2, Pallas kernels: 1.31 us -> 1.64 us  [on_device(): pl.pallas_call(functools.partial(encode_kernel, groups), out_shape=jax.Sh...]
  transfers between devices with their start and end apart: 16 -> 26, of which waited for: 5 -> 5; matrix products, arithmetic and copies ran while one was open for 2% -> 3% of each run, Pallas kernels for 12% -> 23%
where the time goes in v2:
time: 73.4 us; the launch traced here: 73.1 us
  starting transfers between devices  34.9 us (48%)
  Pallas kernels  17.4 us (24%)
  waiting for transfers between devices  14.6 us (20%)
  local copies, waits for them, and re-layouts  4.91 us (7%)
  between operations  0.78 us (1%)
    ppermute x18, starting transfers between devices, swap(): return lax.ppermute(value, 'tok', pairs)  23.1 us
    ppermute x6, starting transfers between devices, lift(): return lax.ppermute(value, 'feat', [(i, i ^ m) for i in range(groups)])  11.2 us
    ppermute x18, waiting for transfers between devices, swap(): return lax.ppermute(value, 'tok', pairs)  7.56 us
    ppermute x6, waiting for transfers between devices, lift(): return lax.ppermute(value, 'feat', [(i, i ^ m) for i in range(groups)])  6.98 us
    pallas_call x2, Pallas kernels, columns(): pl.pallas_call(functools.partial(columns_kernel, groups), out_shape=jax.S...  6.88 us
    pallas_call x1, Pallas kernels, on_device(): pl.pallas_call(functools.partial(rows_kernel, groups), out_shape=[listed]...  4.65 us
    unnamed x10, local copies, waits for them, and re-layouts  3.43 us
    pallas_call x2, Pallas kernels, on_device(): pl.pallas_call(functools.partial(decode_kernel, groups), out_shape=[jax.S...  2.99 us
  transfers between devices with their start and end apart: 26, of which 5 were waited for; matrix products, arithmetic and copies ran while one was open for 3% of the time, Pallas kernels for 23%

profile of v2, /device:TPU:0, one launch (start us, length us, event | category | flops | bytes accessed | tf_op | source)
XLA Modules:
  0.0 73.1 jit_solution(8652863746342730618)
XLA Ops:
  2.0 1.2 %copy-done.2 = bf16[64,8192]{1,0:T(8,128)(2,1)S(1)} copy-done((bf16[64,8192]{1,0:T(8,128)(2,1)S(1)}, bf16[64,8192]{1,0:T(8,128)(2,1)}, u32[]{:S(2)}) %copy-start.2) | copy-done | bytes 1048600
  3.4 3.0 %collective-permute-start.8 = (bf16[2,32,1024]{2,1,0:T(8,128)(2,1)S(1)}, bf16[2,32,1024]{2,1,0:T(8,128)(2,1)S(1)}, u32[]{:S(2)}, u32[]{:S(2)}) collective-permute-start(bf16[2,32,1024]{2,1,0:T(8,128)(2,1)S(1)} %get-tuple-element.38), channel_id=1, source_target_pairs={{0,2},{1,3},{2,0},{3,1},{4,6},{5,7},{6,4},{7,5},{8,10},{9,11},{10,... | collective-permute-start | bytes 393224 | tf_op jit(solution)/shard_map/ppermute | solution.py:172
  6.4 1.5 %collective-permute-start.9 = (bf16[2,32,1024]{2,1,0:T(8,128)(2,1)S(1)}, bf16[2,32,1024]{2,1,0:T(8,128)(2,1)S(1)}, u32[]{:S(2)}, u32[]{:S(2)}) collective-permute-start(bf16[2,32,1024]{2,1,0:T(8,128)(2,1)S(1)} %get-tuple-element.39), channel_id=1, source_target_pairs={{0,4},{1,5},{2,6},{3,7},{4,0},{5,1},{6,2},{7,3},{8,12},{9,13},{10,... | collective-permute-start | bytes 393224 | tf_op jit(solution)/shard_map/ppermute | solution.py:172
  7.9 2.3 %collective-permute-done.8.refs_1_ = bf16[2,32,1024]{2,1,0:T(8,128)(2,1)S(1)} collective-permute-done((bf16[2,32,1024]{2,1,0:T(8,128)(2,1)S(1)}, bf16[2,32,1024]{2,1,0:T(8,128)(2,1)S(1)}, u32[]{:S(2)}, u32[]{:S(2)}) %collective-permute-start.8) | collective-permute-done | bytes 131104 | tf_op jit(solution)/shard_map/ppermute | solution.py:172
  10.2 2.5 %collective-permute-start = (bf16[2,32,1024]{2,1,0:T(8,128)(2,1)S(1)}, bf16[2,32,1024]{2,1,0:T(8,128)(2,1)S(1)}, u32[]{:S(2)}, u32[]{:S(2)}) collective-permute-start(bf16[2,32,1024]{2,1,0:T(8,128)(2,1)S(1)} %get-tuple-element.31), channel_id=1, source_target_pairs={{0,2},{1,3},{2,0},{3,1},{4,6},{5,7},{6,4},{7,5},{8,10},{9,11},{10,... | collective-permute-start | bytes 393224 | tf_op jit(solution)/shard_map/ppermute | solution.py:172
  12.7 1.5 %collective-permute-start.1 = (bf16[2,32,1024]{2,1,0:T(8,128)(2,1)S(1)}, bf16[2,32,1024]{2,1,0:T(8,128)(2,1)S(1)}, u32[]{:S(2)}, u32[]{:S(2)}) collective-permute-start(bf16[2,32,1024]{2,1,0:T(8,128)(2,1)S(1)} %get-tuple-element.32), channel_id=1, source_target_pairs={{0,4},{1,5},{2,6},{3,7},{4,0},{5,1},{6,2},{7,3},{8,12},{9,13},{10,... | collective-permute-start | bytes 393224 | tf_op jit(solution)/shard_map/ppermute | solution.py:172
  15.0 2.2 %copy-done = bf16[1024,2048]{1,0:T(8,128)(2,1)S(1)} copy-done((bf16[1024,2048]{1,0:T(8,128)(2,1)S(1)}, bf16[1024,2048]{1,0:T(8,128)(2,1)}, u32[]{:S(2)}) %copy-start) | copy-done | bytes 4194328
  17.2 2.6 %columns.2.refs_4_ = bf16[4,1024,256]{2,1,0:T(8,128)(2,1)S(1)} custom-call(s32[8,4]{1,0:T(8,128)S(1)} %copy.12.ids_ref.refs_0_, bf16[1024,2048]{1,0:T(8,128)(2,1)S(1)} %copy-done), custom_call_target="tpu_custom_call" | custom-call | bytes 6291456 | tf_op jit(solution)/shard_map/columns/pallas_call | solution.py:193
  19.8 4.3 %columns.3.refs_5_ = bf16[4,1024,256]{2,1,0:T(8,128)(2,1)S(1)} custom-call(s32[8,4]{1,0:T(8,128)S(1)} %copy.12.ids_ref.refs_0_, bf16[1024,2048]{1,0:T(8,128)(2,1)} %collective-permute-done.3.w_ref), custom_call_target="tpu_custom_call" | custom-call | bytes 6291456 | tf_op jit(solution)/shard_map/columns/pallas_call | solution.py:193
  24.2 0.8 %encode.3.refs_3_ = bf16[4,32,256]{2,1,0:T(8,128)(2,1)S(1)} custom-call(bf16[2,32,1024]{2,1,0:T(8,128)(2,1)S(1)} %get-tuple-element.37.refs_0_, bf16[2,32,1024]{2,1,0:T(8,128)(2,1)S(1)} %collective-permute-done.8.refs_1_, bf16[2,32,1024]{2,1,0:T(8,128)(2,1)S(1)} %collective-permute-done.9.refs_2_, bf16[2,32,1024]{2,1,0:T(8,128)(2,1)S(1)} %collective-permute-done.10.refs_3_, ...), custom_call_target="tpu_custom_call" | custom-call | flops 134217728 | bytes 4194304 | tf_op jit(solution)/shard_map/encode/pallas_call | solution.py:224
  25.0 2.9 %collective-permute-start.13 = (bf16[4,32,256]{2,1,0:T(8,128)(2,1)S(1)}, bf16[4,32,256]{2,1,0:T(8,128)(2,1)S(1)}, u32[]{:S(2)}, u32[]{:S(2)}) collective-permute-start(bf16[4,32,256]{2,1,0:T(8,128)(2,1)S(1)} %encode.3.refs_3_), channel_id=1, source_target_pairs={{0,6},{1,7},{2,4},{3,5},{4,2},{5,3},{6,0},{7,1},{8,14},{9,15},{10,... | collective-permute-start | bytes 196616 | tf_op jit(solution)/shard_map/ppermute | solution.py:172
  28.6 2.1 %collective-permute-done.2.refs_3_ = bf16[2,32,1024]{2,1,0:T(8,128)(2,1)S(1)} collective-permute-done((bf16[2,32,1024]{2,1,0:T(8,128)(2,1)S(1)}, bf16[2,32,1024]{2,1,0:T(8,128)(2,1)S(1)}, u32[]{:S(2)}, u32[]{:S(2)}) %collective-permute-start.2) | collective-permute-done | bytes 131104 | tf_op jit(solution)/shard_map/ppermute | solution.py:172
  30.7 0.8 %encode.2.refs_3_ = bf16[4,32,256]{2,1,0:T(8,128)(2,1)S(1)} custom-call(bf16[2,32,1024]{2,1,0:T(8,128)(2,1)S(1)} %get-tuple-element.30.refs_0_, bf16[2,32,1024]{2,1,0:T(8,128)(2,1)S(1)} %collective-permute-done.refs_1_, bf16[2,32,1024]{2,1,0:T(8,128)(2,1)S(1)} %collective-permute-done.1.refs_2_, bf16[2,32,1024]{2,1,0:T(8,128)(2,1)S(1)} %collective-permute-done.2.refs_3_, ...), custom_call_target="tpu_custom_call" | custom-call | flops 134217728 | bytes 4194304 | tf_op jit(solution)/shard_map/encode/pallas_call | solution.py:224
  32.4 4.7 %rows.1 = (bf16[4,256,1024]{2,1,0:T(8,128)(2,1)S(1)}, bf16[4,256,1024]{2,1,0:T(8,128)(2,1)S(1)}) custom-call(s32[8,4]{1,0:T(8,128)S(1)} %copy.12.ids_ref.refs_0_, bf16[2048,1024]{1,0:T(8,128)(2,1)S(1)} %copy-done.1, bf16[2048,1024]{1,0:T(8,128)(2,1)} %collective-permute-done.7.oth_ref), custom_call_target="tpu_custom_call" | custom-call | bytes 8388608 | tf_op jit(solution)/shard_map/rows/pallas_call | solution.py:207
  37.1 1.5 %decode.3 = (bf16[32,256]{1,0:T(8,128)(2,1)S(1)}, bf16[2,32,1024]{2,1,0:T(8,128)(2,1)S(1)}, bf16[2,32,1024]{2,1,0:T(8,128)(2,1)S(1)}, bf16[2,32,1024]{2,1,0:T(8,128)(2,1)S(1)}, bf16[2,32,1024]{2,1,0:T(8,128)(2,1)S(1)}) custom-call(s32[8,4]{1,0:T(8,128)S(1)} %copy.12.ids_ref.refs_0_, s32[8]{0:T(128)S(1)} %bitcast.5, ...), custom_call_target="tpu_custom_call" | custom-call | flops 134217728 | bytes 4194304 | tf_op jit(solution)/shard_map/decode/pallas_call | solution.py:234
  38.6 1.3 %collective-permute-start.20 = (bf16[2,32,1024]{2,1,0:T(8,128)(2,1)S(1)}, bf16[2,32,1024]{2,1,0:T(8,128)(2,1)S(1)}, u32[]{:S(2)}, u32[]{:S(2)}) collective-permute-start(bf16[2,32,1024]{2,1,0:T(8,128)(2,1)S(1)} %get-tuple-element.51), channel_id=1, source_target_pairs={{0,2},{1,3},{2,0},{3,1},{4,6},{5,7},{6,4},{7,5},{8,10},{9,11},{10,... | collective-permute-start | bytes 393224 | tf_op jit(solution)/shard_map/ppermute | solution.py:172
  39.9 1.5 %collective-permute-start.21 = (bf16[2,32,1024]{2,1,0:T(8,128)(2,1)S(1)}, bf16[2,32,1024]{2,1,0:T(8,128)(2,1)S(1)}, u32[]{:S(2)}, u32[]{:S(2)}) collective-permute-start(bf16[2,32,1024]{2,1,0:T(8,128)(2,1)S(1)} %get-tuple-element.52), channel_id=1, source_target_pairs={{0,4},{1,5},{2,6},{3,7},{4,0},{5,1},{6,2},{7,3},{8,12},{9,13},{10,... | collective-permute-start | bytes 393224 | tf_op jit(solution)/shard_map/ppermute | solution.py:172
  42.1 0.8 %collective-permute-start.5 = (bf16[4,32,256]{2,1,0:T(8,128)(2,1)S(1)}, bf16[4,32,256]{2,1,0:T(8,128)(2,1)S(1)}, u32[]{:S(2)}, u32[]{:S(2)}) collective-permute-start(bf16[4,32,256]{2,1,0:T(8,128)(2,1)S(1)} %encode.2.refs_3_), channel_id=1, source_target_pairs={{0,4},{1,5},{2,6},{3,7},{4,0},{5,1},{6,2},{7,3},{8,12},{9,13},{10,... | collective-permute-start | bytes 196616 | tf_op jit(solution)/shard_map/ppermute | solution.py:172
  42.9 1.9 %collective-permute-start.4 = (bf16[4,32,256]{2,1,0:T(8,128)(2,1)S(1)}, bf16[4,32,256]{2,1,0:T(8,128)(2,1)S(1)}, u32[]{:S(2)}, u32[]{:S(2)}) collective-permute-start(bf16[4,32,256]{2,1,0:T(8,128)(2,1)S(1)} %encode.2.refs_3_), channel_id=1, source_target_pairs={{0,2},{1,3},{2,0},{3,1},{4,6},{5,7},{6,4},{7,5},{8,10},{9,11},{10,... | collective-permute-start | bytes 196616 | tf_op jit(solution)/shard_map/ppermute | solution.py:172
  44.9 3.1 %collective-permute-done.5.refs_5_ = bf16[4,32,256]{2,1,0:T(8,128)(2,1)S(1)} collective-permute-done((bf16[4,32,256]{2,1,0:T(8,128)(2,1)S(1)}, bf16[4,32,256]{2,1,0:T(8,128)(2,1)S(1)}, u32[]{:S(2)}, u32[]{:S(2)}) %collective-permute-start.5) | collective-permute-done | bytes 65568 | tf_op jit(solution)/shard_map/ppermute | solution.py:172
  47.9 1.5 %decode.2 = (bf16[32,256]{1,0:T(8,128)(2,1)S(1)}, bf16[2,32,1024]{2,1,0:T(8,128)(2,1)S(1)}, bf16[2,32,1024]{2,1,0:T(8,128)(2,1)S(1)}, bf16[2,32,1024]{2,1,0:T(8,128)(2,1)S(1)}, bf16[2,32,1024]{2,1,0:T(8,128)(2,1)S(1)}) custom-call(s32[8,4]{1,0:T(8,128)S(1)} %copy.12.ids_ref.refs_0_, s32[8]{0:T(128)S(1)} %bitcast.6, ...), custom_call_target="tpu_custom_call" | custom-call | flops 134217728 | bytes 4194304 | tf_op jit(solution)/shard_map/decode/pallas_call | solution.py:234
  49.4 1.5 %collective-permute-start.14 = (bf16[2,32,1024]{2,1,0:T(8,128)(2,1)S(1)}, bf16[2,32,1024]{2,1,0:T(8,128)(2,1)S(1)}, u32[]{:S(2)}, u32[]{:S(2)}) collective-permute-start(bf16[2,32,1024]{2,1,0:T(8,128)(2,1)S(1)} %get-tuple-element.43), channel_id=1, source_target_pairs={{0,2},{1,3},{2,0},{3,1},{4,6},{5,7},{6,4},{7,5},{8,10},{9,11},{10,... | collective-permute-start | bytes 393224 | tf_op jit(solution)/shard_map/ppermute | solution.py:172
  50.9 0.9 %collective-permute-start.15 = (bf16[2,32,1024]{2,1,0:T(8,128)(2,1)S(1)}, bf16[2,32,1024]{2,1,0:T(8,128)(2,1)S(1)}, u32[]{:S(2)}, u32[]{:S(2)}) collective-permute-start(bf16[2,32,1024]{2,1,0:T(8,128)(2,1)S(1)} %get-tuple-element.44), channel_id=1, source_target_pairs={{0,4},{1,5},{2,6},{3,7},{4,0},{5,1},{6,2},{7,3},{8,12},{9,13},{10,... | collective-permute-start | bytes 393224 | tf_op jit(solution)/shard_map/ppermute | solution.py:172
  51.9 1.4 %collective-permute-start.16 = (bf16[2,32,1024]{2,1,0:T(8,128)(2,1)S(1)}, bf16[2,32,1024]{2,1,0:T(8,128)(2,1)S(1)}, u32[]{:S(2)}, u32[]{:S(2)}) collective-permute-start(bf16[2,32,1024]{2,1,0:T(8,128)(2,1)S(1)} %get-tuple-element.45), channel_id=1, source_target_pairs={{0,6},{1,7},{2,4},{3,5},{4,2},{5,3},{6,0},{7,1},{8,14},{9,15},{10,... | collective-permute-start | bytes 393224 | tf_op jit(solution)/shard_map/ppermute | solution.py:172
  53.4 1.6 %collective-permute-start.23 = (bf16[2,32,1024]{2,1,0:T(8,128)(2,1)S(1)}, bf16[2,32,1024]{2,1,0:T(8,128)(2,1)S(1)}, u32[]{:S(2)}, u32[]{:S(2)}) collective-permute-start(bf16[2,32,1024]{2,1,0:T(8,128)(2,1)S(1)} %get-tuple-element.55), channel_id=1, source_target_pairs={{0,8},{8,0},{16,24},{24,16},{1,9},{9,1},{17,25},{25,17},{2,10},{10... | collective-permute-start | bytes 393224 | tf_op jit(solution)/shard_map/ppermute | solution.py:175
  55.0 2.6 %collective-permute-start.24 = (bf16[2,32,1024]{2,1,0:T(8,128)(2,1)S(1)}, bf16[2,32,1024]{2,1,0:T(8,128)(2,1)S(1)}, u32[]{:S(2)}, u32[]{:S(2)}) collective-permute-start(bf16[2,32,1024]{2,1,0:T(8,128)(2,1)S(1)} %get-tuple-element.56), channel_id=1, source_target_pairs={{0,16},{8,24},{16,0},{24,8},{1,17},{9,25},{17,1},{25,9},{2,18},{10... | collective-permute-start | bytes 393224 | tf_op jit(solution)/shard_map/ppermute | solution.py:175
  58.2 1.3 %collective-permute-start.17 = (bf16[2,32,1024]{2,1,0:T(8,128)(2,1)S(1)}, bf16[2,32,1024]{2,1,0:T(8,128)(2,1)S(1)}, u32[]{:S(2)}, u32[]{:S(2)}) collective-permute-start(bf16[2,32,1024]{2,1,0:T(8,128)(2,1)S(1)} %get-tuple-element.47), channel_id=1, source_target_pairs={{0,8},{8,0},{16,24},{24,16},{1,9},{9,1},{17,25},{25,17},{2,10},{10... | collective-permute-start | bytes 393224 | tf_op jit(solution)/shard_map/ppermute | solution.py:175
  59.4 2.6 %collective-permute-start.18 = (bf16[2,32,1024]{2,1,0:T(8,128)(2,1)S(1)}, bf16[2,32,1024]{2,1,0:T(8,128)(2,1)S(1)}, u32[]{:S(2)}, u32[]{:S(2)}) collective-permute-start(bf16[2,32,1024]{2,1,0:T(8,128)(2,1)S(1)} %get-tuple-element.48), channel_id=1, source_target_pairs={{0,16},{8,24},{16,0},{24,8},{1,17},{9,25},{17,1},{25,9},{2,18},{10... | collective-permute-start | bytes 393224 | tf_op jit(solution)/shard_map/ppermute | solution.py:175
  62.1 2.5 %collective-permute-start.19 = (bf16[2,32,1024]{2,1,0:T(8,128)(2,1)S(1)}, bf16[2,32,1024]{2,1,0:T(8,128)(2,1)S(1)}, u32[]{:S(2)}, u32[]{:S(2)}) collective-permute-start(bf16[2,32,1024]{2,1,0:T(8,128)(2,1)S(1)} %get-tuple-element.49), channel_id=1, source_target_pairs={{0,24},{8,16},{16,8},{24,0},{1,25},{9,17},{17,9},{25,1},{2,26},{10... | collective-permute-start | bytes 393224 | tf_op jit(solution)/shard_map/ppermute | solution.py:175
  65.3 3.6 %collective-permute-done.24.refs_6_ = bf16[2,32,1024]{2,1,0:T(8,128)(2,1)S(1)} collective-permute-done((bf16[2,32,1024]{2,1,0:T(8,128)(2,1)S(1)}, bf16[2,32,1024]{2,1,0:T(8,128)(2,1)S(1)}, u32[]{:S(2)}, u32[]{:S(2)}) %collective-permute-start.24) | collective-permute-done | bytes 131104 | tf_op jit(solution)/shard_map/ppermute | solution.py:175
  68.9 3.3 %collective-permute-done.18.refs_2_ = bf16[2,32,1024]{2,1,0:T(8,128)(2,1)S(1)} collective-permute-done((bf16[2,32,1024]{2,1,0:T(8,128)(2,1)S(1)}, bf16[2,32,1024]{2,1,0:T(8,128)(2,1)S(1)}, u32[]{:S(2)}, u32[]{:S(2)}) %collective-permute-start.18) | collective-permute-done | bytes 131104 | tf_op jit(solution)/shard_map/ppermute | solution.py:175
  72.2 0.9 %finish.1 = bf16[64,2048]{1,0:T(8,128)(2,1)} custom-call(bf16[2,32,1024]{2,1,0:T(8,128)(2,1)S(1)} %get-tuple-element.46.refs_0_, bf16[2,32,1024]{2,1,0:T(8,128)(2,1)S(1)} %collective-permute-done.17.refs_1_, bf16[2,32,1024]{2,1,0:T(8,128)(2,1)S(1)} %collective-permute-done.18.refs_2_, bf16[2,32,1024]{2,1,0:T(8,128)(2,1)S(1)} %collective-permute-done.19.refs_3_, ...), custom_call_target="tpu_custom_call" | custom-call | bytes 1310720 | tf_op jit(solution)/shard_map/finish/pallas_call | solution.py:257
  (45 shorter events, 5.9 us)
Async XLA Ops:
  0.6 12.1 %collective-permute-start.3 = (bf16[1024,2048]{1,0:T(8,128)(2,1)}, bf16[1024,2048]{1,0:T(8,128)(2,1)}, u32[]{:S(2)}, u32[]{:S(2)}) collective-permute-start(bf16[1024,2048]{1,0:T(8,128)(2,1)} %w_ref.1), channel_id=1, source_target_pairs={{0,1},{1,0},{2,3},{3,2},{4,5},{5,4},{6,7},{7,6},{8,9},{9,8},{10,11... | collective-permute-start | bytes 12582920 | tf_op jit(solution)/shard_map/ppermute | solution.py:178
  1.1 31.2 %collective-permute-start.7 = (bf16[2048,1024]{1,0:T(8,128)(2,1)}, bf16[2048,1024]{1,0:T(8,128)(2,1)}, u32[]{:S(2)}, u32[]{:S(2)}) collective-permute-start(bf16[2048,1024]{1,0:T(8,128)(2,1)} %own_ref.1), channel_id=1, source_target_pairs={{0,1},{1,0},{2,3},{3,2},{4,5},{5,4},{6,7},{7,6},{8,9},{9,8},{10,11... | collective-permute-start | bytes 12582920 | tf_op jit(solution)/shard_map/ppermute | solution.py:179
  2.0 1.2 %copy-start.2 = (bf16[64,8192]{1,0:T(8,128)(2,1)S(1)}, bf16[64,8192]{1,0:T(8,128)(2,1)}, u32[]{:S(2)}) copy-start(bf16[64,8192]{1,0:T(8,128)(2,1)} %tok_ref.1) | copy-start | bytes 3145732
  3.4 6.8 %collective-permute-start.8 = (bf16[2,32,1024]{2,1,0:T(8,128)(2,1)S(1)}, bf16[2,32,1024]{2,1,0:T(8,128)(2,1)S(1)}, u32[]{:S(2)}, u32[]{:S(2)}) collective-permute-start(bf16[2,32,1024]{2,1,0:T(8,128)(2,1)S(1)} %get-tuple-element.38), channel_id=1, source_target_pairs={{0,2},{1,3},{2,0},{3,1},{4,6},{5,7},{6,4},{7,5},{8,10},{9,11},{10,... | collective-permute-start | bytes 393224 | tf_op jit(solution)/shard_map/ppermute | solution.py:172
  6.4 17.7 %collective-permute-start.9 = (bf16[2,32,1024]{2,1,0:T(8,128)(2,1)S(1)}, bf16[2,32,1024]{2,1,0:T(8,128)(2,1)S(1)}, u32[]{:S(2)}, u32[]{:S(2)}) collective-permute-start(bf16[2,32,1024]{2,1,0:T(8,128)(2,1)S(1)} %get-tuple-element.39), channel_id=1, source_target_pairs={{0,4},{1,5},{2,6},{3,7},{4,0},{5,1},{6,2},{7,3},{8,12},{9,13},{10,... | collective-permute-start | bytes 393224 | tf_op jit(solution)/shard_map/ppermute | solution.py:172
  7.9 16.3 %collective-permute-start.10 = (bf16[2,32,1024]{2,1,0:T(8,128)(2,1)S(1)}, bf16[2,32,1024]{2,1,0:T(8,128)(2,1)S(1)}, u32[]{:S(2)}, u32[]{:S(2)}) collective-permute-start(bf16[2,32,1024]{2,1,0:T(8,128)(2,1)S(1)} %get-tuple-element.40), channel_id=1, source_target_pairs={{0,6},{1,7},{2,4},{3,5},{4,2},{5,3},{6,0},{7,1},{8,14},{9,15},{10,... | collective-permute-start | bytes 393224 | tf_op jit(solution)/shard_map/ppermute | solution.py:172
  10.2 17.7 %collective-permute-start = (bf16[2,32,1024]{2,1,0:T(8,128)(2,1)S(1)}, bf16[2,32,1024]{2,1,0:T(8,128)(2,1)S(1)}, u32[]{:S(2)}, u32[]{:S(2)}) collective-permute-start(bf16[2,32,1024]{2,1,0:T(8,128)(2,1)S(1)} %get-tuple-element.31), channel_id=1, source_target_pairs={{0,2},{1,3},{2,0},{3,1},{4,6},{5,7},{6,4},{7,5},{8,10},{9,11},{10,... | collective-permute-start | bytes 393224 | tf_op jit(solution)/shard_map/ppermute | solution.py:172
  12.7 15.7 %collective-permute-start.1 = (bf16[2,32,1024]{2,1,0:T(8,128)(2,1)S(1)}, bf16[2,32,1024]{2,1,0:T(8,128)(2,1)S(1)}, u32[]{:S(2)}, u32[]{:S(2)}) collective-permute-start(bf16[2,32,1024]{2,1,0:T(8,128)(2,1)S(1)} %get-tuple-element.32), channel_id=1, source_target_pairs={{0,4},{1,5},{2,6},{3,7},{4,0},{5,1},{6,2},{7,3},{8,12},{9,13},{10,... | collective-permute-start | bytes 393224 | tf_op jit(solution)/shard_map/ppermute | solution.py:172
  15.0 2.2 %copy-start = (bf16[1024,2048]{1,0:T(8,128)(2,1)S(1)}, bf16[1024,2048]{1,0:T(8,128)(2,1)}, u32[]{:S(2)}) copy-start(bf16[1024,2048]{1,0:T(8,128)(2,1)} %w_ref.1) | copy-start | bytes 12582916
  19.8 8.8 %copy-start.4 = (bf16[2048]{0:T(1024)(128)(2,1)S(1)}, bf16[2048]{0:T(1024)(128)(2,1)}, u32[]{:S(2)}) copy-start(bf16[2048]{0:T(1024)(128)(2,1)} %param.10) | copy-start | bytes 12292
  24.1 6.6 %collective-permute-start.2 = (bf16[2,32,1024]{2,1,0:T(8,128)(2,1)S(1)}, bf16[2,32,1024]{2,1,0:T(8,128)(2,1)S(1)}, u32[]{:S(2)}, u32[]{:S(2)}) collective-permute-start(bf16[2,32,1024]{2,1,0:T(8,128)(2,1)S(1)} %get-tuple-element.33), channel_id=1, source_target_pairs={{0,6},{1,7},{2,4},{3,5},{4,2},{5,3},{6,0},{7,1},{8,14},{9,15},{10,... | collective-permute-start | bytes 393224 | tf_op jit(solution)/shard_map/ppermute | solution.py:172
  24.2 8.2 %copy-start.1 = (bf16[2048,1024]{1,0:T(8,128)(2,1)S(1)}, bf16[2048,1024]{1,0:T(8,128)(2,1)}, u32[]{:S(2)}) copy-start(bf16[2048,1024]{1,0:T(8,128)(2,1)} %own_ref.1) | copy-start | bytes 12582916
  25.0 12.0 %collective-permute-start.13 = (bf16[4,32,256]{2,1,0:T(8,128)(2,1)S(1)}, bf16[4,32,256]{2,1,0:T(8,128)(2,1)S(1)}, u32[]{:S(2)}, u32[]{:S(2)}) collective-permute-start(bf16[4,32,256]{2,1,0:T(8,128)(2,1)S(1)} %encode.3.refs_3_), channel_id=1, source_target_pairs={{0,6},{1,7},{2,4},{3,5},{4,2},{5,3},{6,0},{7,1},{8,14},{9,15},{10,... | collective-permute-start | bytes 196616 | tf_op jit(solution)/shard_map/ppermute | solution.py:172
  27.9 9.1 %collective-permute-start.12 = (bf16[4,32,256]{2,1,0:T(8,128)(2,1)S(1)}, bf16[4,32,256]{2,1,0:T(8,128)(2,1)S(1)}, u32[]{:S(2)}, u32[]{:S(2)}) collective-permute-start(bf16[4,32,256]{2,1,0:T(8,128)(2,1)S(1)} %encode.3.refs_3_), channel_id=1, source_target_pairs={{0,4},{1,5},{2,6},{3,7},{4,0},{5,1},{6,2},{7,3},{8,12},{9,13},{10,... | collective-permute-start | bytes 196616 | tf_op jit(solution)/shard_map/ppermute | solution.py:172
  28.4 8.6 %collective-permute-start.11 = (bf16[4,32,256]{2,1,0:T(8,128)(2,1)S(1)}, bf16[4,32,256]{2,1,0:T(8,128)(2,1)S(1)}, u32[]{:S(2)}, u32[]{:S(2)}) collective-permute-start(bf16[4,32,256]{2,1,0:T(8,128)(2,1)S(1)} %encode.3.refs_3_), channel_id=1, source_target_pairs={{0,2},{1,3},{2,0},{3,1},{4,6},{5,7},{6,4},{7,5},{8,10},{9,11},{10,... | collective-permute-start | bytes 196616 | tf_op jit(solution)/shard_map/ppermute | solution.py:172
  31.6 5.5 %copy-start.3 = (s32[8,1]{0,1:T(1,128)S(1)}, s32[8,1]{0,1:T(1,128)}, u32[]{:S(2)}) copy-start(s32[8,1]{0,1:T(1,128)} %param.13) | copy-start | bytes 100
  31.6 11.4 %collective-permute-start.6 = (bf16[4,32,256]{2,1,0:T(8,128)(2,1)S(1)}, bf16[4,32,256]{2,1,0:T(8,128)(2,1)S(1)}, u32[]{:S(2)}, u32[]{:S(2)}) collective-permute-start(bf16[4,32,256]{2,1,0:T(8,128)(2,1)S(1)} %encode.2.refs_3_), channel_id=1, source_target_pairs={{0,6},{1,7},{2,4},{3,5},{4,2},{5,3},{6,0},{7,1},{8,14},{9,15},{10,... | collective-permute-start | bytes 196616 | tf_op jit(solution)/shard_map/ppermute | solution.py:172
  38.6 13.3 %collective-permute-start.20 = (bf16[2,32,1024]{2,1,0:T(8,128)(2,1)S(1)}, bf16[2,32,1024]{2,1,0:T(8,128)(2,1)S(1)}, u32[]{:S(2)}, u32[]{:S(2)}) collective-permute-start(bf16[2,32,1024]{2,1,0:T(8,128)(2,1)S(1)} %get-tuple-element.51), channel_id=1, source_target_pairs={{0,2},{1,3},{2,0},{3,1},{4,6},{5,7},{6,4},{7,5},{8,10},{9,11},{10,... | collective-permute-start | bytes 393224 | tf_op jit(solution)/shard_map/ppermute | solution.py:172
  39.9 13.4 %collective-permute-start.21 = (bf16[2,32,1024]{2,1,0:T(8,128)(2,1)S(1)}, bf16[2,32,1024]{2,1,0:T(8,128)(2,1)S(1)}, u32[]{:S(2)}, u32[]{:S(2)}) collective-permute-start(bf16[2,32,1024]{2,1,0:T(8,128)(2,1)S(1)} %get-tuple-element.52), channel_id=1, source_target_pairs={{0,4},{1,5},{2,6},{3,7},{4,0},{5,1},{6,2},{7,3},{8,12},{9,13},{10,... | collective-permute-start | bytes 393224 | tf_op jit(solution)/shard_map/ppermute | solution.py:172
  41.4 11.9 %collective-permute-start.22 = (bf16[2,32,1024]{2,1,0:T(8,128)(2,1)S(1)}, bf16[2,32,1024]{2,1,0:T(8,128)(2,1)S(1)}, u32[]{:S(2)}, u32[]{:S(2)}) collective-permute-start(bf16[2,32,1024]{2,1,0:T(8,128)(2,1)S(1)} %get-tuple-element.53), channel_id=1, source_target_pairs={{0,6},{1,7},{2,4},{3,5},{4,2},{5,3},{6,0},{7,1},{8,14},{9,15},{10,... | collective-permute-start | bytes 393224 | tf_op jit(solution)/shard_map/ppermute | solution.py:172
  42.1 5.8 %collective-permute-start.5 = (bf16[4,32,256]{2,1,0:T(8,128)(2,1)S(1)}, bf16[4,32,256]{2,1,0:T(8,128)(2,1)S(1)}, u32[]{:S(2)}, u32[]{:S(2)}) collective-permute-start(bf16[4,32,256]{2,1,0:T(8,128)(2,1)S(1)} %encode.2.refs_3_), channel_id=1, source_target_pairs={{0,4},{1,5},{2,6},{3,7},{4,0},{5,1},{6,2},{7,3},{8,12},{9,13},{10,... | collective-permute-start | bytes 196616 | tf_op jit(solution)/shard_map/ppermute | solution.py:172
  42.9 5.0 %collective-permute-start.4 = (bf16[4,32,256]{2,1,0:T(8,128)(2,1)S(1)}, bf16[4,32,256]{2,1,0:T(8,128)(2,1)S(1)}, u32[]{:S(2)}, u32[]{:S(2)}) collective-permute-start(bf16[4,32,256]{2,1,0:T(8,128)(2,1)S(1)} %encode.2.refs_3_), channel_id=1, source_target_pairs={{0,2},{1,3},{2,0},{3,1},{4,6},{5,7},{6,4},{7,5},{8,10},{9,11},{10,... | collective-permute-start | bytes 196616 | tf_op jit(solution)/shard_map/ppermute | solution.py:172
  49.4 8.1 %collective-permute-start.14 = (bf16[2,32,1024]{2,1,0:T(8,128)(2,1)S(1)}, bf16[2,32,1024]{2,1,0:T(8,128)(2,1)S(1)}, u32[]{:S(2)}, u32[]{:S(2)}) collective-permute-start(bf16[2,32,1024]{2,1,0:T(8,128)(2,1)S(1)} %get-tuple-element.43), channel_id=1, source_target_pairs={{0,2},{1,3},{2,0},{3,1},{4,6},{5,7},{6,4},{7,5},{8,10},{9,11},{10,... | collective-permute-start | bytes 393224 | tf_op jit(solution)/shard_map/ppermute | solution.py:172
  50.9 7.2 %collective-permute-start.15 = (bf16[2,32,1024]{2,1,0:T(8,128)(2,1)S(1)}, bf16[2,32,1024]{2,1,0:T(8,128)(2,1)S(1)}, u32[]{:S(2)}, u32[]{:S(2)}) collective-permute-start(bf16[2,32,1024]{2,1,0:T(8,128)(2,1)S(1)} %get-tuple-element.44), channel_id=1, source_target_pairs={{0,4},{1,5},{2,6},{3,7},{4,0},{5,1},{6,2},{7,3},{8,12},{9,13},{10,... | collective-permute-start | bytes 393224 | tf_op jit(solution)/shard_map/ppermute | solution.py:172
  51.9 6.2 %collective-permute-start.16 = (bf16[2,32,1024]{2,1,0:T(8,128)(2,1)S(1)}, bf16[2,32,1024]{2,1,0:T(8,128)(2,1)S(1)}, u32[]{:S(2)}, u32[]{:S(2)}) collective-permute-start(bf16[2,32,1024]{2,1,0:T(8,128)(2,1)S(1)} %get-tuple-element.45), channel_id=1, source_target_pairs={{0,6},{1,7},{2,4},{3,5},{4,2},{5,3},{6,0},{7,1},{8,14},{9,15},{10,... | collective-permute-start | bytes 393224 | tf_op jit(solution)/shard_map/ppermute | solution.py:172
  53.4 8.7 %collective-permute-start.23 = (bf16[2,32,1024]{2,1,0:T(8,128)(2,1)S(1)}, bf16[2,32,1024]{2,1,0:T(8,128)(2,1)S(1)}, u32[]{:S(2)}, u32[]{:S(2)}) collective-permute-start(bf16[2,32,1024]{2,1,0:T(8,128)(2,1)S(1)} %get-tuple-element.55), channel_id=1, source_target_pairs={{0,8},{8,0},{16,24},{24,16},{1,9},{9,1},{17,25},{25,17},{2,10},{10... | collective-permute-start | bytes 393224 | tf_op jit(solution)/shard_map/ppermute | solution.py:175
  55.0 13.9 %collective-permute-start.24 = (bf16[2,32,1024]{2,1,0:T(8,128)(2,1)S(1)}, bf16[2,32,1024]{2,1,0:T(8,128)(2,1)S(1)}, u32[]{:S(2)}, u32[]{:S(2)}) collective-permute-start(bf16[2,32,1024]{2,1,0:T(8,128)(2,1)S(1)} %get-tuple-element.56), channel_id=1, source_target_pairs={{0,16},{8,24},{16,0},{24,8},{1,17},{9,25},{17,1},{25,9},{2,18},{10... | collective-permute-start | bytes 393224 | tf_op jit(solution)/shard_map/ppermute | solution.py:175
  57.6 11.3 %collective-permute-start.25 = (bf16[2,32,1024]{2,1,0:T(8,128)(2,1)S(1)}, bf16[2,32,1024]{2,1,0:T(8,128)(2,1)S(1)}, u32[]{:S(2)}, u32[]{:S(2)}) collective-permute-start(bf16[2,32,1024]{2,1,0:T(8,128)(2,1)S(1)} %get-tuple-element.57), channel_id=1, source_target_pairs={{0,24},{8,16},{16,8},{24,0},{1,25},{9,17},{17,9},{25,1},{2,26},{10... | collective-permute-start | bytes 393224 | tf_op jit(solution)/shard_map/ppermute | solution.py:175
  58.2 10.7 %collective-permute-start.17 = (bf16[2,32,1024]{2,1,0:T(8,128)(2,1)S(1)}, bf16[2,32,1024]{2,1,0:T(8,128)(2,1)S(1)}, u32[]{:S(2)}, u32[]{:S(2)}) collective-permute-start(bf16[2,32,1024]{2,1,0:T(8,128)(2,1)S(1)} %get-tuple-element.47), channel_id=1, source_target_pairs={{0,8},{8,0},{16,24},{24,16},{1,9},{9,1},{17,25},{25,17},{2,10},{10... | collective-permute-start | bytes 393224 | tf_op jit(solution)/shard_map/ppermute | solution.py:175
  59.4 12.8 %collective-permute-start.18 = (bf16[2,32,1024]{2,1,0:T(8,128)(2,1)S(1)}, bf16[2,32,1024]{2,1,0:T(8,128)(2,1)S(1)}, u32[]{:S(2)}, u32[]{:S(2)}) collective-permute-start(bf16[2,32,1024]{2,1,0:T(8,128)(2,1)S(1)} %get-tuple-element.48), channel_id=1, source_target_pairs={{0,16},{8,24},{16,0},{24,8},{1,17},{9,25},{17,1},{25,9},{2,18},{10... | collective-permute-start | bytes 393224 | tf_op jit(solution)/shard_map/ppermute | solution.py:175
  62.1 10.1 %collective-permute-start.19 = (bf16[2,32,1024]{2,1,0:T(8,128)(2,1)S(1)}, bf16[2,32,1024]{2,1,0:T(8,128)(2,1)S(1)}, u32[]{:S(2)}, u32[]{:S(2)}) collective-permute-start(bf16[2,32,1024]{2,1,0:T(8,128)(2,1)S(1)} %get-tuple-element.49), channel_id=1, source_target_pairs={{0,24},{8,16},{16,8},{24,0},{1,25},{9,17},{17,9},{25,1},{2,26},{10... | collective-permute-start | bytes 393224 | tf_op jit(solution)/shard_map/ppermute | solution.py:175

commit v3 on v2

v3 whole, which is shorter than its diff:
```python
import functools

import jax
import jax.numpy as jnp
from jax import lax
from jax.experimental import pallas as pl
from jax.experimental.pallas import tpu as pltpu
from jax.sharding import PartitionSpec as P

BLOCK = 64
SLOTS = 4
LANES = 128
ACTIVE = SLOTS * BLOCK
CHUNKS = 2
VMEM = pltpu.VMEM
SMEM = pltpu.SMEM
HBM = pltpu.HBM
BF16 = jnp.bfloat16
F32 = jnp.float32


def spec(space):
    return pl.BlockSpec(memory_space=space)


def params(mib):
    return pltpu.CompilerParams(vmem_limit_bytes=mib << 20)


def cost(flops, nbytes):
    return pl.CostEstimate(flops=flops, bytes_accessed=nbytes, transcendentals=0)


def pin(value):
    return pltpu.with_memory_space_constraint(value, HBM)


def place():
    tok = lax.axis_index("tok")
    return lax.axis_index("feat"), tok >> 1, tok & 1


def split_kernel(groups, tok_ref, *refs):
    outs, sems = refs[:-1], refs[-1]
    _, c, k = place()
    wslice = outs[0].shape[2]
    copies = []
    for p in range(groups):
        for half in range(2):
            u = ((c ^ p) << 1) + (k ^ half)
            cols = pl.ds(pl.multiple_of(u * wslice, wslice), wslice)
            copy = pltpu.make_async_copy(
                tok_ref.at[:, cols], outs[p].at[half], sems.at[p, half]
            )
            copy.start()
            copies.append(copy)
    for copy in copies:
        copy.wait()


def pick_pair(first, second, odd_first, odd_second):
    low = lax.broadcasted_iota(jnp.int32, first.shape, 1) < BLOCK
    a = jnp.where(odd_first, pltpu.roll(first, BLOCK, 1), first)
    b = jnp.where(odd_second, second, pltpu.roll(second, BLOCK, 1))
    return jnp.where(low, a, b)


def columns_kernel(groups, ids_ref, w_ref, out_ref):
    _, c, k = place()
    for p in range(groups):
        tile = ((c ^ p) << 1) + k
        for pair in range(SLOTS // 2):
            windows = []
            odds = []
            for slot in (2 * pair, 2 * pair + 1):
                block = ids_ref[tile, slot]
                start = pl.multiple_of((block >> 1) * LANES, LANES)
                windows.append(w_ref[:, pl.ds(start, LANES)])
                odds.append((block & 1) == 1)
            picked = pick_pair(windows[0].astype(F32), windows[1].astype(F32), *odds)
            out_ref[p, :, pair * LANES : (pair + 1) * LANES] = picked.astype(BF16)


def stage_kernel(src, dst, sems):
    parts = sems.shape[0]
    height = src.shape[0] // parts
    copies = []
    for i in range(parts):
        some = pl.ds(i * height, height)
        copy = pltpu.make_async_copy(src.at[some, :], dst.at[some, :], sems.at[i])
        copy.start()
        copies.append(copy)
    for copy in copies:
        copy.wait()


def encode_kernel(groups, *refs):
    bias_ref, pieces, (own_ref, oth_ref, out_ref) = refs[0], refs[1 : 1 + groups], refs[1 + groups :]
    _, c, k = place()
    bias = [bias_ref[pl.ds(2 * c + (k ^ half), 1), :] for half in range(2)]
    for p in range(groups):
        mine, other = [
            (pieces[p][half].astype(F32) - bias[half]).astype(BF16) for half in range(2)
        ]
        acc = jnp.dot(mine, own_ref[p], preferred_element_type=F32)
        acc += jnp.dot(other, oth_ref[p], preferred_element_type=F32)
        out_ref[p] = acc.astype(BF16)


def decode_kernel(groups, chunks, *refs):
    ids_ref, counts_ref, bias_ref = refs[:3]
    parts = refs[3 : 3 + groups]
    own_ref, oth_ref, code_ref = refs[3 + groups : 6 + groups]
    outs = refs[6 + groups :]
    _, c, k = place()
    lane = lax.broadcasted_iota(jnp.int32, (1, LANES), 1)
    for p in range(groups):
        tile = ((c ^ p) << 1) + k
        count = counts_ref[tile]
        code = []
        listed = []
        for pair in range(SLOTS // 2):
            cols = slice(pair * LANES, (pair + 1) * LANES)
            pre = parts[0][p, :, cols].astype(F32)
            for q in range(1, groups):
                pre += parts[q][p ^ q, :, cols].astype(F32)
            bias = []
            odds = []
            for slot in (2 * pair, 2 * pair + 1):
                block = ids_ref[tile, slot]
                listed.append(pl.ds(pl.multiple_of(block * BLOCK, BLOCK), BLOCK))
                bias.append(bias_ref[pl.ds(block >> 1, 1), :])
                odds.append((block & 1) == 1)
            row = pick_pair(bias[0], bias[1], *odds)
            live = (lane >= BLOCK).astype(jnp.int32) + 2 * pair < count
            value = jnp.where(live, jnp.maximum(pre + row, 0.0), 0.0).astype(BF16)
            code.append(value)
        code = jnp.concatenate(code, axis=1)
        if p == 0:
            code_ref[...] = code
        height = code.shape[0] // chunks
        for half, ref in ((k, own_ref), (1 - k, oth_ref)):
            rows = jnp.concatenate([ref[some, :] for some in listed], axis=0)
            result = jnp.dot(code, rows, preferred_element_type=F32).astype(BF16)
            for h in range(chunks):
                outs[h * groups + p][half] = result[h * height : (h + 1) * height]


def route_kernel(groups, *refs):
    came, (keep_ref, send_ref, held) = refs[:groups], refs[groups:]
    f, c, _ = place()
    for p in range(groups):
        held[p] = came[p][...]
    for m in range(0, groups, 2):
        keep_ref[m // 2] = held[c ^ f ^ m]
        send_ref[m // 2] = held[c ^ f ^ m ^ 1]


def add_kernel(groups, keep_ref, came_ref, *outs):
    for i in range(1, groups // 2):
        total = keep_ref[i].astype(F32) + came_ref[i].astype(F32)
        outs[i - 1][...] = total.astype(BF16)


def finish_kernel(groups, chunks, *refs):
    bias_ref, out_ref = refs[-2:]
    each = 1 + groups // 2
    f, _, _ = place()
    for h in range(chunks):
        keep_ref, came_ref, *far = refs[h * each : (h + 1) * each]
        _, _, rows, wslice = keep_ref.shape
        for half in range(2):
            total = keep_ref[0, half].astype(F32) + came_ref[0, half].astype(F32)
            for ref in far:
                total += ref[half].astype(F32)
            total += bias_ref[pl.ds(2 * f + half, 1), :]
            out_ref[h * rows : (h + 1) * rows, half * wslice : (half + 1) * wslice] = (
                total.astype(BF16)
            )


def on_device(tokens, dec_bias, enc_weight, enc_bias, dec_weight, block_ids, block_counts):
    tile_count = lax.axis_size("tok")
    groups = lax.axis_size("feat")
    tok_rows, width = tokens.shape
    wslice = width // tile_count
    feats = enc_weight.shape[1]
    rows = tok_rows // CHUNKS
    ids = block_ids[:, 0, :]
    counts = block_counts[:, 0]
    bias_rows = dec_bias.astype(F32).reshape(tile_count, wslice)
    enc_bias_rows = enc_bias.astype(F32).reshape(feats // LANES, LANES)

    def swap(value, p):
        pairs = [(i, i ^ (2 * p)) for i in range(tile_count)]
        return lax.ppermute(value, "tok", pairs)

    def lift(value, m):
        return lax.ppermute(value, "feat", [(i, i ^ m) for i in range(groups)])

    cores = [(i, i ^ 1) for i in range(tile_count)]
    enc_other = lax.ppermute(enc_weight, "tok", cores)
    dec_other = lax.ppermute(dec_weight, "tok", cores)

    sent = pl.pallas_call(
        functools.partial(split_kernel, groups),
        out_shape=[jax.ShapeDtypeStruct((2, tok_rows, wslice), BF16)] * groups,
        in_specs=[spec(pl.ANY)],
        out_specs=[spec(VMEM)] * groups,
        scratch_shapes=[pltpu.SemaphoreType.DMA((groups, 2))],
        compiler_params=params(8),
        cost_estimate=cost(0, 4 * width * tok_rows),
        name="split",
    )(pin(tokens))
    pieces = [sent[0]] + [swap(sent[p], p) for p in range(1, groups)]

    chunk = min(wslice, 256)

    def columns(weight):
        return pl.pallas_call(
            functools.partial(columns_kernel, groups),
            out_shape=jax.ShapeDtypeStruct((groups, wslice, ACTIVE), BF16),
            grid=(wslice // chunk,),
            in_specs=[spec(SMEM), pl.BlockSpec((chunk, feats), lambda i: (i, 0))],
            out_specs=pl.BlockSpec((groups, chunk, ACTIVE), lambda i: (0, i, 0)),
            compiler_params=params(16),
            cost_estimate=cost(0, 2 * wslice * (feats + groups * ACTIVE)),
            name="columns",
        )(ids, weight)

    own_cols = columns(enc_weight)
    oth_cols = columns(enc_other)
    flops = 4 * groups * tok_rows * wslice * ACTIVE
    part = pl.pallas_call(
        functools.partial(encode_kernel, groups),
        out_shape=jax.ShapeDtypeStruct((groups, tok_rows, ACTIVE), BF16),
        in_specs=[spec(VMEM)] * (groups + 3),
        out_specs=spec(VMEM),
        compiler_params=params(16),
        cost_estimate=cost(flops, 4 * groups * wslice * ACTIVE),
        name="encode",
    )(bias_rows, *pieces, own_cols, oth_cols)
    parts = [part] + [swap(part, p) for p in range(1, groups)]

    dec_staged = pl.pallas_call(
        stage_kernel,
        out_shape=jax.ShapeDtypeStruct(dec_weight.shape, BF16),
        in_specs=[spec(pl.ANY)],
        out_specs=spec(VMEM),
        scratch_shapes=[pltpu.SemaphoreType.DMA((8,))],
        compiler_params=params(8),
        cost_estimate=cost(0, 4 * wslice * feats),
        name="stage",
    )(dec_other)
    piece = jax.ShapeDtypeStruct((2, rows, wslice), BF16)
    decoded = pl.pallas_call(
        functools.partial(decode_kernel, groups, CHUNKS),
        out_shape=[jax.ShapeDtypeStruct((tok_rows, ACTIVE), BF16)]
        + [piece] * (groups * CHUNKS),
        in_specs=[spec(SMEM)] * 2 + [spec(VMEM)] * (3 + groups),
        out_specs=[spec(VMEM)] * (1 + groups * CHUNKS),
        compiler_params=params(16),
        cost_estimate=cost(flops, 4 * groups * wslice * ACTIVE),
        name="decode",
    )(ids, counts, enc_bias_rows, *parts, dec_weight, dec_staged)

    both = jax.ShapeDtypeStruct((groups // 2, 2, rows, wslice), BF16)
    moved = []
    for h in range(CHUNKS):
        made = decoded[1 + h * groups : 1 + (h + 1) * groups]
        came = [made[0]] + [swap(made[p], p) for p in range(1, groups)]
        keep, send = pl.pallas_call(
            functools.partial(route_kernel, groups),
            out_shape=[both] * 2,
            in_specs=[spec(VMEM)] * groups,
            out_specs=[spec(VMEM)] * 2,
            scratch_shapes=[VMEM((groups, 2, rows, wslice), BF16)],
            compiler_params=params(8),
            cost_estimate=cost(0, 8 * groups * rows * wslice),
            name="route",
        )(*came)
        near = lift(send, 1)
        sums = pl.pallas_call(
            functools.partial(add_kernel, groups),
            out_shape=[piece] * (groups // 2 - 1),
            in_specs=[spec(VMEM)] * 2,
            out_specs=[spec(VMEM)] * (groups // 2 - 1),
            compiler_params=params(8),
            cost_estimate=cost(groups * rows * wslice, 6 * groups * rows * wslice),
            name="add",
        )(keep, near)
        moved += [keep, near] + [lift(sums[m // 2 - 1], m) for m in range(2, groups, 2)]

    rebuilt = pl.pallas_call(
        functools.partial(finish_kernel, groups, CHUNKS),
        out_shape=jax.ShapeDtypeStruct((tok_rows, 2 * wslice), BF16),
        in_specs=[spec(VMEM)] * (len(moved) + 1),
        out_specs=spec(VMEM),
        compiler_params=params(8),
        cost_estimate=cost(0, 4 * (groups + 1) * tok_rows * wslice),
        name="finish",
    )(*moved, bias_rows)
    return (decoded[0], rebuilt)


def solution(mesh):
    in_specs = (
        P("tok", None),
        P(),
        P("tok", "feat"),
        P("feat"),
        P("feat", "tok"),
        P(None, "feat", None),
        P(None, "feat"),
    )
    out_specs = (P("tok", "feat"), P("tok", "feat"))
    return jax.shard_map(
        on_device, mesh=mesh, in_specs=in_specs, out_specs=out_specs, check_vma=False
    )
```

time: 73.4 us -> 65.6 us (0.89)
  starting transfers between devices: 34.9 us -> 24.5 us
  waiting for transfers between devices: 14.6 us -> 21.4 us
  local copies, waits for them, and re-layouts: 4.91 us -> 2.97 us
  Pallas kernels: 17.4 us -> 15.7 us
    ppermute x18 -> x12, starting transfers between devices: 23.1 us -> 15.7 us  [swap(): return lax.ppermute(value, 'tok', pairs)]
    ppermute x6 -> x4, waiting for transfers between devices: 6.98 us -> 13.3 us  [lift(): return lax.ppermute(value, 'feat', [(i, i ^ m) for i in range(groups)])]
    ppermute x6 -> x4, starting transfers between devices: 11.2 us -> 8.14 us  [lift(): return lax.ppermute(value, 'feat', [(i, i ^ m) for i in range(groups)])]
    pallas_call x6 -> x7, Pallas kernels: 7.98 us -> 6.69 us  [the longest x1 2.37 us: on_device(): pl.pallas_call(stage_kernel, out_shape=jax.ShapeDtypeStruct(dec_weight.sh...]
    unnamed x10, local copies, waits for them, and re-layouts: 3.43 us -> 2.21 us
    pallas_call x2 -> x1, Pallas kernels: 1.64 us -> 0.84 us  [on_device(): pl.pallas_call(functools.partial(encode_kernel, groups), out_shape=jax.Sh...]
    ppermute x18 -> x12, waiting for transfers between devices: 7.56 us -> 8.12 us  [swap(): return lax.ppermute(value, 'tok', pairs)]
  transfers between devices with their start and end apart: 26 -> 18, of which waited for: 5 -> 12; matrix products, arithmetic and copies ran while one was open for 3% -> 1% of each run, Pallas kernels for 23% -> 20%
where the time goes in v3:
time: 65.6 us; the launch traced here: 65.3 us
  starting transfers between devices  24.5 us (37%)
  waiting for transfers between devices  21.4 us (33%)
  Pallas kernels  15.7 us (24%)
  local copies, waits for them, and re-layouts  2.97 us (5%)
  between operations  0.77 us (1%)
    ppermute x12, starting transfers between devices, swap(): return lax.ppermute(value, 'tok', pairs)  15.7 us
    ppermute x4, waiting for transfers between devices, lift(): return lax.ppermute(value, 'feat', [(i, i ^ m) for i in range(groups)])  13.3 us
    ppermute x4, starting transfers between devices, lift(): return lax.ppermute(value, 'feat', [(i, i ^ m) for i in range(groups)])  8.14 us
    ppermute x12, waiting for transfers between devices, swap(): return lax.ppermute(value, 'tok', pairs)  8.12 us
    pallas_call x2, Pallas kernels, columns(): pl.pallas_call(functools.partial(columns_kernel, groups), out_shape=jax.S...  7.34 us
    pallas_call x1, Pallas kernels, on_device(): pl.pallas_call(stage_kernel, out_shape=jax.ShapeDtypeStruct(dec_weight.sh...  2.37 us
    unnamed x10, local copies, waits for them, and re-layouts  2.21 us
    pallas_call x1, Pallas kernels, on_device(): pl.pallas_call(functools.partial(split_kernel, groups), out_shape=[jax.Sh...  2.15 us
  transfers between devices with their start and end apart: 18, of which 12 were waited for; matrix products, arithmetic and copies ran while one was open for 1% of the time, Pallas kernels for 20%

profile of v3, /device:TPU:0, one launch (start us, length us, event | category | flops | bytes accessed | tf_op | source)
XLA Modules:
  0.0 65.3 jit_solution(3057848651704767707)
XLA Ops:
  1.2 2.1 %split.1 = (bf16[2,64,1024]{2,1,0:T(8,128)(2,1)S(1)}, bf16[2,64,1024]{2,1,0:T(8,128)(2,1)}, bf16[2,64,1024]{2,1,0:T(8,128)(2,1)}, bf16[2,64,1024]{2,1,0:T(8,128)(2,1)S(1)}) custom-call(bf16[64,8192]{1,0:T(8,128)(2,1)} %tok_ref.1), custom_call_target="tpu_custom_call" | custom-call | bytes 2097152 | tf_op jit(solution)/shard_map/split/pallas_call | solution.py:205
  3.4 3.0 %collective-permute-start = (bf16[2,64,1024]{2,1,0:T(8,128)(2,1)}, bf16[2,64,1024]{2,1,0:T(8,128)(2,1)S(1)}, u32[]{:S(2)}, u32[]{:S(2)}) collective-permute-start(bf16[2,64,1024]{2,1,0:T(8,128)(2,1)} %get-tuple-element.20), channel_id=1, source_target_pairs={{0,2},{1,3},{2,0},{3,1},{4,6},{5,7},{6,4},{7,5},{8,10},{9,11},{10,... | collective-permute-start | bytes 786440 | tf_op jit(solution)/shard_map/ppermute | solution.py:196
  6.4 1.5 %collective-permute-start.1 = (bf16[2,64,1024]{2,1,0:T(8,128)(2,1)}, bf16[2,64,1024]{2,1,0:T(8,128)(2,1)S(1)}, u32[]{:S(2)}, u32[]{:S(2)}) collective-permute-start(bf16[2,64,1024]{2,1,0:T(8,128)(2,1)} %get-tuple-element.21), channel_id=1, source_target_pairs={{0,4},{1,5},{2,6},{3,7},{4,0},{5,1},{6,2},{7,3},{8,12},{9,13},{10,... | collective-permute-start | bytes 786440 | tf_op jit(solution)/shard_map/ppermute | solution.py:196
  7.9 0.8 %copy.11.ids_ref.refs_0_ = s32[8,4]{1,0:T(8,128)S(1)} copy(s32[8,4]{0,1:T(4,128)} %bitcast.6) | data formatting | bytes 256 | tf_op jit(solution)/shard_map/squeeze | solution.py:189
  8.7 2.2 %copy-done.1 = bf16[1024,2048]{1,0:T(8,128)(2,1)S(1)} copy-done((bf16[1024,2048]{1,0:T(8,128)(2,1)S(1)}, bf16[1024,2048]{1,0:T(8,128)(2,1)}, u32[]{:S(2)}) %copy-start.1) | copy-done | bytes 4194328
  10.9 3.0 %columns.2.refs_5_ = bf16[4,1024,256]{2,1,0:T(8,128)(2,1)S(1)} custom-call(s32[8,4]{1,0:T(8,128)S(1)} %copy.11.ids_ref.refs_0_, bf16[1024,2048]{1,0:T(8,128)(2,1)S(1)} %copy-done.1), custom_call_target="tpu_custom_call" | custom-call | bytes 6291456 | tf_op jit(solution)/shard_map/columns/pallas_call | solution.py:220
  13.9 4.4 %columns.3.refs_6_ = bf16[4,1024,256]{2,1,0:T(8,128)(2,1)S(1)} custom-call(s32[8,4]{1,0:T(8,128)S(1)} %copy.11.ids_ref.refs_0_, bf16[1024,2048]{1,0:T(8,128)(2,1)} %collective-permute-done.3.w_ref), custom_call_target="tpu_custom_call" | custom-call | bytes 6291456 | tf_op jit(solution)/shard_map/columns/pallas_call | solution.py:220
  18.3 1.9 %collective-permute-done.1.refs_3_ = bf16[2,64,1024]{2,1,0:T(8,128)(2,1)S(1)} collective-permute-done((bf16[2,64,1024]{2,1,0:T(8,128)(2,1)}, bf16[2,64,1024]{2,1,0:T(8,128)(2,1)S(1)}, u32[]{:S(2)}, u32[]{:S(2)}) %collective-permute-start.1) | collective-permute-done | bytes 262176 | tf_op jit(solution)/shard_map/ppermute | solution.py:196
  20.2 0.8 %encode.1.refs_3_ = bf16[4,64,256]{2,1,0:T(8,128)(2,1)S(1)} custom-call(f32[8,1024]{1,0:T(8,128)S(1)} %reshape.21.refs_0_.refs_6_, bf16[2,64,1024]{2,1,0:T(8,128)(2,1)S(1)} %get-tuple-element.19.refs_1_, bf16[2,64,1024]{2,1,0:T(8,128)(2,1)S(1)} %collective-permute-done.refs_2_, bf16[2,64,1024]{2,1,0:T(8,128)(2,1)S(1)} %collective-permute-done.1.refs_3_, ...), custom_call_target="tpu_custom_call" | custom-call | flops 268435456 | bytes 4194304 | tf_op jit(solution)/shard_map/encode/pallas_call | solution.py:234
  21.1 1.3 %collective-permute-start.4 = (bf16[4,64,256]{2,1,0:T(8,128)(2,1)S(1)}, bf16[4,64,256]{2,1,0:T(8,128)(2,1)S(1)}, u32[]{:S(2)}, u32[]{:S(2)}) collective-permute-start(bf16[4,64,256]{2,1,0:T(8,128)(2,1)S(1)} %encode.1.refs_3_), channel_id=1, source_target_pairs={{0,2},{1,3},{2,0},{3,1},{4,6},{5,7},{6,4},{7,5},{8,10},{9,11},{10,... | collective-permute-start | bytes 393224 | tf_op jit(solution)/shard_map/ppermute | solution.py:196
  22.4 0.8 %collective-permute-start.5 = (bf16[4,64,256]{2,1,0:T(8,128)(2,1)S(1)}, bf16[4,64,256]{2,1,0:T(8,128)(2,1)S(1)}, u32[]{:S(2)}, u32[]{:S(2)}) collective-permute-start(bf16[4,64,256]{2,1,0:T(8,128)(2,1)S(1)} %encode.1.refs_3_), channel_id=1, source_target_pairs={{0,4},{1,5},{2,6},{3,7},{4,0},{5,1},{6,2},{7,3},{8,12},{9,13},{10,... | collective-permute-start | bytes 393224 | tf_op jit(solution)/shard_map/ppermute | solution.py:196
  23.2 1.4 %collective-permute-start.6 = (bf16[4,64,256]{2,1,0:T(8,128)(2,1)S(1)}, bf16[4,64,256]{2,1,0:T(8,128)(2,1)S(1)}, u32[]{:S(2)}, u32[]{:S(2)}) collective-permute-start(bf16[4,64,256]{2,1,0:T(8,128)(2,1)S(1)} %encode.1.refs_3_), channel_id=1, source_target_pairs={{0,6},{1,7},{2,4},{3,5},{4,2},{5,3},{6,0},{7,1},{8,14},{9,15},{10,... | collective-permute-start | bytes 393224 | tf_op jit(solution)/shard_map/ppermute | solution.py:196
  24.6 2.4 %stage.1.refs_8_ = bf16[2048,1024]{1,0:T(8,128)(2,1)S(1)} custom-call(bf16[2048,1024]{1,0:T(8,128)(2,1)} %collective-permute-done.7.src), custom_call_target="tpu_custom_call" | custom-call | bytes 8388608 | tf_op jit(solution)/shard_map/stage/pallas_call | solution.py:245
  27.2 2.4 %collective-permute-done.5.refs_5_ = bf16[4,64,256]{2,1,0:T(8,128)(2,1)S(1)} collective-permute-done((bf16[4,64,256]{2,1,0:T(8,128)(2,1)S(1)}, bf16[4,64,256]{2,1,0:T(8,128)(2,1)S(1)}, u32[]{:S(2)}, u32[]{:S(2)}) %collective-permute-start.5) | collective-permute-done | bytes 131104 | tf_op jit(solution)/shard_map/ppermute | solution.py:196
  29.5 2.0 %decode.1 = (bf16[64,256]{1,0:T(8,128)(2,1)}, bf16[2,32,1024]{2,1,0:T(8,128)(2,1)S(1)}, bf16[2,32,1024]{2,1,0:T(8,128)(2,1)S(1)}, bf16[2,32,1024]{2,1,0:T(8,128)...) custom-call(s32[8,4]{1,0:T(8,128)S(1)} %copy.11.ids_ref.refs_0_, ...), custom_call_target="tpu_custom_call" | custom-call | flops 268435456 | bytes 4194304 | tf_op jit(solution)/shard_map/decode/pallas_call | solution.py:256
  31.5 1.3 %collective-permute-start.13 = (bf16[2,32,1024]{2,1,0:T(8,128)(2,1)S(1)}, bf16[2,32,1024]{2,1,0:T(8,128)(2,1)S(1)}, u32[]{:S(2)}, u32[]{:S(2)}) collective-permute-start(bf16[2,32,1024]{2,1,0:T(8,128)(2,1)S(1)} %get-tuple-element.31), channel_id=1, source_target_pairs={{0,2},{1,3},{2,0},{3,1},{4,6},{5,7},{6,4},{7,5},{8,10},{9,11},{10,... | collective-permute-start | bytes 393224 | tf_op jit(solution)/shard_map/ppermute | solution.py:196
  32.8 1.0 %collective-permute-start.14 = (bf16[2,32,1024]{2,1,0:T(8,128)(2,1)S(1)}, bf16[2,32,1024]{2,1,0:T(8,128)(2,1)S(1)}, u32[]{:S(2)}, u32[]{:S(2)}) collective-permute-start(bf16[2,32,1024]{2,1,0:T(8,128)(2,1)S(1)} %get-tuple-element.32), channel_id=1, source_target_pairs={{0,4},{1,5},{2,6},{3,7},{4,0},{5,1},{6,2},{7,3},{8,12},{9,13},{10,... | collective-permute-start | bytes 393224 | tf_op jit(solution)/shard_map/ppermute | solution.py:196
  33.8 1.2 %collective-permute-start.15 = (bf16[2,32,1024]{2,1,0:T(8,128)(2,1)S(1)}, bf16[2,32,1024]{2,1,0:T(8,128)(2,1)S(1)}, u32[]{:S(2)}, u32[]{:S(2)}) collective-permute-start(bf16[2,32,1024]{2,1,0:T(8,128)(2,1)S(1)} %get-tuple-element.33), channel_id=1, source_target_pairs={{0,6},{1,7},{2,4},{3,5},{4,2},{5,3},{6,0},{7,1},{8,14},{9,15},{10,... | collective-permute-start | bytes 393224 | tf_op jit(solution)/shard_map/ppermute | solution.py:196
  35.0 1.7 %collective-permute-start.10 = (bf16[2,32,1024]{2,1,0:T(8,128)(2,1)S(1)}, bf16[2,32,1024]{2,1,0:T(8,128)(2,1)S(1)}, u32[]{:S(2)}, u32[]{:S(2)}) collective-permute-start(bf16[2,32,1024]{2,1,0:T(8,128)(2,1)S(1)} %get-tuple-element.27), channel_id=1, source_target_pairs={{0,6},{1,7},{2,4},{3,5},{4,2},{5,3},{6,0},{7,1},{8,14},{9,15},{10,... | collective-permute-start | bytes 393224 | tf_op jit(solution)/shard_map/ppermute | solution.py:196
  36.7 1.1 %collective-permute-start.8 = (bf16[2,32,1024]{2,1,0:T(8,128)(2,1)S(1)}, bf16[2,32,1024]{2,1,0:T(8,128)(2,1)S(1)}, u32[]{:S(2)}, u32[]{:S(2)}) collective-permute-start(bf16[2,32,1024]{2,1,0:T(8,128)(2,1)S(1)} %get-tuple-element.25), channel_id=1, source_target_pairs={{0,2},{1,3},{2,0},{3,1},{4,6},{5,7},{6,4},{7,5},{8,10},{9,11},{10,... | collective-permute-start | bytes 393224 | tf_op jit(solution)/shard_map/ppermute | solution.py:196
  37.8 1.4 %collective-permute-start.9 = (bf16[2,32,1024]{2,1,0:T(8,128)(2,1)S(1)}, bf16[2,32,1024]{2,1,0:T(8,128)(2,1)S(1)}, u32[]{:S(2)}, u32[]{:S(2)}) collective-permute-start(bf16[2,32,1024]{2,1,0:T(8,128)(2,1)S(1)} %get-tuple-element.26), channel_id=1, source_target_pairs={{0,4},{1,5},{2,6},{3,7},{4,0},{5,1},{6,2},{7,3},{8,12},{9,13},{10,... | collective-permute-start | bytes 393224 | tf_op jit(solution)/shard_map/ppermute | solution.py:196
  39.2 2.0 %collective-permute-done.14.refs_2_ = bf16[2,32,1024]{2,1,0:T(8,128)(2,1)S(1)} collective-permute-done((bf16[2,32,1024]{2,1,0:T(8,128)(2,1)S(1)}, bf16[2,32,1024]{2,1,0:T(8,128)(2,1)S(1)}, u32[]{:S(2)}, u32[]{:S(2)}) %collective-permute-start.14) | collective-permute-done | bytes 131104 | tf_op jit(solution)/shard_map/ppermute | solution.py:196
  41.6 1.7 %collective-permute-start.16 = (bf16[2,2,32,1024]{3,2,1,0:T(8,128)(2,1)S(1)}, bf16[2,2,32,1024]{3,2,1,0:T(8,128)(2,1)S(1)}, u32[]{:S(2)}, u32[]{:S(2)}) collective-permute-start(bf16[2,2,32,1024]{3,2,1,0:T(8,128)(2,1)S(1)} %get-tuple-element.35), channel_id=1, source_target_pairs={{0,8},{8,0},{16,24},{24,16},{1,9},{9,1},{17,25},{25,17},{2,10},{10... | collective-permute-start | bytes 786440 | tf_op jit(solution)/shard_map/ppermute | solution.py:199
  43.3 1.0 %collective-permute-done.8.refs_1_ = bf16[2,32,1024]{2,1,0:T(8,128)(2,1)S(1)} collective-permute-done((bf16[2,32,1024]{2,1,0:T(8,128)(2,1)S(1)}, bf16[2,32,1024]{2,1,0:T(8,128)(2,1)S(1)}, u32[]{:S(2)}, u32[]{:S(2)}) %collective-permute-start.8) | collective-permute-done | bytes 131104 | tf_op jit(solution)/shard_map/ppermute | solution.py:196
  44.7 1.5 %collective-permute-start.11 = (bf16[2,2,32,1024]{3,2,1,0:T(8,128)(2,1)S(1)}, bf16[2,2,32,1024]{3,2,1,0:T(8,128)(2,1)S(1)}, u32[]{:S(2)}, u32[]{:S(2)}) collective-permute-start(bf16[2,2,32,1024]{3,2,1,0:T(8,128)(2,1)S(1)} %get-tuple-element.29), channel_id=1, source_target_pairs={{0,8},{8,0},{16,24},{24,16},{1,9},{9,1},{17,25},{25,17},{2,10},{10... | collective-permute-start | bytes 786440 | tf_op jit(solution)/shard_map/ppermute | solution.py:199
  46.2 4.9 %collective-permute-done.16.came_ref.refs_4_ = bf16[2,2,32,1024]{3,2,1,0:T(8,128)(2,1)S(1)} collective-permute-done((bf16[2,2,32,1024]{3,2,1,0:T(8,128)(2,1)S(1)}, bf16[2,2,32,1024]{3,2,1,0:T(8,128)(2,1)S(1)}, u32[]{:S(2)}, u32[]{:S(2)}) %collective-permute-start.16) | collective-permute-done | bytes 262176 | tf_op jit(solution)/shard_map/ppermute | solution.py:199
  51.1 2.2 %collective-permute-start.17 = (bf16[2,32,1024]{2,1,0:T(8,128)(2,1)S(1)}, bf16[2,32,1024]{2,1,0:T(8,128)(2,1)S(1)}, u32[]{:S(2)}, u32[]{:S(2)}) collective-permute-start(bf16[2,32,1024]{2,1,0:T(8,128)(2,1)S(1)} %add.3), channel_id=1, source_target_pairs={{0,16},{8,24},{16,0},{24,8},{1,17},{9,25},{17,1},{25,9},{2,18},{10... | collective-permute-start | bytes 393224 | tf_op jit(solution)/shard_map/ppermute | solution.py:199
  53.3 1.7 %collective-permute-done.11.came_ref.refs_1_ = bf16[2,2,32,1024]{3,2,1,0:T(8,128)(2,1)S(1)} collective-permute-done((bf16[2,2,32,1024]{3,2,1,0:T(8,128)(2,1)S(1)}, bf16[2,2,32,1024]{3,2,1,0:T(8,128)(2,1)S(1)}, u32[]{:S(2)}, u32[]{:S(2)}) %collective-permute-start.11) | collective-permute-done | bytes 262176 | tf_op jit(solution)/shard_map/ppermute | solution.py:199
  55.1 2.7 %collective-permute-start.12 = (bf16[2,32,1024]{2,1,0:T(8,128)(2,1)S(1)}, bf16[2,32,1024]{2,1,0:T(8,128)(2,1)S(1)}, u32[]{:S(2)}, u32[]{:S(2)}) collective-permute-start(bf16[2,32,1024]{2,1,0:T(8,128)(2,1)S(1)} %add.2), channel_id=1, source_target_pairs={{0,16},{8,24},{16,0},{24,8},{1,17},{9,25},{17,1},{25,9},{2,18},{10... | collective-permute-start | bytes 393224 | tf_op jit(solution)/shard_map/ppermute | solution.py:199
  57.8 2.8 %collective-permute-done.17.refs_5_ = bf16[2,32,1024]{2,1,0:T(8,128)(2,1)S(1)} collective-permute-done((bf16[2,32,1024]{2,1,0:T(8,128)(2,1)S(1)}, bf16[2,32,1024]{2,1,0:T(8,128)(2,1)S(1)}, u32[]{:S(2)}, u32[]{:S(2)}) %collective-permute-start.17) | collective-permute-done | bytes 131104 | tf_op jit(solution)/shard_map/ppermute | solution.py:199
  60.6 3.9 %collective-permute-done.12.refs_2_ = bf16[2,32,1024]{2,1,0:T(8,128)(2,1)S(1)} collective-permute-done((bf16[2,32,1024]{2,1,0:T(8,128)(2,1)S(1)}, bf16[2,32,1024]{2,1,0:T(8,128)(2,1)S(1)}, u32[]{:S(2)}, u32[]{:S(2)}) %collective-permute-start.12) | collective-permute-done | bytes 131104 | tf_op jit(solution)/shard_map/ppermute | solution.py:199
  64.5 0.8 %finish.1 = bf16[64,2048]{1,0:T(8,128)(2,1)} custom-call(bf16[2,2,32,1024]{3,2,1,0:T(8,128)(2,1)S(1)} %get-tuple-element.28.keep_ref.refs_0_, bf16[2,2,32,1024]{3,2,1,0:T(8,128)(2,1)S(1)} %collective-permute-done.11.came_ref.refs_1_, bf16[2,32,1024]{2,1,0:T(8,128)(2,1)S(1)} %collective-permute-done.12.refs_2_, ...), custom_call_target="tpu_custom_call" | custom-call | bytes 1310720 | tf_op jit(solution)/shard_map/finish/pallas_call | solution.py:294
  (28 shorter events, 1.7 us)
Async XLA Ops:
  0.6 13.2 %copy-start.3 = (bf16[8192]{0:T(1024)(128)(2,1)S(1)}, bf16[8192]{0:T(1024)(128)(2,1)}, u32[]{:S(2)}) copy-start(bf16[8192]{0:T(1024)(128)(2,1)} %param.8) | copy-start | bytes 49156
  0.6 13.2 %collective-permute-start.3 = (bf16[1024,2048]{1,0:T(8,128)(2,1)}, bf16[1024,2048]{1,0:T(8,128)(2,1)}, u32[]{:S(2)}, u32[]{:S(2)}) collective-permute-start(bf16[1024,2048]{1,0:T(8,128)(2,1)} %w_ref.1), channel_id=1, source_target_pairs={{0,1},{1,0},{2,3},{3,2},{4,5},{5,4},{6,7},{7,6},{8,9},{9,8},{10,11... | collective-permute-start | bytes 12582920 | tf_op jit(solution)/shard_map/ppermute | solution.py:202
  1.2 23.5 %collective-permute-start.7 = (bf16[2048,1024]{1,0:T(8,128)(2,1)}, bf16[2048,1024]{1,0:T(8,128)(2,1)}, u32[]{:S(2)}, u32[]{:S(2)}) collective-permute-start(bf16[2048,1024]{1,0:T(8,128)(2,1)} %refs_7_.1), channel_id=1, source_target_pairs={{0,1},{1,0},{2,3},{3,2},{4,5},{5,4},{6,7},{7,6},{8,9},{9,8},{10,11... | collective-permute-start | bytes 12582920 | tf_op jit(solution)/shard_map/ppermute | solution.py:203
  3.4 14.9 %collective-permute-start = (bf16[2,64,1024]{2,1,0:T(8,128)(2,1)}, bf16[2,64,1024]{2,1,0:T(8,128)(2,1)S(1)}, u32[]{:S(2)}, u32[]{:S(2)}) collective-permute-start(bf16[2,64,1024]{2,1,0:T(8,128)(2,1)} %get-tuple-element.20), channel_id=1, source_target_pairs={{0,2},{1,3},{2,0},{3,1},{4,6},{5,7},{6,4},{7,5},{8,10},{9,11},{10,... | collective-permute-start | bytes 786440 | tf_op jit(solution)/shard_map/ppermute | solution.py:196
  6.4 13.8 %collective-permute-start.1 = (bf16[2,64,1024]{2,1,0:T(8,128)(2,1)}, bf16[2,64,1024]{2,1,0:T(8,128)(2,1)S(1)}, u32[]{:S(2)}, u32[]{:S(2)}) collective-permute-start(bf16[2,64,1024]{2,1,0:T(8,128)(2,1)} %get-tuple-element.21), channel_id=1, source_target_pairs={{0,4},{1,5},{2,6},{3,7},{4,0},{5,1},{6,2},{7,3},{8,12},{9,13},{10,... | collective-permute-start | bytes 786440 | tf_op jit(solution)/shard_map/ppermute | solution.py:196
  7.9 12.3 %collective-permute-start.2 = (bf16[2,64,1024]{2,1,0:T(8,128)(2,1)S(1)}, bf16[2,64,1024]{2,1,0:T(8,128)(2,1)S(1)}, u32[]{:S(2)}, u32[]{:S(2)}) collective-permute-start(bf16[2,64,1024]{2,1,0:T(8,128)(2,1)S(1)} %get-tuple-element.22), channel_id=1, source_target_pairs={{0,6},{1,7},{2,4},{3,5},{4,2},{5,3},{6,0},{7,1},{8,14},{9,15},{10,... | collective-permute-start | bytes 786440 | tf_op jit(solution)/shard_map/ppermute | solution.py:196
  8.7 2.2 %copy-start.1 = (bf16[1024,2048]{1,0:T(8,128)(2,1)S(1)}, bf16[1024,2048]{1,0:T(8,128)(2,1)}, u32[]{:S(2)}) copy-start(bf16[1024,2048]{1,0:T(8,128)(2,1)} %w_ref.1) | copy-start | bytes 12582916
  18.3 6.4 %copy-start.4 = (bf16[2048]{0:T(1024)(128)(2,1)S(1)}, bf16[2048]{0:T(1024)(128)(2,1)}, u32[]{:S(2)}) copy-start(bf16[2048]{0:T(1024)(128)(2,1)} %param.10) | copy-start | bytes 12292
  21.1 6.1 %collective-permute-start.4 = (bf16[4,64,256]{2,1,0:T(8,128)(2,1)S(1)}, bf16[4,64,256]{2,1,0:T(8,128)(2,1)S(1)}, u32[]{:S(2)}, u32[]{:S(2)}) collective-permute-start(bf16[4,64,256]{2,1,0:T(8,128)(2,1)S(1)} %encode.1.refs_3_), channel_id=1, source_target_pairs={{0,2},{1,3},{2,0},{3,1},{4,6},{5,7},{6,4},{7,5},{8,10},{9,11},{10,... | collective-permute-start | bytes 393224 | tf_op jit(solution)/shard_map/ppermute | solution.py:196
  22.4 7.2 %collective-permute-start.5 = (bf16[4,64,256]{2,1,0:T(8,128)(2,1)S(1)}, bf16[4,64,256]{2,1,0:T(8,128)(2,1)S(1)}, u32[]{:S(2)}, u32[]{:S(2)}) collective-permute-start(bf16[4,64,256]{2,1,0:T(8,128)(2,1)S(1)} %encode.1.refs_3_), channel_id=1, source_target_pairs={{0,4},{1,5},{2,6},{3,7},{4,0},{5,1},{6,2},{7,3},{8,12},{9,13},{10,... | collective-permute-start | bytes 393224 | tf_op jit(solution)/shard_map/ppermute | solution.py:196
  23.2 6.4 %collective-permute-start.6 = (bf16[4,64,256]{2,1,0:T(8,128)(2,1)S(1)}, bf16[4,64,256]{2,1,0:T(8,128)(2,1)S(1)}, u32[]{:S(2)}, u32[]{:S(2)}) collective-permute-start(bf16[4,64,256]{2,1,0:T(8,128)(2,1)S(1)} %encode.1.refs_3_), channel_id=1, source_target_pairs={{0,6},{1,7},{2,4},{3,5},{4,2},{5,3},{6,0},{7,1},{8,14},{9,15},{10,... | collective-permute-start | bytes 393224 | tf_op jit(solution)/shard_map/ppermute | solution.py:196
  24.6 4.9 %copy-start = (bf16[2048,1024]{1,0:T(8,128)(2,1)S(1)}, bf16[2048,1024]{1,0:T(8,128)(2,1)}, u32[]{:S(2)}) copy-start(bf16[2048,1024]{1,0:T(8,128)(2,1)} %refs_7_.1) | copy-start | bytes 12582916
  24.6 4.9 %copy-start.2 = (s32[8,1]{0,1:T(1,128)S(1)}, s32[8,1]{0,1:T(1,128)}, u32[]{:S(2)}) copy-start(s32[8,1]{0,1:T(1,128)} %param.13) | copy-start | bytes 100
  31.5 6.3 %collective-permute-start.13 = (bf16[2,32,1024]{2,1,0:T(8,128)(2,1)S(1)}, bf16[2,32,1024]{2,1,0:T(8,128)(2,1)S(1)}, u32[]{:S(2)}, u32[]{:S(2)}) collective-permute-start(bf16[2,32,1024]{2,1,0:T(8,128)(2,1)S(1)} %get-tuple-element.31), channel_id=1, source_target_pairs={{0,2},{1,3},{2,0},{3,1},{4,6},{5,7},{6,4},{7,5},{8,10},{9,11},{10,... | collective-permute-start | bytes 393224 | tf_op jit(solution)/shard_map/ppermute | solution.py:196
  32.8 8.5 %collective-permute-start.14 = (bf16[2,32,1024]{2,1,0:T(8,128)(2,1)S(1)}, bf16[2,32,1024]{2,1,0:T(8,128)(2,1)S(1)}, u32[]{:S(2)}, u32[]{:S(2)}) collective-permute-start(bf16[2,32,1024]{2,1,0:T(8,128)(2,1)S(1)} %get-tuple-element.32), channel_id=1, source_target_pairs={{0,4},{1,5},{2,6},{3,7},{4,0},{5,1},{6,2},{7,3},{8,12},{9,13},{10,... | collective-permute-start | bytes 393224 | tf_op jit(solution)/shard_map/ppermute | solution.py:196
  33.8 7.7 %collective-permute-start.15 = (bf16[2,32,1024]{2,1,0:T(8,128)(2,1)S(1)}, bf16[2,32,1024]{2,1,0:T(8,128)(2,1)S(1)}, u32[]{:S(2)}, u32[]{:S(2)}) collective-permute-start(bf16[2,32,1024]{2,1,0:T(8,128)(2,1)S(1)} %get-tuple-element.33), channel_id=1, source_target_pairs={{0,6},{1,7},{2,4},{3,5},{4,2},{5,3},{6,0},{7,1},{8,14},{9,15},{10,... | collective-permute-start | bytes 393224 | tf_op jit(solution)/shard_map/ppermute | solution.py:196
  35.0 8.3 %collective-permute-start.10 = (bf16[2,32,1024]{2,1,0:T(8,128)(2,1)S(1)}, bf16[2,32,1024]{2,1,0:T(8,128)(2,1)S(1)}, u32[]{:S(2)}, u32[]{:S(2)}) collective-permute-start(bf16[2,32,1024]{2,1,0:T(8,128)(2,1)S(1)} %get-tuple-element.27), channel_id=1, source_target_pairs={{0,6},{1,7},{2,4},{3,5},{4,2},{5,3},{6,0},{7,1},{8,14},{9,15},{10,... | collective-permute-start | bytes 393224 | tf_op jit(solution)/shard_map/ppermute | solution.py:196
  36.7 7.6 %collective-permute-start.8 = (bf16[2,32,1024]{2,1,0:T(8,128)(2,1)S(1)}, bf16[2,32,1024]{2,1,0:T(8,128)(2,1)S(1)}, u32[]{:S(2)}, u32[]{:S(2)}) collective-permute-start(bf16[2,32,1024]{2,1,0:T(8,128)(2,1)S(1)} %get-tuple-element.25), channel_id=1, source_target_pairs={{0,2},{1,3},{2,0},{3,1},{4,6},{5,7},{6,4},{7,5},{8,10},{9,11},{10,... | collective-permute-start | bytes 393224 | tf_op jit(solution)/shard_map/ppermute | solution.py:196
  37.8 6.8 %collective-permute-start.9 = (bf16[2,32,1024]{2,1,0:T(8,128)(2,1)S(1)}, bf16[2,32,1024]{2,1,0:T(8,128)(2,1)S(1)}, u32[]{:S(2)}, u32[]{:S(2)}) collective-permute-start(bf16[2,32,1024]{2,1,0:T(8,128)(2,1)S(1)} %get-tuple-element.26), channel_id=1, source_target_pairs={{0,4},{1,5},{2,6},{3,7},{4,0},{5,1},{6,2},{7,3},{8,12},{9,13},{10,... | collective-permute-start | bytes 393224 | tf_op jit(solution)/shard_map/ppermute | solution.py:196
  41.6 9.5 %collective-permute-start.16 = (bf16[2,2,32,1024]{3,2,1,0:T(8,128)(2,1)S(1)}, bf16[2,2,32,1024]{3,2,1,0:T(8,128)(2,1)S(1)}, u32[]{:S(2)}, u32[]{:S(2)}) collective-permute-start(bf16[2,2,32,1024]{3,2,1,0:T(8,128)(2,1)S(1)} %get-tuple-element.35), channel_id=1, source_target_pairs={{0,8},{8,0},{16,24},{24,16},{1,9},{9,1},{17,25},{25,17},{2,10},{10... | collective-permute-start | bytes 786440 | tf_op jit(solution)/shard_map/ppermute | solution.py:199
  44.7 10.3 %collective-permute-start.11 = (bf16[2,2,32,1024]{3,2,1,0:T(8,128)(2,1)S(1)}, bf16[2,2,32,1024]{3,2,1,0:T(8,128)(2,1)S(1)}, u32[]{:S(2)}, u32[]{:S(2)}) collective-permute-start(bf16[2,2,32,1024]{3,2,1,0:T(8,128)(2,1)S(1)} %get-tuple-element.29), channel_id=1, source_target_pairs={{0,8},{8,0},{16,24},{24,16},{1,9},{9,1},{17,25},{25,17},{2,10},{10... | collective-permute-start | bytes 786440 | tf_op jit(solution)/shard_map/ppermute | solution.py:199
  51.1 9.5 %collective-permute-start.17 = (bf16[2,32,1024]{2,1,0:T(8,128)(2,1)S(1)}, bf16[2,32,1024]{2,1,0:T(8,128)(2,1)S(1)}, u32[]{:S(2)}, u32[]{:S(2)}) collective-permute-start(bf16[2,32,1024]{2,1,0:T(8,128)(2,1)S(1)} %add.3), channel_id=1, source_target_pairs={{0,16},{8,24},{16,0},{24,8},{1,17},{9,25},{17,1},{25,9},{2,18},{10... | collective-permute-start | bytes 393224 | tf_op jit(solution)/shard_map/ppermute | solution.py:199
  55.1 9.4 %collective-permute-start.12 = (bf16[2,32,1024]{2,1,0:T(8,128)(2,1)S(1)}, bf16[2,32,1024]{2,1,0:T(8,128)(2,1)S(1)}, u32[]{:S(2)}, u32[]{:S(2)}) collective-permute-start(bf16[2,32,1024]{2,1,0:T(8,128)(2,1)S(1)} %add.2), channel_id=1, source_target_pairs={{0,16},{8,24},{16,0},{24,8},{1,17},{9,25},{17,1},{25,9},{2,18},{10... | collective-permute-start | bytes 393224 | tf_op jit(solution)/shard_map/ppermute | solution.py:199

commit v4 on v3

--- a/solution.py
+++ b/solution.py
@@ -11,7 +11,6 @@
 SLOTS = 4
 LANES = 128
 ACTIVE = SLOTS * BLOCK
-CHUNKS = 2
 VMEM = pltpu.VMEM
 SMEM = pltpu.SMEM
 HBM = pltpu.HBM
@@ -40,22 +39,14 @@
     return lax.axis_index("feat"), tok >> 1, tok & 1
 
 
-def split_kernel(groups, tok_ref, *refs):
-    outs, sems = refs[:-1], refs[-1]
+def split_kernel(groups, tok_ref, *outs):
     _, c, k = place()
     wslice = outs[0].shape[2]
-    copies = []
     for p in range(groups):
         for half in range(2):
             u = ((c ^ p) << 1) + (k ^ half)
             cols = pl.ds(pl.multiple_of(u * wslice, wslice), wslice)
-            copy = pltpu.make_async_copy(
-                tok_ref.at[:, cols], outs[p].at[half], sems.at[p, half]
-            )
-            copy.start()
-            copies.append(copy)
-    for copy in copies:
-        copy.wait()
+            outs[p][half] = tok_ref[:, cols]
 
 
 def pick_pair(first, second, odd_first, odd_second):
@@ -107,12 +98,14 @@
         out_ref[p] = acc.astype(BF16)
 
 
-def decode_kernel(groups, chunks, *refs):
+def decode_kernel(groups, *refs):
     ids_ref, counts_ref, bias_ref = refs[:3]
     parts = refs[3 : 3 + groups]
     own_ref, oth_ref, code_ref = refs[3 + groups : 6 + groups]
-    outs = refs[6 + groups :]
-    _, c, k = place()
+    firsts = refs[6 + groups : 6 + 2 * groups]
+    keep_ref, send_ref = refs[6 + 2 * groups :]
+    f, c, k = place()
+    even = (f & 1) == 0
     lane = lax.broadcasted_iota(jnp.int32, (1, LANES), 1)
     for p in range(groups):
         tile = ((c ^ p) << 1) + k
@@ -138,12 +131,14 @@
         code = jnp.concatenate(code, axis=1)
         if p == 0:
             code_ref[...] = code
-        height = code.shape[0] // chunks
+        height = code.shape[0] // 4
         for half, ref in ((k, own_ref), (1 - k, oth_ref)):
             rows = jnp.concatenate([ref[some, :] for some in listed], axis=0)
             result = jnp.dot(code, rows, preferred_element_type=F32).astype(BF16)
-            for h in range(chunks):
-                outs[h * groups + p][half] = result[h * height : (h + 1) * height]
+            firsts[p][half] = result[: 2 * height]
+            third, fourth = result[2 * height : 3 * height], result[3 * height :]
+            keep_ref[p, half] = jnp.where(even, third, fourth)
+            send_ref[p, half] = jnp.where(even, fourth, third)
 
 
 def route_kernel(groups, *refs):
@@ -162,21 +157,39 @@
         outs[i - 1][...] = total.astype(BF16)
 
 
-def finish_kernel(groups, chunks, *refs):
+def merge_kernel(groups, keep_ref, came_ref, *outs):
+    for p in range(groups):
+        outs[p][...] = (keep_ref[p].astype(F32) + came_ref[p].astype(F32)).astype(BF16)
+
+
+def direct_kernel(groups, *refs):
+    came, outs, held = refs[:groups], refs[groups : 2 * groups], refs[2 * groups]
+    f, c, _ = place()
+    for p in range(groups):
+        held[p] = came[p][...]
+    for m in range(groups):
+        outs[m][...] = held[c ^ f ^ m]
+
+
+def finish_kernel(groups, *refs):
     bias_ref, out_ref = refs[-2:]
-    each = 1 + groups // 2
+    keep_ref, came_ref, *far = refs[: 1 + groups // 2]
+    direct = refs[1 + groups // 2 : -2]
     f, _, _ = place()
-    for h in range(chunks):
-        keep_ref, came_ref, *far = refs[h * each : (h + 1) * each]
-        _, _, rows, wslice = keep_ref.shape
-        for half in range(2):
-            total = keep_ref[0, half].astype(F32) + came_ref[0, half].astype(F32)
-            for ref in far:
+    _, rows, wslice = direct[0].shape
+    for half in range(2):
+        cols = slice(half * wslice, (half + 1) * wslice)
+        bias = bias_ref[pl.ds(2 * f + half, 1), :]
+        total = keep_ref[0, half].astype(F32) + came_ref[0, half].astype(F32)
+        for ref in far:
+            total += ref[half].astype(F32)
+        out_ref[: 2 * rows, cols] = (total + bias).astype(BF16)
+        for odd in range(2):
+            total = direct[odd][half].astype(F32)
+            for ref in direct[2 + odd :: 2]:
                 total += ref[half].astype(F32)
-            total += bias_ref[pl.ds(2 * f + half, 1), :]
-            out_ref[h * rows : (h + 1) * rows, half * wslice : (half + 1) * wslice] = (
-                total.astype(BF16)
-            )
+            start = pl.multiple_of(2 * rows + ((f & 1) ^ odd) * rows, rows)
+            out_ref[pl.ds(start, rows), cols] = (total + bias).astype(BF16)
 
 
 def on_device(tokens, dec_bias, enc_weight, enc_bias, dec_weight, block_ids, block_counts):
@@ -185,7 +198,6 @@
     tok_rows, width = tokens.shape
     wslice = width // tile_count
     feats = enc_weight.shape[1]
-    rows = tok_rows // CHUNKS
     ids = block_ids[:, 0, :]
     counts = block_counts[:, 0]
     bias_rows = dec_bias.astype(F32).reshape(tile_count, wslice)
@@ -205,13 +217,12 @@
     sent = pl.pallas_call(
         functools.partial(split_kernel, groups),
         out_shape=[jax.ShapeDtypeStruct((2, tok_rows, wslice), BF16)] * groups,
-        in_specs=[spec(pl.ANY)],
+        in_specs=[spec(VMEM)],
         out_specs=[spec(VMEM)] * groups,
-        scratch_shapes=[pltpu.SemaphoreType.DMA((groups, 2))],
         compiler_params=params(8),
         cost_estimate=cost(0, 4 * width * tok_rows),
         name="split",
-    )(pin(tokens))
+    )(tokens)
     pieces = [sent[0]] + [swap(sent[p], p) for p in range(1, groups)]
 
     chunk = min(wslice, 256)
@@ -223,7 +234,7 @@
             grid=(wslice // chunk,),
             in_specs=[spec(SMEM), pl.BlockSpec((chunk, feats), lambda i: (i, 0))],
             out_specs=pl.BlockSpec((groups, chunk, ACTIVE), lambda i: (0, i, 0)),
-            compiler_params=params(16),
+            compiler_params=params(8),
             cost_estimate=cost(0, 2 * wslice * (feats + groups * ACTIVE)),
             name="columns",
         )(ids, weight)
@@ -236,7 +247,7 @@
         out_shape=jax.ShapeDtypeStruct((groups, tok_rows, ACTIVE), BF16),
         in_specs=[spec(VMEM)] * (groups + 3),
         out_specs=spec(VMEM),
-        compiler_params=params(16),
+        compiler_params=params(8),
         cost_estimate=cost(flops, 4 * groups * wslice * ACTIVE),
         name="encode",
     )(bias_rows, *pieces, own_cols, oth_cols)
@@ -252,47 +263,72 @@
         cost_estimate=cost(0, 4 * wslice * feats),
         name="stage",
     )(dec_other)
-    piece = jax.ShapeDtypeStruct((2, rows, wslice), BF16)
-    decoded = pl.pallas_call(
-        functools.partial(decode_kernel, groups, CHUNKS),
+    half_rows = tok_rows // 2
+    quarter_rows = tok_rows // 4
+    piece = jax.ShapeDtypeStruct((2, half_rows, wslice), BF16)
+    small = jax.ShapeDtypeStruct((2, quarter_rows, wslice), BF16)
+    smalls = jax.ShapeDtypeStruct((groups, 2, quarter_rows, wslice), BF16)
+    code_values, *outgoing = pl.pallas_call(
+        functools.partial(decode_kernel, groups),
         out_shape=[jax.ShapeDtypeStruct((tok_rows, ACTIVE), BF16)]
-        + [piece] * (groups * CHUNKS),
+        + [piece] * groups
+        + [smalls] * 2,
         in_specs=[spec(SMEM)] * 2 + [spec(VMEM)] * (3 + groups),
-        out_specs=[spec(VMEM)] * (1 + groups * CHUNKS),
-        compiler_params=params(16),
+        out_specs=[spec(VMEM)] * (3 + groups),
+        compiler_params=params(8),
         cost_estimate=cost(flops, 4 * groups * wslice * ACTIVE),
         name="decode",
     )(ids, counts, enc_bias_rows, *parts, dec_weight, dec_staged)
-
-    both = jax.ShapeDtypeStruct((groups // 2, 2, rows, wslice), BF16)
-    moved = []
-    for h in range(CHUNKS):
-        made = decoded[1 + h * groups : 1 + (h + 1) * groups]
-        came = [made[0]] + [swap(made[p], p) for p in range(1, groups)]
-        keep, send = pl.pallas_call(
-            functools.partial(route_kernel, groups),
-            out_shape=[both] * 2,
-            in_specs=[spec(VMEM)] * groups,
-            out_specs=[spec(VMEM)] * 2,
-            scratch_shapes=[VMEM((groups, 2, rows, wslice), BF16)],
-            compiler_params=params(8),
-            cost_estimate=cost(0, 8 * groups * rows * wslice),
-            name="route",
-        )(*came)
-        near = lift(send, 1)
-        sums = pl.pallas_call(
-            functools.partial(add_kernel, groups),
-            out_shape=[piece] * (groups // 2 - 1),
-            in_specs=[spec(VMEM)] * 2,
-            out_specs=[spec(VMEM)] * (groups // 2 - 1),
-            compiler_params=params(8),
-            cost_estimate=cost(groups * rows * wslice, 6 * groups * rows * wslice),
-            name="add",
-        )(keep, near)
-        moved += [keep, near] + [lift(sums[m // 2 - 1], m) for m in range(2, groups, 2)]
+    firsts, (own_sums, sent_sums) = outgoing[:groups], outgoing[groups:]
+
+    swapped = lift(sent_sums, 1)
+    came = [firsts[0]] + [swap(firsts[p], p) for p in range(1, groups)]
+    both = jax.ShapeDtypeStruct((groups // 2,) + piece.shape, BF16)
+    keep, send = pl.pallas_call(
+        functools.partial(route_kernel, groups),
+        out_shape=[both] * 2,
+        in_specs=[spec(VMEM)] * groups,
+        out_specs=[spec(VMEM)] * 2,
+        scratch_shapes=[VMEM((groups,) + piece.shape, BF16)],
+        compiler_params=params(8),
+        cost_estimate=cost(0, 8 * groups * half_rows * wslice),
+        name="route",
+    )(*came)
+    near = lift(send, 1)
+    merged = pl.pallas_call(
+        functools.partial(merge_kernel, groups),
+        out_shape=[small] * groups,
+        in_specs=[spec(VMEM)] * 2,
+        out_specs=[spec(VMEM)] * groups,
+        compiler_params=params(8),
+        cost_estimate=cost(0, 8 * groups * quarter_rows * wslice),
+        name="merge",
+    )(own_sums, swapped)
+    merged = [merged[0]] + [swap(merged[p], p) for p in range(1, groups)]
+    direct = pl.pallas_call(
+        functools.partial(direct_kernel, groups),
+        out_shape=[small] * groups,
+        in_specs=[spec(VMEM)] * groups,
+        out_specs=[spec(VMEM)] * groups,
+        scratch_shapes=[VMEM((groups,) + small.shape, BF16)],
+        compiler_params=params(8),
+        cost_estimate=cost(0, 8 * groups * quarter_rows * wslice),
+        name="direct",
+    )(*merged)
+    sums = pl.pallas_call(
+        functools.partial(add_kernel, groups),
+        out_shape=[piece] * (groups // 2 - 1),
+        in_specs=[spec(VMEM)] * 2,
+        out_specs=[spec(VMEM)] * (groups // 2 - 1),
+        compiler_params=params(8),
+        cost_estimate=cost(groups * half_rows * wslice, 6 * groups * half_rows * wslice),
+        name="add",
+    )(keep, near)
+    moved = [keep, near] + [lift(sums[m // 2 - 1], m) for m in range(2, groups, 2)]
+    moved += [direct[0]] + [lift(direct[m], m) for m in range(1, groups)]
 
     rebuilt = pl.pallas_call(
-        functools.partial(finish_kernel, groups, CHUNKS),
+        functools.partial(finish_kernel, groups),
         out_shape=jax.ShapeDtypeStruct((tok_rows, 2 * wslice), BF16),
         in_specs=[spec(VMEM)] * (len(moved) + 1),
         out_specs=spec(VMEM),
@@ -300,7 +336,7 @@
         cost_estimate=cost(0, 4 * (groups + 1) * tok_rows * wslice),
         name="finish",
     )(*moved, bias_rows)
-    return (decoded[0], rebuilt)
+    return (code_values, rebuilt)
 
 
 def solution(mesh):

time: 65.6 us -> 62.6 us (0.954)
  waiting for transfers between devices: 21.4 us -> 17 us
  starting transfers between devices: 24.5 us -> 25.9 us
  Pallas kernels: 15.7 us -> 14.4 us
  local copies, waits for them, and re-layouts: 2.97 us -> 4.2 us
    ppermute x4 -> x6, waiting for transfers between devices: 13.3 us -> 8.79 us  [lift(): return lax.ppermute(value, 'feat', [(i, i ^ m) for i in range(groups)])]
    ppermute x4 -> x6, starting transfers between devices: 8.14 us -> 10.3 us  [lift(): return lax.ppermute(value, 'feat', [(i, i ^ m) for i in range(groups)])]
    pallas_call x1, Pallas kernels: 2.15 us -> 0.87 us  [on_device(): pl.pallas_call(functools.partial(split_kernel, groups), out_shape=[jax.Sh...]
    unnamed x10 -> x12, local copies, waits for them, and re-layouts: 2.21 us -> 3.43 us
    ppermute x12, starting transfers between devices: 15.7 us -> 15 us  [swap(): return lax.ppermute(value, 'tok', pairs)]
    pallas_call x2 -> x4, Pallas kernels: 2.79 us -> 2.88 us  [the longest x1 1.97 us: on_device(): pl.pallas_call(functools.partial(decode_kernel, groups), out_shape=[jax.S...]
  transfers between devices with their start and end apart: 18 -> 20, of which waited for: 12 -> 11; matrix products, arithmetic and copies ran while one was open for 1% -> 1% of each run, Pallas kernels for 20% -> 19%
where the time goes in v4:
time: 62.6 us; the launch traced here: 62.3 us
  starting transfers between devices  25.9 us (41%)
  waiting for transfers between devices  17 us (27%)
  Pallas kernels  14.4 us (23%)
  local copies, waits for them, and re-layouts  4.2 us (7%)
  between operations  0.75 us (1%)
    ppermute x12, starting transfers between devices, swap(): return lax.ppermute(value, 'tok', pairs)  15 us
    ppermute x6, starting transfers between devices, lift(): return lax.ppermute(value, 'feat', [(i, i ^ m) for i in range(groups)])  10.3 us
    ppermute x6, waiting for transfers between devices, lift(): return lax.ppermute(value, 'feat', [(i, i ^ m) for i in range(groups)])  8.79 us
    ppermute x12, waiting for transfers between devices, swap(): return lax.ppermute(value, 'tok', pairs)  8.2 us
    pallas_call x2, Pallas kernels, columns(): pl.pallas_call(functools.partial(columns_kernel, groups), out_shape=jax.S...  7.33 us
    unnamed x12, local copies, waits for them, and re-layouts  3.43 us
    pallas_call x1, Pallas kernels, on_device(): pl.pallas_call(stage_kernel, out_shape=jax.ShapeDtypeStruct(dec_weight.sh...  2.37 us
    pallas_call x1, Pallas kernels, on_device(): pl.pallas_call(functools.partial(decode_kernel, groups), out_shape=[jax.S...  1.97 us
  transfers between devices with their start and end apart: 20, of which 11 were waited for; matrix products, arithmetic and copies ran while one was open for 1% of the time, Pallas kernels for 19%

profile of v4, /device:TPU:0, one launch (start us, length us, event | category | flops | bytes accessed | tf_op | source)
XLA Modules:
  0.0 62.3 jit_solution(104967427844063591)
XLA Ops:
  1.2 1.2 %copy-done.2 = bf16[64,8192]{1,0:T(8,128)(2,1)S(1)} copy-done((bf16[64,8192]{1,0:T(8,128)(2,1)S(1)}, bf16[64,8192]{1,0:T(8,128)(2,1)}, u32[]{:S(2)}) %copy-start.2) | copy-done | bytes 1048600
  2.5 0.9 %split.1 = (bf16[2,64,1024]{2,1,0:T(8,128)(2,1)S(1)}, bf16[2,64,1024]{2,1,0:T(8,128)(2,1)}, bf16[2,64,1024]{2,1,0:T(8,128)(2,1)}, bf16[2,64,1024]{2,1,0:T(8,128)(2,1)S(1)}) custom-call(bf16[64,8192]{1,0:T(8,128)(2,1)S(1)} %copy-done.2), custom_call_target="tpu_custom_call" | custom-call | bytes 2097152 | tf_op jit(solution)/shard_map/split/pallas_call | solution.py:217
  3.3 2.9 %collective-permute-start = (bf16[2,64,1024]{2,1,0:T(8,128)(2,1)}, bf16[2,64,1024]{2,1,0:T(8,128)(2,1)S(1)}, u32[]{:S(2)}, u32[]{:S(2)}) collective-permute-start(bf16[2,64,1024]{2,1,0:T(8,128)(2,1)} %get-tuple-element.24), channel_id=1, source_target_pairs={{0,2},{1,3},{2,0},{3,1},{4,6},{5,7},{6,4},{7,5},{8,10},{9,11},{10,... | collective-permute-start | bytes 786440 | tf_op jit(solution)/shard_map/ppermute | solution.py:208
  6.2 1.5 %collective-permute-start.1 = (bf16[2,64,1024]{2,1,0:T(8,128)(2,1)}, bf16[2,64,1024]{2,1,0:T(8,128)(2,1)S(1)}, u32[]{:S(2)}, u32[]{:S(2)}) collective-permute-start(bf16[2,64,1024]{2,1,0:T(8,128)(2,1)} %get-tuple-element.25), channel_id=1, source_target_pairs={{0,4},{1,5},{2,6},{3,7},{4,0},{5,1},{6,2},{7,3},{8,12},{9,13},{10,... | collective-permute-start | bytes 786440 | tf_op jit(solution)/shard_map/ppermute | solution.py:208
  8.5 2.2 %copy-done.1 = bf16[1024,2048]{1,0:T(8,128)(2,1)S(1)} copy-done((bf16[1024,2048]{1,0:T(8,128)(2,1)S(1)}, bf16[1024,2048]{1,0:T(8,128)(2,1)}, u32[]{:S(2)}) %copy-start.1) | copy-done | bytes 4194328
  10.7 3.0 %columns.2.refs_5_ = bf16[4,1024,256]{2,1,0:T(8,128)(2,1)S(1)} custom-call(s32[8,4]{1,0:T(8,128)S(1)} %copy.11.ids_ref.refs_0_, bf16[1024,2048]{1,0:T(8,128)(2,1)S(1)} %copy-done.1), custom_call_target="tpu_custom_call" | custom-call | bytes 6291456 | tf_op jit(solution)/shard_map/columns/pallas_call | solution.py:231
  13.7 4.4 %columns.3.refs_6_ = bf16[4,1024,256]{2,1,0:T(8,128)(2,1)S(1)} custom-call(s32[8,4]{1,0:T(8,128)S(1)} %copy.11.ids_ref.refs_0_, bf16[1024,2048]{1,0:T(8,128)(2,1)} %collective-permute-done.3.w_ref), custom_call_target="tpu_custom_call" | custom-call | bytes 6291456 | tf_op jit(solution)/shard_map/columns/pallas_call | solution.py:231
  18.1 2.0 %collective-permute-done.1.refs_3_ = bf16[2,64,1024]{2,1,0:T(8,128)(2,1)S(1)} collective-permute-done((bf16[2,64,1024]{2,1,0:T(8,128)(2,1)}, bf16[2,64,1024]{2,1,0:T(8,128)(2,1)S(1)}, u32[]{:S(2)}, u32[]{:S(2)}) %collective-permute-start.1) | collective-permute-done | bytes 262176 | tf_op jit(solution)/shard_map/ppermute | solution.py:208
  20.1 0.8 %encode.1.refs_3_ = bf16[4,64,256]{2,1,0:T(8,128)(2,1)S(1)} custom-call(f32[8,1024]{1,0:T(8,128)S(1)} %reshape.21.refs_0_.refs_7_, bf16[2,64,1024]{2,1,0:T(8,128)(2,1)S(1)} %get-tuple-element.23.refs_1_, bf16[2,64,1024]{2,1,0:T(8,128)(2,1)S(1)} %collective-permute-done.refs_2_, bf16[2,64,1024]{2,1,0:T(8,128)(2,1)S(1)} %collective-permute-done.1.refs_3_, ...), custom_call_target="tpu_custom_call" | custom-call | flops 268435456 | bytes 4194304 | tf_op jit(solution)/shard_map/encode/pallas_call | solution.py:245
  20.9 1.3 %collective-permute-start.4 = (bf16[4,64,256]{2,1,0:T(8,128)(2,1)S(1)}, bf16[4,64,256]{2,1,0:T(8,128)(2,1)S(1)}, u32[]{:S(2)}, u32[]{:S(2)}) collective-permute-start(bf16[4,64,256]{2,1,0:T(8,128)(2,1)S(1)} %encode.1.refs_3_), channel_id=1, source_target_pairs={{0,2},{1,3},{2,0},{3,1},{4,6},{5,7},{6,4},{7,5},{8,10},{9,11},{10,... | collective-permute-start | bytes 393224 | tf_op jit(solution)/shard_map/ppermute | solution.py:208
  22.2 0.8 %collective-permute-start.5 = (bf16[4,64,256]{2,1,0:T(8,128)(2,1)S(1)}, bf16[4,64,256]{2,1,0:T(8,128)(2,1)S(1)}, u32[]{:S(2)}, u32[]{:S(2)}) collective-permute-start(bf16[4,64,256]{2,1,0:T(8,128)(2,1)S(1)} %encode.1.refs_3_), channel_id=1, source_target_pairs={{0,4},{1,5},{2,6},{3,7},{4,0},{5,1},{6,2},{7,3},{8,12},{9,13},{10,... | collective-permute-start | bytes 393224 | tf_op jit(solution)/shard_map/ppermute | solution.py:208
  23.1 1.4 %collective-permute-start.6 = (bf16[4,64,256]{2,1,0:T(8,128)(2,1)S(1)}, bf16[4,64,256]{2,1,0:T(8,128)(2,1)S(1)}, u32[]{:S(2)}, u32[]{:S(2)}) collective-permute-start(bf16[4,64,256]{2,1,0:T(8,128)(2,1)S(1)} %encode.1.refs_3_), channel_id=1, source_target_pairs={{0,6},{1,7},{2,4},{3,5},{4,2},{5,3},{6,0},{7,1},{8,14},{9,15},{10,... | collective-permute-start | bytes 393224 | tf_op jit(solution)/shard_map/ppermute | solution.py:208
  24.5 2.4 %stage.1.refs_8_ = bf16[2048,1024]{1,0:T(8,128)(2,1)S(1)} custom-call(bf16[2048,1024]{1,0:T(8,128)(2,1)} %collective-permute-done.7.src), custom_call_target="tpu_custom_call" | custom-call | bytes 8388608 | tf_op jit(solution)/shard_map/stage/pallas_call | solution.py:256
  27.1 2.4 %collective-permute-done.5.refs_5_ = bf16[4,64,256]{2,1,0:T(8,128)(2,1)S(1)} collective-permute-done((bf16[4,64,256]{2,1,0:T(8,128)(2,1)S(1)}, bf16[4,64,256]{2,1,0:T(8,128)(2,1)S(1)}, u32[]{:S(2)}, u32[]{:S(2)}) %collective-permute-start.5) | collective-permute-done | bytes 131104 | tf_op jit(solution)/shard_map/ppermute | solution.py:208
  29.4 2.0 %decode.1 = (bf16[64,256]{1,0:T(8,128)(2,1)}, bf16[2,32,1024]{2,1,0:T(8,128)(2,1)S(1)}, bf16[2,32,1024]{2,1,0:T(8,128)(2,1)S(1)}, bf16[2,32,1024]{2,1,0:T(8,128)...) custom-call(s32[8,4]{1,0:T(8,128)S(1)} %copy.11.ids_ref.refs_0_, ...), custom_call_target="tpu_custom_call" | custom-call | flops 268435456 | bytes 4194304 | tf_op jit(solution)/shard_map/decode/pallas_call | solution.py:271
  31.4 1.7 %collective-permute-start.10 = (bf16[2,32,1024]{2,1,0:T(8,128)(2,1)S(1)}, bf16[2,32,1024]{2,1,0:T(8,128)(2,1)S(1)}, u32[]{:S(2)}, u32[]{:S(2)}) collective-permute-start(bf16[2,32,1024]{2,1,0:T(8,128)(2,1)S(1)} %get-tuple-element.31), channel_id=1, source_target_pairs={{0,6},{1,7},{2,4},{3,5},{4,2},{5,3},{6,0},{7,1},{8,14},{9,15},{10,... | collective-permute-start | bytes 393224 | tf_op jit(solution)/shard_map/ppermute | solution.py:208
  33.1 1.1 %collective-permute-start.8 = (bf16[2,32,1024]{2,1,0:T(8,128)(2,1)S(1)}, bf16[2,32,1024]{2,1,0:T(8,128)(2,1)S(1)}, u32[]{:S(2)}, u32[]{:S(2)}) collective-permute-start(bf16[2,32,1024]{2,1,0:T(8,128)(2,1)S(1)} %get-tuple-element.29), channel_id=1, source_target_pairs={{0,2},{1,3},{2,0},{3,1},{4,6},{5,7},{6,4},{7,5},{8,10},{9,11},{10,... | collective-permute-start | bytes 393224 | tf_op jit(solution)/shard_map/ppermute | solution.py:208
  34.9 1.6 %collective-permute-start.13 = (bf16[4,2,16,1024]{3,2,1,0:T(8,128)(2,1)S(1)}, bf16[4,2,16,1024]{3,2,1,0:T(8,128)(2,1)S(1)}, u32[]{:S(2)}, u32[]{:S(2)}) collective-permute-start(bf16[4,2,16,1024]{3,2,1,0:T(8,128)(2,1)S(1)} %get-tuple-element.35), channel_id=1, source_target_pairs={{0,8},{8,0},{16,24},{24,16},{1,9},{9,1},{17,25},{25,17},{2,10},{10... | collective-permute-start | bytes 786440 | tf_op jit(solution)/shard_map/ppermute | solution.py:211
  36.5 0.8 %collective-permute-done.10.refs_3_ = bf16[2,32,1024]{2,1,0:T(8,128)(2,1)S(1)} collective-permute-done((bf16[2,32,1024]{2,1,0:T(8,128)(2,1)S(1)}, bf16[2,32,1024]{2,1,0:T(8,128)(2,1)S(1)}, u32[]{:S(2)}, u32[]{:S(2)}) %collective-permute-start.10) | collective-permute-done | bytes 131104 | tf_op jit(solution)/shard_map/ppermute | solution.py:208
  37.3 1.3 %collective-permute-done.8.refs_1_ = bf16[2,32,1024]{2,1,0:T(8,128)(2,1)S(1)} collective-permute-done((bf16[2,32,1024]{2,1,0:T(8,128)(2,1)S(1)}, bf16[2,32,1024]{2,1,0:T(8,128)(2,1)S(1)}, u32[]{:S(2)}, u32[]{:S(2)}) %collective-permute-start.8) | collective-permute-done | bytes 131104 | tf_op jit(solution)/shard_map/ppermute | solution.py:208
  39.2 1.6 %collective-permute-start.11 = (bf16[2,2,32,1024]{3,2,1,0:T(8,128)(2,1)S(1)}, bf16[2,2,32,1024]{3,2,1,0:T(8,128)(2,1)S(1)}, u32[]{:S(2)}, u32[]{:S(2)}) collective-permute-start(bf16[2,2,32,1024]{3,2,1,0:T(8,128)(2,1)S(1)} %get-tuple-element.33), channel_id=1, source_target_pairs={{0,8},{8,0},{16,24},{24,16},{1,9},{9,1},{17,25},{25,17},{2,10},{10... | collective-permute-start | bytes 786440 | tf_op jit(solution)/shard_map/ppermute | solution.py:211
  40.8 3.0 %collective-permute-done.13.came_ref = bf16[4,2,16,1024]{3,2,1,0:T(8,128)(2,1)S(1)} collective-permute-done((bf16[4,2,16,1024]{3,2,1,0:T(8,128)(2,1)S(1)}, bf16[4,2,16,1024]{3,2,1,0:T(8,128)(2,1)S(1)}, u32[]{:S(2)}, u32[]{:S(2)}) %collective-permute-start.13) | collective-permute-done | bytes 262176 | tf_op jit(solution)/shard_map/ppermute | solution.py:211
  43.8 1.5 %collective-permute-start.14 = (bf16[2,16,1024]{2,1,0:T(8,128)(2,1)S(1)}, bf16[2,16,1024]{2,1,0:T(8,128)(2,1)S(1)}, u32[]{:S(2)}, u32[]{:S(2)}) collective-permute-start(bf16[2,16,1024]{2,1,0:T(8,128)(2,1)S(1)} %get-tuple-element.37), channel_id=1, source_target_pairs={{0,2},{1,3},{2,0},{3,1},{4,6},{5,7},{6,4},{7,5},{8,10},{9,11},{10,... | collective-permute-start | bytes 196616 | tf_op jit(solution)/shard_map/ppermute | solution.py:208
  46.0 1.4 %collective-permute-start.16 = (bf16[2,16,1024]{2,1,0:T(8,128)(2,1)S(1)}, bf16[2,16,1024]{2,1,0:T(8,128)(2,1)S(1)}, u32[]{:S(2)}, u32[]{:S(2)}) collective-permute-start(bf16[2,16,1024]{2,1,0:T(8,128)(2,1)S(1)} %get-tuple-element.39), channel_id=1, source_target_pairs={{0,6},{1,7},{2,4},{3,5},{4,2},{5,3},{6,0},{7,1},{8,14},{9,15},{10,... | collective-permute-start | bytes 196616 | tf_op jit(solution)/shard_map/ppermute | solution.py:208
  47.4 2.6 %collective-permute-start.12 = (bf16[2,32,1024]{2,1,0:T(8,128)(2,1)S(1)}, bf16[2,32,1024]{2,1,0:T(8,128)(2,1)S(1)}, u32[]{:S(2)}, u32[]{:S(2)}) collective-permute-start(bf16[2,32,1024]{2,1,0:T(8,128)(2,1)S(1)} %add.1), channel_id=1, source_target_pairs={{0,16},{8,24},{16,0},{24,8},{1,17},{9,25},{17,1},{25,9},{2,18},{10... | collective-permute-start | bytes 393224 | tf_op jit(solution)/shard_map/ppermute | solution.py:211
  50.1 1.1 %collective-permute-done.16.refs_3_ = bf16[2,16,1024]{2,1,0:T(8,128)(2,1)S(1)} collective-permute-done((bf16[2,16,1024]{2,1,0:T(8,128)(2,1)S(1)}, bf16[2,16,1024]{2,1,0:T(8,128)(2,1)S(1)}, u32[]{:S(2)}, u32[]{:S(2)}) %collective-permute-start.16) | collective-permute-done | bytes 65568 | tf_op jit(solution)/shard_map/ppermute | solution.py:208
  51.2 1.6 %collective-permute-start.17 = (bf16[2,16,1024]{2,1,0:T(8,128)(2,1)S(1)}, bf16[2,16,1024]{2,1,0:T(8,128)(2,1)S(1)}, u32[]{:S(2)}, u32[]{:S(2)}) collective-permute-start(bf16[2,16,1024]{2,1,0:T(8,128)(2,1)S(1)} %get-tuple-element.41), channel_id=1, source_target_pairs={{0,8},{8,0},{16,24},{24,16},{1,9},{9,1},{17,25},{25,17},{2,10},{10... | collective-permute-start | bytes 196616 | tf_op jit(solution)/shard_map/ppermute | solution.py:211
  52.8 2.6 %collective-permute-start.18 = (bf16[2,16,1024]{2,1,0:T(8,128)(2,1)S(1)}, bf16[2,16,1024]{2,1,0:T(8,128)(2,1)S(1)}, u32[]{:S(2)}, u32[]{:S(2)}) collective-permute-start(bf16[2,16,1024]{2,1,0:T(8,128)(2,1)S(1)} %get-tuple-element.42), channel_id=1, source_target_pairs={{0,16},{8,24},{16,0},{24,8},{1,17},{9,25},{17,1},{25,9},{2,18},{10... | collective-permute-start | bytes 196616 | tf_op jit(solution)/shard_map/ppermute | solution.py:211
  55.6 1.5 %collective-permute-done.17.refs_4_ = bf16[2,16,1024]{2,1,0:T(8,128)(2,1)S(1)} collective-permute-done((bf16[2,16,1024]{2,1,0:T(8,128)(2,1)S(1)}, bf16[2,16,1024]{2,1,0:T(8,128)(2,1)S(1)}, u32[]{:S(2)}, u32[]{:S(2)}) %collective-permute-start.17) | collective-permute-done | bytes 65568 | tf_op jit(solution)/shard_map/ppermute | solution.py:211
  57.2 1.6 %collective-permute-done.18.refs_5_ = bf16[2,16,1024]{2,1,0:T(8,128)(2,1)S(1)} collective-permute-done((bf16[2,16,1024]{2,1,0:T(8,128)(2,1)S(1)}, bf16[2,16,1024]{2,1,0:T(8,128)(2,1)S(1)}, u32[]{:S(2)}, u32[]{:S(2)}) %collective-permute-start.18) | collective-permute-done | bytes 65568 | tf_op jit(solution)/shard_map/ppermute | solution.py:211
  58.7 2.7 %collective-permute-done.19.refs_6_ = bf16[2,16,1024]{2,1,0:T(8,128)(2,1)S(1)} collective-permute-done((bf16[2,16,1024]{2,1,0:T(8,128)(2,1)S(1)}, bf16[2,16,1024]{2,1,0:T(8,128)(2,1)S(1)}, u32[]{:S(2)}, u32[]{:S(2)}) %collective-permute-start.19) | collective-permute-done | bytes 65568 | tf_op jit(solution)/shard_map/ppermute | solution.py:211
  61.5 0.8 %finish.1 = bf16[64,2048]{1,0:T(8,128)(2,1)} custom-call(bf16[2,2,32,1024]{3,2,1,0:T(8,128)(2,1)S(1)} %get-tuple-element.32.keep_ref.refs_0_, bf16[2,2,32,1024]{3,2,1,0:T(8,128)(2,1)S(1)} %collective-permute-done.11.came_ref.refs_1_, bf16[2,32,1024]{2,1,0:T(8,128)(2,1)S(1)} %collective-permute-done.12.refs_2_, ...), custom_call_target="tpu_custom_call" | custom-call | bytes 1310720 | tf_op jit(solution)/shard_map/finish/pallas_call | solution.py:330
  (34 shorter events, 3.9 us)
Async XLA Ops:
  0.6 13.1 %collective-permute-start.3 = (bf16[1024,2048]{1,0:T(8,128)(2,1)}, bf16[1024,2048]{1,0:T(8,128)(2,1)}, u32[]{:S(2)}, u32[]{:S(2)}) collective-permute-start(bf16[1024,2048]{1,0:T(8,128)(2,1)} %w_ref.1), channel_id=1, source_target_pairs={{0,1},{1,0},{2,3},{3,2},{4,5},{5,4},{6,7},{7,6},{8,9},{9,8},{10,11... | collective-permute-start | bytes 12582920 | tf_op jit(solution)/shard_map/ppermute | solution.py:214
  1.1 23.4 %collective-permute-start.7 = (bf16[2048,1024]{1,0:T(8,128)(2,1)}, bf16[2048,1024]{1,0:T(8,128)(2,1)}, u32[]{:S(2)}, u32[]{:S(2)}) collective-permute-start(bf16[2048,1024]{1,0:T(8,128)(2,1)} %refs_7_.1), channel_id=1, source_target_pairs={{0,1},{1,0},{2,3},{3,2},{4,5},{5,4},{6,7},{7,6},{8,9},{9,8},{10,11... | collective-permute-start | bytes 12582920 | tf_op jit(solution)/shard_map/ppermute | solution.py:215
  1.2 1.2 %copy-start.2 = (bf16[64,8192]{1,0:T(8,128)(2,1)S(1)}, bf16[64,8192]{1,0:T(8,128)(2,1)}, u32[]{:S(2)}) copy-start(bf16[64,8192]{1,0:T(8,128)(2,1)} %tok_ref.1) | copy-start | bytes 3145732
  2.5 11.2 %copy-start.4 = (bf16[8192]{0:T(1024)(128)(2,1)S(1)}, bf16[8192]{0:T(1024)(128)(2,1)}, u32[]{:S(2)}) copy-start(bf16[8192]{0:T(1024)(128)(2,1)} %param.8) | copy-start | bytes 49156
  3.3 14.8 %collective-permute-start = (bf16[2,64,1024]{2,1,0:T(8,128)(2,1)}, bf16[2,64,1024]{2,1,0:T(8,128)(2,1)S(1)}, u32[]{:S(2)}, u32[]{:S(2)}) collective-permute-start(bf16[2,64,1024]{2,1,0:T(8,128)(2,1)} %get-tuple-element.24), channel_id=1, source_target_pairs={{0,2},{1,3},{2,0},{3,1},{4,6},{5,7},{6,4},{7,5},{8,10},{9,11},{10,... | collective-permute-start | bytes 786440 | tf_op jit(solution)/shard_map/ppermute | solution.py:208
  6.2 13.8 %collective-permute-start.1 = (bf16[2,64,1024]{2,1,0:T(8,128)(2,1)}, bf16[2,64,1024]{2,1,0:T(8,128)(2,1)S(1)}, u32[]{:S(2)}, u32[]{:S(2)}) collective-permute-start(bf16[2,64,1024]{2,1,0:T(8,128)(2,1)} %get-tuple-element.25), channel_id=1, source_target_pairs={{0,4},{1,5},{2,6},{3,7},{4,0},{5,1},{6,2},{7,3},{8,12},{9,13},{10,... | collective-permute-start | bytes 786440 | tf_op jit(solution)/shard_map/ppermute | solution.py:208
  7.8 12.3 %collective-permute-start.2 = (bf16[2,64,1024]{2,1,0:T(8,128)(2,1)S(1)}, bf16[2,64,1024]{2,1,0:T(8,128)(2,1)S(1)}, u32[]{:S(2)}, u32[]{:S(2)}) collective-permute-start(bf16[2,64,1024]{2,1,0:T(8,128)(2,1)S(1)} %get-tuple-element.26), channel_id=1, source_target_pairs={{0,6},{1,7},{2,4},{3,5},{4,2},{5,3},{6,0},{7,1},{8,14},{9,15},{10,... | collective-permute-start | bytes 786440 | tf_op jit(solution)/shard_map/ppermute | solution.py:208
  8.5 2.2 %copy-start.1 = (bf16[1024,2048]{1,0:T(8,128)(2,1)S(1)}, bf16[1024,2048]{1,0:T(8,128)(2,1)}, u32[]{:S(2)}) copy-start(bf16[1024,2048]{1,0:T(8,128)(2,1)} %w_ref.1) | copy-start | bytes 12582916
  18.1 6.4 %copy-start.5 = (bf16[2048]{0:T(1024)(128)(2,1)S(1)}, bf16[2048]{0:T(1024)(128)(2,1)}, u32[]{:S(2)}) copy-start(bf16[2048]{0:T(1024)(128)(2,1)} %param.10) | copy-start | bytes 12292
  20.9 6.1 %collective-permute-start.4 = (bf16[4,64,256]{2,1,0:T(8,128)(2,1)S(1)}, bf16[4,64,256]{2,1,0:T(8,128)(2,1)S(1)}, u32[]{:S(2)}, u32[]{:S(2)}) collective-permute-start(bf16[4,64,256]{2,1,0:T(8,128)(2,1)S(1)} %encode.1.refs_3_), channel_id=1, source_target_pairs={{0,2},{1,3},{2,0},{3,1},{4,6},{5,7},{6,4},{7,5},{8,10},{9,11},{10,... | collective-permute-start | bytes 393224 | tf_op jit(solution)/shard_map/ppermute | solution.py:208
  22.2 7.2 %collective-permute-start.5 = (bf16[4,64,256]{2,1,0:T(8,128)(2,1)S(1)}, bf16[4,64,256]{2,1,0:T(8,128)(2,1)S(1)}, u32[]{:S(2)}, u32[]{:S(2)}) collective-permute-start(bf16[4,64,256]{2,1,0:T(8,128)(2,1)S(1)} %encode.1.refs_3_), channel_id=1, source_target_pairs={{0,4},{1,5},{2,6},{3,7},{4,0},{5,1},{6,2},{7,3},{8,12},{9,13},{10,... | collective-permute-start | bytes 393224 | tf_op jit(solution)/shard_map/ppermute | solution.py:208
  23.1 6.4 %collective-permute-start.6 = (bf16[4,64,256]{2,1,0:T(8,128)(2,1)S(1)}, bf16[4,64,256]{2,1,0:T(8,128)(2,1)S(1)}, u32[]{:S(2)}, u32[]{:S(2)}) collective-permute-start(bf16[4,64,256]{2,1,0:T(8,128)(2,1)S(1)} %encode.1.refs_3_), channel_id=1, source_target_pairs={{0,6},{1,7},{2,4},{3,5},{4,2},{5,3},{6,0},{7,1},{8,14},{9,15},{10,... | collective-permute-start | bytes 393224 | tf_op jit(solution)/shard_map/ppermute | solution.py:208
  24.5 4.9 %copy-start = (bf16[2048,1024]{1,0:T(8,128)(2,1)S(1)}, bf16[2048,1024]{1,0:T(8,128)(2,1)}, u32[]{:S(2)}) copy-start(bf16[2048,1024]{1,0:T(8,128)(2,1)} %refs_7_.1) | copy-start | bytes 12582916
  24.5 4.9 %copy-start.3 = (s32[8,1]{0,1:T(1,128)S(1)}, s32[8,1]{0,1:T(1,128)}, u32[]{:S(2)}) copy-start(s32[8,1]{0,1:T(1,128)} %param.13) | copy-start | bytes 100
  31.4 5.9 %collective-permute-start.10 = (bf16[2,32,1024]{2,1,0:T(8,128)(2,1)S(1)}, bf16[2,32,1024]{2,1,0:T(8,128)(2,1)S(1)}, u32[]{:S(2)}, u32[]{:S(2)}) collective-permute-start(bf16[2,32,1024]{2,1,0:T(8,128)(2,1)S(1)} %get-tuple-element.31), channel_id=1, source_target_pairs={{0,6},{1,7},{2,4},{3,5},{4,2},{5,3},{6,0},{7,1},{8,14},{9,15},{10,... | collective-permute-start | bytes 393224 | tf_op jit(solution)/shard_map/ppermute | solution.py:208
  33.1 5.5 %collective-permute-start.8 = (bf16[2,32,1024]{2,1,0:T(8,128)(2,1)S(1)}, bf16[2,32,1024]{2,1,0:T(8,128)(2,1)S(1)}, u32[]{:S(2)}, u32[]{:S(2)}) collective-permute-start(bf16[2,32,1024]{2,1,0:T(8,128)(2,1)S(1)} %get-tuple-element.29), channel_id=1, source_target_pairs={{0,2},{1,3},{2,0},{3,1},{4,6},{5,7},{6,4},{7,5},{8,10},{9,11},{10,... | collective-permute-start | bytes 393224 | tf_op jit(solution)/shard_map/ppermute | solution.py:208
  34.1 5.0 %collective-permute-start.9 = (bf16[2,32,1024]{2,1,0:T(8,128)(2,1)S(1)}, bf16[2,32,1024]{2,1,0:T(8,128)(2,1)S(1)}, u32[]{:S(2)}, u32[]{:S(2)}) collective-permute-start(bf16[2,32,1024]{2,1,0:T(8,128)(2,1)S(1)} %get-tuple-element.30), channel_id=1, source_target_pairs={{0,4},{1,5},{2,6},{3,7},{4,0},{5,1},{6,2},{7,3},{8,12},{9,13},{10,... | collective-permute-start | bytes 393224 | tf_op jit(solution)/shard_map/ppermute | solution.py:208
  34.9 8.9 %collective-permute-start.13 = (bf16[4,2,16,1024]{3,2,1,0:T(8,128)(2,1)S(1)}, bf16[4,2,16,1024]{3,2,1,0:T(8,128)(2,1)S(1)}, u32[]{:S(2)}, u32[]{:S(2)}) collective-permute-start(bf16[4,2,16,1024]{3,2,1,0:T(8,128)(2,1)S(1)} %get-tuple-element.35), channel_id=1, source_target_pairs={{0,8},{8,0},{16,24},{24,16},{1,9},{9,1},{17,25},{25,17},{2,10},{10... | collective-permute-start | bytes 786440 | tf_op jit(solution)/shard_map/ppermute | solution.py:211
  39.2 8.2 %collective-permute-start.11 = (bf16[2,2,32,1024]{3,2,1,0:T(8,128)(2,1)S(1)}, bf16[2,2,32,1024]{3,2,1,0:T(8,128)(2,1)S(1)}, u32[]{:S(2)}, u32[]{:S(2)}) collective-permute-start(bf16[2,2,32,1024]{3,2,1,0:T(8,128)(2,1)S(1)} %get-tuple-element.33), channel_id=1, source_target_pairs={{0,8},{8,0},{16,24},{24,16},{1,9},{9,1},{17,25},{25,17},{2,10},{10... | collective-permute-start | bytes 786440 | tf_op jit(solution)/shard_map/ppermute | solution.py:211
  43.8 6.2 %collective-permute-start.14 = (bf16[2,16,1024]{2,1,0:T(8,128)(2,1)S(1)}, bf16[2,16,1024]{2,1,0:T(8,128)(2,1)S(1)}, u32[]{:S(2)}, u32[]{:S(2)}) collective-permute-start(bf16[2,16,1024]{2,1,0:T(8,128)(2,1)S(1)} %get-tuple-element.37), channel_id=1, source_target_pairs={{0,2},{1,3},{2,0},{3,1},{4,6},{5,7},{6,4},{7,5},{8,10},{9,11},{10,... | collective-permute-start | bytes 196616 | tf_op jit(solution)/shard_map/ppermute | solution.py:208
  45.4 4.7 %collective-permute-start.15 = (bf16[2,16,1024]{2,1,0:T(8,128)(2,1)S(1)}, bf16[2,16,1024]{2,1,0:T(8,128)(2,1)S(1)}, u32[]{:S(2)}, u32[]{:S(2)}) collective-permute-start(bf16[2,16,1024]{2,1,0:T(8,128)(2,1)S(1)} %get-tuple-element.38), channel_id=1, source_target_pairs={{0,4},{1,5},{2,6},{3,7},{4,0},{5,1},{6,2},{7,3},{8,12},{9,13},{10,... | collective-permute-start | bytes 196616 | tf_op jit(solution)/shard_map/ppermute | solution.py:208
  46.0 5.2 %collective-permute-start.16 = (bf16[2,16,1024]{2,1,0:T(8,128)(2,1)S(1)}, bf16[2,16,1024]{2,1,0:T(8,128)(2,1)S(1)}, u32[]{:S(2)}, u32[]{:S(2)}) collective-permute-start(bf16[2,16,1024]{2,1,0:T(8,128)(2,1)S(1)} %get-tuple-element.39), channel_id=1, source_target_pairs={{0,6},{1,7},{2,4},{3,5},{4,2},{5,3},{6,0},{7,1},{8,14},{9,15},{10,... | collective-permute-start | bytes 196616 | tf_op jit(solution)/shard_map/ppermute | solution.py:208
  47.4 14.0 %collective-permute-start.12 = (bf16[2,32,1024]{2,1,0:T(8,128)(2,1)S(1)}, bf16[2,32,1024]{2,1,0:T(8,128)(2,1)S(1)}, u32[]{:S(2)}, u32[]{:S(2)}) collective-permute-start(bf16[2,32,1024]{2,1,0:T(8,128)(2,1)S(1)} %add.1), channel_id=1, source_target_pairs={{0,16},{8,24},{16,0},{24,8},{1,17},{9,25},{17,1},{25,9},{2,18},{10... | collective-permute-start | bytes 393224 | tf_op jit(solution)/shard_map/ppermute | solution.py:211
  51.2 6.0 %collective-permute-start.17 = (bf16[2,16,1024]{2,1,0:T(8,128)(2,1)S(1)}, bf16[2,16,1024]{2,1,0:T(8,128)(2,1)S(1)}, u32[]{:S(2)}, u32[]{:S(2)}) collective-permute-start(bf16[2,16,1024]{2,1,0:T(8,128)(2,1)S(1)} %get-tuple-element.41), channel_id=1, source_target_pairs={{0,8},{8,0},{16,24},{24,16},{1,9},{9,1},{17,25},{25,17},{2,10},{10... | collective-permute-start | bytes 196616 | tf_op jit(solution)/shard_map/ppermute | solution.py:211
  52.8 5.9 %collective-permute-start.18 = (bf16[2,16,1024]{2,1,0:T(8,128)(2,1)S(1)}, bf16[2,16,1024]{2,1,0:T(8,128)(2,1)S(1)}, u32[]{:S(2)}, u32[]{:S(2)}) collective-permute-start(bf16[2,16,1024]{2,1,0:T(8,128)(2,1)S(1)} %get-tuple-element.42), channel_id=1, source_target_pairs={{0,16},{8,24},{16,0},{24,8},{1,17},{9,25},{17,1},{25,9},{2,18},{10... | collective-permute-start | bytes 196616 | tf_op jit(solution)/shard_map/ppermute | solution.py:211
  55.4 6.1 %collective-permute-start.19 = (bf16[2,16,1024]{2,1,0:T(8,128)(2,1)S(1)}, bf16[2,16,1024]{2,1,0:T(8,128)(2,1)S(1)}, u32[]{:S(2)}, u32[]{:S(2)}) collective-permute-start(bf16[2,16,1024]{2,1,0:T(8,128)(2,1)S(1)} %get-tuple-element.43), channel_id=1, source_target_pairs={{0,24},{8,16},{16,8},{24,0},{1,25},{9,17},{17,9},{25,1},{2,26},{10... | collective-permute-start | bytes 196616 | tf_op jit(solution)/shard_map/ppermute | solution.py:211

commit v5 on v4

--- a/solution.py
+++ b/solution.py
@@ -283,6 +283,16 @@
 
     swapped = lift(sent_sums, 1)
     came = [firsts[0]] + [swap(firsts[p], p) for p in range(1, groups)]
+    merged = pl.pallas_call(
+        functools.partial(merge_kernel, groups),
+        out_shape=[small] * groups,
+        in_specs=[spec(VMEM)] * 2,
+        out_specs=[spec(VMEM)] * groups,
+        compiler_params=params(8),
+        cost_estimate=cost(0, 8 * groups * quarter_rows * wslice),
+        name="merge",
+    )(own_sums, swapped)
+    came[0], *merged = lax.optimization_barrier((came[0], *merged))
     both = jax.ShapeDtypeStruct((groups // 2,) + piece.shape, BF16)
     keep, send = pl.pallas_call(
         functools.partial(route_kernel, groups),
@@ -295,15 +305,6 @@
         name="route",
     )(*came)
     near = lift(send, 1)
-    merged = pl.pallas_call(
-        functools.partial(merge_kernel, groups),
-        out_shape=[small] * groups,
-        in_specs=[spec(VMEM)] * 2,
-        out_specs=[spec(VMEM)] * groups,
-        compiler_params=params(8),
-        cost_estimate=cost(0, 8 * groups * quarter_rows * wslice),
-        name="merge",
-    )(own_sums, swapped)
     merged = [merged[0]] + [swap(merged[p], p) for p in range(1, groups)]
     direct = pl.pallas_call(
         functools.partial(direct_kernel, groups),

time: 62.6 us -> 61.5 us (0.982)
  starting transfers between devices: 25.9 us -> 24.1 us
  waiting for transfers between devices: 17 us -> 17.7 us
    ppermute x6, starting transfers between devices: 10.3 us -> 8.48 us  [lift(): return lax.ppermute(value, 'feat', [(i, i ^ m) for i in range(groups)])]
    ppermute x6, waiting for transfers between devices: 8.79 us -> 9.65 us  [lift(): return lax.ppermute(value, 'feat', [(i, i ^ m) for i in range(groups)])]
where the time goes in v5:
time: 61.5 us; the launch traced here: 61.2 us
  starting transfers between devices  24.1 us (39%)
  waiting for transfers between devices  17.7 us (29%)
  Pallas kernels  14.4 us (23%)
  local copies, waits for them, and re-layouts  4.2 us (7%)
  between operations  0.77 us (1%)
    ppermute x12, starting transfers between devices, swap(): return lax.ppermute(value, 'tok', pairs)  15 us
    ppermute x6, waiting for transfers between devices, lift(): return lax.ppermute(value, 'feat', [(i, i ^ m) for i in range(groups)])  9.65 us
    ppermute x6, starting transfers between devices, lift(): return lax.ppermute(value, 'feat', [(i, i ^ m) for i in range(groups)])  8.48 us
    ppermute x12, waiting for transfers between devices, swap(): return lax.ppermute(value, 'tok', pairs)  8.05 us
    pallas_call x2, Pallas kernels, columns(): pl.pallas_call(functools.partial(columns_kernel, groups), out_shape=jax.S...  7.32 us
    unnamed x12, local copies, waits for them, and re-layouts  3.43 us
    pallas_call x1, Pallas kernels, on_device(): pl.pallas_call(stage_kernel, out_shape=jax.ShapeDtypeStruct(dec_weight.sh...  2.37 us
    pallas_call x1, Pallas kernels, on_device(): pl.pallas_call(functools.partial(decode_kernel, groups), out_shape=[jax.S...  1.97 us
  transfers between devices with their start and end apart: 20, of which 11 were waited for; matrix products, arithmetic and copies ran while one was open for 1% of the time, Pallas kernels for 19%

profile of v5, /device:TPU:0, one launch (start us, length us, event | category | flops | bytes accessed | tf_op | source)
XLA Modules:
  0.0 61.2 jit_solution(13977082521161423587)
XLA Ops:
  1.2 1.2 %copy-done.2 = bf16[64,8192]{1,0:T(8,128)(2,1)S(1)} copy-done((bf16[64,8192]{1,0:T(8,128)(2,1)S(1)}, bf16[64,8192]{1,0:T(8,128)(2,1)}, u32[]{:S(2)}) %copy-start.2) | copy-done | bytes 1048600
  2.5 0.9 %split.1 = (bf16[2,64,1024]{2,1,0:T(8,128)(2,1)S(1)}, bf16[2,64,1024]{2,1,0:T(8,128)(2,1)}, bf16[2,64,1024]{2,1,0:T(8,128)(2,1)}, bf16[2,64,1024]{2,1,0:T(8,128)(2,1)S(1)}) custom-call(bf16[64,8192]{1,0:T(8,128)(2,1)S(1)} %copy-done.2), custom_call_target="tpu_custom_call" | custom-call | bytes 2097152 | tf_op jit(solution)/shard_map/split/pallas_call | solution.py:217
  3.3 2.9 %collective-permute-start = (bf16[2,64,1024]{2,1,0:T(8,128)(2,1)}, bf16[2,64,1024]{2,1,0:T(8,128)(2,1)S(1)}, u32[]{:S(2)}, u32[]{:S(2)}) collective-permute-start(bf16[2,64,1024]{2,1,0:T(8,128)(2,1)} %get-tuple-element.29), channel_id=1, source_target_pairs={{0,2},{1,3},{2,0},{3,1},{4,6},{5,7},{6,4},{7,5},{8,10},{9,11},{10,... | collective-permute-start | bytes 786440 | tf_op jit(solution)/shard_map/ppermute | solution.py:208
  6.2 1.5 %collective-permute-start.1 = (bf16[2,64,1024]{2,1,0:T(8,128)(2,1)}, bf16[2,64,1024]{2,1,0:T(8,128)(2,1)S(1)}, u32[]{:S(2)}, u32[]{:S(2)}) collective-permute-start(bf16[2,64,1024]{2,1,0:T(8,128)(2,1)} %get-tuple-element.30), channel_id=1, source_target_pairs={{0,4},{1,5},{2,6},{3,7},{4,0},{5,1},{6,2},{7,3},{8,12},{9,13},{10,... | collective-permute-start | bytes 786440 | tf_op jit(solution)/shard_map/ppermute | solution.py:208
  7.8 0.8 %copy.11.ids_ref.refs_0_ = s32[8,4]{1,0:T(8,128)S(1)} copy(s32[8,4]{0,1:T(4,128)} %bitcast.6) | data formatting | bytes 256 | tf_op jit(solution)/shard_map/squeeze | solution.py:201
  8.5 2.2 %copy-done.1 = bf16[1024,2048]{1,0:T(8,128)(2,1)S(1)} copy-done((bf16[1024,2048]{1,0:T(8,128)(2,1)S(1)}, bf16[1024,2048]{1,0:T(8,128)(2,1)}, u32[]{:S(2)}) %copy-start.1) | copy-done | bytes 4194328
  10.7 3.0 %columns.2.refs_5_ = bf16[4,1024,256]{2,1,0:T(8,128)(2,1)S(1)} custom-call(s32[8,4]{1,0:T(8,128)S(1)} %copy.11.ids_ref.refs_0_, bf16[1024,2048]{1,0:T(8,128)(2,1)S(1)} %copy-done.1), custom_call_target="tpu_custom_call" | custom-call | bytes 6291456 | tf_op jit(solution)/shard_map/columns/pallas_call | solution.py:231
  13.8 4.3 %columns.3.refs_6_ = bf16[4,1024,256]{2,1,0:T(8,128)(2,1)S(1)} custom-call(s32[8,4]{1,0:T(8,128)S(1)} %copy.11.ids_ref.refs_0_, bf16[1024,2048]{1,0:T(8,128)(2,1)} %collective-permute-done.3.w_ref), custom_call_target="tpu_custom_call" | custom-call | bytes 6291456 | tf_op jit(solution)/shard_map/columns/pallas_call | solution.py:231
  18.1 2.0 %collective-permute-done.1.refs_3_ = bf16[2,64,1024]{2,1,0:T(8,128)(2,1)S(1)} collective-permute-done((bf16[2,64,1024]{2,1,0:T(8,128)(2,1)}, bf16[2,64,1024]{2,1,0:T(8,128)(2,1)S(1)}, u32[]{:S(2)}, u32[]{:S(2)}) %collective-permute-start.1) | collective-permute-done | bytes 262176 | tf_op jit(solution)/shard_map/ppermute | solution.py:208
  20.1 0.8 %encode.1.refs_3_ = bf16[4,64,256]{2,1,0:T(8,128)(2,1)S(1)} custom-call(f32[8,1024]{1,0:T(8,128)S(1)} %reshape.21.refs_0_.refs_7_, bf16[2,64,1024]{2,1,0:T(8,128)(2,1)S(1)} %get-tuple-element.28.refs_1_, bf16[2,64,1024]{2,1,0:T(8,128)(2,1)S(1)} %collective-permute-done.refs_2_, bf16[2,64,1024]{2,1,0:T(8,128)(2,1)S(1)} %collective-permute-done.1.refs_3_, ...), custom_call_target="tpu_custom_call" | custom-call | flops 268435456 | bytes 4194304 | tf_op jit(solution)/shard_map/encode/pallas_call | solution.py:245
  20.9 1.3 %collective-permute-start.4 = (bf16[4,64,256]{2,1,0:T(8,128)(2,1)S(1)}, bf16[4,64,256]{2,1,0:T(8,128)(2,1)S(1)}, u32[]{:S(2)}, u32[]{:S(2)}) collective-permute-start(bf16[4,64,256]{2,1,0:T(8,128)(2,1)S(1)} %encode.1.refs_3_), channel_id=1, source_target_pairs={{0,2},{1,3},{2,0},{3,1},{4,6},{5,7},{6,4},{7,5},{8,10},{9,11},{10,... | collective-permute-start | bytes 393224 | tf_op jit(solution)/shard_map/ppermute | solution.py:208
  22.2 0.8 %collective-permute-start.5 = (bf16[4,64,256]{2,1,0:T(8,128)(2,1)S(1)}, bf16[4,64,256]{2,1,0:T(8,128)(2,1)S(1)}, u32[]{:S(2)}, u32[]{:S(2)}) collective-permute-start(bf16[4,64,256]{2,1,0:T(8,128)(2,1)S(1)} %encode.1.refs_3_), channel_id=1, source_target_pairs={{0,4},{1,5},{2,6},{3,7},{4,0},{5,1},{6,2},{7,3},{8,12},{9,13},{10,... | collective-permute-start | bytes 393224 | tf_op jit(solution)/shard_map/ppermute | solution.py:208
  23.1 1.4 %collective-permute-start.6 = (bf16[4,64,256]{2,1,0:T(8,128)(2,1)S(1)}, bf16[4,64,256]{2,1,0:T(8,128)(2,1)S(1)}, u32[]{:S(2)}, u32[]{:S(2)}) collective-permute-start(bf16[4,64,256]{2,1,0:T(8,128)(2,1)S(1)} %encode.1.refs_3_), channel_id=1, source_target_pairs={{0,6},{1,7},{2,4},{3,5},{4,2},{5,3},{6,0},{7,1},{8,14},{9,15},{10,... | collective-permute-start | bytes 393224 | tf_op jit(solution)/shard_map/ppermute | solution.py:208
  24.5 2.4 %stage.1.refs_8_ = bf16[2048,1024]{1,0:T(8,128)(2,1)S(1)} custom-call(bf16[2048,1024]{1,0:T(8,128)(2,1)} %collective-permute-done.7.src), custom_call_target="tpu_custom_call" | custom-call | bytes 8388608 | tf_op jit(solution)/shard_map/stage/pallas_call | solution.py:256
  27.1 2.4 %collective-permute-done.5.refs_5_ = bf16[4,64,256]{2,1,0:T(8,128)(2,1)S(1)} collective-permute-done((bf16[4,64,256]{2,1,0:T(8,128)(2,1)S(1)}, bf16[4,64,256]{2,1,0:T(8,128)(2,1)S(1)}, u32[]{:S(2)}, u32[]{:S(2)}) %collective-permute-start.5) | collective-permute-done | bytes 131104 | tf_op jit(solution)/shard_map/ppermute | solution.py:208
  29.4 2.0 %decode.1 = (bf16[64,256]{1,0:T(8,128)(2,1)}, bf16[2,32,1024]{2,1,0:T(8,128)(2,1)S(1)}, bf16[2,32,1024]{2,1,0:T(8,128)(2,1)S(1)}, bf16[2,32,1024]{2,1,0:T(8,128)...) custom-call(s32[8,4]{1,0:T(8,128)S(1)} %copy.11.ids_ref.refs_0_, ...), custom_call_target="tpu_custom_call" | custom-call | flops 268435456 | bytes 4194304 | tf_op jit(solution)/shard_map/decode/pallas_call | solution.py:271
  31.4 1.6 %collective-permute-start.8 = (bf16[4,2,16,1024]{3,2,1,0:T(8,128)(2,1)S(1)}, bf16[4,2,16,1024]{3,2,1,0:T(8,128)(2,1)S(1)}, u32[]{:S(2)}, u32[]{:S(2)}) collective-permute-start(bf16[4,2,16,1024]{3,2,1,0:T(8,128)(2,1)S(1)} %get-tuple-element.35), channel_id=1, source_target_pairs={{0,8},{8,0},{16,24},{24,16},{1,9},{9,1},{17,25},{25,17},{2,10},{10... | collective-permute-start | bytes 786440 | tf_op jit(solution)/shard_map/ppermute | solution.py:211
  33.0 1.3 %collective-permute-start.10 = (bf16[2,32,1024]{2,1,0:T(8,128)(2,1)S(1)}, bf16[2,32,1024]{2,1,0:T(8,128)(2,1)S(1)}, u32[]{:S(2)}, u32[]{:S(2)}) collective-permute-start(bf16[2,32,1024]{2,1,0:T(8,128)(2,1)S(1)} %get-tuple-element.42), channel_id=1, source_target_pairs={{0,4},{1,5},{2,6},{3,7},{4,0},{5,1},{6,2},{7,3},{8,12},{9,13},{10,... | collective-permute-start | bytes 393224 | tf_op jit(solution)/shard_map/ppermute | solution.py:208
  34.3 1.2 %collective-permute-start.11 = (bf16[2,32,1024]{2,1,0:T(8,128)(2,1)S(1)}, bf16[2,32,1024]{2,1,0:T(8,128)(2,1)S(1)}, u32[]{:S(2)}, u32[]{:S(2)}) collective-permute-start(bf16[2,32,1024]{2,1,0:T(8,128)(2,1)S(1)} %get-tuple-element.43), channel_id=1, source_target_pairs={{0,6},{1,7},{2,4},{3,5},{4,2},{5,3},{6,0},{7,1},{8,14},{9,15},{10,... | collective-permute-start | bytes 393224 | tf_op jit(solution)/shard_map/ppermute | solution.py:208
  35.4 1.0 %collective-permute-start.9 = (bf16[2,32,1024]{2,1,0:T(8,128)(2,1)S(1)}, bf16[2,32,1024]{2,1,0:T(8,128)(2,1)S(1)}, u32[]{:S(2)}, u32[]{:S(2)}) collective-permute-start(bf16[2,32,1024]{2,1,0:T(8,128)(2,1)S(1)} %get-tuple-element.41), channel_id=1, source_target_pairs={{0,2},{1,3},{2,0},{3,1},{4,6},{5,7},{6,4},{7,5},{8,10},{9,11},{10,... | collective-permute-start | bytes 393224 | tf_op jit(solution)/shard_map/ppermute | solution.py:208
  36.5 1.3 %collective-permute-done.8.came_ref = bf16[4,2,16,1024]{3,2,1,0:T(8,128)(2,1)S(1)} collective-permute-done((bf16[4,2,16,1024]{3,2,1,0:T(8,128)(2,1)S(1)}, bf16[4,2,16,1024]{3,2,1,0:T(8,128)(2,1)S(1)}, u32[]{:S(2)}, u32[]{:S(2)}) %collective-permute-start.8) | collective-permute-done | bytes 262176 | tf_op jit(solution)/shard_map/ppermute | solution.py:211
  38.3 1.8 %collective-permute-done.11.refs_3_ = bf16[2,32,1024]{2,1,0:T(8,128)(2,1)S(1)} collective-permute-done((bf16[2,32,1024]{2,1,0:T(8,128)(2,1)S(1)}, bf16[2,32,1024]{2,1,0:T(8,128)(2,1)S(1)}, u32[]{:S(2)}, u32[]{:S(2)}) %collective-permute-start.11) | collective-permute-done | bytes 131104 | tf_op jit(solution)/shard_map/ppermute | solution.py:208
  40.1 1.2 %collective-permute-done.9.refs_1_ = bf16[2,32,1024]{2,1,0:T(8,128)(2,1)S(1)} collective-permute-done((bf16[2,32,1024]{2,1,0:T(8,128)(2,1)S(1)}, bf16[2,32,1024]{2,1,0:T(8,128)(2,1)S(1)}, u32[]{:S(2)}, u32[]{:S(2)}) %collective-permute-start.9) | collective-permute-done | bytes 131104 | tf_op jit(solution)/shard_map/ppermute | solution.py:208
  41.5 1.3 %collective-permute-start.14 = (bf16[2,16,1024]{2,1,0:T(8,128)(2,1)S(1)}, bf16[2,16,1024]{2,1,0:T(8,128)(2,1)S(1)}, u32[]{:S(2)}, u32[]{:S(2)}) collective-permute-start(bf16[2,16,1024]{2,1,0:T(8,128)(2,1)S(1)} %get-tuple-element.47), channel_id=1, source_target_pairs={{0,2},{1,3},{2,0},{3,1},{4,6},{5,7},{6,4},{7,5},{8,10},{9,11},{10,... | collective-permute-start | bytes 196616 | tf_op jit(solution)/shard_map/ppermute | solution.py:208
  42.8 1.2 %collective-permute-start.15 = (bf16[2,16,1024]{2,1,0:T(8,128)(2,1)S(1)}, bf16[2,16,1024]{2,1,0:T(8,128)(2,1)S(1)}, u32[]{:S(2)}, u32[]{:S(2)}) collective-permute-start(bf16[2,16,1024]{2,1,0:T(8,128)(2,1)S(1)} %get-tuple-element.48), channel_id=1, source_target_pairs={{0,4},{1,5},{2,6},{3,7},{4,0},{5,1},{6,2},{7,3},{8,12},{9,13},{10,... | collective-permute-start | bytes 196616 | tf_op jit(solution)/shard_map/ppermute | solution.py:208
  43.9 1.1 %collective-permute-start.16 = (bf16[2,16,1024]{2,1,0:T(8,128)(2,1)S(1)}, bf16[2,16,1024]{2,1,0:T(8,128)(2,1)S(1)}, u32[]{:S(2)}, u32[]{:S(2)}) collective-permute-start(bf16[2,16,1024]{2,1,0:T(8,128)(2,1)S(1)} %get-tuple-element.49), channel_id=1, source_target_pairs={{0,6},{1,7},{2,4},{3,5},{4,2},{5,3},{6,0},{7,1},{8,14},{9,15},{10,... | collective-permute-start | bytes 196616 | tf_op jit(solution)/shard_map/ppermute | solution.py:208
  45.1 5.3 %collective-permute-done.12.came_ref.refs_1_ = bf16[2,2,32,1024]{3,2,1,0:T(8,128)(2,1)S(1)} collective-permute-done((bf16[2,2,32,1024]{3,2,1,0:T(8,128)(2,1)S(1)}, bf16[2,2,32,1024]{3,2,1,0:T(8,128)(2,1)S(1)}, u32[]{:S(2)}, u32[]{:S(2)}) %collective-permute-start.12) | collective-permute-done | bytes 262176 | tf_op jit(solution)/shard_map/ppermute | solution.py:211
  50.4 2.4 %collective-permute-start.13 = (bf16[2,32,1024]{2,1,0:T(8,128)(2,1)S(1)}, bf16[2,32,1024]{2,1,0:T(8,128)(2,1)S(1)}, u32[]{:S(2)}, u32[]{:S(2)}) collective-permute-start(bf16[2,32,1024]{2,1,0:T(8,128)(2,1)S(1)} %add.1), channel_id=1, source_target_pairs={{0,16},{8,24},{16,0},{24,8},{1,17},{9,25},{17,1},{25,9},{2,18},{10... | collective-permute-start | bytes 393224 | tf_op jit(solution)/shard_map/ppermute | solution.py:211
  53.8 3.5 %collective-permute-start.19 = (bf16[2,16,1024]{2,1,0:T(8,128)(2,1)S(1)}, bf16[2,16,1024]{2,1,0:T(8,128)(2,1)S(1)}, u32[]{:S(2)}, u32[]{:S(2)}) collective-permute-start(bf16[2,16,1024]{2,1,0:T(8,128)(2,1)S(1)} %get-tuple-element.53), channel_id=1, source_target_pairs={{0,24},{8,16},{16,8},{24,0},{1,25},{9,17},{17,9},{25,1},{2,26},{10... | collective-permute-start | bytes 196616 | tf_op jit(solution)/shard_map/ppermute | solution.py:211
  57.6 0.8 %collective-permute-done.18.refs_5_ = bf16[2,16,1024]{2,1,0:T(8,128)(2,1)S(1)} collective-permute-done((bf16[2,16,1024]{2,1,0:T(8,128)(2,1)S(1)}, bf16[2,16,1024]{2,1,0:T(8,128)(2,1)S(1)}, u32[]{:S(2)}, u32[]{:S(2)}) %collective-permute-start.18) | collective-permute-done | bytes 65568 | tf_op jit(solution)/shard_map/ppermute | solution.py:211
  58.4 2.0 %collective-permute-done.19.refs_6_ = bf16[2,16,1024]{2,1,0:T(8,128)(2,1)S(1)} collective-permute-done((bf16[2,16,1024]{2,1,0:T(8,128)(2,1)S(1)}, bf16[2,16,1024]{2,1,0:T(8,128)(2,1)S(1)}, u32[]{:S(2)}, u32[]{:S(2)}) %collective-permute-start.19) | collective-permute-done | bytes 65568 | tf_op jit(solution)/shard_map/ppermute | solution.py:211
  60.4 0.8 %finish.1 = bf16[64,2048]{1,0:T(8,128)(2,1)} custom-call(bf16[2,2,32,1024]{3,2,1,0:T(8,128)(2,1)S(1)} %get-tuple-element.44.keep_ref.refs_0_, bf16[2,2,32,1024]{3,2,1,0:T(8,128)(2,1)S(1)} %collective-permute-done.12.came_ref.refs_1_, bf16[2,32,1024]{2,1,0:T(8,128)(2,1)S(1)} %collective-permute-done.13.refs_2_, ...), custom_call_target="tpu_custom_call" | custom-call | bytes 1310720 | tf_op jit(solution)/shard_map/finish/pallas_call | solution.py:331
  (34 shorter events, 2.7 us)
Async XLA Ops:
  0.6 13.1 %collective-permute-start.3 = (bf16[1024,2048]{1,0:T(8,128)(2,1)}, bf16[1024,2048]{1,0:T(8,128)(2,1)}, u32[]{:S(2)}, u32[]{:S(2)}) collective-permute-start(bf16[1024,2048]{1,0:T(8,128)(2,1)} %w_ref.1), channel_id=1, source_target_pairs={{0,1},{1,0},{2,3},{3,2},{4,5},{5,4},{6,7},{7,6},{8,9},{9,8},{10,11... | collective-permute-start | bytes 12582920 | tf_op jit(solution)/shard_map/ppermute | solution.py:214
  1.1 23.4 %collective-permute-start.7 = (bf16[2048,1024]{1,0:T(8,128)(2,1)}, bf16[2048,1024]{1,0:T(8,128)(2,1)}, u32[]{:S(2)}, u32[]{:S(2)}) collective-permute-start(bf16[2048,1024]{1,0:T(8,128)(2,1)} %refs_7_.1), channel_id=1, source_target_pairs={{0,1},{1,0},{2,3},{3,2},{4,5},{5,4},{6,7},{7,6},{8,9},{9,8},{10,11... | collective-permute-start | bytes 12582920 | tf_op jit(solution)/shard_map/ppermute | solution.py:215
  1.2 1.2 %copy-start.2 = (bf16[64,8192]{1,0:T(8,128)(2,1)S(1)}, bf16[64,8192]{1,0:T(8,128)(2,1)}, u32[]{:S(2)}) copy-start(bf16[64,8192]{1,0:T(8,128)(2,1)} %tok_ref.1) | copy-start | bytes 3145732
  2.5 11.3 %copy-start.4 = (bf16[8192]{0:T(1024)(128)(2,1)S(1)}, bf16[8192]{0:T(1024)(128)(2,1)}, u32[]{:S(2)}) copy-start(bf16[8192]{0:T(1024)(128)(2,1)} %param.8) | copy-start | bytes 49156
  3.3 14.8 %collective-permute-start = (bf16[2,64,1024]{2,1,0:T(8,128)(2,1)}, bf16[2,64,1024]{2,1,0:T(8,128)(2,1)S(1)}, u32[]{:S(2)}, u32[]{:S(2)}) collective-permute-start(bf16[2,64,1024]{2,1,0:T(8,128)(2,1)} %get-tuple-element.29), channel_id=1, source_target_pairs={{0,2},{1,3},{2,0},{3,1},{4,6},{5,7},{6,4},{7,5},{8,10},{9,11},{10,... | collective-permute-start | bytes 786440 | tf_op jit(solution)/shard_map/ppermute | solution.py:208
  6.2 13.8 %collective-permute-start.1 = (bf16[2,64,1024]{2,1,0:T(8,128)(2,1)}, bf16[2,64,1024]{2,1,0:T(8,128)(2,1)S(1)}, u32[]{:S(2)}, u32[]{:S(2)}) collective-permute-start(bf16[2,64,1024]{2,1,0:T(8,128)(2,1)} %get-tuple-element.30), channel_id=1, source_target_pairs={{0,4},{1,5},{2,6},{3,7},{4,0},{5,1},{6,2},{7,3},{8,12},{9,13},{10,... | collective-permute-start | bytes 786440 | tf_op jit(solution)/shard_map/ppermute | solution.py:208
  7.8 12.3 %collective-permute-start.2 = (bf16[2,64,1024]{2,1,0:T(8,128)(2,1)S(1)}, bf16[2,64,1024]{2,1,0:T(8,128)(2,1)S(1)}, u32[]{:S(2)}, u32[]{:S(2)}) collective-permute-start(bf16[2,64,1024]{2,1,0:T(8,128)(2,1)S(1)} %get-tuple-element.31), channel_id=1, source_target_pairs={{0,6},{1,7},{2,4},{3,5},{4,2},{5,3},{6,0},{7,1},{8,14},{9,15},{10,... | collective-permute-start | bytes 786440 | tf_op jit(solution)/shard_map/ppermute | solution.py:208
  8.5 2.2 %copy-start.1 = (bf16[1024,2048]{1,0:T(8,128)(2,1)S(1)}, bf16[1024,2048]{1,0:T(8,128)(2,1)}, u32[]{:S(2)}) copy-start(bf16[1024,2048]{1,0:T(8,128)(2,1)} %w_ref.1) | copy-start | bytes 12582916
  18.1 6.4 %copy-start.5 = (bf16[2048]{0:T(1024)(128)(2,1)S(1)}, bf16[2048]{0:T(1024)(128)(2,1)}, u32[]{:S(2)}) copy-start(bf16[2048]{0:T(1024)(128)(2,1)} %param.10) | copy-start | bytes 12292
  20.9 6.1 %collective-permute-start.4 = (bf16[4,64,256]{2,1,0:T(8,128)(2,1)S(1)}, bf16[4,64,256]{2,1,0:T(8,128)(2,1)S(1)}, u32[]{:S(2)}, u32[]{:S(2)}) collective-permute-start(bf16[4,64,256]{2,1,0:T(8,128)(2,1)S(1)} %encode.1.refs_3_), channel_id=1, source_target_pairs={{0,2},{1,3},{2,0},{3,1},{4,6},{5,7},{6,4},{7,5},{8,10},{9,11},{10,... | collective-permute-start | bytes 393224 | tf_op jit(solution)/shard_map/ppermute | solution.py:208
  22.2 7.2 %collective-permute-start.5 = (bf16[4,64,256]{2,1,0:T(8,128)(2,1)S(1)}, bf16[4,64,256]{2,1,0:T(8,128)(2,1)S(1)}, u32[]{:S(2)}, u32[]{:S(2)}) collective-permute-start(bf16[4,64,256]{2,1,0:T(8,128)(2,1)S(1)} %encode.1.refs_3_), channel_id=1, source_target_pairs={{0,4},{1,5},{2,6},{3,7},{4,0},{5,1},{6,2},{7,3},{8,12},{9,13},{10,... | collective-permute-start | bytes 393224 | tf_op jit(solution)/shard_map/ppermute | solution.py:208
  23.1 6.4 %collective-permute-start.6 = (bf16[4,64,256]{2,1,0:T(8,128)(2,1)S(1)}, bf16[4,64,256]{2,1,0:T(8,128)(2,1)S(1)}, u32[]{:S(2)}, u32[]{:S(2)}) collective-permute-start(bf16[4,64,256]{2,1,0:T(8,128)(2,1)S(1)} %encode.1.refs_3_), channel_id=1, source_target_pairs={{0,6},{1,7},{2,4},{3,5},{4,2},{5,3},{6,0},{7,1},{8,14},{9,15},{10,... | collective-permute-start | bytes 393224 | tf_op jit(solution)/shard_map/ppermute | solution.py:208
  24.5 4.9 %copy-start = (bf16[2048,1024]{1,0:T(8,128)(2,1)S(1)}, bf16[2048,1024]{1,0:T(8,128)(2,1)}, u32[]{:S(2)}) copy-start(bf16[2048,1024]{1,0:T(8,128)(2,1)} %refs_7_.1) | copy-start | bytes 12582916
  24.5 4.9 %copy-start.3 = (s32[8,1]{0,1:T(1,128)S(1)}, s32[8,1]{0,1:T(1,128)}, u32[]{:S(2)}) copy-start(s32[8,1]{0,1:T(1,128)} %param.13) | copy-start | bytes 100
  31.4 6.4 %collective-permute-start.8 = (bf16[4,2,16,1024]{3,2,1,0:T(8,128)(2,1)S(1)}, bf16[4,2,16,1024]{3,2,1,0:T(8,128)(2,1)S(1)}, u32[]{:S(2)}, u32[]{:S(2)}) collective-permute-start(bf16[4,2,16,1024]{3,2,1,0:T(8,128)(2,1)S(1)} %get-tuple-element.35), channel_id=1, source_target_pairs={{0,8},{8,0},{16,24},{24,16},{1,9},{9,1},{17,25},{25,17},{2,10},{10... | collective-permute-start | bytes 786440 | tf_op jit(solution)/shard_map/ppermute | solution.py:211
  33.0 5.3 %collective-permute-start.10 = (bf16[2,32,1024]{2,1,0:T(8,128)(2,1)S(1)}, bf16[2,32,1024]{2,1,0:T(8,128)(2,1)S(1)}, u32[]{:S(2)}, u32[]{:S(2)}) collective-permute-start(bf16[2,32,1024]{2,1,0:T(8,128)(2,1)S(1)} %get-tuple-element.42), channel_id=1, source_target_pairs={{0,4},{1,5},{2,6},{3,7},{4,0},{5,1},{6,2},{7,3},{8,12},{9,13},{10,... | collective-permute-start | bytes 393224 | tf_op jit(solution)/shard_map/ppermute | solution.py:208
  34.3 5.9 %collective-permute-start.11 = (bf16[2,32,1024]{2,1,0:T(8,128)(2,1)S(1)}, bf16[2,32,1024]{2,1,0:T(8,128)(2,1)S(1)}, u32[]{:S(2)}, u32[]{:S(2)}) collective-permute-start(bf16[2,32,1024]{2,1,0:T(8,128)(2,1)S(1)} %get-tuple-element.43), channel_id=1, source_target_pairs={{0,6},{1,7},{2,4},{3,5},{4,2},{5,3},{6,0},{7,1},{8,14},{9,15},{10,... | collective-permute-start | bytes 393224 | tf_op jit(solution)/shard_map/ppermute | solution.py:208
  35.4 6.0 %collective-permute-start.9 = (bf16[2,32,1024]{2,1,0:T(8,128)(2,1)S(1)}, bf16[2,32,1024]{2,1,0:T(8,128)(2,1)S(1)}, u32[]{:S(2)}, u32[]{:S(2)}) collective-permute-start(bf16[2,32,1024]{2,1,0:T(8,128)(2,1)S(1)} %get-tuple-element.41), channel_id=1, source_target_pairs={{0,2},{1,3},{2,0},{3,1},{4,6},{5,7},{6,4},{7,5},{8,10},{9,11},{10,... | collective-permute-start | bytes 393224 | tf_op jit(solution)/shard_map/ppermute | solution.py:208
  41.4 8.9 %collective-permute-start.12 = (bf16[2,2,32,1024]{3,2,1,0:T(8,128)(2,1)S(1)}, bf16[2,2,32,1024]{3,2,1,0:T(8,128)(2,1)S(1)}, u32[]{:S(2)}, u32[]{:S(2)}) collective-permute-start(bf16[2,2,32,1024]{3,2,1,0:T(8,128)(2,1)S(1)} %get-tuple-element.45), channel_id=1, source_target_pairs={{0,8},{8,0},{16,24},{24,16},{1,9},{9,1},{17,25},{25,17},{2,10},{10... | collective-permute-start | bytes 786440 | tf_op jit(solution)/shard_map/ppermute | solution.py:211
  41.5 11.3 %collective-permute-start.14 = (bf16[2,16,1024]{2,1,0:T(8,128)(2,1)S(1)}, bf16[2,16,1024]{2,1,0:T(8,128)(2,1)S(1)}, u32[]{:S(2)}, u32[]{:S(2)}) collective-permute-start(bf16[2,16,1024]{2,1,0:T(8,128)(2,1)S(1)} %get-tuple-element.47), channel_id=1, source_target_pairs={{0,2},{1,3},{2,0},{3,1},{4,6},{5,7},{6,4},{7,5},{8,10},{9,11},{10,... | collective-permute-start | bytes 196616 | tf_op jit(solution)/shard_map/ppermute | solution.py:208
  42.8 10.0 %collective-permute-start.15 = (bf16[2,16,1024]{2,1,0:T(8,128)(2,1)S(1)}, bf16[2,16,1024]{2,1,0:T(8,128)(2,1)S(1)}, u32[]{:S(2)}, u32[]{:S(2)}) collective-permute-start(bf16[2,16,1024]{2,1,0:T(8,128)(2,1)S(1)} %get-tuple-element.48), channel_id=1, source_target_pairs={{0,4},{1,5},{2,6},{3,7},{4,0},{5,1},{6,2},{7,3},{8,12},{9,13},{10,... | collective-permute-start | bytes 196616 | tf_op jit(solution)/shard_map/ppermute | solution.py:208
  43.9 8.9 %collective-permute-start.16 = (bf16[2,16,1024]{2,1,0:T(8,128)(2,1)S(1)}, bf16[2,16,1024]{2,1,0:T(8,128)(2,1)S(1)}, u32[]{:S(2)}, u32[]{:S(2)}) collective-permute-start(bf16[2,16,1024]{2,1,0:T(8,128)(2,1)S(1)} %get-tuple-element.49), channel_id=1, source_target_pairs={{0,6},{1,7},{2,4},{3,5},{4,2},{5,3},{6,0},{7,1},{8,14},{9,15},{10,... | collective-permute-start | bytes 196616 | tf_op jit(solution)/shard_map/ppermute | solution.py:208
  50.4 9.9 %collective-permute-start.13 = (bf16[2,32,1024]{2,1,0:T(8,128)(2,1)S(1)}, bf16[2,32,1024]{2,1,0:T(8,128)(2,1)S(1)}, u32[]{:S(2)}, u32[]{:S(2)}) collective-permute-start(bf16[2,32,1024]{2,1,0:T(8,128)(2,1)S(1)} %add.1), channel_id=1, source_target_pairs={{0,16},{8,24},{16,0},{24,8},{1,17},{9,25},{17,1},{25,9},{2,18},{10... | collective-permute-start | bytes 393224 | tf_op jit(solution)/shard_map/ppermute | solution.py:211
  52.9 4.7 %collective-permute-start.17 = (bf16[2,16,1024]{2,1,0:T(8,128)(2,1)S(1)}, bf16[2,16,1024]{2,1,0:T(8,128)(2,1)S(1)}, u32[]{:S(2)}, u32[]{:S(2)}) collective-permute-start(bf16[2,16,1024]{2,1,0:T(8,128)(2,1)S(1)} %get-tuple-element.51), channel_id=1, source_target_pairs={{0,8},{8,0},{16,24},{24,16},{1,9},{9,1},{17,25},{25,17},{2,10},{10... | collective-permute-start | bytes 196616 | tf_op jit(solution)/shard_map/ppermute | solution.py:211
  53.2 5.2 %collective-permute-start.18 = (bf16[2,16,1024]{2,1,0:T(8,128)(2,1)S(1)}, bf16[2,16,1024]{2,1,0:T(8,128)(2,1)S(1)}, u32[]{:S(2)}, u32[]{:S(2)}) collective-permute-start(bf16[2,16,1024]{2,1,0:T(8,128)(2,1)S(1)} %get-tuple-element.52), channel_id=1, source_target_pairs={{0,16},{8,24},{16,0},{24,8},{1,17},{9,25},{17,1},{25,9},{2,18},{10... | collective-permute-start | bytes 196616 | tf_op jit(solution)/shard_map/ppermute | solution.py:211
  53.8 6.6 %collective-permute-start.19 = (bf16[2,16,1024]{2,1,0:T(8,128)(2,1)S(1)}, bf16[2,16,1024]{2,1,0:T(8,128)(2,1)S(1)}, u32[]{:S(2)}, u32[]{:S(2)}) collective-permute-start(bf16[2,16,1024]{2,1,0:T(8,128)(2,1)S(1)} %get-tuple-element.53), channel_id=1, source_target_pairs={{0,24},{8,16},{16,8},{24,0},{1,25},{9,17},{17,9},{25,1},{2,26},{10... | collective-permute-start | bytes 196616 | tf_op jit(solution)/shard_map/ppermute | solution.py:211

commit v6 on v5

--- a/solution.py
+++ b/solution.py
@@ -151,10 +151,14 @@
         send_ref[m // 2] = held[c ^ f ^ m ^ 1]
 
 
-def add_kernel(groups, keep_ref, came_ref, *outs):
+def add_kernel(groups, *refs):
+    keep_ref, came_ref, *rest = refs
+    straight, outs = rest[: groups // 2 - 1], rest[groups // 2 - 1 :]
     for i in range(1, groups // 2):
         total = keep_ref[i].astype(F32) + came_ref[i].astype(F32)
-        outs[i - 1][...] = total.astype(BF16)
+        rows = total.shape[1]
+        outs[i - 1][:, :rows] = total.astype(BF16)
+        outs[i - 1][:, rows:] = straight[i - 1][...]
 
 
 def merge_kernel(groups, keep_ref, came_ref, *outs):
@@ -172,23 +176,25 @@
 
 
 def finish_kernel(groups, *refs):
+    keep_ref, came_ref, mine_ref, *rest = refs[:-2]
     bias_ref, out_ref = refs[-2:]
-    keep_ref, came_ref, *far = refs[: 1 + groups // 2]
-    direct = refs[1 + groups // 2 : -2]
+    far, odd = rest[: groups // 2 - 1], rest[groups // 2 - 1 :]
     f, _, _ = place()
-    _, rows, wslice = direct[0].shape
+    _, rows, wslice = mine_ref.shape
     for half in range(2):
         cols = slice(half * wslice, (half + 1) * wslice)
         bias = bias_ref[pl.ds(2 * f + half, 1), :]
-        total = keep_ref[0, half].astype(F32) + came_ref[0, half].astype(F32)
+        first = keep_ref[0, half].astype(F32) + came_ref[0, half].astype(F32)
+        same = mine_ref[half].astype(F32)
         for ref in far:
-            total += ref[half].astype(F32)
-        out_ref[: 2 * rows, cols] = (total + bias).astype(BF16)
-        for odd in range(2):
-            total = direct[odd][half].astype(F32)
-            for ref in direct[2 + odd :: 2]:
-                total += ref[half].astype(F32)
-            start = pl.multiple_of(2 * rows + ((f & 1) ^ odd) * rows, rows)
+            first += ref[half, : 2 * rows].astype(F32)
+            same += ref[half, 2 * rows :].astype(F32)
+        out_ref[: 2 * rows, cols] = (first + bias).astype(BF16)
+        other = odd[0][half].astype(F32)
+        for ref in odd[1:]:
+            other += ref[half].astype(F32)
+        for total, parity in ((same, f & 1), (other, 1 - (f & 1))):
+            start = pl.multiple_of(2 * rows + parity * rows, rows)
             out_ref[pl.ds(start, rows), cols] = (total + bias).astype(BF16)
 
 
@@ -316,17 +322,19 @@
         cost_estimate=cost(0, 8 * groups * quarter_rows * wslice),
         name="direct",
     )(*merged)
+    far = jax.ShapeDtypeStruct((2, half_rows + quarter_rows, wslice), BF16)
     sums = pl.pallas_call(
         functools.partial(add_kernel, groups),
-        out_shape=[piece] * (groups // 2 - 1),
-        in_specs=[spec(VMEM)] * 2,
+        out_shape=[far] * (groups // 2 - 1),
+        in_specs=[spec(VMEM)] * (1 + groups // 2),
         out_specs=[spec(VMEM)] * (groups // 2 - 1),
         compiler_params=params(8),
         cost_estimate=cost(groups * half_rows * wslice, 6 * groups * half_rows * wslice),
         name="add",
-    )(keep, near)
-    moved = [keep, near] + [lift(sums[m // 2 - 1], m) for m in range(2, groups, 2)]
-    moved += [direct[0]] + [lift(direct[m], m) for m in range(1, groups)]
+    )(keep, near, *direct[2::2])
+    moved = [keep, near, direct[0]]
+    moved += [lift(sums[m // 2 - 1], m) for m in range(2, groups, 2)]
+    moved += [lift(direct[m], m) for m in range(1, groups, 2)]
 
     rebuilt = pl.pallas_call(
         functools.partial(finish_kernel, groups),

time: 61.5 us -> 61.1 us (level)
  starting transfers between devices: 24.1 us -> 21.7 us
  waiting for transfers between devices: 17.7 us -> 19.7 us
    ppermute x12, waiting for transfers between devices: 8.05 us -> 12 us  [swap(): return lax.ppermute(value, 'tok', pairs)]
    ppermute x6 -> x5, starting transfers between devices: 8.48 us -> 6.1 us  [lift(): return lax.ppermute(value, 'feat', [(i, i ^ m) for i in range(groups)])]
    ppermute x6 -> x5, waiting for transfers between devices: 9.65 us -> 7.69 us  [lift(): return lax.ppermute(value, 'feat', [(i, i ^ m) for i in range(groups)])]
  transfers between devices with their start and end apart: 20 -> 19, of which waited for: 11 -> 13; matrix products, arithmetic and copies ran while one was open for 1% -> 1% of each run, Pallas kernels for 19% -> 19%
where the time goes in v6:
time: 61.1 us; the launch traced here: 60.8 us
  starting transfers between devices  21.7 us (36%)
  waiting for transfers between devices  19.7 us (32%)
  Pallas kernels  14.4 us (24%)
  local copies, waits for them, and re-layouts  4.2 us (7%)
  between operations  0.76 us (1%)
    ppermute x12, starting transfers between devices, swap(): return lax.ppermute(value, 'tok', pairs)  15 us
    ppermute x12, waiting for transfers between devices, swap(): return lax.ppermute(value, 'tok', pairs)  12 us
    ppermute x5, waiting for transfers between devices, lift(): return lax.ppermute(value, 'feat', [(i, i ^ m) for i in range(groups)])  7.69 us
    pallas_call x2, Pallas kernels, columns(): pl.pallas_call(functools.partial(columns_kernel, groups), out_shape=jax.S...  7.37 us
    ppermute x5, starting transfers between devices, lift(): return lax.ppermute(value, 'feat', [(i, i ^ m) for i in range(groups)])  6.1 us
    unnamed x12, local copies, waits for them, and re-layouts  3.43 us
    pallas_call x1, Pallas kernels, on_device(): pl.pallas_call(stage_kernel, out_shape=jax.ShapeDtypeStruct(dec_weight.sh...  2.37 us
    pallas_call x1, Pallas kernels, on_device(): pl.pallas_call(functools.partial(decode_kernel, groups), out_shape=[jax.S...  1.97 us
  transfers between devices with their start and end apart: 19, of which 13 were waited for; matrix products, arithmetic and copies ran while one was open for 1% of the time, Pallas kernels for 19%

profile of v6, /device:TPU:0, one launch (start us, length us, event | category | flops | bytes accessed | tf_op | source)
XLA Modules:
  0.0 60.8 jit_solution(17168584187326209660)
XLA Ops:
  1.2 1.2 %copy-done.2 = bf16[64,8192]{1,0:T(8,128)(2,1)S(1)} copy-done((bf16[64,8192]{1,0:T(8,128)(2,1)S(1)}, bf16[64,8192]{1,0:T(8,128)(2,1)}, u32[]{:S(2)}) %copy-start.2) | copy-done | bytes 1048600
  2.5 0.9 %split.1 = (bf16[2,64,1024]{2,1,0:T(8,128)(2,1)S(1)}, bf16[2,64,1024]{2,1,0:T(8,128)(2,1)}, bf16[2,64,1024]{2,1,0:T(8,128)(2,1)}, bf16[2,64,1024]{2,1,0:T(8,128)(2,1)S(1)}) custom-call(bf16[64,8192]{1,0:T(8,128)(2,1)S(1)} %copy-done.2), custom_call_target="tpu_custom_call" | custom-call | bytes 2097152 | tf_op jit(solution)/shard_map/split/pallas_call | solution.py:223
  3.3 2.9 %collective-permute-start = (bf16[2,64,1024]{2,1,0:T(8,128)(2,1)}, bf16[2,64,1024]{2,1,0:T(8,128)(2,1)S(1)}, u32[]{:S(2)}, u32[]{:S(2)}) collective-permute-start(bf16[2,64,1024]{2,1,0:T(8,128)(2,1)} %get-tuple-element.29), channel_id=1, source_target_pairs={{0,2},{1,3},{2,0},{3,1},{4,6},{5,7},{6,4},{7,5},{8,10},{9,11},{10,... | collective-permute-start | bytes 786440 | tf_op jit(solution)/shard_map/ppermute | solution.py:214
  6.2 1.5 %collective-permute-start.1 = (bf16[2,64,1024]{2,1,0:T(8,128)(2,1)}, bf16[2,64,1024]{2,1,0:T(8,128)(2,1)S(1)}, u32[]{:S(2)}, u32[]{:S(2)}) collective-permute-start(bf16[2,64,1024]{2,1,0:T(8,128)(2,1)} %get-tuple-element.30), channel_id=1, source_target_pairs={{0,4},{1,5},{2,6},{3,7},{4,0},{5,1},{6,2},{7,3},{8,12},{9,13},{10,... | collective-permute-start | bytes 786440 | tf_op jit(solution)/shard_map/ppermute | solution.py:214
  8.5 2.2 %copy-done.1 = bf16[1024,2048]{1,0:T(8,128)(2,1)S(1)} copy-done((bf16[1024,2048]{1,0:T(8,128)(2,1)S(1)}, bf16[1024,2048]{1,0:T(8,128)(2,1)}, u32[]{:S(2)}) %copy-start.1) | copy-done | bytes 4194328
  10.7 3.0 %columns.2.refs_5_ = bf16[4,1024,256]{2,1,0:T(8,128)(2,1)S(1)} custom-call(s32[8,4]{1,0:T(8,128)S(1)} %copy.11.ids_ref.refs_0_, bf16[1024,2048]{1,0:T(8,128)(2,1)S(1)} %copy-done.1), custom_call_target="tpu_custom_call" | custom-call | bytes 6291456 | tf_op jit(solution)/shard_map/columns/pallas_call | solution.py:237
  13.8 4.4 %columns.3.refs_6_ = bf16[4,1024,256]{2,1,0:T(8,128)(2,1)S(1)} custom-call(s32[8,4]{1,0:T(8,128)S(1)} %copy.11.ids_ref.refs_0_, bf16[1024,2048]{1,0:T(8,128)(2,1)} %collective-permute-done.3.w_ref), custom_call_target="tpu_custom_call" | custom-call | bytes 6291456 | tf_op jit(solution)/shard_map/columns/pallas_call | solution.py:237
  18.2 1.9 %collective-permute-done.1.refs_3_ = bf16[2,64,1024]{2,1,0:T(8,128)(2,1)S(1)} collective-permute-done((bf16[2,64,1024]{2,1,0:T(8,128)(2,1)}, bf16[2,64,1024]{2,1,0:T(8,128)(2,1)S(1)}, u32[]{:S(2)}, u32[]{:S(2)}) %collective-permute-start.1) | collective-permute-done | bytes 262176 | tf_op jit(solution)/shard_map/ppermute | solution.py:214
  20.1 0.8 %encode.1.refs_3_ = bf16[4,64,256]{2,1,0:T(8,128)(2,1)S(1)} custom-call(f32[8,1024]{1,0:T(8,128)S(1)} %reshape.21.refs_0_.refs_6_, bf16[2,64,1024]{2,1,0:T(8,128)(2,1)S(1)} %get-tuple-element.28.refs_1_, bf16[2,64,1024]{2,1,0:T(8,128)(2,1)S(1)} %collective-permute-done.refs_2_, bf16[2,64,1024]{2,1,0:T(8,128)(2,1)S(1)} %collective-permute-done.1.refs_3_, ...), custom_call_target="tpu_custom_call" | custom-call | flops 268435456 | bytes 4194304 | tf_op jit(solution)/shard_map/encode/pallas_call | solution.py:251
  20.9 1.3 %collective-permute-start.4 = (bf16[4,64,256]{2,1,0:T(8,128)(2,1)S(1)}, bf16[4,64,256]{2,1,0:T(8,128)(2,1)S(1)}, u32[]{:S(2)}, u32[]{:S(2)}) collective-permute-start(bf16[4,64,256]{2,1,0:T(8,128)(2,1)S(1)} %encode.1.refs_3_), channel_id=1, source_target_pairs={{0,2},{1,3},{2,0},{3,1},{4,6},{5,7},{6,4},{7,5},{8,10},{9,11},{10,... | collective-permute-start | bytes 393224 | tf_op jit(solution)/shard_map/ppermute | solution.py:214
  23.1 1.4 %collective-permute-start.6 = (bf16[4,64,256]{2,1,0:T(8,128)(2,1)S(1)}, bf16[4,64,256]{2,1,0:T(8,128)(2,1)S(1)}, u32[]{:S(2)}, u32[]{:S(2)}) collective-permute-start(bf16[4,64,256]{2,1,0:T(8,128)(2,1)S(1)} %encode.1.refs_3_), channel_id=1, source_target_pairs={{0,6},{1,7},{2,4},{3,5},{4,2},{5,3},{6,0},{7,1},{8,14},{9,15},{10,... | collective-permute-start | bytes 393224 | tf_op jit(solution)/shard_map/ppermute | solution.py:214
  24.5 2.4 %stage.1.refs_8_ = bf16[2048,1024]{1,0:T(8,128)(2,1)S(1)} custom-call(bf16[2048,1024]{1,0:T(8,128)(2,1)} %collective-permute-done.7.src), custom_call_target="tpu_custom_call" | custom-call | bytes 8388608 | tf_op jit(solution)/shard_map/stage/pallas_call | solution.py:262
  27.1 2.4 %collective-permute-done.5.refs_5_ = bf16[4,64,256]{2,1,0:T(8,128)(2,1)S(1)} collective-permute-done((bf16[4,64,256]{2,1,0:T(8,128)(2,1)S(1)}, bf16[4,64,256]{2,1,0:T(8,128)(2,1)S(1)}, u32[]{:S(2)}, u32[]{:S(2)}) %collective-permute-start.5) | collective-permute-done | bytes 131104 | tf_op jit(solution)/shard_map/ppermute | solution.py:214
  29.4 2.0 %decode.1 = (bf16[64,256]{1,0:T(8,128)(2,1)}, bf16[2,32,1024]{2,1,0:T(8,128)(2,1)S(1)}, bf16[2,32,1024]{2,1,0:T(8,128)(2,1)S(1)}, bf16[2,32,1024]{2,1,0:T(8,128)...) custom-call(s32[8,4]{1,0:T(8,128)S(1)} %copy.11.ids_ref.refs_0_, ...), custom_call_target="tpu_custom_call" | custom-call | flops 268435456 | bytes 4194304 | tf_op jit(solution)/shard_map/decode/pallas_call | solution.py:277
  31.4 1.6 %collective-permute-start.8 = (bf16[4,2,16,1024]{3,2,1,0:T(8,128)(2,1)S(1)}, bf16[4,2,16,1024]{3,2,1,0:T(8,128)(2,1)S(1)}, u32[]{:S(2)}, u32[]{:S(2)}) collective-permute-start(bf16[4,2,16,1024]{3,2,1,0:T(8,128)(2,1)S(1)} %get-tuple-element.35), channel_id=1, source_target_pairs={{0,8},{8,0},{16,24},{24,16},{1,9},{9,1},{17,25},{25,17},{2,10},{10... | collective-permute-start | bytes 786440 | tf_op jit(solution)/shard_map/ppermute | solution.py:217
  33.0 1.3 %collective-permute-start.10 = (bf16[2,32,1024]{2,1,0:T(8,128)(2,1)S(1)}, bf16[2,32,1024]{2,1,0:T(8,128)(2,1)S(1)}, u32[]{:S(2)}, u32[]{:S(2)}) collective-permute-start(bf16[2,32,1024]{2,1,0:T(8,128)(2,1)S(1)} %get-tuple-element.42), channel_id=1, source_target_pairs={{0,4},{1,5},{2,6},{3,7},{4,0},{5,1},{6,2},{7,3},{8,12},{9,13},{10,... | collective-permute-start | bytes 393224 | tf_op jit(solution)/shard_map/ppermute | solution.py:214
  34.3 1.2 %collective-permute-start.11 = (bf16[2,32,1024]{2,1,0:T(8,128)(2,1)S(1)}, bf16[2,32,1024]{2,1,0:T(8,128)(2,1)S(1)}, u32[]{:S(2)}, u32[]{:S(2)}) collective-permute-start(bf16[2,32,1024]{2,1,0:T(8,128)(2,1)S(1)} %get-tuple-element.43), channel_id=1, source_target_pairs={{0,6},{1,7},{2,4},{3,5},{4,2},{5,3},{6,0},{7,1},{8,14},{9,15},{10,... | collective-permute-start | bytes 393224 | tf_op jit(solution)/shard_map/ppermute | solution.py:214
  35.4 1.0 %collective-permute-start.9 = (bf16[2,32,1024]{2,1,0:T(8,128)(2,1)S(1)}, bf16[2,32,1024]{2,1,0:T(8,128)(2,1)S(1)}, u32[]{:S(2)}, u32[]{:S(2)}) collective-permute-start(bf16[2,32,1024]{2,1,0:T(8,128)(2,1)S(1)} %get-tuple-element.41), channel_id=1, source_target_pairs={{0,2},{1,3},{2,0},{3,1},{4,6},{5,7},{6,4},{7,5},{8,10},{9,11},{10,... | collective-permute-start | bytes 393224 | tf_op jit(solution)/shard_map/ppermute | solution.py:214
  36.5 1.3 %collective-permute-done.8.came_ref = bf16[4,2,16,1024]{3,2,1,0:T(8,128)(2,1)S(1)} collective-permute-done((bf16[4,2,16,1024]{3,2,1,0:T(8,128)(2,1)S(1)}, bf16[4,2,16,1024]{3,2,1,0:T(8,128)(2,1)S(1)}, u32[]{:S(2)}, u32[]{:S(2)}) %collective-permute-start.8) | collective-permute-done | bytes 262176 | tf_op jit(solution)/shard_map/ppermute | solution.py:217
  38.3 1.8 %collective-permute-done.11.refs_3_ = bf16[2,32,1024]{2,1,0:T(8,128)(2,1)S(1)} collective-permute-done((bf16[2,32,1024]{2,1,0:T(8,128)(2,1)S(1)}, bf16[2,32,1024]{2,1,0:T(8,128)(2,1)S(1)}, u32[]{:S(2)}, u32[]{:S(2)}) %collective-permute-start.11) | collective-permute-done | bytes 131104 | tf_op jit(solution)/shard_map/ppermute | solution.py:214
  40.1 1.2 %collective-permute-done.9.refs_1_ = bf16[2,32,1024]{2,1,0:T(8,128)(2,1)S(1)} collective-permute-done((bf16[2,32,1024]{2,1,0:T(8,128)(2,1)S(1)}, bf16[2,32,1024]{2,1,0:T(8,128)(2,1)S(1)}, u32[]{:S(2)}, u32[]{:S(2)}) %collective-permute-start.9) | collective-permute-done | bytes 131104 | tf_op jit(solution)/shard_map/ppermute | solution.py:214
  41.5 1.3 %collective-permute-start.13 = (bf16[2,16,1024]{2,1,0:T(8,128)(2,1)S(1)}, bf16[2,16,1024]{2,1,0:T(8,128)(2,1)S(1)}, u32[]{:S(2)}, u32[]{:S(2)}) collective-permute-start(bf16[2,16,1024]{2,1,0:T(8,128)(2,1)S(1)} %get-tuple-element.47), channel_id=1, source_target_pairs={{0,2},{1,3},{2,0},{3,1},{4,6},{5,7},{6,4},{7,5},{8,10},{9,11},{10,... | collective-permute-start | bytes 196616 | tf_op jit(solution)/shard_map/ppermute | solution.py:214
  42.8 1.2 %collective-permute-start.14 = (bf16[2,16,1024]{2,1,0:T(8,128)(2,1)S(1)}, bf16[2,16,1024]{2,1,0:T(8,128)(2,1)S(1)}, u32[]{:S(2)}, u32[]{:S(2)}) collective-permute-start(bf16[2,16,1024]{2,1,0:T(8,128)(2,1)S(1)} %get-tuple-element.48), channel_id=1, source_target_pairs={{0,4},{1,5},{2,6},{3,7},{4,0},{5,1},{6,2},{7,3},{8,12},{9,13},{10,... | collective-permute-start | bytes 196616 | tf_op jit(solution)/shard_map/ppermute | solution.py:214
  43.9 1.1 %collective-permute-start.15 = (bf16[2,16,1024]{2,1,0:T(8,128)(2,1)S(1)}, bf16[2,16,1024]{2,1,0:T(8,128)(2,1)S(1)}, u32[]{:S(2)}, u32[]{:S(2)}) collective-permute-start(bf16[2,16,1024]{2,1,0:T(8,128)(2,1)S(1)} %get-tuple-element.49), channel_id=1, source_target_pairs={{0,6},{1,7},{2,4},{3,5},{4,2},{5,3},{6,0},{7,1},{8,14},{9,15},{10,... | collective-permute-start | bytes 196616 | tf_op jit(solution)/shard_map/ppermute | solution.py:214
  45.9 1.2 %collective-permute-done.14.refs_2_ = bf16[2,16,1024]{2,1,0:T(8,128)(2,1)S(1)} collective-permute-done((bf16[2,16,1024]{2,1,0:T(8,128)(2,1)S(1)}, bf16[2,16,1024]{2,1,0:T(8,128)(2,1)S(1)}, u32[]{:S(2)}, u32[]{:S(2)}) %collective-permute-start.14) | collective-permute-done | bytes 65568 | tf_op jit(solution)/shard_map/ppermute | solution.py:214
  47.1 2.1 %collective-permute-done.15.refs_3_ = bf16[2,16,1024]{2,1,0:T(8,128)(2,1)S(1)} collective-permute-done((bf16[2,16,1024]{2,1,0:T(8,128)(2,1)S(1)}, bf16[2,16,1024]{2,1,0:T(8,128)(2,1)S(1)}, u32[]{:S(2)}, u32[]{:S(2)}) %collective-permute-start.15) | collective-permute-done | bytes 65568 | tf_op jit(solution)/shard_map/ppermute | solution.py:214
  49.1 1.5 %collective-permute-done.12.refs_1_ = bf16[2,2,32,1024]{3,2,1,0:T(8,128)(2,1)S(1)} collective-permute-done((bf16[2,2,32,1024]{3,2,1,0:T(8,128)(2,1)S(1)}, bf16[2,2,32,1024]{3,2,1,0:T(8,128)(2,1)S(1)}, u32[]{:S(2)}, u32[]{:S(2)}) %collective-permute-start.12) | collective-permute-done | bytes 262176 | tf_op jit(solution)/shard_map/ppermute | solution.py:217
  50.7 2.0 %collective-permute-start.16 = (bf16[2,48,1024]{2,1,0:T(8,128)(2,1)S(1)}, bf16[2,48,1024]{2,1,0:T(8,128)(2,1)S(1)}, u32[]{:S(2)}, u32[]{:S(2)}) collective-permute-start(bf16[2,48,1024]{2,1,0:T(8,128)(2,1)S(1)} %add.1), channel_id=1, source_target_pairs={{0,16},{8,24},{16,0},{24,8},{1,17},{9,25},{17,1},{25,9},{2,18},{10... | collective-permute-start | bytes 589832 | tf_op jit(solution)/shard_map/ppermute | solution.py:217
  52.7 1.1 %collective-permute-start.17 = (bf16[2,16,1024]{2,1,0:T(8,128)(2,1)S(1)}, bf16[2,16,1024]{2,1,0:T(8,128)(2,1)S(1)}, u32[]{:S(2)}, u32[]{:S(2)}) collective-permute-start(bf16[2,16,1024]{2,1,0:T(8,128)(2,1)S(1)} %get-tuple-element.52), channel_id=1, source_target_pairs={{0,8},{8,0},{16,24},{24,16},{1,9},{9,1},{17,25},{25,17},{2,10},{10... | collective-permute-start | bytes 196616 | tf_op jit(solution)/shard_map/ppermute | solution.py:217
  53.8 1.3 %collective-permute-start.18 = (bf16[2,16,1024]{2,1,0:T(8,128)(2,1)S(1)}, bf16[2,16,1024]{2,1,0:T(8,128)(2,1)S(1)}, u32[]{:S(2)}, u32[]{:S(2)}) collective-permute-start(bf16[2,16,1024]{2,1,0:T(8,128)(2,1)S(1)} %get-tuple-element.53), channel_id=1, source_target_pairs={{0,24},{8,16},{16,8},{24,0},{1,25},{9,17},{17,9},{25,1},{2,26},{10... | collective-permute-start | bytes 196616 | tf_op jit(solution)/shard_map/ppermute | solution.py:217
  55.2 1.8 %collective-permute-done.17.refs_4_ = bf16[2,16,1024]{2,1,0:T(8,128)(2,1)S(1)} collective-permute-done((bf16[2,16,1024]{2,1,0:T(8,128)(2,1)S(1)}, bf16[2,16,1024]{2,1,0:T(8,128)(2,1)S(1)}, u32[]{:S(2)}, u32[]{:S(2)}) %collective-permute-start.17) | collective-permute-done | bytes 65568 | tf_op jit(solution)/shard_map/ppermute | solution.py:217
  57.0 3.0 %collective-permute-done.18.refs_5_ = bf16[2,16,1024]{2,1,0:T(8,128)(2,1)S(1)} collective-permute-done((bf16[2,16,1024]{2,1,0:T(8,128)(2,1)S(1)}, bf16[2,16,1024]{2,1,0:T(8,128)(2,1)S(1)}, u32[]{:S(2)}, u32[]{:S(2)}) %collective-permute-start.18) | collective-permute-done | bytes 65568 | tf_op jit(solution)/shard_map/ppermute | solution.py:217
  (32 shorter events, 4.7 us)
Async XLA Ops:
  0.6 13.1 %collective-permute-start.3 = (bf16[1024,2048]{1,0:T(8,128)(2,1)}, bf16[1024,2048]{1,0:T(8,128)(2,1)}, u32[]{:S(2)}, u32[]{:S(2)}) collective-permute-start(bf16[1024,2048]{1,0:T(8,128)(2,1)} %w_ref.1), channel_id=1, source_target_pairs={{0,1},{1,0},{2,3},{3,2},{4,5},{5,4},{6,7},{7,6},{8,9},{9,8},{10,11... | collective-permute-start | bytes 12582920 | tf_op jit(solution)/shard_map/ppermute | solution.py:220
  1.1 23.4 %collective-permute-start.7 = (bf16[2048,1024]{1,0:T(8,128)(2,1)}, bf16[2048,1024]{1,0:T(8,128)(2,1)}, u32[]{:S(2)}, u32[]{:S(2)}) collective-permute-start(bf16[2048,1024]{1,0:T(8,128)(2,1)} %refs_7_.1), channel_id=1, source_target_pairs={{0,1},{1,0},{2,3},{3,2},{4,5},{5,4},{6,7},{7,6},{8,9},{9,8},{10,11... | collective-permute-start | bytes 12582920 | tf_op jit(solution)/shard_map/ppermute | solution.py:221
  1.2 1.2 %copy-start.2 = (bf16[64,8192]{1,0:T(8,128)(2,1)S(1)}, bf16[64,8192]{1,0:T(8,128)(2,1)}, u32[]{:S(2)}) copy-start(bf16[64,8192]{1,0:T(8,128)(2,1)} %tok_ref.1) | copy-start | bytes 3145732
  2.5 11.3 %copy-start.4 = (bf16[8192]{0:T(1024)(128)(2,1)S(1)}, bf16[8192]{0:T(1024)(128)(2,1)}, u32[]{:S(2)}) copy-start(bf16[8192]{0:T(1024)(128)(2,1)} %param.8) | copy-start | bytes 49156
  3.3 14.8 %collective-permute-start = (bf16[2,64,1024]{2,1,0:T(8,128)(2,1)}, bf16[2,64,1024]{2,1,0:T(8,128)(2,1)S(1)}, u32[]{:S(2)}, u32[]{:S(2)}) collective-permute-start(bf16[2,64,1024]{2,1,0:T(8,128)(2,1)} %get-tuple-element.29), channel_id=1, source_target_pairs={{0,2},{1,3},{2,0},{3,1},{4,6},{5,7},{6,4},{7,5},{8,10},{9,11},{10,... | collective-permute-start | bytes 786440 | tf_op jit(solution)/shard_map/ppermute | solution.py:214
  6.2 13.8 %collective-permute-start.1 = (bf16[2,64,1024]{2,1,0:T(8,128)(2,1)}, bf16[2,64,1024]{2,1,0:T(8,128)(2,1)S(1)}, u32[]{:S(2)}, u32[]{:S(2)}) collective-permute-start(bf16[2,64,1024]{2,1,0:T(8,128)(2,1)} %get-tuple-element.30), channel_id=1, source_target_pairs={{0,4},{1,5},{2,6},{3,7},{4,0},{5,1},{6,2},{7,3},{8,12},{9,13},{10,... | collective-permute-start | bytes 786440 | tf_op jit(solution)/shard_map/ppermute | solution.py:214
  7.8 12.3 %collective-permute-start.2 = (bf16[2,64,1024]{2,1,0:T(8,128)(2,1)S(1)}, bf16[2,64,1024]{2,1,0:T(8,128)(2,1)S(1)}, u32[]{:S(2)}, u32[]{:S(2)}) collective-permute-start(bf16[2,64,1024]{2,1,0:T(8,128)(2,1)S(1)} %get-tuple-element.31), channel_id=1, source_target_pairs={{0,6},{1,7},{2,4},{3,5},{4,2},{5,3},{6,0},{7,1},{8,14},{9,15},{10,... | collective-permute-start | bytes 786440 | tf_op jit(solution)/shard_map/ppermute | solution.py:214
  8.5 2.2 %copy-start.1 = (bf16[1024,2048]{1,0:T(8,128)(2,1)S(1)}, bf16[1024,2048]{1,0:T(8,128)(2,1)}, u32[]{:S(2)}) copy-start(bf16[1024,2048]{1,0:T(8,128)(2,1)} %w_ref.1) | copy-start | bytes 12582916
  18.1 6.3 %copy-start.5 = (bf16[2048]{0:T(1024)(128)(2,1)S(1)}, bf16[2048]{0:T(1024)(128)(2,1)}, u32[]{:S(2)}) copy-start(bf16[2048]{0:T(1024)(128)(2,1)} %param.10) | copy-start | bytes 12292
  20.9 6.1 %collective-permute-start.4 = (bf16[4,64,256]{2,1,0:T(8,128)(2,1)S(1)}, bf16[4,64,256]{2,1,0:T(8,128)(2,1)S(1)}, u32[]{:S(2)}, u32[]{:S(2)}) collective-permute-start(bf16[4,64,256]{2,1,0:T(8,128)(2,1)S(1)} %encode.1.refs_3_), channel_id=1, source_target_pairs={{0,2},{1,3},{2,0},{3,1},{4,6},{5,7},{6,4},{7,5},{8,10},{9,11},{10,... | collective-permute-start | bytes 393224 | tf_op jit(solution)/shard_map/ppermute | solution.py:214
  22.2 7.2 %collective-permute-start.5 = (bf16[4,64,256]{2,1,0:T(8,128)(2,1)S(1)}, bf16[4,64,256]{2,1,0:T(8,128)(2,1)S(1)}, u32[]{:S(2)}, u32[]{:S(2)}) collective-permute-start(bf16[4,64,256]{2,1,0:T(8,128)(2,1)S(1)} %encode.1.refs_3_), channel_id=1, source_target_pairs={{0,4},{1,5},{2,6},{3,7},{4,0},{5,1},{6,2},{7,3},{8,12},{9,13},{10,... | collective-permute-start | bytes 393224 | tf_op jit(solution)/shard_map/ppermute | solution.py:214
  23.1 6.4 %collective-permute-start.6 = (bf16[4,64,256]{2,1,0:T(8,128)(2,1)S(1)}, bf16[4,64,256]{2,1,0:T(8,128)(2,1)S(1)}, u32[]{:S(2)}, u32[]{:S(2)}) collective-permute-start(bf16[4,64,256]{2,1,0:T(8,128)(2,1)S(1)} %encode.1.refs_3_), channel_id=1, source_target_pairs={{0,6},{1,7},{2,4},{3,5},{4,2},{5,3},{6,0},{7,1},{8,14},{9,15},{10,... | collective-permute-start | bytes 393224 | tf_op jit(solution)/shard_map/ppermute | solution.py:214
  24.5 4.9 %copy-start = (bf16[2048,1024]{1,0:T(8,128)(2,1)S(1)}, bf16[2048,1024]{1,0:T(8,128)(2,1)}, u32[]{:S(2)}) copy-start(bf16[2048,1024]{1,0:T(8,128)(2,1)} %refs_7_.1) | copy-start | bytes 12582916
  24.5 4.9 %copy-start.3 = (s32[8,1]{0,1:T(1,128)S(1)}, s32[8,1]{0,1:T(1,128)}, u32[]{:S(2)}) copy-start(s32[8,1]{0,1:T(1,128)} %param.13) | copy-start | bytes 100
  31.4 6.4 %collective-permute-start.8 = (bf16[4,2,16,1024]{3,2,1,0:T(8,128)(2,1)S(1)}, bf16[4,2,16,1024]{3,2,1,0:T(8,128)(2,1)S(1)}, u32[]{:S(2)}, u32[]{:S(2)}) collective-permute-start(bf16[4,2,16,1024]{3,2,1,0:T(8,128)(2,1)S(1)} %get-tuple-element.35), channel_id=1, source_target_pairs={{0,8},{8,0},{16,24},{24,16},{1,9},{9,1},{17,25},{25,17},{2,10},{10... | collective-permute-start | bytes 786440 | tf_op jit(solution)/shard_map/ppermute | solution.py:217
  33.0 5.3 %collective-permute-start.10 = (bf16[2,32,1024]{2,1,0:T(8,128)(2,1)S(1)}, bf16[2,32,1024]{2,1,0:T(8,128)(2,1)S(1)}, u32[]{:S(2)}, u32[]{:S(2)}) collective-permute-start(bf16[2,32,1024]{2,1,0:T(8,128)(2,1)S(1)} %get-tuple-element.42), channel_id=1, source_target_pairs={{0,4},{1,5},{2,6},{3,7},{4,0},{5,1},{6,2},{7,3},{8,12},{9,13},{10,... | collective-permute-start | bytes 393224 | tf_op jit(solution)/shard_map/ppermute | solution.py:214
  34.3 5.9 %collective-permute-start.11 = (bf16[2,32,1024]{2,1,0:T(8,128)(2,1)S(1)}, bf16[2,32,1024]{2,1,0:T(8,128)(2,1)S(1)}, u32[]{:S(2)}, u32[]{:S(2)}) collective-permute-start(bf16[2,32,1024]{2,1,0:T(8,128)(2,1)S(1)} %get-tuple-element.43), channel_id=1, source_target_pairs={{0,6},{1,7},{2,4},{3,5},{4,2},{5,3},{6,0},{7,1},{8,14},{9,15},{10,... | collective-permute-start | bytes 393224 | tf_op jit(solution)/shard_map/ppermute | solution.py:214
  35.4 6.0 %collective-permute-start.9 = (bf16[2,32,1024]{2,1,0:T(8,128)(2,1)S(1)}, bf16[2,32,1024]{2,1,0:T(8,128)(2,1)S(1)}, u32[]{:S(2)}, u32[]{:S(2)}) collective-permute-start(bf16[2,32,1024]{2,1,0:T(8,128)(2,1)S(1)} %get-tuple-element.41), channel_id=1, source_target_pairs={{0,2},{1,3},{2,0},{3,1},{4,6},{5,7},{6,4},{7,5},{8,10},{9,11},{10,... | collective-permute-start | bytes 393224 | tf_op jit(solution)/shard_map/ppermute | solution.py:214
  41.5 9.2 %collective-permute-start.12 = (bf16[2,2,32,1024]{3,2,1,0:T(8,128)(2,1)S(1)}, bf16[2,2,32,1024]{3,2,1,0:T(8,128)(2,1)S(1)}, u32[]{:S(2)}, u32[]{:S(2)}) collective-permute-start(bf16[2,2,32,1024]{3,2,1,0:T(8,128)(2,1)S(1)} %get-tuple-element.45), channel_id=1, source_target_pairs={{0,8},{8,0},{16,24},{24,16},{1,9},{9,1},{17,25},{25,17},{2,10},{10... | collective-permute-start | bytes 786440 | tf_op jit(solution)/shard_map/ppermute | solution.py:217
  41.5 4.3 %collective-permute-start.13 = (bf16[2,16,1024]{2,1,0:T(8,128)(2,1)S(1)}, bf16[2,16,1024]{2,1,0:T(8,128)(2,1)S(1)}, u32[]{:S(2)}, u32[]{:S(2)}) collective-permute-start(bf16[2,16,1024]{2,1,0:T(8,128)(2,1)S(1)} %get-tuple-element.47), channel_id=1, source_target_pairs={{0,2},{1,3},{2,0},{3,1},{4,6},{5,7},{6,4},{7,5},{8,10},{9,11},{10,... | collective-permute-start | bytes 196616 | tf_op jit(solution)/shard_map/ppermute | solution.py:214
  42.8 4.3 %collective-permute-start.14 = (bf16[2,16,1024]{2,1,0:T(8,128)(2,1)S(1)}, bf16[2,16,1024]{2,1,0:T(8,128)(2,1)S(1)}, u32[]{:S(2)}, u32[]{:S(2)}) collective-permute-start(bf16[2,16,1024]{2,1,0:T(8,128)(2,1)S(1)} %get-tuple-element.48), channel_id=1, source_target_pairs={{0,4},{1,5},{2,6},{3,7},{4,0},{5,1},{6,2},{7,3},{8,12},{9,13},{10,... | collective-permute-start | bytes 196616 | tf_op jit(solution)/shard_map/ppermute | solution.py:214
  43.9 5.2 %collective-permute-start.15 = (bf16[2,16,1024]{2,1,0:T(8,128)(2,1)S(1)}, bf16[2,16,1024]{2,1,0:T(8,128)(2,1)S(1)}, u32[]{:S(2)}, u32[]{:S(2)}) collective-permute-start(bf16[2,16,1024]{2,1,0:T(8,128)(2,1)S(1)} %get-tuple-element.49), channel_id=1, source_target_pairs={{0,6},{1,7},{2,4},{3,5},{4,2},{5,3},{6,0},{7,1},{8,14},{9,15},{10,... | collective-permute-start | bytes 196616 | tf_op jit(solution)/shard_map/ppermute | solution.py:214
  50.7 9.3 %collective-permute-start.16 = (bf16[2,48,1024]{2,1,0:T(8,128)(2,1)S(1)}, bf16[2,48,1024]{2,1,0:T(8,128)(2,1)S(1)}, u32[]{:S(2)}, u32[]{:S(2)}) collective-permute-start(bf16[2,48,1024]{2,1,0:T(8,128)(2,1)S(1)} %add.1), channel_id=1, source_target_pairs={{0,16},{8,24},{16,0},{24,8},{1,17},{9,25},{17,1},{25,9},{2,18},{10... | collective-permute-start | bytes 589832 | tf_op jit(solution)/shard_map/ppermute | solution.py:217
  52.7 4.3 %collective-permute-start.17 = (bf16[2,16,1024]{2,1,0:T(8,128)(2,1)S(1)}, bf16[2,16,1024]{2,1,0:T(8,128)(2,1)S(1)}, u32[]{:S(2)}, u32[]{:S(2)}) collective-permute-start(bf16[2,16,1024]{2,1,0:T(8,128)(2,1)S(1)} %get-tuple-element.52), channel_id=1, source_target_pairs={{0,8},{8,0},{16,24},{24,16},{1,9},{9,1},{17,25},{25,17},{2,10},{10... | collective-permute-start | bytes 196616 | tf_op jit(solution)/shard_map/ppermute | solution.py:217
  53.8 6.2 %collective-permute-start.18 = (bf16[2,16,1024]{2,1,0:T(8,128)(2,1)S(1)}, bf16[2,16,1024]{2,1,0:T(8,128)(2,1)S(1)}, u32[]{:S(2)}, u32[]{:S(2)}) collective-permute-start(bf16[2,16,1024]{2,1,0:T(8,128)(2,1)S(1)} %get-tuple-element.53), channel_id=1, source_target_pairs={{0,24},{8,16},{16,8},{24,0},{1,25},{9,17},{17,9},{25,1},{2,26},{10... | collective-permute-start | bytes 196616 | tf_op jit(solution)/shard_map/ppermute | solution.py:217

commit v7 on v6

--- a/solution.py
+++ b/solution.py
@@ -58,18 +58,17 @@
 
 def columns_kernel(groups, ids_ref, w_ref, out_ref):
     _, c, k = place()
+    low = lax.broadcasted_iota(jnp.int32, (w_ref.shape[0], LANES), 1) < BLOCK
     for p in range(groups):
         tile = ((c ^ p) << 1) + k
         for pair in range(SLOTS // 2):
-            windows = []
-            odds = []
-            for slot in (2 * pair, 2 * pair + 1):
-                block = ids_ref[tile, slot]
+            halves = []
+            for slot in range(2):
+                block = ids_ref[tile, 2 * pair + slot]
                 start = pl.multiple_of((block >> 1) * LANES, LANES)
-                windows.append(w_ref[:, pl.ds(start, LANES)])
-                odds.append((block & 1) == 1)
-            picked = pick_pair(windows[0].astype(F32), windows[1].astype(F32), *odds)
-            out_ref[p, :, pair * LANES : (pair + 1) * LANES] = picked.astype(BF16)
+                turn = ((block & 1) ^ slot) * BLOCK
+                halves.append(pltpu.roll(w_ref[:, pl.ds(start, LANES)], turn, 1))
+            out_ref[p, :, pair * LANES : (pair + 1) * LANES] = jnp.where(low, *halves)
 
 
 def stage_kernel(src, dst, sems):
@@ -85,13 +84,17 @@
         copy.wait()
 
 
-def encode_kernel(groups, *refs):
-    bias_ref, pieces, (own_ref, oth_ref, out_ref) = refs[0], refs[1 : 1 + groups], refs[1 + groups :]
+def encode_kernel(groups, low, *refs):
+    bias_ref, own_ref, oth_ref = refs[:3]
+    done, pieces, out_ref = refs[3 : 3 + bool(low)], refs[3 + bool(low) : -1], refs[-1]
     _, c, k = place()
+    for ref in done:
+        out_ref[:low] = ref[...]
+    wslice = own_ref.shape[1]
     bias = [bias_ref[pl.ds(2 * c + (k ^ half), 1), :] for half in range(2)]
-    for p in range(groups):
+    for p, ref in enumerate(pieces, low):
         mine, other = [
-            (pieces[p][half].astype(F32) - bias[half]).astype(BF16) for half in range(2)
+            (ref[half].astype(F32) - bias[half]).astype(BF16) for half in range(2)
         ]
         acc = jnp.dot(mine, own_ref[p], preferred_element_type=F32)
         acc += jnp.dot(other, oth_ref[p], preferred_element_type=F32)
@@ -231,15 +234,12 @@
     )(tokens)
     pieces = [sent[0]] + [swap(sent[p], p) for p in range(1, groups)]
 
-    chunk = min(wslice, 256)
-
     def columns(weight):
         return pl.pallas_call(
             functools.partial(columns_kernel, groups),
             out_shape=jax.ShapeDtypeStruct((groups, wslice, ACTIVE), BF16),
-            grid=(wslice // chunk,),
-            in_specs=[spec(SMEM), pl.BlockSpec((chunk, feats), lambda i: (i, 0))],
-            out_specs=pl.BlockSpec((groups, chunk, ACTIVE), lambda i: (0, i, 0)),
+            in_specs=[spec(SMEM), spec(VMEM)],
+            out_specs=spec(VMEM),
             compiler_params=params(8),
             cost_estimate=cost(0, 2 * wslice * (feats + groups * ACTIVE)),
             name="columns",
@@ -248,15 +248,20 @@
     own_cols = columns(enc_weight)
     oth_cols = columns(enc_other)
     flops = 4 * groups * tok_rows * wslice * ACTIVE
-    part = pl.pallas_call(
-        functools.partial(encode_kernel, groups),
-        out_shape=jax.ShapeDtypeStruct((groups, tok_rows, ACTIVE), BF16),
-        in_specs=[spec(VMEM)] * (groups + 3),
-        out_specs=spec(VMEM),
-        compiler_params=params(8),
-        cost_estimate=cost(flops, 4 * groups * wslice * ACTIVE),
-        name="encode",
-    )(bias_rows, *pieces, own_cols, oth_cols)
+    part = []
+    for low, high in ((0, groups // 2), (groups // 2, groups)):
+        part = [
+            pl.pallas_call(
+                functools.partial(encode_kernel, groups, low),
+                out_shape=jax.ShapeDtypeStruct((high, tok_rows, ACTIVE), BF16),
+                in_specs=[spec(VMEM)] * (3 + len(part) + high - low),
+                out_specs=spec(VMEM),
+                compiler_params=params(8),
+                cost_estimate=cost(flops // 2, 2 * groups * wslice * ACTIVE),
+                name="encode",
+            )(bias_rows, own_cols, oth_cols, *part, *pieces[low:high])
+        ]
+    part = part[0]
     parts = [part] + [swap(part, p) for p in range(1, groups)]
 
     dec_staged = pl.pallas_call(

time: 61.1 us -> 60.7 us (level)
  Pallas kernels: 14.4 us -> 12.4 us
  waiting for transfers between devices: 19.7 us -> 21.4 us
    pallas_call x2, Pallas kernels: 7.37 us -> 5.21 us  [columns(): pl.pallas_call(functools.partial(columns_kernel, groups), out_shape=jax.S...]
    ppermute x12, waiting for transfers between devices: 12 us -> 13.7 us  [swap(): return lax.ppermute(value, 'tok', pairs)]
  transfers between devices with their start and end apart: 19 -> 19, of which waited for: 13 -> 13; matrix products, arithmetic and copies ran while one was open for 1% -> 1% of each run, Pallas kernels for 19% -> 16%
where the time goes in v7:
time: 60.7 us; the launch traced here: 60.5 us
  starting transfers between devices  21.7 us (36%)
  waiting for transfers between devices  21.4 us (35%)
  Pallas kernels  12.4 us (20%)
  local copies, waits for them, and re-layouts  4.2 us (7%)
  between operations  0.77 us (1%)
    ppermute x12, starting transfers between devices, swap(): return lax.ppermute(value, 'tok', pairs)  15 us
    ppermute x12, waiting for transfers between devices, swap(): return lax.ppermute(value, 'tok', pairs)  13.7 us
    ppermute x5, waiting for transfers between devices, lift(): return lax.ppermute(value, 'feat', [(i, i ^ m) for i in range(groups)])  7.69 us
    ppermute x5, starting transfers between devices, lift(): return lax.ppermute(value, 'feat', [(i, i ^ m) for i in range(groups)])  6.1 us
    pallas_call x2, Pallas kernels, columns(): pl.pallas_call(functools.partial(columns_kernel, groups), out_shape=jax.S...  5.21 us
    unnamed x12, local copies, waits for them, and re-layouts  3.43 us
    pallas_call x1, Pallas kernels, on_device(): pl.pallas_call(stage_kernel, out_shape=jax.ShapeDtypeStruct(dec_weight.sh...  2.37 us
    pallas_call x1, Pallas kernels, on_device(): pl.pallas_call(functools.partial(decode_kernel, groups), out_shape=[jax.S...  1.97 us
  transfers between devices with their start and end apart: 19, of which 13 were waited for; matrix products, arithmetic and copies ran while one was open for 1% of the time, Pallas kernels for 16%

profile of v7, /device:TPU:0, one launch (start us, length us, event | category | flops | bytes accessed | tf_op | source)
XLA Modules:
  0.0 60.5 jit_solution(689506049691471570)
XLA Ops:
  1.2 1.2 %copy-done.2 = bf16[64,8192]{1,0:T(8,128)(2,1)S(1)} copy-done((bf16[64,8192]{1,0:T(8,128)(2,1)S(1)}, bf16[64,8192]{1,0:T(8,128)(2,1)}, u32[]{:S(2)}) %copy-start.2) | copy-done | bytes 1048600
  2.5 0.9 %split.1 = (bf16[2,64,1024]{2,1,0:T(8,128)(2,1)S(1)}, bf16[2,64,1024]{2,1,0:T(8,128)(2,1)}, bf16[2,64,1024]{2,1,0:T(8,128)(2,1)}, bf16[2,64,1024]{2,1,0:T(8,128)(2,1)S(1)}) custom-call(bf16[64,8192]{1,0:T(8,128)(2,1)S(1)} %copy-done.2), custom_call_target="tpu_custom_call" | custom-call | bytes 2097152 | tf_op jit(solution)/shard_map/split/pallas_call | solution.py:226
  3.3 2.9 %collective-permute-start.1 = (bf16[2,64,1024]{2,1,0:T(8,128)(2,1)}, bf16[2,64,1024]{2,1,0:T(8,128)(2,1)S(1)}, u32[]{:S(2)}, u32[]{:S(2)}) collective-permute-start(bf16[2,64,1024]{2,1,0:T(8,128)(2,1)} %get-tuple-element.29), channel_id=1, source_target_pairs={{0,2},{1,3},{2,0},{3,1},{4,6},{5,7},{6,4},{7,5},{8,10},{9,11},{10,... | collective-permute-start | bytes 786440 | tf_op jit(solution)/shard_map/ppermute | solution.py:217
  6.2 1.5 %collective-permute-start.2 = (bf16[2,64,1024]{2,1,0:T(8,128)(2,1)}, bf16[2,64,1024]{2,1,0:T(8,128)(2,1)S(1)}, u32[]{:S(2)}, u32[]{:S(2)}) collective-permute-start(bf16[2,64,1024]{2,1,0:T(8,128)(2,1)} %get-tuple-element.30), channel_id=1, source_target_pairs={{0,4},{1,5},{2,6},{3,7},{4,0},{5,1},{6,2},{7,3},{8,12},{9,13},{10,... | collective-permute-start | bytes 786440 | tf_op jit(solution)/shard_map/ppermute | solution.py:217
  8.5 2.2 %copy-done.1 = bf16[1024,2048]{1,0:T(8,128)(2,1)S(1)} copy-done((bf16[1024,2048]{1,0:T(8,128)(2,1)S(1)}, bf16[1024,2048]{1,0:T(8,128)(2,1)}, u32[]{:S(2)}) %copy-start.1) | copy-done | bytes 4194328
  10.7 1.8 %columns.2.refs_1_ = bf16[4,1024,256]{2,1,0:T(8,128)(2,1)S(1)} custom-call(s32[8,4]{1,0:T(8,128)S(1)} %copy.11.ids_ref.refs_0_, bf16[1024,2048]{1,0:T(8,128)(2,1)S(1)} %copy-done.1), custom_call_target="tpu_custom_call" | custom-call | bytes 6291456 | tf_op jit(solution)/shard_map/columns/pallas_call | solution.py:238
  12.6 3.4 %columns.3.refs_2_ = bf16[4,1024,256]{2,1,0:T(8,128)(2,1)S(1)} custom-call(s32[8,4]{1,0:T(8,128)S(1)} %copy.11.ids_ref.refs_0_, bf16[1024,2048]{1,0:T(8,128)(2,1)} %collective-permute-done.w_ref), custom_call_target="tpu_custom_call" | custom-call | bytes 6291456 | tf_op jit(solution)/shard_map/columns/pallas_call | solution.py:238
  16.5 3.6 %collective-permute-done.2.refs_4_ = bf16[2,64,1024]{2,1,0:T(8,128)(2,1)S(1)} collective-permute-done((bf16[2,64,1024]{2,1,0:T(8,128)(2,1)}, bf16[2,64,1024]{2,1,0:T(8,128)(2,1)S(1)}, u32[]{:S(2)}, u32[]{:S(2)}) %collective-permute-start.2) | collective-permute-done | bytes 262176 | tf_op jit(solution)/shard_map/ppermute | solution.py:217
  20.6 1.3 %collective-permute-start.4 = (bf16[4,64,256]{2,1,0:T(8,128)(2,1)S(1)}, bf16[4,64,256]{2,1,0:T(8,128)(2,1)S(1)}, u32[]{:S(2)}, u32[]{:S(2)}) collective-permute-start(bf16[4,64,256]{2,1,0:T(8,128)(2,1)S(1)} %encode.3.refs_3_), channel_id=1, source_target_pairs={{0,2},{1,3},{2,0},{3,1},{4,6},{5,7},{6,4},{7,5},{8,10},{9,11},{10,... | collective-permute-start | bytes 393224 | tf_op jit(solution)/shard_map/ppermute | solution.py:217
  21.9 0.8 %collective-permute-start.5 = (bf16[4,64,256]{2,1,0:T(8,128)(2,1)S(1)}, bf16[4,64,256]{2,1,0:T(8,128)(2,1)S(1)}, u32[]{:S(2)}, u32[]{:S(2)}) collective-permute-start(bf16[4,64,256]{2,1,0:T(8,128)(2,1)S(1)} %encode.3.refs_3_), channel_id=1, source_target_pairs={{0,4},{1,5},{2,6},{3,7},{4,0},{5,1},{6,2},{7,3},{8,12},{9,13},{10,... | collective-permute-start | bytes 393224 | tf_op jit(solution)/shard_map/ppermute | solution.py:217
  22.7 1.4 %collective-permute-start.6 = (bf16[4,64,256]{2,1,0:T(8,128)(2,1)S(1)}, bf16[4,64,256]{2,1,0:T(8,128)(2,1)S(1)}, u32[]{:S(2)}, u32[]{:S(2)}) collective-permute-start(bf16[4,64,256]{2,1,0:T(8,128)(2,1)S(1)} %encode.3.refs_3_), channel_id=1, source_target_pairs={{0,6},{1,7},{2,4},{3,5},{4,2},{5,3},{6,0},{7,1},{8,14},{9,15},{10,... | collective-permute-start | bytes 393224 | tf_op jit(solution)/shard_map/ppermute | solution.py:217
  24.2 2.4 %stage.1.refs_8_ = bf16[2048,1024]{1,0:T(8,128)(2,1)S(1)} custom-call(bf16[2048,1024]{1,0:T(8,128)(2,1)} %collective-permute-done.7.src), custom_call_target="tpu_custom_call" | custom-call | bytes 8388608 | tf_op jit(solution)/shard_map/stage/pallas_call | solution.py:267
  26.7 2.4 %collective-permute-done.5.refs_5_ = bf16[4,64,256]{2,1,0:T(8,128)(2,1)S(1)} collective-permute-done((bf16[4,64,256]{2,1,0:T(8,128)(2,1)S(1)}, bf16[4,64,256]{2,1,0:T(8,128)(2,1)S(1)}, u32[]{:S(2)}, u32[]{:S(2)}) %collective-permute-start.5) | collective-permute-done | bytes 131104 | tf_op jit(solution)/shard_map/ppermute | solution.py:217
  29.1 2.0 %decode.1 = (bf16[64,256]{1,0:T(8,128)(2,1)}, bf16[2,32,1024]{2,1,0:T(8,128)(2,1)S(1)}, bf16[2,32,1024]{2,1,0:T(8,128)(2,1)S(1)}, bf16[2,32,1024]{2,1,0:T(8,128)...) custom-call(s32[8,4]{1,0:T(8,128)S(1)} %copy.11.ids_ref.refs_0_, ...), custom_call_target="tpu_custom_call" | custom-call | flops 268435456 | bytes 4194304 | tf_op jit(solution)/shard_map/decode/pallas_call | solution.py:282
  31.0 1.6 %collective-permute-start.8 = (bf16[4,2,16,1024]{3,2,1,0:T(8,128)(2,1)S(1)}, bf16[4,2,16,1024]{3,2,1,0:T(8,128)(2,1)S(1)}, u32[]{:S(2)}, u32[]{:S(2)}) collective-permute-start(bf16[4,2,16,1024]{3,2,1,0:T(8,128)(2,1)S(1)} %get-tuple-element.35), channel_id=1, source_target_pairs={{0,8},{8,0},{16,24},{24,16},{1,9},{9,1},{17,25},{25,17},{2,10},{10... | collective-permute-start | bytes 786440 | tf_op jit(solution)/shard_map/ppermute | solution.py:220
  32.6 1.3 %collective-permute-start.10 = (bf16[2,32,1024]{2,1,0:T(8,128)(2,1)S(1)}, bf16[2,32,1024]{2,1,0:T(8,128)(2,1)S(1)}, u32[]{:S(2)}, u32[]{:S(2)}) collective-permute-start(bf16[2,32,1024]{2,1,0:T(8,128)(2,1)S(1)} %get-tuple-element.42), channel_id=1, source_target_pairs={{0,4},{1,5},{2,6},{3,7},{4,0},{5,1},{6,2},{7,3},{8,12},{9,13},{10,... | collective-permute-start | bytes 393224 | tf_op jit(solution)/shard_map/ppermute | solution.py:217
  33.9 1.2 %collective-permute-start.11 = (bf16[2,32,1024]{2,1,0:T(8,128)(2,1)S(1)}, bf16[2,32,1024]{2,1,0:T(8,128)(2,1)S(1)}, u32[]{:S(2)}, u32[]{:S(2)}) collective-permute-start(bf16[2,32,1024]{2,1,0:T(8,128)(2,1)S(1)} %get-tuple-element.43), channel_id=1, source_target_pairs={{0,6},{1,7},{2,4},{3,5},{4,2},{5,3},{6,0},{7,1},{8,14},{9,15},{10,... | collective-permute-start | bytes 393224 | tf_op jit(solution)/shard_map/ppermute | solution.py:217
  35.1 1.0 %collective-permute-start.9 = (bf16[2,32,1024]{2,1,0:T(8,128)(2,1)S(1)}, bf16[2,32,1024]{2,1,0:T(8,128)(2,1)S(1)}, u32[]{:S(2)}, u32[]{:S(2)}) collective-permute-start(bf16[2,32,1024]{2,1,0:T(8,128)(2,1)S(1)} %get-tuple-element.41), channel_id=1, source_target_pairs={{0,2},{1,3},{2,0},{3,1},{4,6},{5,7},{6,4},{7,5},{8,10},{9,11},{10,... | collective-permute-start | bytes 393224 | tf_op jit(solution)/shard_map/ppermute | solution.py:217
  36.1 1.3 %collective-permute-done.8.came_ref = bf16[4,2,16,1024]{3,2,1,0:T(8,128)(2,1)S(1)} collective-permute-done((bf16[4,2,16,1024]{3,2,1,0:T(8,128)(2,1)S(1)}, bf16[4,2,16,1024]{3,2,1,0:T(8,128)(2,1)S(1)}, u32[]{:S(2)}, u32[]{:S(2)}) %collective-permute-start.8) | collective-permute-done | bytes 262176 | tf_op jit(solution)/shard_map/ppermute | solution.py:220
  37.9 1.8 %collective-permute-done.11.refs_3_ = bf16[2,32,1024]{2,1,0:T(8,128)(2,1)S(1)} collective-permute-done((bf16[2,32,1024]{2,1,0:T(8,128)(2,1)S(1)}, bf16[2,32,1024]{2,1,0:T(8,128)(2,1)S(1)}, u32[]{:S(2)}, u32[]{:S(2)}) %collective-permute-start.11) | collective-permute-done | bytes 131104 | tf_op jit(solution)/shard_map/ppermute | solution.py:217
  39.8 1.2 %collective-permute-done.9.refs_1_ = bf16[2,32,1024]{2,1,0:T(8,128)(2,1)S(1)} collective-permute-done((bf16[2,32,1024]{2,1,0:T(8,128)(2,1)S(1)}, bf16[2,32,1024]{2,1,0:T(8,128)(2,1)S(1)}, u32[]{:S(2)}, u32[]{:S(2)}) %collective-permute-start.9) | collective-permute-done | bytes 131104 | tf_op jit(solution)/shard_map/ppermute | solution.py:217
  41.2 1.3 %collective-permute-start.13 = (bf16[2,16,1024]{2,1,0:T(8,128)(2,1)S(1)}, bf16[2,16,1024]{2,1,0:T(8,128)(2,1)S(1)}, u32[]{:S(2)}, u32[]{:S(2)}) collective-permute-start(bf16[2,16,1024]{2,1,0:T(8,128)(2,1)S(1)} %get-tuple-element.47), channel_id=1, source_target_pairs={{0,2},{1,3},{2,0},{3,1},{4,6},{5,7},{6,4},{7,5},{8,10},{9,11},{10,... | collective-permute-start | bytes 196616 | tf_op jit(solution)/shard_map/ppermute | solution.py:217
  42.4 1.1 %collective-permute-start.14 = (bf16[2,16,1024]{2,1,0:T(8,128)(2,1)S(1)}, bf16[2,16,1024]{2,1,0:T(8,128)(2,1)S(1)}, u32[]{:S(2)}, u32[]{:S(2)}) collective-permute-start(bf16[2,16,1024]{2,1,0:T(8,128)(2,1)S(1)} %get-tuple-element.48), channel_id=1, source_target_pairs={{0,4},{1,5},{2,6},{3,7},{4,0},{5,1},{6,2},{7,3},{8,12},{9,13},{10,... | collective-permute-start | bytes 196616 | tf_op jit(solution)/shard_map/ppermute | solution.py:217
  43.6 1.1 %collective-permute-start.15 = (bf16[2,16,1024]{2,1,0:T(8,128)(2,1)S(1)}, bf16[2,16,1024]{2,1,0:T(8,128)(2,1)S(1)}, u32[]{:S(2)}, u32[]{:S(2)}) collective-permute-start(bf16[2,16,1024]{2,1,0:T(8,128)(2,1)S(1)} %get-tuple-element.49), channel_id=1, source_target_pairs={{0,6},{1,7},{2,4},{3,5},{4,2},{5,3},{6,0},{7,1},{8,14},{9,15},{10,... | collective-permute-start | bytes 196616 | tf_op jit(solution)/shard_map/ppermute | solution.py:217
  45.5 1.2 %collective-permute-done.14.refs_2_ = bf16[2,16,1024]{2,1,0:T(8,128)(2,1)S(1)} collective-permute-done((bf16[2,16,1024]{2,1,0:T(8,128)(2,1)S(1)}, bf16[2,16,1024]{2,1,0:T(8,128)(2,1)S(1)}, u32[]{:S(2)}, u32[]{:S(2)}) %collective-permute-start.14) | collective-permute-done | bytes 65568 | tf_op jit(solution)/shard_map/ppermute | solution.py:217
  46.7 2.0 %collective-permute-done.15.refs_3_ = bf16[2,16,1024]{2,1,0:T(8,128)(2,1)S(1)} collective-permute-done((bf16[2,16,1024]{2,1,0:T(8,128)(2,1)S(1)}, bf16[2,16,1024]{2,1,0:T(8,128)(2,1)S(1)}, u32[]{:S(2)}, u32[]{:S(2)}) %collective-permute-start.15) | collective-permute-done | bytes 65568 | tf_op jit(solution)/shard_map/ppermute | solution.py:217
  48.8 1.5 %collective-permute-done.12.refs_1_ = bf16[2,2,32,1024]{3,2,1,0:T(8,128)(2,1)S(1)} collective-permute-done((bf16[2,2,32,1024]{3,2,1,0:T(8,128)(2,1)S(1)}, bf16[2,2,32,1024]{3,2,1,0:T(8,128)(2,1)S(1)}, u32[]{:S(2)}, u32[]{:S(2)}) %collective-permute-start.12) | collective-permute-done | bytes 262176 | tf_op jit(solution)/shard_map/ppermute | solution.py:220
  50.4 2.0 %collective-permute-start.16 = (bf16[2,48,1024]{2,1,0:T(8,128)(2,1)S(1)}, bf16[2,48,1024]{2,1,0:T(8,128)(2,1)S(1)}, u32[]{:S(2)}, u32[]{:S(2)}) collective-permute-start(bf16[2,48,1024]{2,1,0:T(8,128)(2,1)S(1)} %add.1), channel_id=1, source_target_pairs={{0,16},{8,24},{16,0},{24,8},{1,17},{9,25},{17,1},{25,9},{2,18},{10... | collective-permute-start | bytes 589832 | tf_op jit(solution)/shard_map/ppermute | solution.py:220
  52.4 1.1 %collective-permute-start.17 = (bf16[2,16,1024]{2,1,0:T(8,128)(2,1)S(1)}, bf16[2,16,1024]{2,1,0:T(8,128)(2,1)S(1)}, u32[]{:S(2)}, u32[]{:S(2)}) collective-permute-start(bf16[2,16,1024]{2,1,0:T(8,128)(2,1)S(1)} %get-tuple-element.52), channel_id=1, source_target_pairs={{0,8},{8,0},{16,24},{24,16},{1,9},{9,1},{17,25},{25,17},{2,10},{10... | collective-permute-start | bytes 196616 | tf_op jit(solution)/shard_map/ppermute | solution.py:220
  53.5 1.3 %collective-permute-start.18 = (bf16[2,16,1024]{2,1,0:T(8,128)(2,1)S(1)}, bf16[2,16,1024]{2,1,0:T(8,128)(2,1)S(1)}, u32[]{:S(2)}, u32[]{:S(2)}) collective-permute-start(bf16[2,16,1024]{2,1,0:T(8,128)(2,1)S(1)} %get-tuple-element.53), channel_id=1, source_target_pairs={{0,24},{8,16},{16,8},{24,0},{1,25},{9,17},{17,9},{25,1},{2,26},{10... | collective-permute-start | bytes 196616 | tf_op jit(solution)/shard_map/ppermute | solution.py:220
  54.8 1.8 %collective-permute-done.17.refs_4_ = bf16[2,16,1024]{2,1,0:T(8,128)(2,1)S(1)} collective-permute-done((bf16[2,16,1024]{2,1,0:T(8,128)(2,1)S(1)}, bf16[2,16,1024]{2,1,0:T(8,128)(2,1)S(1)}, u32[]{:S(2)}, u32[]{:S(2)}) %collective-permute-start.17) | collective-permute-done | bytes 65568 | tf_op jit(solution)/shard_map/ppermute | solution.py:220
  56.6 3.0 %collective-permute-done.18.refs_5_ = bf16[2,16,1024]{2,1,0:T(8,128)(2,1)S(1)} collective-permute-done((bf16[2,16,1024]{2,1,0:T(8,128)(2,1)S(1)}, bf16[2,16,1024]{2,1,0:T(8,128)(2,1)S(1)}, u32[]{:S(2)}, u32[]{:S(2)}) %collective-permute-start.18) | collective-permute-done | bytes 65568 | tf_op jit(solution)/shard_map/ppermute | solution.py:220
  (33 shorter events, 4.8 us)
Async XLA Ops:
  0.6 11.9 %collective-permute-start = (bf16[1024,2048]{1,0:T(8,128)(2,1)}, bf16[1024,2048]{1,0:T(8,128)(2,1)}, u32[]{:S(2)}, u32[]{:S(2)}) collective-permute-start(bf16[1024,2048]{1,0:T(8,128)(2,1)} %w_ref.1), channel_id=1, source_target_pairs={{0,1},{1,0},{2,3},{3,2},{4,5},{5,4},{6,7},{7,6},{8,9},{9,8},{10,11... | collective-permute-start | bytes 12582920 | tf_op jit(solution)/shard_map/ppermute | solution.py:223
  1.1 23.0 %collective-permute-start.7 = (bf16[2048,1024]{1,0:T(8,128)(2,1)}, bf16[2048,1024]{1,0:T(8,128)(2,1)}, u32[]{:S(2)}, u32[]{:S(2)}) collective-permute-start(bf16[2048,1024]{1,0:T(8,128)(2,1)} %refs_7_.1), channel_id=1, source_target_pairs={{0,1},{1,0},{2,3},{3,2},{4,5},{5,4},{6,7},{7,6},{8,9},{9,8},{10,11... | collective-permute-start | bytes 12582920 | tf_op jit(solution)/shard_map/ppermute | solution.py:224
  1.2 1.2 %copy-start.2 = (bf16[64,8192]{1,0:T(8,128)(2,1)S(1)}, bf16[64,8192]{1,0:T(8,128)(2,1)}, u32[]{:S(2)}) copy-start(bf16[64,8192]{1,0:T(8,128)(2,1)} %tok_ref.1) | copy-start | bytes 3145732
  2.5 10.1 %copy-start.4 = (bf16[8192]{0:T(1024)(128)(2,1)S(1)}, bf16[8192]{0:T(1024)(128)(2,1)}, u32[]{:S(2)}) copy-start(bf16[8192]{0:T(1024)(128)(2,1)} %param.8) | copy-start | bytes 49156
  3.3 12.7 %collective-permute-start.1 = (bf16[2,64,1024]{2,1,0:T(8,128)(2,1)}, bf16[2,64,1024]{2,1,0:T(8,128)(2,1)S(1)}, u32[]{:S(2)}, u32[]{:S(2)}) collective-permute-start(bf16[2,64,1024]{2,1,0:T(8,128)(2,1)} %get-tuple-element.29), channel_id=1, source_target_pairs={{0,2},{1,3},{2,0},{3,1},{4,6},{5,7},{6,4},{7,5},{8,10},{9,11},{10,... | collective-permute-start | bytes 786440 | tf_op jit(solution)/shard_map/ppermute | solution.py:217
  6.2 13.8 %collective-permute-start.2 = (bf16[2,64,1024]{2,1,0:T(8,128)(2,1)}, bf16[2,64,1024]{2,1,0:T(8,128)(2,1)S(1)}, u32[]{:S(2)}, u32[]{:S(2)}) collective-permute-start(bf16[2,64,1024]{2,1,0:T(8,128)(2,1)} %get-tuple-element.30), channel_id=1, source_target_pairs={{0,4},{1,5},{2,6},{3,7},{4,0},{5,1},{6,2},{7,3},{8,12},{9,13},{10,... | collective-permute-start | bytes 786440 | tf_op jit(solution)/shard_map/ppermute | solution.py:217
  7.8 12.3 %collective-permute-start.3 = (bf16[2,64,1024]{2,1,0:T(8,128)(2,1)S(1)}, bf16[2,64,1024]{2,1,0:T(8,128)(2,1)S(1)}, u32[]{:S(2)}, u32[]{:S(2)}) collective-permute-start(bf16[2,64,1024]{2,1,0:T(8,128)(2,1)S(1)} %get-tuple-element.31), channel_id=1, source_target_pairs={{0,6},{1,7},{2,4},{3,5},{4,2},{5,3},{6,0},{7,1},{8,14},{9,15},{10,... | collective-permute-start | bytes 786440 | tf_op jit(solution)/shard_map/ppermute | solution.py:217
  8.5 2.2 %copy-start.1 = (bf16[1024,2048]{1,0:T(8,128)(2,1)S(1)}, bf16[1024,2048]{1,0:T(8,128)(2,1)}, u32[]{:S(2)}) copy-start(bf16[1024,2048]{1,0:T(8,128)(2,1)} %w_ref.1) | copy-start | bytes 12582916
  16.0 8.1 %copy-start.5 = (bf16[2048]{0:T(1024)(128)(2,1)S(1)}, bf16[2048]{0:T(1024)(128)(2,1)}, u32[]{:S(2)}) copy-start(bf16[2048]{0:T(1024)(128)(2,1)} %param.10) | copy-start | bytes 12292
  20.6 6.1 %collective-permute-start.4 = (bf16[4,64,256]{2,1,0:T(8,128)(2,1)S(1)}, bf16[4,64,256]{2,1,0:T(8,128)(2,1)S(1)}, u32[]{:S(2)}, u32[]{:S(2)}) collective-permute-start(bf16[4,64,256]{2,1,0:T(8,128)(2,1)S(1)} %encode.3.refs_3_), channel_id=1, source_target_pairs={{0,2},{1,3},{2,0},{3,1},{4,6},{5,7},{6,4},{7,5},{8,10},{9,11},{10,... | collective-permute-start | bytes 393224 | tf_op jit(solution)/shard_map/ppermute | solution.py:217
  21.9 7.2 %collective-permute-start.5 = (bf16[4,64,256]{2,1,0:T(8,128)(2,1)S(1)}, bf16[4,64,256]{2,1,0:T(8,128)(2,1)S(1)}, u32[]{:S(2)}, u32[]{:S(2)}) collective-permute-start(bf16[4,64,256]{2,1,0:T(8,128)(2,1)S(1)} %encode.3.refs_3_), channel_id=1, source_target_pairs={{0,4},{1,5},{2,6},{3,7},{4,0},{5,1},{6,2},{7,3},{8,12},{9,13},{10,... | collective-permute-start | bytes 393224 | tf_op jit(solution)/shard_map/ppermute | solution.py:217
  22.7 6.4 %collective-permute-start.6 = (bf16[4,64,256]{2,1,0:T(8,128)(2,1)S(1)}, bf16[4,64,256]{2,1,0:T(8,128)(2,1)S(1)}, u32[]{:S(2)}, u32[]{:S(2)}) collective-permute-start(bf16[4,64,256]{2,1,0:T(8,128)(2,1)S(1)} %encode.3.refs_3_), channel_id=1, source_target_pairs={{0,6},{1,7},{2,4},{3,5},{4,2},{5,3},{6,0},{7,1},{8,14},{9,15},{10,... | collective-permute-start | bytes 393224 | tf_op jit(solution)/shard_map/ppermute | solution.py:217
  24.1 4.9 %copy-start = (bf16[2048,1024]{1,0:T(8,128)(2,1)S(1)}, bf16[2048,1024]{1,0:T(8,128)(2,1)}, u32[]{:S(2)}) copy-start(bf16[2048,1024]{1,0:T(8,128)(2,1)} %refs_7_.1) | copy-start | bytes 12582916
  24.1 4.9 %copy-start.3 = (s32[8,1]{0,1:T(1,128)S(1)}, s32[8,1]{0,1:T(1,128)}, u32[]{:S(2)}) copy-start(s32[8,1]{0,1:T(1,128)} %param.13) | copy-start | bytes 100
  31.0 6.4 %collective-permute-start.8 = (bf16[4,2,16,1024]{3,2,1,0:T(8,128)(2,1)S(1)}, bf16[4,2,16,1024]{3,2,1,0:T(8,128)(2,1)S(1)}, u32[]{:S(2)}, u32[]{:S(2)}) collective-permute-start(bf16[4,2,16,1024]{3,2,1,0:T(8,128)(2,1)S(1)} %get-tuple-element.35), channel_id=1, source_target_pairs={{0,8},{8,0},{16,24},{24,16},{1,9},{9,1},{17,25},{25,17},{2,10},{10... | collective-permute-start | bytes 786440 | tf_op jit(solution)/shard_map/ppermute | solution.py:220
  32.6 5.3 %collective-permute-start.10 = (bf16[2,32,1024]{2,1,0:T(8,128)(2,1)S(1)}, bf16[2,32,1024]{2,1,0:T(8,128)(2,1)S(1)}, u32[]{:S(2)}, u32[]{:S(2)}) collective-permute-start(bf16[2,32,1024]{2,1,0:T(8,128)(2,1)S(1)} %get-tuple-element.42), channel_id=1, source_target_pairs={{0,4},{1,5},{2,6},{3,7},{4,0},{5,1},{6,2},{7,3},{8,12},{9,13},{10,... | collective-permute-start | bytes 393224 | tf_op jit(solution)/shard_map/ppermute | solution.py:217
  33.9 5.9 %collective-permute-start.11 = (bf16[2,32,1024]{2,1,0:T(8,128)(2,1)S(1)}, bf16[2,32,1024]{2,1,0:T(8,128)(2,1)S(1)}, u32[]{:S(2)}, u32[]{:S(2)}) collective-permute-start(bf16[2,32,1024]{2,1,0:T(8,128)(2,1)S(1)} %get-tuple-element.43), channel_id=1, source_target_pairs={{0,6},{1,7},{2,4},{3,5},{4,2},{5,3},{6,0},{7,1},{8,14},{9,15},{10,... | collective-permute-start | bytes 393224 | tf_op jit(solution)/shard_map/ppermute | solution.py:217
  35.1 5.9 %collective-permute-start.9 = (bf16[2,32,1024]{2,1,0:T(8,128)(2,1)S(1)}, bf16[2,32,1024]{2,1,0:T(8,128)(2,1)S(1)}, u32[]{:S(2)}, u32[]{:S(2)}) collective-permute-start(bf16[2,32,1024]{2,1,0:T(8,128)(2,1)S(1)} %get-tuple-element.41), channel_id=1, source_target_pairs={{0,2},{1,3},{2,0},{3,1},{4,6},{5,7},{6,4},{7,5},{8,10},{9,11},{10,... | collective-permute-start | bytes 393224 | tf_op jit(solution)/shard_map/ppermute | solution.py:217
  41.1 9.2 %collective-permute-start.12 = (bf16[2,2,32,1024]{3,2,1,0:T(8,128)(2,1)S(1)}, bf16[2,2,32,1024]{3,2,1,0:T(8,128)(2,1)S(1)}, u32[]{:S(2)}, u32[]{:S(2)}) collective-permute-start(bf16[2,2,32,1024]{3,2,1,0:T(8,128)(2,1)S(1)} %get-tuple-element.45), channel_id=1, source_target_pairs={{0,8},{8,0},{16,24},{24,16},{1,9},{9,1},{17,25},{25,17},{2,10},{10... | collective-permute-start | bytes 786440 | tf_op jit(solution)/shard_map/ppermute | solution.py:220
  41.2 4.3 %collective-permute-start.13 = (bf16[2,16,1024]{2,1,0:T(8,128)(2,1)S(1)}, bf16[2,16,1024]{2,1,0:T(8,128)(2,1)S(1)}, u32[]{:S(2)}, u32[]{:S(2)}) collective-permute-start(bf16[2,16,1024]{2,1,0:T(8,128)(2,1)S(1)} %get-tuple-element.47), channel_id=1, source_target_pairs={{0,2},{1,3},{2,0},{3,1},{4,6},{5,7},{6,4},{7,5},{8,10},{9,11},{10,... | collective-permute-start | bytes 196616 | tf_op jit(solution)/shard_map/ppermute | solution.py:217
  42.4 4.3 %collective-permute-start.14 = (bf16[2,16,1024]{2,1,0:T(8,128)(2,1)S(1)}, bf16[2,16,1024]{2,1,0:T(8,128)(2,1)S(1)}, u32[]{:S(2)}, u32[]{:S(2)}) collective-permute-start(bf16[2,16,1024]{2,1,0:T(8,128)(2,1)S(1)} %get-tuple-element.48), channel_id=1, source_target_pairs={{0,4},{1,5},{2,6},{3,7},{4,0},{5,1},{6,2},{7,3},{8,12},{9,13},{10,... | collective-permute-start | bytes 196616 | tf_op jit(solution)/shard_map/ppermute | solution.py:217
  43.6 5.2 %collective-permute-start.15 = (bf16[2,16,1024]{2,1,0:T(8,128)(2,1)S(1)}, bf16[2,16,1024]{2,1,0:T(8,128)(2,1)S(1)}, u32[]{:S(2)}, u32[]{:S(2)}) collective-permute-start(bf16[2,16,1024]{2,1,0:T(8,128)(2,1)S(1)} %get-tuple-element.49), channel_id=1, source_target_pairs={{0,6},{1,7},{2,4},{3,5},{4,2},{5,3},{6,0},{7,1},{8,14},{9,15},{10,... | collective-permute-start | bytes 196616 | tf_op jit(solution)/shard_map/ppermute | solution.py:217
  50.4 9.3 %collective-permute-start.16 = (bf16[2,48,1024]{2,1,0:T(8,128)(2,1)S(1)}, bf16[2,48,1024]{2,1,0:T(8,128)(2,1)S(1)}, u32[]{:S(2)}, u32[]{:S(2)}) collective-permute-start(bf16[2,48,1024]{2,1,0:T(8,128)(2,1)S(1)} %add.1), channel_id=1, source_target_pairs={{0,16},{8,24},{16,0},{24,8},{1,17},{9,25},{17,1},{25,9},{2,18},{10... | collective-permute-start | bytes 589832 | tf_op jit(solution)/shard_map/ppermute | solution.py:220
  52.4 4.3 %collective-permute-start.17 = (bf16[2,16,1024]{2,1,0:T(8,128)(2,1)S(1)}, bf16[2,16,1024]{2,1,0:T(8,128)(2,1)S(1)}, u32[]{:S(2)}, u32[]{:S(2)}) collective-permute-start(bf16[2,16,1024]{2,1,0:T(8,128)(2,1)S(1)} %get-tuple-element.52), channel_id=1, source_target_pairs={{0,8},{8,0},{16,24},{24,16},{1,9},{9,1},{17,25},{25,17},{2,10},{10... | collective-permute-start | bytes 196616 | tf_op jit(solution)/shard_map/ppermute | solution.py:220
  53.5 6.2 %collective-permute-start.18 = (bf16[2,16,1024]{2,1,0:T(8,128)(2,1)S(1)}, bf16[2,16,1024]{2,1,0:T(8,128)(2,1)S(1)}, u32[]{:S(2)}, u32[]{:S(2)}) collective-permute-start(bf16[2,16,1024]{2,1,0:T(8,128)(2,1)S(1)} %get-tuple-element.53), channel_id=1, source_target_pairs={{0,24},{8,16},{16,8},{24,0},{1,25},{9,17},{17,9},{25,1},{2,26},{10... | collective-permute-start | bytes 196616 | tf_op jit(solution)/shard_map/ppermute | solution.py:220

commit v8 on v7

--- a/solution.py
+++ b/solution.py
@@ -39,14 +39,26 @@
     return lax.axis_index("feat"), tok >> 1, tok & 1
 
 
-def split_kernel(groups, tok_ref, *outs):
+def split_kernel(groups, tok_ref, bias_ref, *refs):
+    outs, (held, bias, sems) = refs[:groups], refs[groups:]
     _, c, k = place()
     wslice = outs[0].shape[2]
+    parts = sems.shape[0] - 1
+    height = held.shape[0] // parts
+    copies = [pltpu.make_async_copy(bias_ref, bias, sems.at[parts])]
+    for i in range(parts):
+        some = pl.ds(i * height, height)
+        copies.append(pltpu.make_async_copy(tok_ref.at[some, :], held.at[some, :], sems.at[i]))
+    for copy in copies:
+        copy.start()
+    for copy in copies:
+        copy.wait()
     for p in range(groups):
         for half in range(2):
             u = ((c ^ p) << 1) + (k ^ half)
             cols = pl.ds(pl.multiple_of(u * wslice, wslice), wslice)
-            outs[p][half] = tok_ref[:, cols]
+            value = held[:, cols].astype(F32) - bias[cols].astype(F32)[None, :]
+            outs[p][half] = value.astype(BF16)
 
 
 def pick_pair(first, second, odd_first, odd_second):
@@ -85,19 +97,13 @@
 
 
 def encode_kernel(groups, low, *refs):
-    bias_ref, own_ref, oth_ref = refs[:3]
-    done, pieces, out_ref = refs[3 : 3 + bool(low)], refs[3 + bool(low) : -1], refs[-1]
-    _, c, k = place()
+    own_ref, oth_ref = refs[:2]
+    done, pieces, out_ref = refs[2 : 2 + bool(low)], refs[2 + bool(low) : -1], refs[-1]
     for ref in done:
         out_ref[:low] = ref[...]
-    wslice = own_ref.shape[1]
-    bias = [bias_ref[pl.ds(2 * c + (k ^ half), 1), :] for half in range(2)]
     for p, ref in enumerate(pieces, low):
-        mine, other = [
-            (ref[half].astype(F32) - bias[half]).astype(BF16) for half in range(2)
-        ]
-        acc = jnp.dot(mine, own_ref[p], preferred_element_type=F32)
-        acc += jnp.dot(other, oth_ref[p], preferred_element_type=F32)
+        acc = jnp.dot(ref[0], own_ref[p], preferred_element_type=F32)
+        acc += jnp.dot(ref[1], oth_ref[p], preferred_element_type=F32)
         out_ref[p] = acc.astype(BF16)
 
 
@@ -226,12 +232,17 @@
     sent = pl.pallas_call(
         functools.partial(split_kernel, groups),
         out_shape=[jax.ShapeDtypeStruct((2, tok_rows, wslice), BF16)] * groups,
-        in_specs=[spec(VMEM)],
+        in_specs=[spec(pl.ANY)] * 2,
         out_specs=[spec(VMEM)] * groups,
+        scratch_shapes=[
+            VMEM((tok_rows, width), BF16),
+            VMEM((width,), BF16),
+            pltpu.SemaphoreType.DMA((5,)),
+        ],
         compiler_params=params(8),
         cost_estimate=cost(0, 4 * width * tok_rows),
         name="split",
-    )(tokens)
+    )(pin(tokens), pin(dec_bias))
     pieces = [sent[0]] + [swap(sent[p], p) for p in range(1, groups)]
 
     def columns(weight):
@@ -254,12 +265,12 @@
             pl.pallas_call(
                 functools.partial(encode_kernel, groups, low),
                 out_shape=jax.ShapeDtypeStruct((high, tok_rows, ACTIVE), BF16),
-                in_specs=[spec(VMEM)] * (3 + len(part) + high - low),
+                in_specs=[spec(VMEM)] * (2 + len(part) + high - low),
                 out_specs=spec(VMEM),
                 compiler_params=params(8),
                 cost_estimate=cost(flops // 2, 2 * groups * wslice * ACTIVE),
                 name="encode",
-            )(bias_rows, own_cols, oth_cols, *part, *pieces[low:high])
+            )(own_cols, oth_cols, *part, *pieces[low:high])
         ]
     part = part[0]
     parts = [part] + [swap(part, p) for p in range(1, groups)]

time: 60.7 us -> 59.9 us (0.987)
  local copies, waits for them, and re-layouts: 4.2 us -> 2.98 us
    unnamed x12 -> x10, local copies, waits for them, and re-layouts: 3.43 us -> 2.21 us
  transfers between devices with their start and end apart: 19 -> 19, of which waited for: 13 -> 13; matrix products, arithmetic and copies ran while one was open for 1% -> 1% of each run, Pallas kernels for 16% -> 17%
where the time goes in v8:
time: 59.9 us; the launch traced here: 59.7 us
  starting transfers between devices  21.8 us (36%)
  waiting for transfers between devices  21.1 us (35%)
  Pallas kernels  13 us (22%)
  local copies, waits for them, and re-layouts  2.98 us (5%)
  between operations  0.77 us (1%)
    ppermute x12, starting transfers between devices, swap(): return lax.ppermute(value, 'tok', pairs)  15.1 us
    ppermute x12, waiting for transfers between devices, swap(): return lax.ppermute(value, 'tok', pairs)  13.5 us
    ppermute x5, waiting for transfers between devices, lift(): return lax.ppermute(value, 'feat', [(i, i ^ m) for i in range(groups)])  7.67 us
    ppermute x5, starting transfers between devices, lift(): return lax.ppermute(value, 'feat', [(i, i ^ m) for i in range(groups)])  6.1 us
    pallas_call x2, Pallas kernels, columns(): pl.pallas_call(functools.partial(columns_kernel, groups), out_shape=jax.S...  5.23 us
    pallas_call x1, Pallas kernels, on_device(): pl.pallas_call(stage_kernel, out_shape=jax.ShapeDtypeStruct(dec_weight.sh...  2.37 us
    unnamed x10, local copies, waits for them, and re-layouts  2.21 us
    pallas_call x1, Pallas kernels, on_device(): pl.pallas_call(functools.partial(decode_kernel, groups), out_shape=[jax.S...  1.97 us
  transfers between devices with their start and end apart: 19, of which 13 were waited for; matrix products, arithmetic and copies ran while one was open for 1% of the time, Pallas kernels for 17%

profile of v8, /device:TPU:0, one launch (start us, length us, event | category | flops | bytes accessed | tf_op | source)
XLA Modules:
  0.0 59.7 jit_solution(12009702038845015746)
XLA Ops:
  1.2 1.4 %split.1 = (bf16[2,64,1024]{2,1,0:T(8,128)(2,1)S(1)}, bf16[2,64,1024]{2,1,0:T(8,128)(2,1)S(1)}, bf16[2,64,1024]{2,1,0:T(8,128)(2,1)S(1)}, bf16[2,64,1024]{2,1,0:T(8,128)(2,1)S(1)}) custom-call(bf16[64,8192]{1,0:T(8,128)(2,1)} %tok_ref.1, bf16[8192]{0:T(1024)(128)(2,1)} %bias_ref.1), custom_call_target="tpu_custom_call" | custom-call | bytes 2097152 | tf_op jit(solution)/shard_map/split/pallas_call | solution.py:232
  2.7 3.0 %collective-permute-start.1 = (bf16[2,64,1024]{2,1,0:T(8,128)(2,1)S(1)}, bf16[2,64,1024]{2,1,0:T(8,128)(2,1)S(1)}, u32[]{:S(2)}, u32[]{:S(2)}) collective-permute-start(bf16[2,64,1024]{2,1,0:T(8,128)(2,1)S(1)} %get-tuple-element.29), channel_id=1, source_target_pairs={{0,2},{1,3},{2,0},{3,1},{4,6},{5,7},{6,4},{7,5},{8,10},{9,11},{10,... | collective-permute-start | bytes 786440 | tf_op jit(solution)/shard_map/ppermute | solution.py:223
  5.7 1.5 %collective-permute-start.2 = (bf16[2,64,1024]{2,1,0:T(8,128)(2,1)S(1)}, bf16[2,64,1024]{2,1,0:T(8,128)(2,1)S(1)}, u32[]{:S(2)}, u32[]{:S(2)}) collective-permute-start(bf16[2,64,1024]{2,1,0:T(8,128)(2,1)S(1)} %get-tuple-element.30), channel_id=1, source_target_pairs={{0,4},{1,5},{2,6},{3,7},{4,0},{5,1},{6,2},{7,3},{8,12},{9,13},{10,... | collective-permute-start | bytes 786440 | tf_op jit(solution)/shard_map/ppermute | solution.py:223
  8.0 2.2 %copy-done.1 = bf16[1024,2048]{1,0:T(8,128)(2,1)S(1)} copy-done((bf16[1024,2048]{1,0:T(8,128)(2,1)S(1)}, bf16[1024,2048]{1,0:T(8,128)(2,1)}, u32[]{:S(2)}) %copy-start.1) | copy-done | bytes 4194328
  10.1 1.8 %columns.2.refs_0_ = bf16[4,1024,256]{2,1,0:T(8,128)(2,1)S(1)} custom-call(s32[8,4]{1,0:T(8,128)S(1)} %copy.11.ids_ref.refs_0_, bf16[1024,2048]{1,0:T(8,128)(2,1)S(1)} %copy-done.1), custom_call_target="tpu_custom_call" | custom-call | bytes 6291456 | tf_op jit(solution)/shard_map/columns/pallas_call | solution.py:249
  12.0 3.4 %columns.3.refs_1_ = bf16[4,1024,256]{2,1,0:T(8,128)(2,1)S(1)} custom-call(s32[8,4]{1,0:T(8,128)S(1)} %copy.11.ids_ref.refs_0_, bf16[1024,2048]{1,0:T(8,128)(2,1)} %collective-permute-done.w_ref), custom_call_target="tpu_custom_call" | custom-call | bytes 6291456 | tf_op jit(solution)/shard_map/columns/pallas_call | solution.py:249
  15.9 3.4 %collective-permute-done.2.refs_3_ = bf16[2,64,1024]{2,1,0:T(8,128)(2,1)S(1)} collective-permute-done((bf16[2,64,1024]{2,1,0:T(8,128)(2,1)S(1)}, bf16[2,64,1024]{2,1,0:T(8,128)(2,1)S(1)}, u32[]{:S(2)}, u32[]{:S(2)}) %collective-permute-start.2) | collective-permute-done | bytes 262176 | tf_op jit(solution)/shard_map/ppermute | solution.py:223
  19.8 1.3 %collective-permute-start.4 = (bf16[4,64,256]{2,1,0:T(8,128)(2,1)S(1)}, bf16[4,64,256]{2,1,0:T(8,128)(2,1)S(1)}, u32[]{:S(2)}, u32[]{:S(2)}) collective-permute-start(bf16[4,64,256]{2,1,0:T(8,128)(2,1)S(1)} %encode.3.refs_3_), channel_id=1, source_target_pairs={{0,2},{1,3},{2,0},{3,1},{4,6},{5,7},{6,4},{7,5},{8,10},{9,11},{10,... | collective-permute-start | bytes 393224 | tf_op jit(solution)/shard_map/ppermute | solution.py:223
  21.1 0.8 %collective-permute-start.5 = (bf16[4,64,256]{2,1,0:T(8,128)(2,1)S(1)}, bf16[4,64,256]{2,1,0:T(8,128)(2,1)S(1)}, u32[]{:S(2)}, u32[]{:S(2)}) collective-permute-start(bf16[4,64,256]{2,1,0:T(8,128)(2,1)S(1)} %encode.3.refs_3_), channel_id=1, source_target_pairs={{0,4},{1,5},{2,6},{3,7},{4,0},{5,1},{6,2},{7,3},{8,12},{9,13},{10,... | collective-permute-start | bytes 393224 | tf_op jit(solution)/shard_map/ppermute | solution.py:223
  21.9 1.4 %collective-permute-start.6 = (bf16[4,64,256]{2,1,0:T(8,128)(2,1)S(1)}, bf16[4,64,256]{2,1,0:T(8,128)(2,1)S(1)}, u32[]{:S(2)}, u32[]{:S(2)}) collective-permute-start(bf16[4,64,256]{2,1,0:T(8,128)(2,1)S(1)} %encode.3.refs_3_), channel_id=1, source_target_pairs={{0,6},{1,7},{2,4},{3,5},{4,2},{5,3},{6,0},{7,1},{8,14},{9,15},{10,... | collective-permute-start | bytes 393224 | tf_op jit(solution)/shard_map/ppermute | solution.py:223
  23.4 2.4 %stage.1.refs_8_ = bf16[2048,1024]{1,0:T(8,128)(2,1)S(1)} custom-call(bf16[2048,1024]{1,0:T(8,128)(2,1)} %collective-permute-done.7.src), custom_call_target="tpu_custom_call" | custom-call | bytes 8388608 | tf_op jit(solution)/shard_map/stage/pallas_call | solution.py:278
  25.9 2.4 %collective-permute-done.5.refs_5_ = bf16[4,64,256]{2,1,0:T(8,128)(2,1)S(1)} collective-permute-done((bf16[4,64,256]{2,1,0:T(8,128)(2,1)S(1)}, bf16[4,64,256]{2,1,0:T(8,128)(2,1)S(1)}, u32[]{:S(2)}, u32[]{:S(2)}) %collective-permute-start.5) | collective-permute-done | bytes 131104 | tf_op jit(solution)/shard_map/ppermute | solution.py:223
  28.3 2.0 %decode.1 = (bf16[64,256]{1,0:T(8,128)(2,1)}, bf16[2,32,1024]{2,1,0:T(8,128)(2,1)S(1)}, bf16[2,32,1024]{2,1,0:T(8,128)(2,1)S(1)}, bf16[2,32,1024]{2,1,0:T(8,128)...) custom-call(s32[8,4]{1,0:T(8,128)S(1)} %copy.11.ids_ref.refs_0_, ...), custom_call_target="tpu_custom_call" | custom-call | flops 268435456 | bytes 4194304 | tf_op jit(solution)/shard_map/decode/pallas_call | solution.py:293
  30.3 1.6 %collective-permute-start.8 = (bf16[4,2,16,1024]{3,2,1,0:T(8,128)(2,1)S(1)}, bf16[4,2,16,1024]{3,2,1,0:T(8,128)(2,1)S(1)}, u32[]{:S(2)}, u32[]{:S(2)}) collective-permute-start(bf16[4,2,16,1024]{3,2,1,0:T(8,128)(2,1)S(1)} %get-tuple-element.35), channel_id=1, source_target_pairs={{0,8},{8,0},{16,24},{24,16},{1,9},{9,1},{17,25},{25,17},{2,10},{10... | collective-permute-start | bytes 786440 | tf_op jit(solution)/shard_map/ppermute | solution.py:226
  31.8 1.3 %collective-permute-start.10 = (bf16[2,32,1024]{2,1,0:T(8,128)(2,1)S(1)}, bf16[2,32,1024]{2,1,0:T(8,128)(2,1)S(1)}, u32[]{:S(2)}, u32[]{:S(2)}) collective-permute-start(bf16[2,32,1024]{2,1,0:T(8,128)(2,1)S(1)} %get-tuple-element.42), channel_id=1, source_target_pairs={{0,4},{1,5},{2,6},{3,7},{4,0},{5,1},{6,2},{7,3},{8,12},{9,13},{10,... | collective-permute-start | bytes 393224 | tf_op jit(solution)/shard_map/ppermute | solution.py:223
  33.1 1.2 %collective-permute-start.11 = (bf16[2,32,1024]{2,1,0:T(8,128)(2,1)S(1)}, bf16[2,32,1024]{2,1,0:T(8,128)(2,1)S(1)}, u32[]{:S(2)}, u32[]{:S(2)}) collective-permute-start(bf16[2,32,1024]{2,1,0:T(8,128)(2,1)S(1)} %get-tuple-element.43), channel_id=1, source_target_pairs={{0,6},{1,7},{2,4},{3,5},{4,2},{5,3},{6,0},{7,1},{8,14},{9,15},{10,... | collective-permute-start | bytes 393224 | tf_op jit(solution)/shard_map/ppermute | solution.py:223
  34.3 1.0 %collective-permute-start.9 = (bf16[2,32,1024]{2,1,0:T(8,128)(2,1)S(1)}, bf16[2,32,1024]{2,1,0:T(8,128)(2,1)S(1)}, u32[]{:S(2)}, u32[]{:S(2)}) collective-permute-start(bf16[2,32,1024]{2,1,0:T(8,128)(2,1)S(1)} %get-tuple-element.41), channel_id=1, source_target_pairs={{0,2},{1,3},{2,0},{3,1},{4,6},{5,7},{6,4},{7,5},{8,10},{9,11},{10,... | collective-permute-start | bytes 393224 | tf_op jit(solution)/shard_map/ppermute | solution.py:223
  35.3 1.3 %collective-permute-done.8.came_ref = bf16[4,2,16,1024]{3,2,1,0:T(8,128)(2,1)S(1)} collective-permute-done((bf16[4,2,16,1024]{3,2,1,0:T(8,128)(2,1)S(1)}, bf16[4,2,16,1024]{3,2,1,0:T(8,128)(2,1)S(1)}, u32[]{:S(2)}, u32[]{:S(2)}) %collective-permute-start.8) | collective-permute-done | bytes 262176 | tf_op jit(solution)/shard_map/ppermute | solution.py:226
  37.1 1.8 %collective-permute-done.11.refs_3_ = bf16[2,32,1024]{2,1,0:T(8,128)(2,1)S(1)} collective-permute-done((bf16[2,32,1024]{2,1,0:T(8,128)(2,1)S(1)}, bf16[2,32,1024]{2,1,0:T(8,128)(2,1)S(1)}, u32[]{:S(2)}, u32[]{:S(2)}) %collective-permute-start.11) | collective-permute-done | bytes 131104 | tf_op jit(solution)/shard_map/ppermute | solution.py:223
  39.0 1.3 %collective-permute-done.9.refs_1_ = bf16[2,32,1024]{2,1,0:T(8,128)(2,1)S(1)} collective-permute-done((bf16[2,32,1024]{2,1,0:T(8,128)(2,1)S(1)}, bf16[2,32,1024]{2,1,0:T(8,128)(2,1)S(1)}, u32[]{:S(2)}, u32[]{:S(2)}) %collective-permute-start.9) | collective-permute-done | bytes 131104 | tf_op jit(solution)/shard_map/ppermute | solution.py:223
  40.4 1.3 %collective-permute-start.13 = (bf16[2,16,1024]{2,1,0:T(8,128)(2,1)S(1)}, bf16[2,16,1024]{2,1,0:T(8,128)(2,1)S(1)}, u32[]{:S(2)}, u32[]{:S(2)}) collective-permute-start(bf16[2,16,1024]{2,1,0:T(8,128)(2,1)S(1)} %get-tuple-element.47), channel_id=1, source_target_pairs={{0,2},{1,3},{2,0},{3,1},{4,6},{5,7},{6,4},{7,5},{8,10},{9,11},{10,... | collective-permute-start | bytes 196616 | tf_op jit(solution)/shard_map/ppermute | solution.py:223
  41.7 1.2 %collective-permute-start.14 = (bf16[2,16,1024]{2,1,0:T(8,128)(2,1)S(1)}, bf16[2,16,1024]{2,1,0:T(8,128)(2,1)S(1)}, u32[]{:S(2)}, u32[]{:S(2)}) collective-permute-start(bf16[2,16,1024]{2,1,0:T(8,128)(2,1)S(1)} %get-tuple-element.48), channel_id=1, source_target_pairs={{0,4},{1,5},{2,6},{3,7},{4,0},{5,1},{6,2},{7,3},{8,12},{9,13},{10,... | collective-permute-start | bytes 196616 | tf_op jit(solution)/shard_map/ppermute | solution.py:223
  42.8 1.1 %collective-permute-start.15 = (bf16[2,16,1024]{2,1,0:T(8,128)(2,1)S(1)}, bf16[2,16,1024]{2,1,0:T(8,128)(2,1)S(1)}, u32[]{:S(2)}, u32[]{:S(2)}) collective-permute-start(bf16[2,16,1024]{2,1,0:T(8,128)(2,1)S(1)} %get-tuple-element.49), channel_id=1, source_target_pairs={{0,6},{1,7},{2,4},{3,5},{4,2},{5,3},{6,0},{7,1},{8,14},{9,15},{10,... | collective-permute-start | bytes 196616 | tf_op jit(solution)/shard_map/ppermute | solution.py:223
  44.7 1.2 %collective-permute-done.14.refs_2_ = bf16[2,16,1024]{2,1,0:T(8,128)(2,1)S(1)} collective-permute-done((bf16[2,16,1024]{2,1,0:T(8,128)(2,1)S(1)}, bf16[2,16,1024]{2,1,0:T(8,128)(2,1)S(1)}, u32[]{:S(2)}, u32[]{:S(2)}) %collective-permute-start.14) | collective-permute-done | bytes 65568 | tf_op jit(solution)/shard_map/ppermute | solution.py:223
  45.9 2.1 %collective-permute-done.15.refs_3_ = bf16[2,16,1024]{2,1,0:T(8,128)(2,1)S(1)} collective-permute-done((bf16[2,16,1024]{2,1,0:T(8,128)(2,1)S(1)}, bf16[2,16,1024]{2,1,0:T(8,128)(2,1)S(1)}, u32[]{:S(2)}, u32[]{:S(2)}) %collective-permute-start.15) | collective-permute-done | bytes 65568 | tf_op jit(solution)/shard_map/ppermute | solution.py:223
  48.0 1.6 %collective-permute-done.12.refs_1_ = bf16[2,2,32,1024]{3,2,1,0:T(8,128)(2,1)S(1)} collective-permute-done((bf16[2,2,32,1024]{3,2,1,0:T(8,128)(2,1)S(1)}, bf16[2,2,32,1024]{3,2,1,0:T(8,128)(2,1)S(1)}, u32[]{:S(2)}, u32[]{:S(2)}) %collective-permute-start.12) | collective-permute-done | bytes 262176 | tf_op jit(solution)/shard_map/ppermute | solution.py:226
  49.6 2.0 %collective-permute-start.16 = (bf16[2,48,1024]{2,1,0:T(8,128)(2,1)S(1)}, bf16[2,48,1024]{2,1,0:T(8,128)(2,1)S(1)}, u32[]{:S(2)}, u32[]{:S(2)}) collective-permute-start(bf16[2,48,1024]{2,1,0:T(8,128)(2,1)S(1)} %add.1), channel_id=1, source_target_pairs={{0,16},{8,24},{16,0},{24,8},{1,17},{9,25},{17,1},{25,9},{2,18},{10... | collective-permute-start | bytes 589832 | tf_op jit(solution)/shard_map/ppermute | solution.py:226
  51.6 1.1 %collective-permute-start.17 = (bf16[2,16,1024]{2,1,0:T(8,128)(2,1)S(1)}, bf16[2,16,1024]{2,1,0:T(8,128)(2,1)S(1)}, u32[]{:S(2)}, u32[]{:S(2)}) collective-permute-start(bf16[2,16,1024]{2,1,0:T(8,128)(2,1)S(1)} %get-tuple-element.52), channel_id=1, source_target_pairs={{0,8},{8,0},{16,24},{24,16},{1,9},{9,1},{17,25},{25,17},{2,10},{10... | collective-permute-start | bytes 196616 | tf_op jit(solution)/shard_map/ppermute | solution.py:226
  52.7 1.4 %collective-permute-start.18 = (bf16[2,16,1024]{2,1,0:T(8,128)(2,1)S(1)}, bf16[2,16,1024]{2,1,0:T(8,128)(2,1)S(1)}, u32[]{:S(2)}, u32[]{:S(2)}) collective-permute-start(bf16[2,16,1024]{2,1,0:T(8,128)(2,1)S(1)} %get-tuple-element.53), channel_id=1, source_target_pairs={{0,24},{8,16},{16,8},{24,0},{1,25},{9,17},{17,9},{25,1},{2,26},{10... | collective-permute-start | bytes 196616 | tf_op jit(solution)/shard_map/ppermute | solution.py:226
  54.1 1.8 %collective-permute-done.17.refs_4_ = bf16[2,16,1024]{2,1,0:T(8,128)(2,1)S(1)} collective-permute-done((bf16[2,16,1024]{2,1,0:T(8,128)(2,1)S(1)}, bf16[2,16,1024]{2,1,0:T(8,128)(2,1)S(1)}, u32[]{:S(2)}, u32[]{:S(2)}) %collective-permute-start.17) | collective-permute-done | bytes 65568 | tf_op jit(solution)/shard_map/ppermute | solution.py:226
  55.9 3.0 %collective-permute-done.18.refs_5_ = bf16[2,16,1024]{2,1,0:T(8,128)(2,1)S(1)} collective-permute-done((bf16[2,16,1024]{2,1,0:T(8,128)(2,1)S(1)}, bf16[2,16,1024]{2,1,0:T(8,128)(2,1)S(1)}, u32[]{:S(2)}, u32[]{:S(2)}) %collective-permute-start.18) | collective-permute-done | bytes 65568 | tf_op jit(solution)/shard_map/ppermute | solution.py:226
  58.9 0.8 %finish.1 = bf16[64,2048]{1,0:T(8,128)(2,1)} custom-call(bf16[2,2,32,1024]{3,2,1,0:T(8,128)(2,1)S(1)} %get-tuple-element.44.refs_0_, bf16[2,2,32,1024]{3,2,1,0:T(8,128)(2,1)S(1)} %collective-permute-done.12.refs_1_, bf16[2,16,1024]{2,1,0:T(8,128)(2,1)S(1)} %get-tuple-element.50.refs_2_, bf16[2,48,1024]{2,1,0:T(8,128)(2,1)S(1)} %collective-permute-done.16.refs_3_, ...), custom_call_target="tpu_custom_call" | custom-call | bytes 1310720 | tf_op jit(solution)/shard_map/finish/pallas_call | solution.py:355
  (31 shorter events, 4.1 us)
Async XLA Ops:
  0.6 11.3 %collective-permute-start = (bf16[1024,2048]{1,0:T(8,128)(2,1)}, bf16[1024,2048]{1,0:T(8,128)(2,1)}, u32[]{:S(2)}, u32[]{:S(2)}) collective-permute-start(bf16[1024,2048]{1,0:T(8,128)(2,1)} %w_ref.1), channel_id=1, source_target_pairs={{0,1},{1,0},{2,3},{3,2},{4,5},{5,4},{6,7},{7,6},{8,9},{9,8},{10,11... | collective-permute-start | bytes 12582920 | tf_op jit(solution)/shard_map/ppermute | solution.py:229
  1.1 22.2 %collective-permute-start.7 = (bf16[2048,1024]{1,0:T(8,128)(2,1)}, bf16[2048,1024]{1,0:T(8,128)(2,1)}, u32[]{:S(2)}, u32[]{:S(2)}) collective-permute-start(bf16[2048,1024]{1,0:T(8,128)(2,1)} %refs_7_.1), channel_id=1, source_target_pairs={{0,1},{1,0},{2,3},{3,2},{4,5},{5,4},{6,7},{7,6},{8,9},{9,8},{10,11... | collective-permute-start | bytes 12582920 | tf_op jit(solution)/shard_map/ppermute | solution.py:230
  2.7 12.7 %collective-permute-start.1 = (bf16[2,64,1024]{2,1,0:T(8,128)(2,1)S(1)}, bf16[2,64,1024]{2,1,0:T(8,128)(2,1)S(1)}, u32[]{:S(2)}, u32[]{:S(2)}) collective-permute-start(bf16[2,64,1024]{2,1,0:T(8,128)(2,1)S(1)} %get-tuple-element.29), channel_id=1, source_target_pairs={{0,2},{1,3},{2,0},{3,1},{4,6},{5,7},{6,4},{7,5},{8,10},{9,11},{10,... | collective-permute-start | bytes 786440 | tf_op jit(solution)/shard_map/ppermute | solution.py:223
  5.7 13.6 %collective-permute-start.2 = (bf16[2,64,1024]{2,1,0:T(8,128)(2,1)S(1)}, bf16[2,64,1024]{2,1,0:T(8,128)(2,1)S(1)}, u32[]{:S(2)}, u32[]{:S(2)}) collective-permute-start(bf16[2,64,1024]{2,1,0:T(8,128)(2,1)S(1)} %get-tuple-element.30), channel_id=1, source_target_pairs={{0,4},{1,5},{2,6},{3,7},{4,0},{5,1},{6,2},{7,3},{8,12},{9,13},{10,... | collective-permute-start | bytes 786440 | tf_op jit(solution)/shard_map/ppermute | solution.py:223
  7.2 12.1 %collective-permute-start.3 = (bf16[2,64,1024]{2,1,0:T(8,128)(2,1)S(1)}, bf16[2,64,1024]{2,1,0:T(8,128)(2,1)S(1)}, u32[]{:S(2)}, u32[]{:S(2)}) collective-permute-start(bf16[2,64,1024]{2,1,0:T(8,128)(2,1)S(1)} %get-tuple-element.31), channel_id=1, source_target_pairs={{0,6},{1,7},{2,4},{3,5},{4,2},{5,3},{6,0},{7,1},{8,14},{9,15},{10,... | collective-permute-start | bytes 786440 | tf_op jit(solution)/shard_map/ppermute | solution.py:223
  8.0 2.2 %copy-start.1 = (bf16[1024,2048]{1,0:T(8,128)(2,1)S(1)}, bf16[1024,2048]{1,0:T(8,128)(2,1)}, u32[]{:S(2)}) copy-start(bf16[1024,2048]{1,0:T(8,128)(2,1)} %w_ref.1) | copy-start | bytes 12582916
  15.4 7.9 %copy-start.4 = (bf16[2048]{0:T(1024)(128)(2,1)S(1)}, bf16[2048]{0:T(1024)(128)(2,1)}, u32[]{:S(2)}) copy-start(bf16[2048]{0:T(1024)(128)(2,1)} %param.10) | copy-start | bytes 12292
  19.8 6.1 %collective-permute-start.4 = (bf16[4,64,256]{2,1,0:T(8,128)(2,1)S(1)}, bf16[4,64,256]{2,1,0:T(8,128)(2,1)S(1)}, u32[]{:S(2)}, u32[]{:S(2)}) collective-permute-start(bf16[4,64,256]{2,1,0:T(8,128)(2,1)S(1)} %encode.3.refs_3_), channel_id=1, source_target_pairs={{0,2},{1,3},{2,0},{3,1},{4,6},{5,7},{6,4},{7,5},{8,10},{9,11},{10,... | collective-permute-start | bytes 393224 | tf_op jit(solution)/shard_map/ppermute | solution.py:223
  21.1 7.2 %collective-permute-start.5 = (bf16[4,64,256]{2,1,0:T(8,128)(2,1)S(1)}, bf16[4,64,256]{2,1,0:T(8,128)(2,1)S(1)}, u32[]{:S(2)}, u32[]{:S(2)}) collective-permute-start(bf16[4,64,256]{2,1,0:T(8,128)(2,1)S(1)} %encode.3.refs_3_), channel_id=1, source_target_pairs={{0,4},{1,5},{2,6},{3,7},{4,0},{5,1},{6,2},{7,3},{8,12},{9,13},{10,... | collective-permute-start | bytes 393224 | tf_op jit(solution)/shard_map/ppermute | solution.py:223
  21.9 6.4 %collective-permute-start.6 = (bf16[4,64,256]{2,1,0:T(8,128)(2,1)S(1)}, bf16[4,64,256]{2,1,0:T(8,128)(2,1)S(1)}, u32[]{:S(2)}, u32[]{:S(2)}) collective-permute-start(bf16[4,64,256]{2,1,0:T(8,128)(2,1)S(1)} %encode.3.refs_3_), channel_id=1, source_target_pairs={{0,6},{1,7},{2,4},{3,5},{4,2},{5,3},{6,0},{7,1},{8,14},{9,15},{10,... | collective-permute-start | bytes 393224 | tf_op jit(solution)/shard_map/ppermute | solution.py:223
  23.3 4.9 %copy-start = (bf16[2048,1024]{1,0:T(8,128)(2,1)S(1)}, bf16[2048,1024]{1,0:T(8,128)(2,1)}, u32[]{:S(2)}) copy-start(bf16[2048,1024]{1,0:T(8,128)(2,1)} %refs_7_.1) | copy-start | bytes 12582916
  23.4 4.9 %copy-start.2 = (s32[8,1]{0,1:T(1,128)S(1)}, s32[8,1]{0,1:T(1,128)}, u32[]{:S(2)}) copy-start(s32[8,1]{0,1:T(1,128)} %param.13) | copy-start | bytes 100
  28.3 25.8 %copy-start.3 = (bf16[8192]{0:T(1024)(128)(2,1)S(1)}, bf16[8192]{0:T(1024)(128)(2,1)}, u32[]{:S(2)}) copy-start(bf16[8192]{0:T(1024)(128)(2,1)} %bias_ref.1) | copy-start | bytes 49156
  30.3 6.4 %collective-permute-start.8 = (bf16[4,2,16,1024]{3,2,1,0:T(8,128)(2,1)S(1)}, bf16[4,2,16,1024]{3,2,1,0:T(8,128)(2,1)S(1)}, u32[]{:S(2)}, u32[]{:S(2)}) collective-permute-start(bf16[4,2,16,1024]{3,2,1,0:T(8,128)(2,1)S(1)} %get-tuple-element.35), channel_id=1, source_target_pairs={{0,8},{8,0},{16,24},{24,16},{1,9},{9,1},{17,25},{25,17},{2,10},{10... | collective-permute-start | bytes 786440 | tf_op jit(solution)/shard_map/ppermute | solution.py:226
  31.8 5.3 %collective-permute-start.10 = (bf16[2,32,1024]{2,1,0:T(8,128)(2,1)S(1)}, bf16[2,32,1024]{2,1,0:T(8,128)(2,1)S(1)}, u32[]{:S(2)}, u32[]{:S(2)}) collective-permute-start(bf16[2,32,1024]{2,1,0:T(8,128)(2,1)S(1)} %get-tuple-element.42), channel_id=1, source_target_pairs={{0,4},{1,5},{2,6},{3,7},{4,0},{5,1},{6,2},{7,3},{8,12},{9,13},{10,... | collective-permute-start | bytes 393224 | tf_op jit(solution)/shard_map/ppermute | solution.py:223
  33.1 5.9 %collective-permute-start.11 = (bf16[2,32,1024]{2,1,0:T(8,128)(2,1)S(1)}, bf16[2,32,1024]{2,1,0:T(8,128)(2,1)S(1)}, u32[]{:S(2)}, u32[]{:S(2)}) collective-permute-start(bf16[2,32,1024]{2,1,0:T(8,128)(2,1)S(1)} %get-tuple-element.43), channel_id=1, source_target_pairs={{0,6},{1,7},{2,4},{3,5},{4,2},{5,3},{6,0},{7,1},{8,14},{9,15},{10,... | collective-permute-start | bytes 393224 | tf_op jit(solution)/shard_map/ppermute | solution.py:223
  34.3 6.0 %collective-permute-start.9 = (bf16[2,32,1024]{2,1,0:T(8,128)(2,1)S(1)}, bf16[2,32,1024]{2,1,0:T(8,128)(2,1)S(1)}, u32[]{:S(2)}, u32[]{:S(2)}) collective-permute-start(bf16[2,32,1024]{2,1,0:T(8,128)(2,1)S(1)} %get-tuple-element.41), channel_id=1, source_target_pairs={{0,2},{1,3},{2,0},{3,1},{4,6},{5,7},{6,4},{7,5},{8,10},{9,11},{10,... | collective-permute-start | bytes 393224 | tf_op jit(solution)/shard_map/ppermute | solution.py:223
  40.3 9.2 %collective-permute-start.12 = (bf16[2,2,32,1024]{3,2,1,0:T(8,128)(2,1)S(1)}, bf16[2,2,32,1024]{3,2,1,0:T(8,128)(2,1)S(1)}, u32[]{:S(2)}, u32[]{:S(2)}) collective-permute-start(bf16[2,2,32,1024]{3,2,1,0:T(8,128)(2,1)S(1)} %get-tuple-element.45), channel_id=1, source_target_pairs={{0,8},{8,0},{16,24},{24,16},{1,9},{9,1},{17,25},{25,17},{2,10},{10... | collective-permute-start | bytes 786440 | tf_op jit(solution)/shard_map/ppermute | solution.py:226
  40.4 4.3 %collective-permute-start.13 = (bf16[2,16,1024]{2,1,0:T(8,128)(2,1)S(1)}, bf16[2,16,1024]{2,1,0:T(8,128)(2,1)S(1)}, u32[]{:S(2)}, u32[]{:S(2)}) collective-permute-start(bf16[2,16,1024]{2,1,0:T(8,128)(2,1)S(1)} %get-tuple-element.47), channel_id=1, source_target_pairs={{0,2},{1,3},{2,0},{3,1},{4,6},{5,7},{6,4},{7,5},{8,10},{9,11},{10,... | collective-permute-start | bytes 196616 | tf_op jit(solution)/shard_map/ppermute | solution.py:223
  41.7 4.3 %collective-permute-start.14 = (bf16[2,16,1024]{2,1,0:T(8,128)(2,1)S(1)}, bf16[2,16,1024]{2,1,0:T(8,128)(2,1)S(1)}, u32[]{:S(2)}, u32[]{:S(2)}) collective-permute-start(bf16[2,16,1024]{2,1,0:T(8,128)(2,1)S(1)} %get-tuple-element.48), channel_id=1, source_target_pairs={{0,4},{1,5},{2,6},{3,7},{4,0},{5,1},{6,2},{7,3},{8,12},{9,13},{10,... | collective-permute-start | bytes 196616 | tf_op jit(solution)/shard_map/ppermute | solution.py:223
  42.8 5.2 %collective-permute-start.15 = (bf16[2,16,1024]{2,1,0:T(8,128)(2,1)S(1)}, bf16[2,16,1024]{2,1,0:T(8,128)(2,1)S(1)}, u32[]{:S(2)}, u32[]{:S(2)}) collective-permute-start(bf16[2,16,1024]{2,1,0:T(8,128)(2,1)S(1)} %get-tuple-element.49), channel_id=1, source_target_pairs={{0,6},{1,7},{2,4},{3,5},{4,2},{5,3},{6,0},{7,1},{8,14},{9,15},{10,... | collective-permute-start | bytes 196616 | tf_op jit(solution)/shard_map/ppermute | solution.py:223
  49.6 9.3 %collective-permute-start.16 = (bf16[2,48,1024]{2,1,0:T(8,128)(2,1)S(1)}, bf16[2,48,1024]{2,1,0:T(8,128)(2,1)S(1)}, u32[]{:S(2)}, u32[]{:S(2)}) collective-permute-start(bf16[2,48,1024]{2,1,0:T(8,128)(2,1)S(1)} %add.1), channel_id=1, source_target_pairs={{0,16},{8,24},{16,0},{24,8},{1,17},{9,25},{17,1},{25,9},{2,18},{10... | collective-permute-start | bytes 589832 | tf_op jit(solution)/shard_map/ppermute | solution.py:226
  51.6 4.3 %collective-permute-start.17 = (bf16[2,16,1024]{2,1,0:T(8,128)(2,1)S(1)}, bf16[2,16,1024]{2,1,0:T(8,128)(2,1)S(1)}, u32[]{:S(2)}, u32[]{:S(2)}) collective-permute-start(bf16[2,16,1024]{2,1,0:T(8,128)(2,1)S(1)} %get-tuple-element.52), channel_id=1, source_target_pairs={{0,8},{8,0},{16,24},{24,16},{1,9},{9,1},{17,25},{25,17},{2,10},{10... | collective-permute-start | bytes 196616 | tf_op jit(solution)/shard_map/ppermute | solution.py:226
  52.7 6.2 %collective-permute-start.18 = (bf16[2,16,1024]{2,1,0:T(8,128)(2,1)S(1)}, bf16[2,16,1024]{2,1,0:T(8,128)(2,1)S(1)}, u32[]{:S(2)}, u32[]{:S(2)}) collective-permute-start(bf16[2,16,1024]{2,1,0:T(8,128)(2,1)S(1)} %get-tuple-element.53), channel_id=1, source_target_pairs={{0,24},{8,16},{16,8},{24,0},{1,25},{9,17},{17,9},{25,1},{2,26},{10... | collective-permute-start | bytes 196616 | tf_op jit(solution)/shard_map/ppermute | solution.py:226

commit v9 on v8

--- a/solution.py
+++ b/solution.py
@@ -51,14 +51,16 @@
         copies.append(pltpu.make_async_copy(tok_ref.at[some, :], held.at[some, :], sems.at[i]))
     for copy in copies:
         copy.start()
-    for copy in copies:
+    copies[0].wait()
+    for i, copy in enumerate(copies[1:]):
         copy.wait()
-    for p in range(groups):
-        for half in range(2):
-            u = ((c ^ p) << 1) + (k ^ half)
-            cols = pl.ds(pl.multiple_of(u * wslice, wslice), wslice)
-            value = held[:, cols].astype(F32) - bias[cols].astype(F32)[None, :]
-            outs[p][half] = value.astype(BF16)
+        some = slice(i * height, (i + 1) * height)
+        for p in range(groups):
+            for half in range(2):
+                u = ((c ^ p) << 1) + (k ^ half)
+                cols = pl.ds(pl.multiple_of(u * wslice, wslice), wslice)
+                value = held[some, cols].astype(F32) - bias[cols].astype(F32)[None, :]
+                outs[p][half, some] = value.astype(BF16)
 
 
 def pick_pair(first, second, odd_first, odd_second):

time: 59.9 us -> 59.8 us (level)
  no operation moved by 1% of the time
where the time goes in v9:
time: 59.8 us; the launch traced here: 59.6 us
  starting transfers between devices  21.8 us (36%)
  waiting for transfers between devices  21.2 us (35%)
  Pallas kernels  12.8 us (21%)
  local copies, waits for them, and re-layouts  2.98 us (5%)
  between operations  0.77 us (1%)
    ppermute x12, starting transfers between devices, swap(): return lax.ppermute(value, 'tok', pairs)  15.1 us
    ppermute x12, waiting for transfers between devices, swap(): return lax.ppermute(value, 'tok', pairs)  13.5 us
    ppermute x5, waiting for transfers between devices, lift(): return lax.ppermute(value, 'feat', [(i, i ^ m) for i in range(groups)])  7.67 us
    ppermute x5, starting transfers between devices, lift(): return lax.ppermute(value, 'feat', [(i, i ^ m) for i in range(groups)])  6.1 us
    pallas_call x2, Pallas kernels, columns(): pl.pallas_call(functools.partial(columns_kernel, groups), out_shape=jax.S...  5.2 us
    pallas_call x1, Pallas kernels, on_device(): pl.pallas_call(stage_kernel, out_shape=jax.ShapeDtypeStruct(dec_weight.sh...  2.37 us
    unnamed x10, local copies, waits for them, and re-layouts  2.21 us
    pallas_call x1, Pallas kernels, on_device(): pl.pallas_call(functools.partial(decode_kernel, groups), out_shape=[jax.S...  1.97 us
  transfers between devices with their start and end apart: 19, of which 13 were waited for; matrix products, arithmetic and copies ran while one was open for 1% of the time, Pallas kernels for 17%

profile of v9, /device:TPU:0, one launch (start us, length us, event | category | flops | bytes accessed | tf_op | source)
XLA Modules:
  0.0 59.6 jit_solution(3691189146845794112)
XLA Ops:
  1.2 1.3 %split.1 = (bf16[2,64,1024]{2,1,0:T(8,128)(2,1)S(1)}, bf16[2,64,1024]{2,1,0:T(8,128)(2,1)S(1)}, bf16[2,64,1024]{2,1,0:T(8,128)(2,1)S(1)}, bf16[2,64,1024]{2,1,0:T(8,128)(2,1)S(1)}) custom-call(bf16[64,8192]{1,0:T(8,128)(2,1)} %tok_ref.1, bf16[8192]{0:T(1024)(128)(2,1)} %bias_ref.1), custom_call_target="tpu_custom_call" | custom-call | bytes 2097152 | tf_op jit(solution)/shard_map/split/pallas_call | solution.py:234
  2.5 3.0 %collective-permute-start.1 = (bf16[2,64,1024]{2,1,0:T(8,128)(2,1)S(1)}, bf16[2,64,1024]{2,1,0:T(8,128)(2,1)S(1)}, u32[]{:S(2)}, u32[]{:S(2)}) collective-permute-start(bf16[2,64,1024]{2,1,0:T(8,128)(2,1)S(1)} %get-tuple-element.29), channel_id=1, source_target_pairs={{0,2},{1,3},{2,0},{3,1},{4,6},{5,7},{6,4},{7,5},{8,10},{9,11},{10,... | collective-permute-start | bytes 786440 | tf_op jit(solution)/shard_map/ppermute | solution.py:225
  5.5 1.5 %collective-permute-start.2 = (bf16[2,64,1024]{2,1,0:T(8,128)(2,1)S(1)}, bf16[2,64,1024]{2,1,0:T(8,128)(2,1)S(1)}, u32[]{:S(2)}, u32[]{:S(2)}) collective-permute-start(bf16[2,64,1024]{2,1,0:T(8,128)(2,1)S(1)} %get-tuple-element.30), channel_id=1, source_target_pairs={{0,4},{1,5},{2,6},{3,7},{4,0},{5,1},{6,2},{7,3},{8,12},{9,13},{10,... | collective-permute-start | bytes 786440 | tf_op jit(solution)/shard_map/ppermute | solution.py:225
  7.8 2.2 %copy-done.1 = bf16[1024,2048]{1,0:T(8,128)(2,1)S(1)} copy-done((bf16[1024,2048]{1,0:T(8,128)(2,1)S(1)}, bf16[1024,2048]{1,0:T(8,128)(2,1)}, u32[]{:S(2)}) %copy-start.1) | copy-done | bytes 4194328
  10.0 1.8 %columns.2.refs_0_ = bf16[4,1024,256]{2,1,0:T(8,128)(2,1)S(1)} custom-call(s32[8,4]{1,0:T(8,128)S(1)} %copy.11.ids_ref.refs_0_, bf16[1024,2048]{1,0:T(8,128)(2,1)S(1)} %copy-done.1), custom_call_target="tpu_custom_call" | custom-call | bytes 6291456 | tf_op jit(solution)/shard_map/columns/pallas_call | solution.py:251
  11.8 3.4 %columns.3.refs_1_ = bf16[4,1024,256]{2,1,0:T(8,128)(2,1)S(1)} custom-call(s32[8,4]{1,0:T(8,128)S(1)} %copy.11.ids_ref.refs_0_, bf16[1024,2048]{1,0:T(8,128)(2,1)} %collective-permute-done.w_ref), custom_call_target="tpu_custom_call" | custom-call | bytes 6291456 | tf_op jit(solution)/shard_map/columns/pallas_call | solution.py:251
  15.8 3.4 %collective-permute-done.2.refs_3_ = bf16[2,64,1024]{2,1,0:T(8,128)(2,1)S(1)} collective-permute-done((bf16[2,64,1024]{2,1,0:T(8,128)(2,1)S(1)}, bf16[2,64,1024]{2,1,0:T(8,128)(2,1)S(1)}, u32[]{:S(2)}, u32[]{:S(2)}) %collective-permute-start.2) | collective-permute-done | bytes 262176 | tf_op jit(solution)/shard_map/ppermute | solution.py:225
  19.7 1.3 %collective-permute-start.4 = (bf16[4,64,256]{2,1,0:T(8,128)(2,1)S(1)}, bf16[4,64,256]{2,1,0:T(8,128)(2,1)S(1)}, u32[]{:S(2)}, u32[]{:S(2)}) collective-permute-start(bf16[4,64,256]{2,1,0:T(8,128)(2,1)S(1)} %encode.3.refs_3_), channel_id=1, source_target_pairs={{0,2},{1,3},{2,0},{3,1},{4,6},{5,7},{6,4},{7,5},{8,10},{9,11},{10,... | collective-permute-start | bytes 393224 | tf_op jit(solution)/shard_map/ppermute | solution.py:225
  21.0 0.8 %collective-permute-start.5 = (bf16[4,64,256]{2,1,0:T(8,128)(2,1)S(1)}, bf16[4,64,256]{2,1,0:T(8,128)(2,1)S(1)}, u32[]{:S(2)}, u32[]{:S(2)}) collective-permute-start(bf16[4,64,256]{2,1,0:T(8,128)(2,1)S(1)} %encode.3.refs_3_), channel_id=1, source_target_pairs={{0,4},{1,5},{2,6},{3,7},{4,0},{5,1},{6,2},{7,3},{8,12},{9,13},{10,... | collective-permute-start | bytes 393224 | tf_op jit(solution)/shard_map/ppermute | solution.py:225
  21.8 1.4 %collective-permute-start.6 = (bf16[4,64,256]{2,1,0:T(8,128)(2,1)S(1)}, bf16[4,64,256]{2,1,0:T(8,128)(2,1)S(1)}, u32[]{:S(2)}, u32[]{:S(2)}) collective-permute-start(bf16[4,64,256]{2,1,0:T(8,128)(2,1)S(1)} %encode.3.refs_3_), channel_id=1, source_target_pairs={{0,6},{1,7},{2,4},{3,5},{4,2},{5,3},{6,0},{7,1},{8,14},{9,15},{10,... | collective-permute-start | bytes 393224 | tf_op jit(solution)/shard_map/ppermute | solution.py:225
  23.2 2.4 %stage.1.refs_8_ = bf16[2048,1024]{1,0:T(8,128)(2,1)S(1)} custom-call(bf16[2048,1024]{1,0:T(8,128)(2,1)} %collective-permute-done.7.src), custom_call_target="tpu_custom_call" | custom-call | bytes 8388608 | tf_op jit(solution)/shard_map/stage/pallas_call | solution.py:280
  25.8 2.4 %collective-permute-done.5.refs_5_ = bf16[4,64,256]{2,1,0:T(8,128)(2,1)S(1)} collective-permute-done((bf16[4,64,256]{2,1,0:T(8,128)(2,1)S(1)}, bf16[4,64,256]{2,1,0:T(8,128)(2,1)S(1)}, u32[]{:S(2)}, u32[]{:S(2)}) %collective-permute-start.5) | collective-permute-done | bytes 131104 | tf_op jit(solution)/shard_map/ppermute | solution.py:225
  28.2 2.0 %decode.1 = (bf16[64,256]{1,0:T(8,128)(2,1)}, bf16[2,32,1024]{2,1,0:T(8,128)(2,1)S(1)}, bf16[2,32,1024]{2,1,0:T(8,128)(2,1)S(1)}, bf16[2,32,1024]{2,1,0:T(8,128)...) custom-call(s32[8,4]{1,0:T(8,128)S(1)} %copy.11.ids_ref.refs_0_, ...), custom_call_target="tpu_custom_call" | custom-call | flops 268435456 | bytes 4194304 | tf_op jit(solution)/shard_map/decode/pallas_call | solution.py:295
  30.1 1.6 %collective-permute-start.8 = (bf16[4,2,16,1024]{3,2,1,0:T(8,128)(2,1)S(1)}, bf16[4,2,16,1024]{3,2,1,0:T(8,128)(2,1)S(1)}, u32[]{:S(2)}, u32[]{:S(2)}) collective-permute-start(bf16[4,2,16,1024]{3,2,1,0:T(8,128)(2,1)S(1)} %get-tuple-element.35), channel_id=1, source_target_pairs={{0,8},{8,0},{16,24},{24,16},{1,9},{9,1},{17,25},{25,17},{2,10},{10... | collective-permute-start | bytes 786440 | tf_op jit(solution)/shard_map/ppermute | solution.py:228
  31.7 1.3 %collective-permute-start.10 = (bf16[2,32,1024]{2,1,0:T(8,128)(2,1)S(1)}, bf16[2,32,1024]{2,1,0:T(8,128)(2,1)S(1)}, u32[]{:S(2)}, u32[]{:S(2)}) collective-permute-start(bf16[2,32,1024]{2,1,0:T(8,128)(2,1)S(1)} %get-tuple-element.42), channel_id=1, source_target_pairs={{0,4},{1,5},{2,6},{3,7},{4,0},{5,1},{6,2},{7,3},{8,12},{9,13},{10,... | collective-permute-start | bytes 393224 | tf_op jit(solution)/shard_map/ppermute | solution.py:225
  33.0 1.2 %collective-permute-start.11 = (bf16[2,32,1024]{2,1,0:T(8,128)(2,1)S(1)}, bf16[2,32,1024]{2,1,0:T(8,128)(2,1)S(1)}, u32[]{:S(2)}, u32[]{:S(2)}) collective-permute-start(bf16[2,32,1024]{2,1,0:T(8,128)(2,1)S(1)} %get-tuple-element.43), channel_id=1, source_target_pairs={{0,6},{1,7},{2,4},{3,5},{4,2},{5,3},{6,0},{7,1},{8,14},{9,15},{10,... | collective-permute-start | bytes 393224 | tf_op jit(solution)/shard_map/ppermute | solution.py:225
  34.2 1.0 %collective-permute-start.9 = (bf16[2,32,1024]{2,1,0:T(8,128)(2,1)S(1)}, bf16[2,32,1024]{2,1,0:T(8,128)(2,1)S(1)}, u32[]{:S(2)}, u32[]{:S(2)}) collective-permute-start(bf16[2,32,1024]{2,1,0:T(8,128)(2,1)S(1)} %get-tuple-element.41), channel_id=1, source_target_pairs={{0,2},{1,3},{2,0},{3,1},{4,6},{5,7},{6,4},{7,5},{8,10},{9,11},{10,... | collective-permute-start | bytes 393224 | tf_op jit(solution)/shard_map/ppermute | solution.py:225
  35.2 1.3 %collective-permute-done.8.came_ref = bf16[4,2,16,1024]{3,2,1,0:T(8,128)(2,1)S(1)} collective-permute-done((bf16[4,2,16,1024]{3,2,1,0:T(8,128)(2,1)S(1)}, bf16[4,2,16,1024]{3,2,1,0:T(8,128)(2,1)S(1)}, u32[]{:S(2)}, u32[]{:S(2)}) %collective-permute-start.8) | collective-permute-done | bytes 262176 | tf_op jit(solution)/shard_map/ppermute | solution.py:228
  37.0 1.8 %collective-permute-done.11.refs_3_ = bf16[2,32,1024]{2,1,0:T(8,128)(2,1)S(1)} collective-permute-done((bf16[2,32,1024]{2,1,0:T(8,128)(2,1)S(1)}, bf16[2,32,1024]{2,1,0:T(8,128)(2,1)S(1)}, u32[]{:S(2)}, u32[]{:S(2)}) %collective-permute-start.11) | collective-permute-done | bytes 131104 | tf_op jit(solution)/shard_map/ppermute | solution.py:225
  38.9 1.3 %collective-permute-done.9.refs_1_ = bf16[2,32,1024]{2,1,0:T(8,128)(2,1)S(1)} collective-permute-done((bf16[2,32,1024]{2,1,0:T(8,128)(2,1)S(1)}, bf16[2,32,1024]{2,1,0:T(8,128)(2,1)S(1)}, u32[]{:S(2)}, u32[]{:S(2)}) %collective-permute-start.9) | collective-permute-done | bytes 131104 | tf_op jit(solution)/shard_map/ppermute | solution.py:225
  40.3 1.3 %collective-permute-start.13 = (bf16[2,16,1024]{2,1,0:T(8,128)(2,1)S(1)}, bf16[2,16,1024]{2,1,0:T(8,128)(2,1)S(1)}, u32[]{:S(2)}, u32[]{:S(2)}) collective-permute-start(bf16[2,16,1024]{2,1,0:T(8,128)(2,1)S(1)} %get-tuple-element.47), channel_id=1, source_target_pairs={{0,2},{1,3},{2,0},{3,1},{4,6},{5,7},{6,4},{7,5},{8,10},{9,11},{10,... | collective-permute-start | bytes 196616 | tf_op jit(solution)/shard_map/ppermute | solution.py:225
  41.5 1.1 %collective-permute-start.14 = (bf16[2,16,1024]{2,1,0:T(8,128)(2,1)S(1)}, bf16[2,16,1024]{2,1,0:T(8,128)(2,1)S(1)}, u32[]{:S(2)}, u32[]{:S(2)}) collective-permute-start(bf16[2,16,1024]{2,1,0:T(8,128)(2,1)S(1)} %get-tuple-element.48), channel_id=1, source_target_pairs={{0,4},{1,5},{2,6},{3,7},{4,0},{5,1},{6,2},{7,3},{8,12},{9,13},{10,... | collective-permute-start | bytes 196616 | tf_op jit(solution)/shard_map/ppermute | solution.py:225
  42.7 1.2 %collective-permute-start.15 = (bf16[2,16,1024]{2,1,0:T(8,128)(2,1)S(1)}, bf16[2,16,1024]{2,1,0:T(8,128)(2,1)S(1)}, u32[]{:S(2)}, u32[]{:S(2)}) collective-permute-start(bf16[2,16,1024]{2,1,0:T(8,128)(2,1)S(1)} %get-tuple-element.49), channel_id=1, source_target_pairs={{0,6},{1,7},{2,4},{3,5},{4,2},{5,3},{6,0},{7,1},{8,14},{9,15},{10,... | collective-permute-start | bytes 196616 | tf_op jit(solution)/shard_map/ppermute | solution.py:225
  44.6 1.2 %collective-permute-done.14.refs_2_ = bf16[2,16,1024]{2,1,0:T(8,128)(2,1)S(1)} collective-permute-done((bf16[2,16,1024]{2,1,0:T(8,128)(2,1)S(1)}, bf16[2,16,1024]{2,1,0:T(8,128)(2,1)S(1)}, u32[]{:S(2)}, u32[]{:S(2)}) %collective-permute-start.14) | collective-permute-done | bytes 65568 | tf_op jit(solution)/shard_map/ppermute | solution.py:225
  45.8 2.0 %collective-permute-done.15.refs_3_ = bf16[2,16,1024]{2,1,0:T(8,128)(2,1)S(1)} collective-permute-done((bf16[2,16,1024]{2,1,0:T(8,128)(2,1)S(1)}, bf16[2,16,1024]{2,1,0:T(8,128)(2,1)S(1)}, u32[]{:S(2)}, u32[]{:S(2)}) %collective-permute-start.15) | collective-permute-done | bytes 65568 | tf_op jit(solution)/shard_map/ppermute | solution.py:225
  47.9 1.6 %collective-permute-done.12.refs_1_ = bf16[2,2,32,1024]{3,2,1,0:T(8,128)(2,1)S(1)} collective-permute-done((bf16[2,2,32,1024]{3,2,1,0:T(8,128)(2,1)S(1)}, bf16[2,2,32,1024]{3,2,1,0:T(8,128)(2,1)S(1)}, u32[]{:S(2)}, u32[]{:S(2)}) %collective-permute-start.12) | collective-permute-done | bytes 262176 | tf_op jit(solution)/shard_map/ppermute | solution.py:228
  49.5 2.0 %collective-permute-start.16 = (bf16[2,48,1024]{2,1,0:T(8,128)(2,1)S(1)}, bf16[2,48,1024]{2,1,0:T(8,128)(2,1)S(1)}, u32[]{:S(2)}, u32[]{:S(2)}) collective-permute-start(bf16[2,48,1024]{2,1,0:T(8,128)(2,1)S(1)} %add.1), channel_id=1, source_target_pairs={{0,16},{8,24},{16,0},{24,8},{1,17},{9,25},{17,1},{25,9},{2,18},{10... | collective-permute-start | bytes 589832 | tf_op jit(solution)/shard_map/ppermute | solution.py:228
  51.5 1.1 %collective-permute-start.17 = (bf16[2,16,1024]{2,1,0:T(8,128)(2,1)S(1)}, bf16[2,16,1024]{2,1,0:T(8,128)(2,1)S(1)}, u32[]{:S(2)}, u32[]{:S(2)}) collective-permute-start(bf16[2,16,1024]{2,1,0:T(8,128)(2,1)S(1)} %get-tuple-element.52), channel_id=1, source_target_pairs={{0,8},{8,0},{16,24},{24,16},{1,9},{9,1},{17,25},{25,17},{2,10},{10... | collective-permute-start | bytes 196616 | tf_op jit(solution)/shard_map/ppermute | solution.py:228
  52.6 1.4 %collective-permute-start.18 = (bf16[2,16,1024]{2,1,0:T(8,128)(2,1)S(1)}, bf16[2,16,1024]{2,1,0:T(8,128)(2,1)S(1)}, u32[]{:S(2)}, u32[]{:S(2)}) collective-permute-start(bf16[2,16,1024]{2,1,0:T(8,128)(2,1)S(1)} %get-tuple-element.53), channel_id=1, source_target_pairs={{0,24},{8,16},{16,8},{24,0},{1,25},{9,17},{17,9},{25,1},{2,26},{10... | collective-permute-start | bytes 196616 | tf_op jit(solution)/shard_map/ppermute | solution.py:228
  53.9 1.8 %collective-permute-done.17.refs_4_ = bf16[2,16,1024]{2,1,0:T(8,128)(2,1)S(1)} collective-permute-done((bf16[2,16,1024]{2,1,0:T(8,128)(2,1)S(1)}, bf16[2,16,1024]{2,1,0:T(8,128)(2,1)S(1)}, u32[]{:S(2)}, u32[]{:S(2)}) %collective-permute-start.17) | collective-permute-done | bytes 65568 | tf_op jit(solution)/shard_map/ppermute | solution.py:228
  55.7 3.0 %collective-permute-done.18.refs_5_ = bf16[2,16,1024]{2,1,0:T(8,128)(2,1)S(1)} collective-permute-done((bf16[2,16,1024]{2,1,0:T(8,128)(2,1)S(1)}, bf16[2,16,1024]{2,1,0:T(8,128)(2,1)S(1)}, u32[]{:S(2)}, u32[]{:S(2)}) %collective-permute-start.18) | collective-permute-done | bytes 65568 | tf_op jit(solution)/shard_map/ppermute | solution.py:228
  58.8 0.8 %finish.1 = bf16[64,2048]{1,0:T(8,128)(2,1)} custom-call(bf16[2,2,32,1024]{3,2,1,0:T(8,128)(2,1)S(1)} %get-tuple-element.44.refs_0_, bf16[2,2,32,1024]{3,2,1,0:T(8,128)(2,1)S(1)} %collective-permute-done.12.refs_1_, bf16[2,16,1024]{2,1,0:T(8,128)(2,1)S(1)} %get-tuple-element.50.refs_2_, bf16[2,48,1024]{2,1,0:T(8,128)(2,1)S(1)} %collective-permute-done.16.refs_3_, ...), custom_call_target="tpu_custom_call" | custom-call | bytes 1310720 | tf_op jit(solution)/shard_map/finish/pallas_call | solution.py:357
  (31 shorter events, 4.1 us)
Async XLA Ops:
  0.6 11.2 %collective-permute-start = (bf16[1024,2048]{1,0:T(8,128)(2,1)}, bf16[1024,2048]{1,0:T(8,128)(2,1)}, u32[]{:S(2)}, u32[]{:S(2)}) collective-permute-start(bf16[1024,2048]{1,0:T(8,128)(2,1)} %w_ref.1), channel_id=1, source_target_pairs={{0,1},{1,0},{2,3},{3,2},{4,5},{5,4},{6,7},{7,6},{8,9},{9,8},{10,11... | collective-permute-start | bytes 12582920 | tf_op jit(solution)/shard_map/ppermute | solution.py:231
  1.1 22.1 %collective-permute-start.7 = (bf16[2048,1024]{1,0:T(8,128)(2,1)}, bf16[2048,1024]{1,0:T(8,128)(2,1)}, u32[]{:S(2)}, u32[]{:S(2)}) collective-permute-start(bf16[2048,1024]{1,0:T(8,128)(2,1)} %refs_7_.1), channel_id=1, source_target_pairs={{0,1},{1,0},{2,3},{3,2},{4,5},{5,4},{6,7},{7,6},{8,9},{9,8},{10,11... | collective-permute-start | bytes 12582920 | tf_op jit(solution)/shard_map/ppermute | solution.py:232
  2.5 12.7 %collective-permute-start.1 = (bf16[2,64,1024]{2,1,0:T(8,128)(2,1)S(1)}, bf16[2,64,1024]{2,1,0:T(8,128)(2,1)S(1)}, u32[]{:S(2)}, u32[]{:S(2)}) collective-permute-start(bf16[2,64,1024]{2,1,0:T(8,128)(2,1)S(1)} %get-tuple-element.29), channel_id=1, source_target_pairs={{0,2},{1,3},{2,0},{3,1},{4,6},{5,7},{6,4},{7,5},{8,10},{9,11},{10,... | collective-permute-start | bytes 786440 | tf_op jit(solution)/shard_map/ppermute | solution.py:225
  5.5 13.6 %collective-permute-start.2 = (bf16[2,64,1024]{2,1,0:T(8,128)(2,1)S(1)}, bf16[2,64,1024]{2,1,0:T(8,128)(2,1)S(1)}, u32[]{:S(2)}, u32[]{:S(2)}) collective-permute-start(bf16[2,64,1024]{2,1,0:T(8,128)(2,1)S(1)} %get-tuple-element.30), channel_id=1, source_target_pairs={{0,4},{1,5},{2,6},{3,7},{4,0},{5,1},{6,2},{7,3},{8,12},{9,13},{10,... | collective-permute-start | bytes 786440 | tf_op jit(solution)/shard_map/ppermute | solution.py:225
  7.1 12.1 %collective-permute-start.3 = (bf16[2,64,1024]{2,1,0:T(8,128)(2,1)S(1)}, bf16[2,64,1024]{2,1,0:T(8,128)(2,1)S(1)}, u32[]{:S(2)}, u32[]{:S(2)}) collective-permute-start(bf16[2,64,1024]{2,1,0:T(8,128)(2,1)S(1)} %get-tuple-element.31), channel_id=1, source_target_pairs={{0,6},{1,7},{2,4},{3,5},{4,2},{5,3},{6,0},{7,1},{8,14},{9,15},{10,... | collective-permute-start | bytes 786440 | tf_op jit(solution)/shard_map/ppermute | solution.py:225
  7.8 2.2 %copy-start.1 = (bf16[1024,2048]{1,0:T(8,128)(2,1)S(1)}, bf16[1024,2048]{1,0:T(8,128)(2,1)}, u32[]{:S(2)}) copy-start(bf16[1024,2048]{1,0:T(8,128)(2,1)} %w_ref.1) | copy-start | bytes 12582916
  15.2 8.0 %copy-start.4 = (bf16[2048]{0:T(1024)(128)(2,1)S(1)}, bf16[2048]{0:T(1024)(128)(2,1)}, u32[]{:S(2)}) copy-start(bf16[2048]{0:T(1024)(128)(2,1)} %param.10) | copy-start | bytes 12292
  19.7 6.1 %collective-permute-start.4 = (bf16[4,64,256]{2,1,0:T(8,128)(2,1)S(1)}, bf16[4,64,256]{2,1,0:T(8,128)(2,1)S(1)}, u32[]{:S(2)}, u32[]{:S(2)}) collective-permute-start(bf16[4,64,256]{2,1,0:T(8,128)(2,1)S(1)} %encode.3.refs_3_), channel_id=1, source_target_pairs={{0,2},{1,3},{2,0},{3,1},{4,6},{5,7},{6,4},{7,5},{8,10},{9,11},{10,... | collective-permute-start | bytes 393224 | tf_op jit(solution)/shard_map/ppermute | solution.py:225
  21.0 7.2 %collective-permute-start.5 = (bf16[4,64,256]{2,1,0:T(8,128)(2,1)S(1)}, bf16[4,64,256]{2,1,0:T(8,128)(2,1)S(1)}, u32[]{:S(2)}, u32[]{:S(2)}) collective-permute-start(bf16[4,64,256]{2,1,0:T(8,128)(2,1)S(1)} %encode.3.refs_3_), channel_id=1, source_target_pairs={{0,4},{1,5},{2,6},{3,7},{4,0},{5,1},{6,2},{7,3},{8,12},{9,13},{10,... | collective-permute-start | bytes 393224 | tf_op jit(solution)/shard_map/ppermute | solution.py:225
  21.8 6.4 %collective-permute-start.6 = (bf16[4,64,256]{2,1,0:T(8,128)(2,1)S(1)}, bf16[4,64,256]{2,1,0:T(8,128)(2,1)S(1)}, u32[]{:S(2)}, u32[]{:S(2)}) collective-permute-start(bf16[4,64,256]{2,1,0:T(8,128)(2,1)S(1)} %encode.3.refs_3_), channel_id=1, source_target_pairs={{0,6},{1,7},{2,4},{3,5},{4,2},{5,3},{6,0},{7,1},{8,14},{9,15},{10,... | collective-permute-start | bytes 393224 | tf_op jit(solution)/shard_map/ppermute | solution.py:225
  23.2 4.9 %copy-start = (bf16[2048,1024]{1,0:T(8,128)(2,1)S(1)}, bf16[2048,1024]{1,0:T(8,128)(2,1)}, u32[]{:S(2)}) copy-start(bf16[2048,1024]{1,0:T(8,128)(2,1)} %refs_7_.1) | copy-start | bytes 12582916
  23.2 4.9 %copy-start.2 = (s32[8,1]{0,1:T(1,128)S(1)}, s32[8,1]{0,1:T(1,128)}, u32[]{:S(2)}) copy-start(s32[8,1]{0,1:T(1,128)} %param.13) | copy-start | bytes 100
  28.1 25.8 %copy-start.3 = (bf16[8192]{0:T(1024)(128)(2,1)S(1)}, bf16[8192]{0:T(1024)(128)(2,1)}, u32[]{:S(2)}) copy-start(bf16[8192]{0:T(1024)(128)(2,1)} %bias_ref.1) | copy-start | bytes 49156
  30.1 6.4 %collective-permute-start.8 = (bf16[4,2,16,1024]{3,2,1,0:T(8,128)(2,1)S(1)}, bf16[4,2,16,1024]{3,2,1,0:T(8,128)(2,1)S(1)}, u32[]{:S(2)}, u32[]{:S(2)}) collective-permute-start(bf16[4,2,16,1024]{3,2,1,0:T(8,128)(2,1)S(1)} %get-tuple-element.35), channel_id=1, source_target_pairs={{0,8},{8,0},{16,24},{24,16},{1,9},{9,1},{17,25},{25,17},{2,10},{10... | collective-permute-start | bytes 786440 | tf_op jit(solution)/shard_map/ppermute | solution.py:228
  31.7 5.3 %collective-permute-start.10 = (bf16[2,32,1024]{2,1,0:T(8,128)(2,1)S(1)}, bf16[2,32,1024]{2,1,0:T(8,128)(2,1)S(1)}, u32[]{:S(2)}, u32[]{:S(2)}) collective-permute-start(bf16[2,32,1024]{2,1,0:T(8,128)(2,1)S(1)} %get-tuple-element.42), channel_id=1, source_target_pairs={{0,4},{1,5},{2,6},{3,7},{4,0},{5,1},{6,2},{7,3},{8,12},{9,13},{10,... | collective-permute-start | bytes 393224 | tf_op jit(solution)/shard_map/ppermute | solution.py:225
  33.0 5.9 %collective-permute-start.11 = (bf16[2,32,1024]{2,1,0:T(8,128)(2,1)S(1)}, bf16[2,32,1024]{2,1,0:T(8,128)(2,1)S(1)}, u32[]{:S(2)}, u32[]{:S(2)}) collective-permute-start(bf16[2,32,1024]{2,1,0:T(8,128)(2,1)S(1)} %get-tuple-element.43), channel_id=1, source_target_pairs={{0,6},{1,7},{2,4},{3,5},{4,2},{5,3},{6,0},{7,1},{8,14},{9,15},{10,... | collective-permute-start | bytes 393224 | tf_op jit(solution)/shard_map/ppermute | solution.py:225
  34.2 6.0 %collective-permute-start.9 = (bf16[2,32,1024]{2,1,0:T(8,128)(2,1)S(1)}, bf16[2,32,1024]{2,1,0:T(8,128)(2,1)S(1)}, u32[]{:S(2)}, u32[]{:S(2)}) collective-permute-start(bf16[2,32,1024]{2,1,0:T(8,128)(2,1)S(1)} %get-tuple-element.41), channel_id=1, source_target_pairs={{0,2},{1,3},{2,0},{3,1},{4,6},{5,7},{6,4},{7,5},{8,10},{9,11},{10,... | collective-permute-start | bytes 393224 | tf_op jit(solution)/shard_map/ppermute | solution.py:225
  40.2 9.2 %collective-permute-start.12 = (bf16[2,2,32,1024]{3,2,1,0:T(8,128)(2,1)S(1)}, bf16[2,2,32,1024]{3,2,1,0:T(8,128)(2,1)S(1)}, u32[]{:S(2)}, u32[]{:S(2)}) collective-permute-start(bf16[2,2,32,1024]{3,2,1,0:T(8,128)(2,1)S(1)} %get-tuple-element.45), channel_id=1, source_target_pairs={{0,8},{8,0},{16,24},{24,16},{1,9},{9,1},{17,25},{25,17},{2,10},{10... | collective-permute-start | bytes 786440 | tf_op jit(solution)/shard_map/ppermute | solution.py:228
  40.3 4.3 %collective-permute-start.13 = (bf16[2,16,1024]{2,1,0:T(8,128)(2,1)S(1)}, bf16[2,16,1024]{2,1,0:T(8,128)(2,1)S(1)}, u32[]{:S(2)}, u32[]{:S(2)}) collective-permute-start(bf16[2,16,1024]{2,1,0:T(8,128)(2,1)S(1)} %get-tuple-element.47), channel_id=1, source_target_pairs={{0,2},{1,3},{2,0},{3,1},{4,6},{5,7},{6,4},{7,5},{8,10},{9,11},{10,... | collective-permute-start | bytes 196616 | tf_op jit(solution)/shard_map/ppermute | solution.py:225
  41.5 4.3 %collective-permute-start.14 = (bf16[2,16,1024]{2,1,0:T(8,128)(2,1)S(1)}, bf16[2,16,1024]{2,1,0:T(8,128)(2,1)S(1)}, u32[]{:S(2)}, u32[]{:S(2)}) collective-permute-start(bf16[2,16,1024]{2,1,0:T(8,128)(2,1)S(1)} %get-tuple-element.48), channel_id=1, source_target_pairs={{0,4},{1,5},{2,6},{3,7},{4,0},{5,1},{6,2},{7,3},{8,12},{9,13},{10,... | collective-permute-start | bytes 196616 | tf_op jit(solution)/shard_map/ppermute | solution.py:225
  42.7 5.2 %collective-permute-start.15 = (bf16[2,16,1024]{2,1,0:T(8,128)(2,1)S(1)}, bf16[2,16,1024]{2,1,0:T(8,128)(2,1)S(1)}, u32[]{:S(2)}, u32[]{:S(2)}) collective-permute-start(bf16[2,16,1024]{2,1,0:T(8,128)(2,1)S(1)} %get-tuple-element.49), channel_id=1, source_target_pairs={{0,6},{1,7},{2,4},{3,5},{4,2},{5,3},{6,0},{7,1},{8,14},{9,15},{10,... | collective-permute-start | bytes 196616 | tf_op jit(solution)/shard_map/ppermute | solution.py:225
  49.5 9.3 %collective-permute-start.16 = (bf16[2,48,1024]{2,1,0:T(8,128)(2,1)S(1)}, bf16[2,48,1024]{2,1,0:T(8,128)(2,1)S(1)}, u32[]{:S(2)}, u32[]{:S(2)}) collective-permute-start(bf16[2,48,1024]{2,1,0:T(8,128)(2,1)S(1)} %add.1), channel_id=1, source_target_pairs={{0,16},{8,24},{16,0},{24,8},{1,17},{9,25},{17,1},{25,9},{2,18},{10... | collective-permute-start | bytes 589832 | tf_op jit(solution)/shard_map/ppermute | solution.py:228
  51.5 4.3 %collective-permute-start.17 = (bf16[2,16,1024]{2,1,0:T(8,128)(2,1)S(1)}, bf16[2,16,1024]{2,1,0:T(8,128)(2,1)S(1)}, u32[]{:S(2)}, u32[]{:S(2)}) collective-permute-start(bf16[2,16,1024]{2,1,0:T(8,128)(2,1)S(1)} %get-tuple-element.52), channel_id=1, source_target_pairs={{0,8},{8,0},{16,24},{24,16},{1,9},{9,1},{17,25},{25,17},{2,10},{10... | collective-permute-start | bytes 196616 | tf_op jit(solution)/shard_map/ppermute | solution.py:228
  52.6 6.2 %collective-permute-start.18 = (bf16[2,16,1024]{2,1,0:T(8,128)(2,1)S(1)}, bf16[2,16,1024]{2,1,0:T(8,128)(2,1)S(1)}, u32[]{:S(2)}, u32[]{:S(2)}) collective-permute-start(bf16[2,16,1024]{2,1,0:T(8,128)(2,1)S(1)} %get-tuple-element.53), channel_id=1, source_target_pairs={{0,24},{8,16},{16,8},{24,0},{1,25},{9,17},{17,9},{25,1},{2,26},{10... | collective-permute-start | bytes 196616 | tf_op jit(solution)/shard_map/ppermute | solution.py:228
